TPU v7x, 32 devices: a whole 2x2x4 slice. The times are simulated.
32 devices in a mesh: row: 4 (over z), col: 8 (over y, x, core).
Axes of the slice: x: 2, y: 2, z: 4, core: 2. Of those that a mesh axis runs over, the one named last changes fastest.
Arguments:
- gaussian_sketch: bfloat16 [16384, 256], P(('col', 'row')), may hold values from -6 to 6
- block_values: bfloat16 [8192, 128, 128], P(('row', 'col')), may hold values from -6 to 6
- block_rows: int32 [8192], P(('row', 'col')), may hold values from 0 to 127, as said below
- block_columns: int32 [8192], P(('row', 'col')), may hold values from 0 to 127, as said below
Outputs:
- range_basis: float32 [16384, 256], P(('row', 'col'))
- upper_factor: float32 [256, 256], replicated
Inputs may be any that keep to these rules, and one draw needn't show every extreme that they name: `block_rows`: entry k * 256 + m, k = i * 8 + j, names a block row in [i * 32, (i + 1) * 32); no (row, column) pair is named twice. `block_columns`: entry k * 256 + m, k = i * 8 + j, names a block column in [j * 16, (j + 1) * 16).
All inputs are finite; a program needn't handle non-finite values.
Results may differ from a plain program's by a relative error of at most 0.0003.
Values may be sent and summed in bfloat16 or wider, within the bound.
No kernel may reach another device: no remote copies, remote signals or barrier semaphores. Data moves between devices by JAX's collectives and lax.ppermute only.
A program may use at most 128 MiB of HBM per device.

v0:
```python
import math

import jax
import jax.numpy as jnp
from jax import lax
from jax.sharding import PartitionSpec as P

PANEL = 128


def upper_parts(gram):
    lower_factor = jnp.linalg.cholesky(gram)
    identity = jnp.eye(gram.shape[0], dtype=gram.dtype)
    inverse = lax.linalg.triangular_solve(lower_factor, identity, left_side=True, lower=True)
    return (lower_factor.T, inverse.T)


def tile_product(sketch_blocks, block_values, local_rows, local_cols, tile_rows):
    group_size = math.gcd(block_values.shape[0], 64)
    col_width = sketch_blocks.shape[2]

    def advance(counter, summed):
        offset = (counter * group_size).astype(jnp.int32)
        values = lax.dynamic_slice_in_dim(block_values, offset, group_size, 0)
        row_ids = lax.dynamic_slice_in_dim(local_rows, offset, group_size, 0)
        col_ids = lax.dynamic_slice_in_dim(local_cols, offset, group_size, 0)
        picked = jnp.take(sketch_blocks, col_ids, axis=0)
        product = jnp.einsum("gab,gbs->gas", values, picked, preferred_element_type=jnp.float32)
        return summed.at[row_ids].add(product)

    initial = jnp.zeros((tile_rows, block_values.shape[1], col_width), jnp.float32)
    summed = lax.fori_loop(0, block_values.shape[0] // group_size, advance, initial)
    return summed.reshape(tile_rows * block_values.shape[1], col_width)


def on_device(gaussian_sketch, block_values, block_rows, block_columns):
    high = lax.Precision.HIGHEST
    size_row = lax.axis_size("row")
    size_col = lax.axis_size("col")
    shard_rows = gaussian_sketch.shape[0]
    block_size = block_values.shape[1]
    grid_rows = shard_rows * size_col // block_size
    grid_cols = shard_rows * size_row // block_size
    local_rows = block_rows - lax.axis_index("row") * grid_rows
    local_cols = block_columns - lax.axis_index("col") * grid_cols
    gathered = lax.all_gather(gaussian_sketch, "row", axis=0, tiled=True)
    sketch_blocks = gathered.reshape(grid_cols, block_size, gathered.shape[1])
    partial_value = tile_product(sketch_blocks, block_values, local_rows, local_cols, grid_rows)
    sketched = lax.psum_scatter(partial_value, "col", scatter_dimension=0, tiled=True)
    first_part = sketched[:, :PANEL]
    second_part = sketched[:, PANEL:]
    order_total = shard_rows * size_row * size_col
    gram_one = (
        lax.psum(jnp.dot(first_part.T, first_part, precision=high), ("row", "col")) / order_total
    )
    upper_one, inverse_one = upper_parts(gram_one)
    basis_one = jnp.dot(first_part, inverse_one, precision=high)
    coupling = (
        lax.psum(jnp.dot(basis_one.T, second_part, precision=high), ("row", "col")) / order_total
    )
    remainder = second_part - jnp.dot(basis_one, coupling, precision=high)
    gram_two = (
        lax.psum(jnp.dot(remainder.T, remainder, precision=high), ("row", "col")) / order_total
    )
    upper_two, inverse_two = upper_parts(gram_two)
    basis_two = jnp.dot(remainder, inverse_two, precision=high)
    range_basis = jnp.concatenate([basis_one, basis_two], axis=1)
    top_rows = jnp.concatenate([upper_one, coupling], axis=1)
    bottom_rows = jnp.concatenate([jnp.zeros_like(upper_two), upper_two], axis=1)
    upper_factor = jnp.concatenate([top_rows, bottom_rows], axis=0)
    return (range_basis, upper_factor)


def solution(mesh):
    return jax.shard_map(
        on_device,
        mesh=mesh,
        in_specs=(
            P(("col", "row"), None),
            P(("row", "col"), None, None),
            P(("row", "col")),
            P(("row", "col")),
        ),
        out_specs=(P(("row", "col"), None), P()),
        check_vma=False,
    )
```

profile of v0, /device:TPU:0, one launch (start us, length us, event | category | flops | bytes accessed | tf_op | source)
XLA Modules:
  0.0 643.1 jit_solution(3256187784970648376)
XLA Ops:
  8.7 31.6 %all-gather.2.cloned.1.call-done = bf16[2048,256]{1,0:T(8,128)(2,1)} async-done(((bf16[512,256]{1,0:T(8,128)(2,1)}), bf16[2048,256]{1,0:T(8,128)(2,1)}) %all-gather.2.cloned.1.call-update) | async-done | bytes 1048592 | tf_op jit(solution)/shard_map/all_gather | solution.py:46
  40.2 2.5 broadcast_in_dim.36
  42.7 118.3 %while.13 = (s32[]{:T(128)}, f32[32,128,256]{2,1,0:T(8,128)}, s32[256]{0:T(256)S(1)}, bf16[256,128,128]{2,1,0:T(8,128)(2,1)}, s32[256]{0:T(256)S(1)}, /*index=5*...) while((s32[]{:T(128)}, f32[32,128,256]{2,1,0:T(8,128)}, s32[256]{0:T(256)S(1)}, ...), condition=%wide.region_2.3_spmd, body=%wide.region_0.2_spmd.sunk | while | flops 541066816 | bytes 48240672 | solution.py:32
  42.8 2.8 gather_fusion
  45.6 7.4 %fusion.38 = f32[64,128,256]{2,1,0:T(8,128)} fusion(bf16[64,128,256]{2,1,0:T(8,128)(2,1)} %gather_fusion, pred[64]{0:T(512)(128)(4,1)S(1)} %get-tuple-element.176, bf16[256,128,128]{2,1,0:T(8,128)(2,1)} %get-tuple-element.200, s32[]{:T(128)S(6)} %select_n.59), kind=kOutput, calls=%fused_computation.2.clone.1 | convolution fusion | flops 538968064 | bytes 14680132 | tf_op jit(solution)/shard_map/while/body/eval_jaxpr/gab,gbs->gas/dot_general | solution.py:28
  53.0 19.5 %scatter_fusion = f32[32,128,256]{2,1,0:T(8,128)} fusion(f32[32,128,256]{2,1,0:T(8,128)} %get-tuple-element.188, s32[64]{0:T(128)S(1)} %compare_select_fusion.4, f32[64,128,256]{2,1,0:T(8,128)} %fusion.38), kind=kCustom, calls=%fused_computation.1.clone.1 | custom fusion | flops 2097152 | bytes 25166080 | tf_op jit(solution)/shard_map/while/body/eval_jaxpr/scatter-add | solution.py:29
  72.6 2.8 gather_fusion
  75.4 7.4 %fusion.38 = f32[64,128,256]{2,1,0:T(8,128)} fusion(bf16[64,128,256]{2,1,0:T(8,128)(2,1)} %gather_fusion, pred[64]{0:T(512)(128)(4,1)S(1)} %get-tuple-element.176, bf16[256,128,128]{2,1,0:T(8,128)(2,1)} %get-tuple-element.200, s32[]{:T(128)S(6)} %select_n.59), kind=kOutput, calls=%fused_computation.2.clone.1 | convolution fusion | flops 538968064 | bytes 14680132 | tf_op jit(solution)/shard_map/while/body/eval_jaxpr/gab,gbs->gas/dot_general | solution.py:28
  82.9 19.2 %scatter_fusion = f32[32,128,256]{2,1,0:T(8,128)} fusion(f32[32,128,256]{2,1,0:T(8,128)} %get-tuple-element.188, s32[64]{0:T(128)S(1)} %compare_select_fusion.4, f32[64,128,256]{2,1,0:T(8,128)} %fusion.38), kind=kCustom, calls=%fused_computation.1.clone.1 | custom fusion | flops 2097152 | bytes 25166080 | tf_op jit(solution)/shard_map/while/body/eval_jaxpr/scatter-add | solution.py:29
  102.1 2.8 gather_fusion
  104.9 7.4 %fusion.38 = f32[64,128,256]{2,1,0:T(8,128)} fusion(bf16[64,128,256]{2,1,0:T(8,128)(2,1)} %gather_fusion, pred[64]{0:T(512)(128)(4,1)S(1)} %get-tuple-element.176, bf16[256,128,128]{2,1,0:T(8,128)(2,1)} %get-tuple-element.200, s32[]{:T(128)S(6)} %select_n.59), kind=kOutput, calls=%fused_computation.2.clone.1 | convolution fusion | flops 538968064 | bytes 14680132 | tf_op jit(solution)/shard_map/while/body/eval_jaxpr/gab,gbs->gas/dot_general | solution.py:28
  112.3 19.2 %scatter_fusion = f32[32,128,256]{2,1,0:T(8,128)} fusion(f32[32,128,256]{2,1,0:T(8,128)} %get-tuple-element.188, s32[64]{0:T(128)S(1)} %compare_select_fusion.4, f32[64,128,256]{2,1,0:T(8,128)} %fusion.38), kind=kCustom, calls=%fused_computation.1.clone.1 | custom fusion | flops 2097152 | bytes 25166080 | tf_op jit(solution)/shard_map/while/body/eval_jaxpr/scatter-add | solution.py:29
  131.6 2.8 gather_fusion
  134.4 7.4 %fusion.38 = f32[64,128,256]{2,1,0:T(8,128)} fusion(bf16[64,128,256]{2,1,0:T(8,128)(2,1)} %gather_fusion, pred[64]{0:T(512)(128)(4,1)S(1)} %get-tuple-element.176, bf16[256,128,128]{2,1,0:T(8,128)(2,1)} %get-tuple-element.200, s32[]{:T(128)S(6)} %select_n.59), kind=kOutput, calls=%fused_computation.2.clone.1 | convolution fusion | flops 538968064 | bytes 14680132 | tf_op jit(solution)/shard_map/while/body/eval_jaxpr/gab,gbs->gas/dot_general | solution.py:28
  141.8 19.2 %scatter_fusion = f32[32,128,256]{2,1,0:T(8,128)} fusion(f32[32,128,256]{2,1,0:T(8,128)} %get-tuple-element.188, s32[64]{0:T(128)S(1)} %compare_select_fusion.4, f32[64,128,256]{2,1,0:T(8,128)} %fusion.38), kind=kCustom, calls=%fused_computation.1.clone.1 | custom fusion | flops 2097152 | bytes 25166080 | tf_op jit(solution)/shard_map/while/body/eval_jaxpr/scatter-add | solution.py:29
  161.1 51.3 %reduce-scatter.2.cloned.1.call-done = f32[512,256]{1,0:T(8,128)} async-done(((f32[4096,256]{1,0:T(8,128)}), f32[512,256]{1,0:T(8,128)}) %reduce-scatter.2.cloned.1.call-update) | async-done | bytes 524304 | tf_op jit(solution)/shard_map/reduce_scatter | solution.py:49
  212.4 2.2 fusion.11
  214.7 122.3 %all-reduce.5.cloned.1.call-done = f32[128,128]{0,1:T(8,128)} async-done(((f32[128,128]{0,1:T(8,128)}), f32[128,128]{0,1:T(8,128)}) %all-reduce.5.cloned.1.call-update) | async-done | bytes 65552 | tf_op jit(solution)/shard_map/psum | solution.py:54
  338.0 0.9 fusion.20
  338.8 11.7 %cholesky.44 = f32[128,128]{1,0:T(8,128)S(1)} custom-call(f32[128,128]{1,0:T(8,128)S(1)} %fusion.20), custom_call_target="Cholesky" | custom-call | tf_op jit(solution)/shard_map/jit(cholesky)/cholesky | solution.py:12
  351.9 9.8 %custom-call.6 = f32[1,128,128]{1,2,0:T(8,128)S(1)} custom-call(f32[1,128,128]{2,1,0:T(8,128)S(1)} %get-tuple-element.131), custom_call_target="InvertDiagBlocksLowerTriangular" | custom-call | tf_op jit(solution)/shard_map/triangular_solve/custom-call.0 | solution.py:14
  362.0 1.3 fusion.9
  363.4 2.2 fusion.7
  365.8 118.2 %all-reduce.7.cloned.1.call-done = f32[128,128]{0,1:T(8,128)} async-done(((f32[128,128]{0,1:T(8,128)}), f32[128,128]{0,1:T(8,128)}) %all-reduce.7.cloned.1.call-update) | async-done | bytes 65552 | tf_op jit(solution)/shard_map/psum | solution.py:59
  484.0 1.6 convolution_subtract_fusion
  485.6 1.2 fusion.24
  486.9 0.8 broadcast_multiply_fusion.1
  487.7 121.6 %all-reduce.9.cloned.1.call-done = f32[128,128]{0,1:T(8,128)} async-done(((f32[128,128]{0,1:T(8,128)}), f32[128,128]{0,1:T(8,128)}) %all-reduce.9.cloned.1.call-update) | async-done | bytes 65552 | tf_op jit(solution)/shard_map/psum | solution.py:63
  610.3 0.9 fusion.18
  611.1 11.7 %cholesky.55 = f32[128,128]{1,0:T(8,128)S(1)} custom-call(f32[128,128]{1,0:T(8,128)S(1)} %fusion.18), custom_call_target="Cholesky" | custom-call | tf_op jit(solution)/shard_map/jit(cholesky)/cholesky | solution.py:12
  625.0 9.8 %custom-call.7 = f32[1,128,128]{1,2,0:T(8,128)S(1)} custom-call(f32[1,128,128]{2,1,0:T(8,128)S(1)} %get-tuple-element.133), custom_call_target="InvertDiagBlocksLowerTriangular" | custom-call | tf_op jit(solution)/shard_map/triangular_solve/custom-call.0 | solution.py:14
  635.6 1.0 copy.11
  (41 shorter events, 8.9 us)
Async XLA Ops:
  7.2 33.1 %all-gather.2.cloned.1.call-start = ((), (), s32[]{:S(2)}) async-start(), calls=%async_computation.1 | async-start | bytes 1310720 | tf_op jit(solution)/shard_map/all_gather | solution.py:46
  7.9 204.5 %reduce-scatter.2.cloned.1.call-start = ((), (), s32[]{:S(2)}) async-start(), calls=%async_computation.2 | async-start | bytes 4718592 | tf_op jit(solution)/shard_map/reduce_scatter | solution.py:49
  40.2 2.5 copy-start
  161.1 176.0 %all-reduce.5.cloned.1.call-start = ((), (), s32[]{:S(2)}) async-start(), calls=%async_computation.3 | async-start | bytes 131072 | tf_op jit(solution)/shard_map/psum | solution.py:54
  214.7 269.4 %all-reduce.7.cloned.1.call-start = ((), (), s32[]{:S(2)}) async-start(), calls=%async_computation.4 | async-start | bytes 131072 | tf_op jit(solution)/shard_map/psum | solution.py:59
  365.6 243.8 %all-reduce.9.cloned.1.call-start = ((), (), s32[]{:S(2)}) async-start(), calls=%async_computation.5 | async-start | bytes 131072 | tf_op jit(solution)/shard_map/psum | solution.py:63
Sparse Core Ops, SparseCore 0:
  9.6 30.6 all-gather.1
  161.2 51.1 reduce-scatter.1
  219.5 117.5 all-reduce.4
  365.7 118.3 all-reduce.6
  491.0 118.3 all-reduce.8
where the time goes:
time: 645 us; the launch traced here: 643 us
  waiting for transfers between devices  446 us (69%)
  other arithmetic  128 us (20%)
  matrix products  39 us (6%)
  local copies, waits for them, and re-layouts  15.6 us (2%)
  between operations  13.9 us (2%)
    psum x1, waiting for transfers between devices, on_device(): lax.psum(jnp.dot(first_part.T, first_part, precision=high), ('row', 'col'))  122 us
    psum x1, waiting for transfers between devices, on_device(): lax.psum(jnp.dot(remainder.T, remainder, precision=high), ('row', 'col'))  122 us
    psum x1, waiting for transfers between devices, on_device(): lax.psum(jnp.dot(basis_one.T, second_part, precision=high), ('row', 'col'))  118 us
    scatter-add x4, other arithmetic, advance(): return summed.at[row_ids].add(product)  77.1 us
    reduce_scatter x1, waiting for transfers between devices, on_device(): lax.psum_scatter(partial_value, 'col', scatter_dimension=0, tiled=True)  51.3 us
    all_gather x1, waiting for transfers between devices, on_device(): gathered = lax.all_gather(gaussian_sketch, 'row', axis=0, tiled=True)  31.6 us
    dot_general x4, matrix products, advance(): jnp.einsum('gab,gbs->gas', values, picked, preferred_element_type=jnp.flo...  29.5 us
    another operation x6, other arithmetic, upper_parts(): lower_factor = jnp.linalg.cholesky(gram)  24.8 us
  transfers between devices with their start and end apart: 5, of which 5 were waited for; matrix products, arithmetic and copies ran while one was open for 0% of the time, Pallas kernels for 0%

commit v1 on v0

v1 whole, which is shorter than its diff:
```python
import functools
import math

import jax
import jax.numpy as jnp
from jax import lax
from jax.experimental import pallas as pl
from jax.experimental.pallas import tpu as pltpu
from jax.sharding import PartitionSpec as P

PANEL = 128
BS = 128
LEVELS = 32700.0
OCTAVE = 64.0
DENSE_BYTES = 32 * 2**20


def upper_parts(gram):
    lower_factor = jnp.linalg.cholesky(gram)
    identity = jnp.eye(gram.shape[0], dtype=gram.dtype)
    inverse = lax.linalg.triangular_solve(lower_factor, identity, left_side=True, lower=True)
    return (lower_factor.T, inverse.T)


def exchange(value, axis, mask):
    size = lax.axis_size(axis)
    return lax.ppermute(value, axis, [(i, i ^ mask) for i in range(size)])


def scatter_kernel(slots, values, dense, zeros, taken, sem):
    n_slots = dense.shape[0]
    n_blocks = values.shape[0]
    zeros[...] = jnp.zeros_like(zeros)

    @pl.loop(0, n_slots)
    def _(s):
        taken[s] = 0

    @pl.loop(0, n_blocks)
    def _(b):
        slot = slots[b]
        taken[slot] = 1
        pltpu.make_async_copy(values.at[b], dense.at[slot], sem).start()

    @pl.loop(0, n_slots)
    def _(s):
        @pl.when(taken[s] == 0)
        def _():
            pltpu.make_async_copy(zeros, dense.at[s], sem).start()

    pltpu.make_async_copy(dense, dense, sem).wait()


def scatter_blocks(slots, values, n_slots):
    return pl.pallas_call(
        scatter_kernel,
        out_shape=jax.ShapeDtypeStruct((n_slots, BS, BS), values.dtype),
        grid_spec=pltpu.PrefetchScalarGridSpec(
            num_scalar_prefetch=1,
            grid=(),
            in_specs=[pl.BlockSpec(memory_space=pl.ANY)],
            out_specs=pl.BlockSpec(memory_space=pl.ANY),
            scratch_shapes=[
                pltpu.VMEM((BS, BS), values.dtype),
                pltpu.SMEM((n_slots,), jnp.int32),
                pltpu.SemaphoreType.DMA,
            ],
        ),
        compiler_params=pltpu.CompilerParams(vmem_limit_bytes=8 * 2**20),
        cost_estimate=pl.CostEstimate(flops=0, bytes_accessed=48 * 2**20, transcendentals=0),
    )(slots, values)


def dense_dot(a_ref, x_ref):
    rows, cols = a_ref.shape[:2]
    lhs = jnp.concatenate(
        [jnp.concatenate([a_ref[r, c] for c in range(cols)], axis=1) for r in range(rows)], axis=0
    )
    return jnp.dot(lhs, x_ref[...], preferred_element_type=jnp.float32)


def far_kernel(a_ref, x_ref, o_ref):
    o_ref[0] = dense_dot(a_ref, x_ref)


def quantize(total, o_ref):
    n = total.shape[0] // BS
    width = total.shape[1]
    row = lax.broadcasted_iota(jnp.int32, (16, width), 0)
    tail = jnp.zeros((16, width), jnp.float32)
    for b in range(n):
        part = total[b * BS : (b + 1) * BS]
        top = jnp.maximum(jnp.max(jnp.abs(part), axis=0, keepdims=True), 1e-30)
        step = jnp.ceil(jnp.log(top) * (OCTAVE / math.log(2.0)))
        scaled = part * (jnp.exp(step * (-math.log(2.0) / OCTAVE)) * LEVELS)
        o_ref[b * BS : (b + 1) * BS, :] = jnp.round(scaled).astype(jnp.int32).astype(jnp.int16)
        tail = jnp.where(row == b, jnp.broadcast_to(step, tail.shape), tail)
    o_ref[n * BS :, :] = tail.astype(jnp.int32).astype(jnp.int16)


def dequantize(q_ref):
    n = (q_ref.shape[0] - 16) // BS
    tail = q_ref[n * BS :, :].astype(jnp.int32).astype(jnp.float32)
    parts = []
    for b in range(n):
        scale = jnp.exp(tail[b : b + 1] * (math.log(2.0) / OCTAVE)) * (1.0 / LEVELS)
        parts.append(q_ref[b * BS : (b + 1) * BS, :].astype(jnp.int32).astype(jnp.float32) * scale)
    return jnp.concatenate(parts, axis=0)


def send_kernel(a_ref, x_ref, r_ref, *o_refs):
    total = dense_dot(a_ref, x_ref) + r_ref[0]
    for i, o_ref in enumerate(o_refs):

        @pl.when(pl.program_id(0) == i)
        def _(o_ref=o_ref):
            quantize(total, o_ref)


def own_kernel(a_ref, x_ref, r_ref, o_ref):
    o_ref[...] = dense_dot(a_ref, x_ref) + r_ref[0]


def reduce_kernel(core, own_ref, *refs):
    *q_refs, s_ref, mine_ref, other_ref, pack = refs
    total = own_ref[...]
    for q_ref in q_refs:
        total = total + dequantize(q_ref)
    s_ref[...] = total
    gram_store(total, pack)
    half = pack.shape[0] // 2
    c = core[0]
    mine_ref[...] = pack[pl.ds(pl.multiple_of(c * half, 8), half), :]
    other_ref[...] = pack[pl.ds(pl.multiple_of((1 - c) * half, 8), half), :]


def gram_store(total, pack):
    high = total.astype(jnp.bfloat16)
    low = (total - high.astype(jnp.float32)).astype(jnp.bfloat16)
    dims = (((0,), (0,)), ((), ()))
    dot = functools.partial(lax.dot_general, dimension_numbers=dims, preferred_element_type=jnp.float32)
    cross = dot(high, low)
    gram = dot(high, high) + dot(low, low) + cross + cross.T
    pack[0:PANEL, :] = gram[:PANEL, :PANEL]
    pack[PANEL : 2 * PANEL, :] = gram[:PANEL, PANEL:]
    pack[2 * PANEL : 3 * PANEL, :] = gram[PANEL:, PANEL:]


def whole(shape):
    return pl.BlockSpec(shape, lambda *_: (0,) * len(shape))


def dense_sketch(gaussian_sketch, block_values, local_rows, local_cols, grid_rows, grid_cols):
    size_col = lax.axis_size("col")
    chips = size_col // 2
    shard_rows, width = gaussian_sketch.shape
    group = shard_rows // BS
    me = lax.axis_index("col")
    owner = local_rows // group
    peer_core = (owner + me) % 2
    near = (owner // 2) ^ (me // 2)
    place = ((1 - peer_core) * chips + near) * group + local_rows % group
    slots = place * grid_cols + local_cols
    dense = scatter_blocks(slots, block_values, grid_rows * grid_cols)
    dense = dense.reshape(2 * chips * group, grid_cols, BS, BS)
    sketch = lax.all_gather(gaussian_sketch, "row", axis=0, tiled=True)

    params = pltpu.CompilerParams(vmem_limit_bytes=32 * 2**20)
    flops = 2 * shard_rows * grid_cols * BS * width
    bytes_a = 2 * shard_rows * grid_cols * BS

    def cost(n):
        return pl.CostEstimate(flops=n * flops, bytes_accessed=n * bytes_a, transcendentals=0)

    def a_spec(first):
        return pl.BlockSpec((group, grid_cols, BS, BS), lambda i: (i + first, 0, 0, 0))

    x_spec = whole(sketch.shape)
    r_block = (1, shard_rows, width)
    far = pl.pallas_call(
        far_kernel,
        grid=(chips,),
        in_specs=[a_spec(0), x_spec],
        out_specs=pl.BlockSpec(r_block, lambda i: (i, 0, 0)),
        out_shape=jax.ShapeDtypeStruct((chips, shard_rows, width), jnp.float32),
        compiler_params=params,
        cost_estimate=cost(chips),
    )(dense, sketch)
    near_sum = exchange(far, "col", 1)
    sent = jax.ShapeDtypeStruct((shard_rows + 16, width), jnp.int16)
    coded = pl.pallas_call(
        send_kernel,
        grid=(chips - 1,),
        in_specs=[a_spec(chips + 1), x_spec, pl.BlockSpec(r_block, lambda i: (i + 1, 0, 0))],
        out_specs=[whole(sent.shape)] * (chips - 1),
        out_shape=[sent] * (chips - 1),
        compiler_params=params,
        cost_estimate=cost(chips - 1),
    )(dense, sketch, near_sum)
    got = [exchange(q, "col", 2 * (i + 1)) for i, q in enumerate(coded)]
    own = pl.pallas_call(
        own_kernel,
        grid=(1,),
        in_specs=[a_spec(chips), x_spec, pl.BlockSpec(r_block, lambda i: (0, 0, 0))],
        out_specs=whole((shard_rows, width)),
        out_shape=jax.ShapeDtypeStruct((shard_rows, width), jnp.float32),
        compiler_params=params,
        cost_estimate=cost(1),
    )(dense, sketch, near_sum)
    return own, got


def tile_product(sketch_blocks, block_values, local_rows, local_cols, tile_rows):
    group_size = math.gcd(block_values.shape[0], 64)
    col_width = sketch_blocks.shape[2]

    def advance(counter, summed):
        offset = (counter * group_size).astype(jnp.int32)
        values = lax.dynamic_slice_in_dim(block_values, offset, group_size, 0)
        row_ids = lax.dynamic_slice_in_dim(local_rows, offset, group_size, 0)
        col_ids = lax.dynamic_slice_in_dim(local_cols, offset, group_size, 0)
        picked = jnp.take(sketch_blocks, col_ids, axis=0)
        product = jnp.einsum("gab,gbs->gas", values, picked, preferred_element_type=jnp.float32)
        return summed.at[row_ids].add(product)

    initial = jnp.zeros((tile_rows, block_values.shape[1], col_width), jnp.float32)
    summed = lax.fori_loop(0, block_values.shape[0] // group_size, advance, initial)
    return summed.reshape(tile_rows * block_values.shape[1], col_width)


def looped_sketch(gaussian_sketch, block_values, local_rows, local_cols, grid_rows, grid_cols):
    gathered = lax.all_gather(gaussian_sketch, "row", axis=0, tiled=True)
    sketch_blocks = gathered.reshape(grid_cols, BS, gathered.shape[1])
    partial_value = tile_product(sketch_blocks, block_values, local_rows, local_cols, grid_rows)
    return lax.psum_scatter(partial_value, "col", scatter_dimension=0, tiled=True), []


def direct_sum(value, axis, low_bit, bits):
    total = value
    for mask in range(1, 2**bits):
        total = total + exchange(value, axis, mask << low_bit)
    return total


def sum_over_axis(value, axis, low_bit):
    bits = lax.axis_size(axis).bit_length() - 1
    while low_bit < bits:
        take = min(2, bits - low_bit)
        value = direct_sum(value, axis, low_bit, take)
        low_bit += take
    return value


def sum_over_mesh(mine, other, core):
    mine = mine + exchange(other, "col", 1)
    mine = sum_over_axis(mine, "col", 1)
    mine = sum_over_axis(mine, "row", 0)
    other = exchange(mine, "col", 1)
    first = core == 0
    return jnp.concatenate([jnp.where(first, mine, other), jnp.where(first, other, mine)], axis=0)


def on_device(gaussian_sketch, block_values, block_rows, block_columns):
    high = lax.Precision.HIGHEST
    size_row = lax.axis_size("row")
    size_col = lax.axis_size("col")
    shard_rows, width = gaussian_sketch.shape
    grid_rows = shard_rows * size_col // BS
    grid_cols = shard_rows * size_row // BS
    local_rows = block_rows - lax.axis_index("row") * grid_rows
    local_cols = block_columns - lax.axis_index("col") * grid_cols
    dense = 2 * grid_rows * grid_cols * BS * BS <= DENSE_BYTES
    sketch = dense_sketch if dense else looped_sketch
    own, got = sketch(
        gaussian_sketch, block_values, local_rows, local_cols, grid_rows, grid_cols
    )
    core = lax.axis_index("col") % 2
    half = jax.ShapeDtypeStruct((3 * PANEL // 2, PANEL), jnp.float32)
    sketched, mine, other = pl.pallas_call(
        reduce_kernel,
        grid_spec=pltpu.PrefetchScalarGridSpec(
            num_scalar_prefetch=1,
            grid=(1,),
            in_specs=[whole(own.shape)] + [whole(q.shape) for q in got],
            out_specs=[whole(own.shape), whole(half.shape), whole(half.shape)],
            scratch_shapes=[pltpu.VMEM((3 * PANEL, PANEL), jnp.float32)],
        ),
        out_shape=[jax.ShapeDtypeStruct(own.shape, jnp.float32), half, half],
        compiler_params=pltpu.CompilerParams(vmem_limit_bytes=32 * 2**20),
    )(core.reshape(1), own, *got)
    order_total = shard_rows * size_row * size_col
    gram = sum_over_mesh(mine, other, core) / order_total
    upper_one, inverse_one = upper_parts(gram[:PANEL])
    coupling = jnp.dot(inverse_one.T, gram[PANEL : 2 * PANEL], precision=high)
    gram_two = gram[2 * PANEL :] - jnp.dot(coupling.T, coupling, precision=high)
    upper_two, inverse_two = upper_parts(gram_two)
    mixed = -jnp.dot(inverse_one, jnp.dot(coupling, inverse_two, precision=high), precision=high)
    zero = jnp.zeros_like(upper_two)
    inverse = jnp.block([[inverse_one, mixed], [zero, inverse_two]])
    range_basis = jnp.dot(sketched, inverse, precision=high)
    upper_factor = jnp.block([[upper_one, coupling], [zero, upper_two]])
    return (range_basis, upper_factor)


def solution(mesh):
    return jax.shard_map(
        on_device,
        mesh=mesh,
        in_specs=(
            P(("col", "row"), None),
            P(("row", "col"), None, None),
            P(("row", "col")),
            P(("row", "col")),
        ),
        out_specs=(P(("row", "col"), None), P()),
        check_vma=False,
    )
```

time: 645 us -> 173 us (0.27)
  waiting for transfers between devices: 446 us -> 29.6 us
  other arithmetic: 128 us -> 46.8 us
  Pallas kernels: 0 us -> 42.8 us
  matrix products: 39 us -> 3.06 us
  starting transfers between devices: 0.38 us -> 13.1 us
  local copies, waits for them, and re-layouts: 15.6 us -> 23.2 us
    psum x3 -> x0, waiting for transfers between devices: 362 us -> none  [the longest x1 122 us: on_device(): lax.psum(jnp.dot(first_part.T, first_part, precision=high), ('row', 'col'))]
    scatter-add x4 -> x0, other arithmetic: 77.1 us -> none  [advance(): return summed.at[row_ids].add(product)]
    reduce_scatter x1 -> x0, waiting for transfers between devices: 51.3 us -> none  [on_device(): lax.psum_scatter(partial_value, 'col', scatter_dimension=0, tiled=True)]
    pallas_call x0 -> x5, Pallas kernels: none -> 42.8 us  [the longest x1 34.2 us: scatter_blocks(): pl.pallas_call(scatter_kernel, out_shape=jax.ShapeDtypeStruct((n_slots, B...]
    dot_general x10 -> x5, matrix products: 38.4 us -> 2.52 us  [the longest x1 1.41 us: on_device(): range_basis = jnp.dot(sketched, inverse, precision=high)]
    all_gather x1, waiting for transfers between devices: 31.6 us -> 0.01 us  [dense_sketch(): sketch = lax.all_gather(gaussian_sketch, 'row', axis=0, tiled=True)]
    ppermute x0 -> x12, waiting for transfers between devices: none -> 28.9 us  [exchange(): return lax.ppermute(value, axis, [(i, i ^ mask) for i in range(size)])]
    unnamed x4 -> x13, local copies, waits for them, and re-layouts: 1.84 us -> 22.7 us
  transfers between devices with their start and end apart: 5 -> 13, of which waited for: 5 -> 9; matrix products, arithmetic and copies ran while one was open for 0% -> 0% of each run, Pallas kernels for 0% -> 20%
where the time goes in v1:
time: 173 us
  other arithmetic  46.8 us (27%)
  Pallas kernels  42.8 us (25%)
  waiting for transfers between devices  29.6 us (17%)
  local copies, waits for them, and re-layouts  23.2 us (13%)
  between operations  14.3 us (8%)
  starting transfers between devices  13.1 us (8%)
  matrix products  3.06 us (2%)
    pallas_call x1, Pallas kernels, scatter_blocks(): pl.pallas_call(scatter_kernel, out_shape=jax.ShapeDtypeStruct((n_slots, B...  34.2 us
    ppermute x12, waiting for transfers between devices, exchange(): return lax.ppermute(value, axis, [(i, i ^ mask) for i in range(size)])  28.9 us
    another operation x6, other arithmetic, upper_parts(): lower_factor = jnp.linalg.cholesky(gram)  24.9 us
    unnamed x13, local copies, waits for them, and re-layouts  22.7 us
    another operation x2, other arithmetic, upper_parts(): lax.linalg.triangular_solve(lower_factor, identity, left_side=True, lower...  19.6 us
    ppermute x12, starting transfers between devices, exchange(): return lax.ppermute(value, axis, [(i, i ^ mask) for i in range(size)])  13 us
  transfers between devices with their start and end apart: 13, of which 9 were waited for; matrix products, arithmetic and copies ran while one was open for 0% of the time, Pallas kernels for 20%

profile of v1, /device:TPU:0, one launch (start us, length us, event | category | flops | bytes accessed | tf_op | source)
XLA Modules:
  0.0 172.8 jit_solution(9833700072846166869)
XLA Ops:
  7.9 0.7 subtract_add_fusion.slots
  8.6 3.4 %copy-done.5 = bf16[256,128,128]{2,1,0:T(8,128)(2,1)S(1)} copy-done((bf16[256,128,128]{2,1,0:T(8,128)(2,1)S(1)}, bf16[256,128,128]{2,1,0:T(8,128)(2,1)}, u32[]{:S(2)}) %copy-start.5) | copy-done | bytes 8388632
  12.0 34.2 %shard_map.59 = bf16[512,128,128]{2,1,0:T(8,128)(2,1)S(1)} custom-call(s32[256]{0:T(256)S(1)} %subtract_add_fusion.slots, bf16[256,128,128]{2,1,0:T(8,128)(2,1)S(1)} %copy-done.5), custom_call_target="tpu_custom_call" | custom-call | bytes 50331648 | tf_op jit(solution)/shard_map/pallas_call | solution.py:55
  46.3 5.7 %copy-done = bf16[512,128,128]{2,1,0:T(8,128)(2,1)} copy-done((bf16[512,128,128]{2,1,0:T(8,128)(2,1)}, bf16[512,128,128]{2,1,0:T(8,128)(2,1)S(1)}, u32[]{:S(2)}) %copy-start) | copy-done | bytes 16777240
  52.0 5.8 %copy-done.1 = bf16[512,128,128]{2,1,0:T(8,128)(2,1)S(1)} copy-done((bf16[512,128,128]{2,1,0:T(8,128)(2,1)S(1)}, bf16[512,128,128]{2,1,0:T(8,128)(2,1)}, u32[]{:S(2)}) %copy-start.1) | copy-done | bytes 16777240
  57.8 1.2 copy-done.3
  59.0 2.8 %shard_map.60 = f32[4,512,256]{2,1,0:T(8,128)S(1)} custom-call(bf16[32,16,128,128]{3,2,1,0:T(8,128)(2,1)S(1)} %bitcast.34, bf16[2048,256]{1,0:T(8,128)(2,1)S(1)} %copy-done.3), custom_call_target="tpu_custom_call" | custom-call | flops 2147483648 | bytes 8388608 | tf_op jit(solution)/shard_map/pallas_call | solution.py:180
  62.4 3.8 %collective-permute-done.r_ref = f32[4,512,256]{2,1,0:T(8,128)S(1)} collective-permute-done((f32[4,512,256]{2,1,0:T(8,128)S(1)}, f32[4,512,256]{2,1,0:T(8,128)S(1)}, u32[]{:S(2)}, u32[]{:S(2)}) %collective-permute-start) | collective-permute-done | bytes 2097184 | tf_op jit(solution)/shard_map/ppermute | solution.py:27
  66.2 3.3 %shard_map.62 = (s16[528,256]{1,0:T(8,128)(2,1)}, s16[528,256]{1,0:T(8,128)(2,1)}, s16[528,256]{1,0:T(8,128)(2,1)}) custom-call(bf16[32,16,128,128]{3,2,1,0:T(8,128)(2,1)S(1)} %bitcast.35, bf16[2048,256]{1,0:T(8,128)(2,1)S(1)} %copy-done.3, f32[4,512,256]{2,1,0:T(8,128)S(1)} %collective-permute-done.r_ref), custom_call_target="tpu_custom_call" | custom-call | flops 1610612736 | bytes 6291456 | tf_op jit(solution)/shard_map/pallas_call | solution.py:191
  69.5 2.9 %collective-permute-start.1 = (s16[528,256]{1,0:T(8,128)(2,1)}, s16[528,256]{1,0:T(8,128)(2,1)S(1)}, u32[]{:S(2)}, u32[]{:S(2)}) collective-permute-start(s16[528,256]{1,0:T(8,128)(2,1)} %get-tuple-element.10), channel_id=1, source_target_pairs={{0,2},{1,3},{2,0},{3,1},{4,6},{5,7},{6,4},{7,5},{8,10},{9,11},{10,... | collective-permute-start | bytes 811016 | tf_op jit(solution)/shard_map/ppermute | solution.py:27
  72.4 1.5 collective-permute-start.2
  73.9 5.8 %copy-done.2 = bf16[512,128,128]{2,1,0:T(8,128)(2,1)S(1)} copy-done((bf16[512,128,128]{2,1,0:T(8,128)(2,1)S(1)}, bf16[512,128,128]{2,1,0:T(8,128)(2,1)}, u32[]{:S(2)}) %copy-start.2) | copy-done | bytes 16777240
  79.7 0.7 shard_map.61.own_ref
  80.4 6.3 %collective-permute-done.2.refs_1_ = s16[528,256]{1,0:T(8,128)(2,1)} collective-permute-done((s16[528,256]{1,0:T(8,128)(2,1)}, s16[528,256]{1,0:T(8,128)(2,1)}, u32[]{:S(2)}, u32[]{:S(2)}) %collective-permute-start.2) | collective-permute-done | bytes 270368 | tf_op jit(solution)/shard_map/ppermute | solution.py:27
  86.7 1.7 shard_map.63
  88.7 1.2 collective-permute-done.4
  89.9 1.6 collective-permute-start.7
  91.5 1.2 collective-permute-start.6
  92.7 0.8 collective-permute-start.5
  93.5 3.8 %collective-permute-done.7 = f32[192,128]{0,1:T(8,128)S(1)} collective-permute-done((f32[192,128]{0,1:T(8,128)S(1)}, f32[192,128]{0,1:T(8,128)S(1)}, u32[]{:S(2)}, u32[]{:S(2)}) %collective-permute-start.7) | collective-permute-done | bytes 98336 | tf_op jit(solution)/shard_map/ppermute | solution.py:27
  97.3 2.0 %collective-permute-done.6 = f32[192,128]{0,1:T(8,128)S(1)} collective-permute-done((f32[192,128]{0,1:T(8,128)S(1)}, f32[192,128]{0,1:T(8,128)S(1)}, u32[]{:S(2)}, u32[]{:S(2)}) %collective-permute-start.6) | collective-permute-done | bytes 98336 | tf_op jit(solution)/shard_map/ppermute | solution.py:27
  99.4 3.7 %collective-permute-start.10 = (f32[192,128]{0,1:T(8,128)S(1)}, f32[192,128]{0,1:T(8,128)S(1)}, u32[]{:S(2)}, u32[]{:S(2)}) collective-permute-start(f32[192,128]{0,1:T(8,128)S(1)} %add_add_fusion.1), channel_id=1, source_target_pairs={{0,24},{8,16},{16,8},{24,0},{1,25},{9,17},{17,9},{25,1},{2,26},{10... | collective-permute-start | bytes 294920 | tf_op jit(solution)/shard_map/ppermute | solution.py:27
  103.1 0.8 collective-permute-start.8
  103.8 3.9 %collective-permute-done.10 = f32[192,128]{0,1:T(8,128)S(1)} collective-permute-done((f32[192,128]{0,1:T(8,128)S(1)}, f32[192,128]{0,1:T(8,128)S(1)}, u32[]{:S(2)}, u32[]{:S(2)}) %collective-permute-start.10) | collective-permute-done | bytes 98336 | tf_op jit(solution)/shard_map/ppermute | solution.py:27
  107.7 6.5 %collective-permute-done.9 = f32[192,128]{0,1:T(8,128)S(1)} collective-permute-done((f32[192,128]{0,1:T(8,128)S(1)}, f32[192,128]{0,1:T(8,128)S(1)}, u32[]{:S(2)}, u32[]{:S(2)}) %collective-permute-start.9) | collective-permute-done | bytes 98336 | tf_op jit(solution)/shard_map/ppermute | solution.py:27
  114.3 1.3 collective-permute-done.11
  115.9 11.7 %cholesky.44 = f32[128,128]{1,0:T(8,128)S(1)} custom-call(f32[128,128]{1,0:T(8,128)S(1)} %fusion.16), custom_call_target="Cholesky" | custom-call | tf_op jit(solution)/shard_map/jit(cholesky)/cholesky | solution.py:19
  129.0 9.8 %custom-call.6 = f32[1,128,128]{1,2,0:T(8,128)S(1)} custom-call(f32[1,128,128]{2,1,0:T(8,128)S(1)} %get-tuple-element.21), custom_call_target="InvertDiagBlocksLowerTriangular" | custom-call | tf_op jit(solution)/shard_map/triangular_solve/custom-call.0 | solution.py:21
  139.7 11.8 %cholesky.55 = f32[128,128]{1,0:T(8,128)S(1)} custom-call(f32[128,128]{1,0:T(8,128)S(1)} %fusion.14), custom_call_target="Cholesky" | custom-call | tf_op jit(solution)/shard_map/jit(cholesky)/cholesky | solution.py:19
  152.9 9.8 %custom-call.7 = f32[1,128,128]{1,2,0:T(8,128)S(1)} custom-call(f32[1,128,128]{2,1,0:T(8,128)S(1)} %get-tuple-element.23), custom_call_target="InvertDiagBlocksLowerTriangular" | custom-call | tf_op jit(solution)/shard_map/triangular_solve/custom-call.0 | solution.py:21
  163.7 0.8 copy.12
  164.6 1.4 fusion
  (45 shorter events, 6.5 us)
Async XLA Ops:
  7.2 44.8 %all-gather.2.cloned.1.call-start = ((), (), s32[]{:S(2)}) async-start(), calls=%async_computation | async-start | bytes 1310720 | tf_op jit(solution)/shard_map/all_gather | solution.py:166
  8.6 3.4 %copy-start.5 = (bf16[256,128,128]{2,1,0:T(8,128)(2,1)S(1)}, bf16[256,128,128]{2,1,0:T(8,128)(2,1)}, u32[]{:S(2)}) copy-start(bf16[256,128,128]{2,1,0:T(8,128)(2,1)} %values.1) | copy-start | bytes 25165828
  46.3 5.7 %copy-start = (bf16[512,128,128]{2,1,0:T(8,128)(2,1)}, bf16[512,128,128]{2,1,0:T(8,128)(2,1)S(1)}, u32[]{:S(2)}) copy-start(bf16[512,128,128]{2,1,0:T(8,128)(2,1)S(1)} %shard_map.59) | copy-start | bytes 50331652
  52.0 5.8 %copy-start.1 = (bf16[512,128,128]{2,1,0:T(8,128)(2,1)S(1)}, bf16[512,128,128]{2,1,0:T(8,128)(2,1)}, u32[]{:S(2)}) copy-start(bf16[512,128,128]{2,1,0:T(8,128)(2,1)} %copy-done) | copy-start | bytes 50331652
  57.8 1.2 copy-start.3
  61.9 12.0 %copy-start.4 = (bf16[2048,256]{1,0:T(8,128)(2,1)S(1)}, bf16[2048,256]{1,0:T(8,128)(2,1)}, u32[]{:S(2)}) copy-start(bf16[2048,256]{1,0:T(8,128)(2,1)} %all-gather.2.cloned.1.call-done.x_ref) | copy-start | bytes 3145732
  61.9 4.3 %collective-permute-start = (f32[4,512,256]{2,1,0:T(8,128)S(1)}, f32[4,512,256]{2,1,0:T(8,128)S(1)}, u32[]{:S(2)}, u32[]{:S(2)}) collective-permute-start(f32[4,512,256]{2,1,0:T(8,128)S(1)} %shard_map.60), channel_id=1, source_target_pairs={{0,1},{1,0},{2,3},{3,2},{4,5},{5,4},{6,7},{7,6},{8,9},{9,8},{10,11... | collective-permute-start | bytes 6291464 | tf_op jit(solution)/shard_map/ppermute | solution.py:27
  69.5 10.9 %collective-permute-start.1 = (s16[528,256]{1,0:T(8,128)(2,1)}, s16[528,256]{1,0:T(8,128)(2,1)S(1)}, u32[]{:S(2)}, u32[]{:S(2)}) collective-permute-start(s16[528,256]{1,0:T(8,128)(2,1)} %get-tuple-element.10), channel_id=1, source_target_pairs={{0,2},{1,3},{2,0},{3,1},{4,6},{5,7},{6,4},{7,5},{8,10},{9,11},{10,... | collective-permute-start | bytes 811016 | tf_op jit(solution)/shard_map/ppermute | solution.py:27
  72.4 14.3 %collective-permute-start.2 = (s16[528,256]{1,0:T(8,128)(2,1)}, s16[528,256]{1,0:T(8,128)(2,1)}, u32[]{:S(2)}, u32[]{:S(2)}) collective-permute-start(s16[528,256]{1,0:T(8,128)(2,1)} %get-tuple-element.11), channel_id=1, source_target_pairs={{0,4},{1,5},{2,6},{3,7},{4,0},{5,1},{6,2},{7,3},{8,12},{9,13},{10,... | collective-permute-start | bytes 811016 | tf_op jit(solution)/shard_map/ppermute | solution.py:27
  73.9 12.8 %collective-permute-start.3 = (s16[528,256]{1,0:T(8,128)(2,1)}, s16[528,256]{1,0:T(8,128)(2,1)}, u32[]{:S(2)}, u32[]{:S(2)}) collective-permute-start(s16[528,256]{1,0:T(8,128)(2,1)} %get-tuple-element.12), channel_id=1, source_target_pairs={{0,6},{1,7},{2,4},{3,5},{4,2},{5,3},{6,0},{7,1},{8,14},{9,15},{10,... | collective-permute-start | bytes 811016 | tf_op jit(solution)/shard_map/ppermute | solution.py:27
  73.9 5.8 %copy-start.2 = (bf16[512,128,128]{2,1,0:T(8,128)(2,1)S(1)}, bf16[512,128,128]{2,1,0:T(8,128)(2,1)}, u32[]{:S(2)}) copy-start(bf16[512,128,128]{2,1,0:T(8,128)(2,1)} %copy-done) | copy-start | bytes 50331652
  88.5 1.4 collective-permute-start.4
  89.9 7.3 %collective-permute-start.7 = (f32[192,128]{0,1:T(8,128)S(1)}, f32[192,128]{0,1:T(8,128)S(1)}, u32[]{:S(2)}, u32[]{:S(2)}) collective-permute-start(f32[192,128]{0,1:T(8,128)S(1)} %add.73), channel_id=1, source_target_pairs={{0,6},{1,7},{2,4},{3,5},{4,2},{5,3},{6,0},{7,1},{8,14},{9,15},{10,... | collective-permute-start | bytes 294920 | tf_op jit(solution)/shard_map/ppermute | solution.py:27
  91.5 7.8 %collective-permute-start.6 = (f32[192,128]{0,1:T(8,128)S(1)}, f32[192,128]{0,1:T(8,128)S(1)}, u32[]{:S(2)}, u32[]{:S(2)}) collective-permute-start(f32[192,128]{0,1:T(8,128)S(1)} %add.73), channel_id=1, source_target_pairs={{0,4},{1,5},{2,6},{3,7},{4,0},{5,1},{6,2},{7,3},{8,12},{9,13},{10,... | collective-permute-start | bytes 294920 | tf_op jit(solution)/shard_map/ppermute | solution.py:27
  92.7 6.7 %collective-permute-start.5 = (f32[192,128]{0,1:T(8,128)S(1)}, f32[192,128]{0,1:T(8,128)S(1)}, u32[]{:S(2)}, u32[]{:S(2)}) collective-permute-start(f32[192,128]{0,1:T(8,128)S(1)} %add.73), channel_id=1, source_target_pairs={{0,2},{1,3},{2,0},{3,1},{4,6},{5,7},{6,4},{7,5},{8,10},{9,11},{10,... | collective-permute-start | bytes 294920 | tf_op jit(solution)/shard_map/ppermute | solution.py:27
  99.4 8.3 %collective-permute-start.10 = (f32[192,128]{0,1:T(8,128)S(1)}, f32[192,128]{0,1:T(8,128)S(1)}, u32[]{:S(2)}, u32[]{:S(2)}) collective-permute-start(f32[192,128]{0,1:T(8,128)S(1)} %add_add_fusion.1), channel_id=1, source_target_pairs={{0,24},{8,16},{16,8},{24,0},{1,25},{9,17},{17,9},{25,1},{2,26},{10... | collective-permute-start | bytes 294920 | tf_op jit(solution)/shard_map/ppermute | solution.py:27
  103.1 11.2 %collective-permute-start.9 = (f32[192,128]{0,1:T(8,128)S(1)}, f32[192,128]{0,1:T(8,128)S(1)}, u32[]{:S(2)}, u32[]{:S(2)}) collective-permute-start(f32[192,128]{0,1:T(8,128)S(1)} %add_add_fusion.1), channel_id=1, source_target_pairs={{0,16},{8,24},{16,0},{24,8},{1,17},{9,25},{17,1},{25,9},{2,18},{10... | collective-permute-start | bytes 294920 | tf_op jit(solution)/shard_map/ppermute | solution.py:27
  103.1 11.2 %collective-permute-start.8 = (f32[192,128]{0,1:T(8,128)S(1)}, f32[192,128]{0,1:T(8,128)S(1)}, u32[]{:S(2)}, u32[]{:S(2)}) collective-permute-start(f32[192,128]{0,1:T(8,128)S(1)} %add_add_fusion.1), channel_id=1, source_target_pairs={{0,8},{8,0},{16,24},{24,16},{1,9},{9,1},{17,25},{25,17},{2,10},{10... | collective-permute-start | bytes 294920 | tf_op jit(solution)/shard_map/ppermute | solution.py:27
  114.3 1.4 collective-permute-start.11
Sparse Core Ops, SparseCore 0:
  9.6 30.6 all-gather.1

commit v2 on v1

v2 whole, which is shorter than its diff:
```python
import functools
import math

import jax
import jax.numpy as jnp
from jax import lax
from jax.experimental import pallas as pl
from jax.experimental.pallas import tpu as pltpu
from jax.sharding import PartitionSpec as P

PANEL = 128
BS = 128
LEVELS = 32700.0
OCTAVE = 64.0
DENSE_BYTES = 32 * 2**20
STEP = 4


def exchange(value, axis, mask):
    size = lax.axis_size(axis)
    return lax.ppermute(value, axis, [(i, i ^ mask) for i in range(size)])


def scatter_kernel(slots, values, dense, sem):
    n_slots = dense.shape[0]
    n_blocks = values.shape[0]

    @pl.loop(0, n_slots)
    def _(s):
        dense[s] = jnp.zeros(dense.shape[1:], dense.dtype)

    @pl.loop(0, n_blocks)
    def _(b):
        pltpu.make_async_copy(values.at[b], dense.at[slots[b]], sem).start()

    pltpu.make_async_copy(values, values, sem).wait()


def scatter_blocks(slots, values, n_slots):
    return pl.pallas_call(
        scatter_kernel,
        out_shape=pltpu.VMEM((n_slots, BS, BS), values.dtype),
        grid_spec=pltpu.PrefetchScalarGridSpec(
            num_scalar_prefetch=1,
            grid=(),
            in_specs=[pl.BlockSpec(memory_space=pltpu.HBM)],
            out_specs=pl.BlockSpec(memory_space=pltpu.VMEM),
            scratch_shapes=[pltpu.SemaphoreType.DMA],
        ),
        compiler_params=pltpu.CompilerParams(vmem_limit_bytes=4 * 2**20),
        cost_estimate=pl.CostEstimate(flops=0, bytes_accessed=24 * 2**20, transcendentals=0),
    )(slots, pltpu.with_memory_space_constraint(values, pltpu.HBM))


def dense_dot(a_ref, x_refs, chunk):
    group = a_ref.shape[1]
    span = a_ref.shape[2] // len(x_refs)
    total = None
    for k, x_ref in enumerate(x_refs):
        lhs = jnp.concatenate(
            [
                jnp.concatenate([a_ref[chunk, r, k * span + c] for c in range(span)], axis=1)
                for r in range(group)
            ],
            axis=0,
        )
        part = jnp.dot(lhs, x_ref[...], preferred_element_type=jnp.float32)
        total = part if total is None else total + part
    return total


def product_kernel(first, a_ref, *refs):
    *x_refs, o_ref = refs
    o_ref[0] = dense_dot(a_ref, x_refs, pl.program_id(0) + first)


def quantize(total, o_ref):
    n = total.shape[0] // BS
    width = total.shape[1]
    row = lax.broadcasted_iota(jnp.int32, (16, width), 0)
    tail = jnp.zeros((16, width), jnp.float32)
    for b in range(n):
        part = total[b * BS : (b + 1) * BS]
        top = jnp.maximum(jnp.max(jnp.abs(part), axis=0, keepdims=True), 1e-30)
        step = jnp.ceil(jnp.log(top) * (OCTAVE / math.log(2.0)))
        scaled = part * (jnp.exp(step * (-math.log(2.0) / OCTAVE)) * LEVELS)
        o_ref[b * BS : (b + 1) * BS, :] = jnp.round(scaled).astype(jnp.int32).astype(jnp.int16)
        tail = jnp.where(row == b, jnp.broadcast_to(step, tail.shape), tail)
    o_ref[n * BS :, :] = tail.astype(jnp.int32).astype(jnp.int16)


def dequantize(q_ref):
    n = (q_ref.shape[0] - 16) // BS
    tail = q_ref[n * BS :, :].astype(jnp.int32).astype(jnp.float32)
    parts = []
    for b in range(n):
        scale = jnp.exp(tail[b : b + 1] * (math.log(2.0) / OCTAVE)) * (1.0 / LEVELS)
        parts.append(q_ref[b * BS : (b + 1) * BS, :].astype(jnp.int32).astype(jnp.float32) * scale)
    return jnp.concatenate(parts, axis=0)


def code_kernel(a_ref, b_ref, own_ref, *o_refs):
    total = a_ref[0] + b_ref[0]
    i = pl.program_id(0)
    for j, o_ref in enumerate(o_refs):

        @pl.when(i == j)
        def _(o_ref=o_ref):
            quantize(total, o_ref)

    @pl.when(i == len(o_refs))
    def _():
        own_ref[...] = total


def reduce_kernel(core, *refs):
    *in_refs, s_ref, mine_ref, other_ref, pack = refs
    total = None
    for ref in in_refs:
        term = dequantize(ref) if ref.dtype == jnp.int16 else ref[...]
        total = term if total is None else total + term
    s_ref[...] = total
    gram_store(total, pack)
    half = pack.shape[0] // 2
    c = core[0]
    mine_ref[...] = pack[pl.ds(pl.multiple_of(c * half, 8), half), :]
    other_ref[...] = pack[pl.ds(pl.multiple_of((1 - c) * half, 8), half), :]


def gram_store(total, pack):
    high = total.astype(jnp.bfloat16)
    low = (total - high.astype(jnp.float32)).astype(jnp.bfloat16)
    dims = (((0,), (0,)), ((), ()))
    dot = functools.partial(lax.dot_general, dimension_numbers=dims, preferred_element_type=jnp.float32)
    cross = dot(high, low)
    gram = dot(high, high) + dot(low, low) + cross + cross.T
    pack[0:PANEL, :] = gram[:PANEL, :PANEL]
    pack[PANEL : 2 * PANEL, :] = gram[:PANEL, PANEL:]
    pack[2 * PANEL : 3 * PANEL, :] = gram[PANEL:, PANEL:]


def split(x, terms):
    out = []
    for _ in range(terms):
        part = x.astype(jnp.bfloat16)
        out.append(part)
        x = x - part.astype(jnp.float32)
    return out


PAIRS = ((0, 0), (0, 1), (1, 0), (1, 1), (0, 2), (2, 0))


def factor(gram):
    n = gram.shape[0]
    sub = lax.broadcasted_iota(jnp.int32, (8, n), 0)
    lane = lax.broadcasted_iota(jnp.int32, (8, n), 1)
    left = [gram[8 * i : 8 * i + 8] for i in range(n // 8)]
    right = [(lane == sub + 8 * i).astype(jnp.float32) for i in range(n // 8)]

    def row(x, k):
        return jnp.broadcast_to(x[k : k + 1], x.shape)

    for first in range(0, n // 8, STEP):
        last = first + STEP
        for b in range(first, last):
            cols = {
                t: [jnp.broadcast_to(left[t][:, 8 * b + k : 8 * b + k + 1], (8, n)) for k in range(8)]
                for t in range(b, last)
            }
            for k in range(8):
                pivot = row(cols[b][k], k)
                root = lax.rsqrt(pivot)
                root = root * (1.5 - 0.5 * pivot * root * root)
                mult = {t: cols[t][k] * root for t in range(b, last)}
                for j in range(k + 1, 8):
                    other = row(mult[b], j)
                    for t in range(b, last):
                        cols[t][j] = cols[t][j] - mult[t] * other
                top_left, top_right = row(left[b], k) * root, row(right[b], k) * root
                below = jnp.where(sub > k, mult[b], 0.0)
                left[b] = jnp.where(sub == k, top_left, left[b] - below * top_left)
                right[b] = jnp.where(sub == k, top_right, right[b] - below * top_right)
                for t in range(b + 1, last):
                    left[t] = left[t] - mult[t] * top_left
                    right[t] = right[t] - mult[t] * top_right
        if last < n // 8:
            u = split(jnp.concatenate(left[first:last], axis=0), 3)
            v = split(jnp.concatenate(right[first:last], axis=0), 3)
            lhs = jnp.concatenate([u[i] for i, _ in PAIRS], axis=0)
            rhs = jnp.concatenate(
                [jnp.concatenate([u[j] for _, j in PAIRS], axis=0), jnp.concatenate([v[j] for _, j in PAIRS], axis=0)],
                axis=1,
            )
            change = lax.dot_general(lhs, rhs, (((0,), (0,)), ((), ())), preferred_element_type=jnp.float32)
            for t in range(last, n // 8):
                left[t] = left[t] - change[8 * t : 8 * t + 8, :n]
                right[t] = right[t] - change[8 * t : 8 * t + 8, n:]
    upper = jnp.concatenate([jnp.where(lane >= sub + 8 * i, x, 0.0) for i, x in enumerate(left)], axis=0)
    return upper, jnp.concatenate(right, axis=0)


def dot3(a, b, dims):
    (ah, al), (bh, bl) = split(a, 2), split(b, 2)
    dot = functools.partial(
        lax.dot_general, dimension_numbers=(dims, ((), ())), preferred_element_type=jnp.float32
    )
    return dot(ah, bh) + (dot(ah, bl) + dot(al, bh))


def full_dot(a, b, dims):
    return lax.dot_general(
        a, b, (dims, ((), ())), precision=lax.Precision.HIGHEST, preferred_element_type=jnp.float32
    )


NN, NT, TN = ((1,), (0,)), ((1,), (1,)), ((0,), (0,))


def tail_kernel(scale, core, mine_ref, other_ref, s_ref, basis_ref, upper_ref, pack):
    half = pack.shape[0] // 2
    c = core[0]
    pack[pl.ds(pl.multiple_of(c * half, 8), half), :] = mine_ref[...] * scale
    pack[pl.ds(pl.multiple_of((1 - c) * half, 8), half), :] = other_ref[...] * scale
    gram_one, cross, gram_two = (pack[i * PANEL : (i + 1) * PANEL, :] for i in range(3))
    upper_one, low_one = factor(gram_one)
    coupling = full_dot(low_one, cross, NN)
    upper_two, low_two = factor(gram_two - full_dot(coupling, coupling, TN))
    mixed = -full_dot(low_two, full_dot(coupling, low_one, TN), NN)
    zero = jnp.zeros_like(upper_one)
    upper_ref[0:PANEL, 0:PANEL] = upper_one
    upper_ref[0:PANEL, PANEL:] = coupling
    upper_ref[PANEL:, 0:PANEL] = zero
    upper_ref[PANEL:, PANEL:] = upper_two
    first, second = s_ref[:, 0:PANEL], s_ref[...]
    basis_ref[:, 0:PANEL] = dot3(first, low_one, NT)
    basis_ref[:, PANEL:] = dot3(second, jnp.concatenate([mixed, low_two], axis=1), NT)


def whole(shape):
    return pl.BlockSpec(shape, lambda *_: (0,) * len(shape))


def gather_row(value):
    bits = lax.axis_size("row").bit_length() - 1
    shards = [value]
    for bit in reversed(range(bits)):
        shards = shards + [exchange(v, "row", 1 << bit) for v in shards]
    order = [0]
    for bit in reversed(range(bits)):
        order = order + [k | 1 << bit for k in order]
    return [shards[order.index(k)] for k in range(2**bits)]


def dense_sketch(gaussian_sketch, block_values, local_rows, local_cols, grid_rows, grid_cols):
    size_col = lax.axis_size("col")
    chips = size_col // 2
    shard_rows, width = gaussian_sketch.shape
    group = shard_rows // BS
    me = lax.axis_index("col")
    owner = local_rows // group
    peer_core = (owner + me) % 2
    near = (owner // 2) ^ (me // 2)
    place = ((1 - peer_core) * chips + near) * group + local_rows % group
    shard = (local_cols // group) ^ lax.axis_index("row")
    slots = place * grid_cols + shard * group + local_cols % group
    dense = scatter_blocks(slots, block_values, grid_rows * grid_cols)
    dense = dense.reshape(2 * chips, group, grid_cols, BS, BS)
    shards = gather_row(gaussian_sketch)
    n = len(shards)

    params = pltpu.CompilerParams(vmem_limit_bytes=12 * 2**20)
    flops = 2 * shard_rows * grid_cols * BS * width
    bytes_a = 2 * shard_rows * grid_cols * BS

    def cost(n):
        return pl.CostEstimate(flops=n * flops, bytes_accessed=n * bytes_a, transcendentals=0)

    held = pl.BlockSpec(memory_space=pltpu.VMEM)
    r_block = (1, shard_rows, width)
    def product(first):
        return pl.pallas_call(
            functools.partial(product_kernel, first),
            grid=(chips,),
            in_specs=[held] * (n + 1),
            out_specs=pl.BlockSpec(r_block, lambda i: (i, 0, 0)),
            out_shape=jax.ShapeDtypeStruct((chips, shard_rows, width), jnp.float32),
            compiler_params=params,
            cost_estimate=cost(chips),
        )(dense, *shards)

    peer_sum = exchange(product(0), "col", 1)
    near_sum = product(chips)
    sent = jax.ShapeDtypeStruct((shard_rows + 16, width), jnp.int16)
    own_last = pl.BlockSpec(r_block, lambda i: ((i + 1) % chips, 0, 0))
    own_shape = (shard_rows, width)
    own, *coded = pl.pallas_call(
        code_kernel,
        grid=(chips,),
        in_specs=[own_last, own_last],
        out_specs=[whole(own_shape)] + [whole(sent.shape)] * (chips - 1),
        out_shape=[jax.ShapeDtypeStruct(own_shape, jnp.float32)] + [sent] * (chips - 1),
        compiler_params=params,
    )(near_sum, peer_sum)
    return [own] + [exchange(q, "col", 2 * (i + 1)) for i, q in enumerate(coded)]


def tile_product(sketch_blocks, block_values, local_rows, local_cols, tile_rows):
    group_size = math.gcd(block_values.shape[0], 64)
    col_width = sketch_blocks.shape[2]

    def advance(counter, summed):
        offset = (counter * group_size).astype(jnp.int32)
        values = lax.dynamic_slice_in_dim(block_values, offset, group_size, 0)
        row_ids = lax.dynamic_slice_in_dim(local_rows, offset, group_size, 0)
        col_ids = lax.dynamic_slice_in_dim(local_cols, offset, group_size, 0)
        picked = jnp.take(sketch_blocks, col_ids, axis=0)
        product = jnp.einsum("gab,gbs->gas", values, picked, preferred_element_type=jnp.float32)
        return summed.at[row_ids].add(product)

    initial = jnp.zeros((tile_rows, block_values.shape[1], col_width), jnp.float32)
    summed = lax.fori_loop(0, block_values.shape[0] // group_size, advance, initial)
    return summed.reshape(tile_rows * block_values.shape[1], col_width)


def looped_sketch(gaussian_sketch, block_values, local_rows, local_cols, grid_rows, grid_cols):
    gathered = lax.all_gather(gaussian_sketch, "row", axis=0, tiled=True)
    sketch_blocks = gathered.reshape(grid_cols, BS, gathered.shape[1])
    partial_value = tile_product(sketch_blocks, block_values, local_rows, local_cols, grid_rows)
    return [lax.psum_scatter(partial_value, "col", scatter_dimension=0, tiled=True)]


def direct_sum(value, axis, low_bit, bits):
    terms = [value] + [exchange(value, axis, mask << low_bit) for mask in range(1, 2**bits)]
    while len(terms) > 1:
        terms = [a + b for a, b in zip(terms[0::2], terms[1::2])]
    return terms[0]


def sum_over_axis(value, axis, low_bit):
    bits = lax.axis_size(axis).bit_length() - 1
    while low_bit < bits:
        take = min(2, bits - low_bit)
        value = direct_sum(value, axis, low_bit, take)
        low_bit += take
    return value


def sum_over_mesh(mine, other, core):
    mine = mine + exchange(other, "col", 1)
    mine = sum_over_axis(mine, "col", 1)
    mine = sum_over_axis(mine, "row", 0)
    return mine, exchange(mine, "col", 1)


def on_device(gaussian_sketch, block_values, block_rows, block_columns):
    size_row = lax.axis_size("row")
    size_col = lax.axis_size("col")
    shard_rows, width = gaussian_sketch.shape
    grid_rows = shard_rows * size_col // BS
    grid_cols = shard_rows * size_row // BS
    local_rows = block_rows - lax.axis_index("row") * grid_rows
    local_cols = block_columns - lax.axis_index("col") * grid_cols
    dense = 2 * grid_rows * grid_cols * BS * BS <= DENSE_BYTES
    sketch = dense_sketch if dense else looped_sketch
    terms = sketch(
        gaussian_sketch, block_values, local_rows, local_cols, grid_rows, grid_cols
    )
    core = lax.axis_index("col") % 2
    half = jax.ShapeDtypeStruct((3 * PANEL // 2, PANEL), jnp.float32)
    sketched, mine, other = pl.pallas_call(
        reduce_kernel,
        grid_spec=pltpu.PrefetchScalarGridSpec(
            num_scalar_prefetch=1,
            grid=(1,),
            in_specs=[whole(t.shape) for t in terms],
            out_specs=[whole((shard_rows, width)), whole(half.shape), whole(half.shape)],
            scratch_shapes=[pltpu.VMEM((3 * PANEL, PANEL), jnp.float32)],
        ),
        out_shape=[jax.ShapeDtypeStruct((shard_rows, width), jnp.float32), half, half],
        compiler_params=pltpu.CompilerParams(vmem_limit_bytes=12 * 2**20),
    )(core.reshape(1), *terms)
    order_total = shard_rows * size_row * size_col
    mine, other = sum_over_mesh(mine, other, core)
    range_basis, upper_factor = pl.pallas_call(
        functools.partial(tail_kernel, 1.0 / order_total),
        grid_spec=pltpu.PrefetchScalarGridSpec(
            num_scalar_prefetch=1,
            grid=(1,),
            in_specs=[whole(half.shape), whole(half.shape), whole(sketched.shape)],
            out_specs=[whole(sketched.shape), whole((width, width))],
            scratch_shapes=[pltpu.VMEM((3 * PANEL, PANEL), jnp.float32)],
        ),
        out_shape=[
            jax.ShapeDtypeStruct(sketched.shape, jnp.float32),
            jax.ShapeDtypeStruct((width, width), jnp.float32),
        ],
        compiler_params=pltpu.CompilerParams(vmem_limit_bytes=16 * 2**20),
    )(core.reshape(1), mine, other, sketched)
    return (range_basis, upper_factor)


def solution(mesh):
    return jax.shard_map(
        on_device,
        mesh=mesh,
        in_specs=(
            P(("col", "row"), None),
            P(("row", "col"), None, None),
            P(("row", "col")),
            P(("row", "col")),
        ),
        out_specs=(P(("row", "col"), None), P()),
        check_vma=False,
    )
```

time: 173 us -> 83.7 us (0.48)
  other arithmetic: 46.8 us -> 0.78 us
  local copies, waits for them, and re-layouts: 23.2 us -> 0.01 us
  Pallas kernels: 42.8 us -> 24.6 us
  between operations: 14.3 us -> 0.75 us
  waiting for transfers between devices: 29.6 us -> 39.1 us
  starting transfers between devices: 13.1 us -> 18.2 us
  matrix products: 3.06 us -> 0 us
    another operation x8 -> x0, other arithmetic: 44.5 us -> none  [the longest x6 24.9 us: upper_parts(): lower_factor = jnp.linalg.cholesky(gram)]
    unnamed x13 -> x2, local copies, waits for them, and re-layouts: 22.7 us -> 0.01 us
    pallas_call x4 -> x5, Pallas kernels: 41.1 us -> 24 us  [the longest x1 10.6 us: on_device(): pl.pallas_call(functools.partial(tail_kernel, 1.0 / order_total), grid_sp...]
    ppermute x12 -> x15, waiting for transfers between devices: 28.9 us -> 39.1 us  [exchange(): return lax.ppermute(value, axis, [(i, i ^ mask) for i in range(size)])]
    ppermute x12 -> x15, starting transfers between devices: 13 us -> 18.2 us  [exchange(): return lax.ppermute(value, axis, [(i, i ^ mask) for i in range(size)])]
    dot_general x5 -> x0, matrix products: 2.52 us -> none  [the longest x1 1.41 us: on_device(): range_basis = jnp.dot(sketched, inverse, precision=high)]
  transfers between devices with their start and end apart: 13 -> 15, of which waited for: 9 -> 11; matrix products, arithmetic and copies ran while one was open for 0% -> 1% of each run, Pallas kernels for 20% -> 12%
where the time goes in v2:
time: 83.7 us; the launch traced here: 83.4 us
  waiting for transfers between devices  39.1 us (47%)
  Pallas kernels  24.6 us (29%)
  starting transfers between devices  18.2 us (22%)
    ppermute x15, waiting for transfers between devices, exchange(): return lax.ppermute(value, axis, [(i, i ^ mask) for i in range(size)])  39.1 us
    ppermute x15, starting transfers between devices, exchange(): return lax.ppermute(value, axis, [(i, i ^ mask) for i in range(size)])  18.2 us
    pallas_call x1, Pallas kernels, on_device(): pl.pallas_call(functools.partial(tail_kernel, 1.0 / order_total), grid_sp...  10.6 us
    pallas_call x1, Pallas kernels, scatter_blocks(): pl.pallas_call(scatter_kernel, out_shape=pltpu.VMEM((n_slots, BS, BS), va...  6.95 us
    pallas_call x2, Pallas kernels, product(): pl.pallas_call(functools.partial(product_kernel, first), grid=(chips,), i...  5.73 us
  transfers between devices with their start and end apart: 15, of which 11 were waited for; matrix products, arithmetic and copies ran while one was open for 1% of the time, Pallas kernels for 12%

profile of v2, /device:TPU:0, one launch (start us, length us, event | category | flops | bytes accessed | tf_op | source)
XLA Modules:
  0.0 83.4 jit_solution(10869343202140765927)
XLA Ops:
  0.6 4.1 %collective-permute-start.1 = (bf16[512,256]{1,0:T(8,128)(2,1)}, bf16[512,256]{1,0:T(8,128)(2,1)S(1)}, u32[]{:S(2)}, u32[]{:S(2)}) collective-permute-start(bf16[512,256]{1,0:T(8,128)(2,1)} %refs_0_.3), channel_id=1, source_target_pairs={{0,16},{8,24},{16,0},{24,8},{1,17},{9,25},{17,1},{25,9},{2,18},{10... | collective-permute-start | bytes 786440 | tf_op jit(solution)/shard_map/ppermute | solution.py:21
  4.7 1.6 %collective-permute-start = (bf16[512,256]{1,0:T(8,128)(2,1)}, bf16[512,256]{1,0:T(8,128)(2,1)S(1)}, u32[]{:S(2)}, u32[]{:S(2)}) collective-permute-start(bf16[512,256]{1,0:T(8,128)(2,1)} %refs_0_.3), channel_id=1, source_target_pairs={{0,8},{8,0},{16,24},{24,16},{1,9},{9,1},{17,25},{25,17},{2,10},{10... | collective-permute-start | bytes 786440 | tf_op jit(solution)/shard_map/ppermute | solution.py:21
  6.3 10.7 %collective-permute-done.1.refs_2_ = bf16[512,256]{1,0:T(8,128)(2,1)S(1)} collective-permute-done((bf16[512,256]{1,0:T(8,128)(2,1)}, bf16[512,256]{1,0:T(8,128)(2,1)S(1)}, u32[]{:S(2)}, u32[]{:S(2)}) %collective-permute-start.1) | collective-permute-done | bytes 262176 | tf_op jit(solution)/shard_map/ppermute | solution.py:21
  17.0 0.7 collective-permute-start.2
  17.7 0.7 fusion.4.slots
  18.4 7.0 %shard_map.59 = bf16[512,128,128]{2,1,0:T(8,128)(2,1)S(1)} custom-call(s32[256]{0:T(256)S(1)} %fusion.4.slots, bf16[256,128,128]{2,1,0:T(8,128)(2,1)} %values.1), custom_call_target="tpu_custom_call" | custom-call | bytes 25165824 | tf_op jit(solution)/shard_map/pallas_call | solution.py:40
  25.4 2.9 %shard_map.61 = f32[4,512,256]{2,1,0:T(8,128)S(1)} custom-call(bf16[8,4,16,128,128]{4,3,2,1,0:T(8,128)(2,1)S(1)} %bitcast.2, bf16[512,256]{1,0:T(8,128)(2,1)S(1)} %copy-done, bf16[512,256]{1,0:T(8,128)(2,1)S(1)} %collective-permute-done.refs_1_, bf16[512,256]{1,0:T(8,128)(2,1)S(1)} %collective-permute-done.1.refs_2_, ...), custom_call_target="tpu_custom_call" | custom-call | flops 2147483648 | bytes 8388608 | tf_op jit(solution)/shard_map/pallas_call | solution.py:282
  28.3 0.1 collective-permute-start.3
  28.4 2.9 %shard_map.60.a_ref = f32[4,512,256]{2,1,0:T(8,128)S(1)} custom-call(bf16[8,4,16,128,128]{4,3,2,1,0:T(8,128)(2,1)S(1)} %bitcast.3, bf16[512,256]{1,0:T(8,128)(2,1)S(1)} %copy-done, bf16[512,256]{1,0:T(8,128)(2,1)S(1)} %collective-permute-done.refs_1_, bf16[512,256]{1,0:T(8,128)(2,1)S(1)} %collective-permute-done.1.refs_2_, ...), custom_call_target="tpu_custom_call" | custom-call | flops 2147483648 | bytes 8388608 | tf_op jit(solution)/shard_map/pallas_call | solution.py:282
  31.2 1.3 %collective-permute-done.3.b_ref = f32[4,512,256]{2,1,0:T(8,128)S(1)} collective-permute-done((f32[4,512,256]{2,1,0:T(8,128)S(1)}, f32[4,512,256]{2,1,0:T(8,128)S(1)}, u32[]{:S(2)}, u32[]{:S(2)}) %collective-permute-start.3) | collective-permute-done | bytes 2097184 | tf_op jit(solution)/shard_map/ppermute | solution.py:21
  32.5 0.7 shard_map.62
  33.2 1.6 %collective-permute-start.4 = (s16[528,256]{1,0:T(8,128)(2,1)S(1)}, s16[528,256]{1,0:T(8,128)(2,1)S(1)}, u32[]{:S(2)}, u32[]{:S(2)}) collective-permute-start(s16[528,256]{1,0:T(8,128)(2,1)S(1)} %get-tuple-element.10), channel_id=1, source_target_pairs={{0,2},{1,3},{2,0},{3,1},{4,6},{5,7},{6,4},{7,5},{8,10},{9,11},{10,... | collective-permute-start | bytes 811016 | tf_op jit(solution)/shard_map/ppermute | solution.py:21
  34.8 1.5 %collective-permute-start.5 = (s16[528,256]{1,0:T(8,128)(2,1)S(1)}, s16[528,256]{1,0:T(8,128)(2,1)S(1)}, u32[]{:S(2)}, u32[]{:S(2)}) collective-permute-start(s16[528,256]{1,0:T(8,128)(2,1)S(1)} %get-tuple-element.11), channel_id=1, source_target_pairs={{0,4},{1,5},{2,6},{3,7},{4,0},{5,1},{6,2},{7,3},{8,12},{9,13},{10,... | collective-permute-start | bytes 811016 | tf_op jit(solution)/shard_map/ppermute | solution.py:21
  36.3 0.5 collective-permute-start.6
  36.8 5.8 %collective-permute-done.4.refs_1_ = s16[528,256]{1,0:T(8,128)(2,1)S(1)} collective-permute-done((s16[528,256]{1,0:T(8,128)(2,1)S(1)}, s16[528,256]{1,0:T(8,128)(2,1)S(1)}, u32[]{:S(2)}, u32[]{:S(2)}) %collective-permute-start.4) | collective-permute-done | bytes 270368 | tf_op jit(solution)/shard_map/ppermute | solution.py:21
  42.6 6.2 %collective-permute-done.5.refs_2_ = s16[528,256]{1,0:T(8,128)(2,1)S(1)} collective-permute-done((s16[528,256]{1,0:T(8,128)(2,1)S(1)}, s16[528,256]{1,0:T(8,128)(2,1)S(1)}, u32[]{:S(2)}, u32[]{:S(2)}) %collective-permute-start.5) | collective-permute-done | bytes 270368 | tf_op jit(solution)/shard_map/ppermute | solution.py:21
  48.8 0.6 shard_map.63
  49.4 0.1 collective-permute-start.7
  49.5 1.3 %collective-permute-done.7 = f32[192,128]{1,0:T(8,128)S(1)} collective-permute-done((f32[192,128]{1,0:T(8,128)S(1)}, f32[192,128]{1,0:T(8,128)S(1)}, u32[]{:S(2)}, u32[]{:S(2)}) %collective-permute-start.7) | collective-permute-done | bytes 98336 | tf_op jit(solution)/shard_map/ppermute | solution.py:21
  50.8 1.6 %collective-permute-start.10 = (f32[192,128]{1,0:T(8,128)S(1)}, f32[192,128]{1,0:T(8,128)S(1)}, u32[]{:S(2)}, u32[]{:S(2)}) collective-permute-start(f32[192,128]{1,0:T(8,128)S(1)} %add.71), channel_id=1, source_target_pairs={{0,6},{1,7},{2,4},{3,5},{4,2},{5,3},{6,0},{7,1},{8,14},{9,15},{10,... | collective-permute-start | bytes 294920 | tf_op jit(solution)/shard_map/ppermute | solution.py:21
  52.4 1.2 %collective-permute-start.9 = (f32[192,128]{1,0:T(8,128)S(1)}, f32[192,128]{1,0:T(8,128)S(1)}, u32[]{:S(2)}, u32[]{:S(2)}) collective-permute-start(f32[192,128]{1,0:T(8,128)S(1)} %add.71), channel_id=1, source_target_pairs={{0,4},{1,5},{2,6},{3,7},{4,0},{5,1},{6,2},{7,3},{8,12},{9,13},{10,... | collective-permute-start | bytes 294920 | tf_op jit(solution)/shard_map/ppermute | solution.py:21
  53.6 0.8 collective-permute-start.8
  54.4 2.9 %collective-permute-done.10 = f32[192,128]{1,0:T(8,128)S(1)} collective-permute-done((f32[192,128]{1,0:T(8,128)S(1)}, f32[192,128]{1,0:T(8,128)S(1)}, u32[]{:S(2)}, u32[]{:S(2)}) %collective-permute-start.10) | collective-permute-done | bytes 98336 | tf_op jit(solution)/shard_map/ppermute | solution.py:21
  57.3 1.4 %collective-permute-done.9 = f32[192,128]{1,0:T(8,128)S(1)} collective-permute-done((f32[192,128]{1,0:T(8,128)S(1)}, f32[192,128]{1,0:T(8,128)S(1)}, u32[]{:S(2)}, u32[]{:S(2)}) %collective-permute-start.9) | collective-permute-done | bytes 98336 | tf_op jit(solution)/shard_map/ppermute | solution.py:21
  58.7 0.1 collective-permute-done.8
  58.9 3.3 %collective-permute-start.13 = (f32[192,128]{1,0:T(8,128)S(1)}, f32[192,128]{1,0:T(8,128)S(1)}, u32[]{:S(2)}, u32[]{:S(2)}) collective-permute-start(f32[192,128]{1,0:T(8,128)S(1)} %add_add_fusion.1), channel_id=1, source_target_pairs={{0,24},{8,16},{16,8},{24,0},{1,25},{9,17},{17,9},{25,1},{2,26},{10... | collective-permute-start | bytes 294920 | tf_op jit(solution)/shard_map/ppermute | solution.py:21
  62.1 0.2 collective-permute-start.12
  62.3 1.0 %collective-permute-start.11 = (f32[192,128]{1,0:T(8,128)S(1)}, f32[192,128]{1,0:T(8,128)S(1)}, u32[]{:S(2)}, u32[]{:S(2)}) collective-permute-start(f32[192,128]{1,0:T(8,128)S(1)} %add_add_fusion.1), channel_id=1, source_target_pairs={{0,8},{8,0},{16,24},{24,16},{1,9},{9,1},{17,25},{25,17},{2,10},{10... | collective-permute-start | bytes 294920 | tf_op jit(solution)/shard_map/ppermute | solution.py:21
  63.3 2.2 %collective-permute-done.13 = f32[192,128]{1,0:T(8,128)S(1)} collective-permute-done((f32[192,128]{1,0:T(8,128)S(1)}, f32[192,128]{1,0:T(8,128)S(1)}, u32[]{:S(2)}, u32[]{:S(2)}) %collective-permute-start.13) | collective-permute-done | bytes 98336 | tf_op jit(solution)/shard_map/ppermute | solution.py:21
  65.6 5.9 %collective-permute-done.12 = f32[192,128]{1,0:T(8,128)S(1)} collective-permute-done((f32[192,128]{1,0:T(8,128)S(1)}, f32[192,128]{1,0:T(8,128)S(1)}, u32[]{:S(2)}, u32[]{:S(2)}) %collective-permute-start.12) | collective-permute-done | bytes 98336 | tf_op jit(solution)/shard_map/ppermute | solution.py:21
  71.5 1.3 %collective-permute-done.14.other_ref = f32[192,128]{1,0:T(8,128)S(1)} collective-permute-done((f32[192,128]{1,0:T(8,128)S(1)}, f32[192,128]{1,0:T(8,128)S(1)}, u32[]{:S(2)}, u32[]{:S(2)}) %collective-permute-start.14) | collective-permute-done | bytes 98336 | tf_op jit(solution)/shard_map/ppermute | solution.py:21
  72.8 10.6 %shard_map.64 = (f32[512,256]{1,0:T(8,128)}, f32[256,256]{1,0:T(8,128)}) custom-call(s32[1]{0:T(128)} %bitcast.core, f32[192,128]{1,0:T(8,128)S(1)} %add_add_fusion.mine_ref, f32[192,128]{1,0:T(8,128)S(1)} %collective-permute-done.14.other_ref, f32[512,256]{1,0:T(8,128)S(1)} %get-tuple-element.15.s_ref), custom_call_target="tpu_custom_call" | custom-call | tf_op jit(solution)/shard_map/pallas_call | solution.py:385
  (10 shorter events, 0.1 us)
Async XLA Ops:
  0.6 16.3 %collective-permute-start.1 = (bf16[512,256]{1,0:T(8,128)(2,1)}, bf16[512,256]{1,0:T(8,128)(2,1)S(1)}, u32[]{:S(2)}, u32[]{:S(2)}) collective-permute-start(bf16[512,256]{1,0:T(8,128)(2,1)} %refs_0_.3), channel_id=1, source_target_pairs={{0,16},{8,24},{16,0},{24,8},{1,17},{9,25},{17,1},{25,9},{2,18},{10... | collective-permute-start | bytes 786440 | tf_op jit(solution)/shard_map/ppermute | solution.py:21
  4.7 20.7 %collective-permute-start = (bf16[512,256]{1,0:T(8,128)(2,1)}, bf16[512,256]{1,0:T(8,128)(2,1)S(1)}, u32[]{:S(2)}, u32[]{:S(2)}) collective-permute-start(bf16[512,256]{1,0:T(8,128)(2,1)} %refs_0_.3), channel_id=1, source_target_pairs={{0,8},{8,0},{16,24},{24,16},{1,9},{9,1},{17,25},{25,17},{2,10},{10... | collective-permute-start | bytes 786440 | tf_op jit(solution)/shard_map/ppermute | solution.py:21
  17.0 8.4 %collective-permute-start.2 = (bf16[512,256]{1,0:T(8,128)(2,1)S(1)}, bf16[512,256]{1,0:T(8,128)(2,1)S(1)}, u32[]{:S(2)}, u32[]{:S(2)}) collective-permute-start(bf16[512,256]{1,0:T(8,128)(2,1)S(1)} %collective-permute-done.1.refs_2_), channel_id=1, source_target_pairs={{0,8},{8,0},{16,24},{24,16},{1,9},{9,1},{17,25},{25,17},{2,10},{10... | collective-permute-start | bytes 786440 | tf_op jit(solution)/shard_map/ppermute | solution.py:21
  18.4 7.0 %copy-start = (bf16[512,256]{1,0:T(8,128)(2,1)S(1)}, bf16[512,256]{1,0:T(8,128)(2,1)}, u32[]{:S(2)}) copy-start(bf16[512,256]{1,0:T(8,128)(2,1)} %refs_0_.3) | copy-start | bytes 786436
  28.3 4.2 %collective-permute-start.3 = (f32[4,512,256]{2,1,0:T(8,128)S(1)}, f32[4,512,256]{2,1,0:T(8,128)S(1)}, u32[]{:S(2)}, u32[]{:S(2)}) collective-permute-start(f32[4,512,256]{2,1,0:T(8,128)S(1)} %shard_map.61), channel_id=1, source_target_pairs={{0,1},{1,0},{2,3},{3,2},{4,5},{5,4},{6,7},{7,6},{8,9},{9,8},{10,11... | collective-permute-start | bytes 6291464 | tf_op jit(solution)/shard_map/ppermute | solution.py:21
  33.2 9.4 %collective-permute-start.4 = (s16[528,256]{1,0:T(8,128)(2,1)S(1)}, s16[528,256]{1,0:T(8,128)(2,1)S(1)}, u32[]{:S(2)}, u32[]{:S(2)}) collective-permute-start(s16[528,256]{1,0:T(8,128)(2,1)S(1)} %get-tuple-element.10), channel_id=1, source_target_pairs={{0,2},{1,3},{2,0},{3,1},{4,6},{5,7},{6,4},{7,5},{8,10},{9,11},{10,... | collective-permute-start | bytes 811016 | tf_op jit(solution)/shard_map/ppermute | solution.py:21
  34.8 14.0 %collective-permute-start.5 = (s16[528,256]{1,0:T(8,128)(2,1)S(1)}, s16[528,256]{1,0:T(8,128)(2,1)S(1)}, u32[]{:S(2)}, u32[]{:S(2)}) collective-permute-start(s16[528,256]{1,0:T(8,128)(2,1)S(1)} %get-tuple-element.11), channel_id=1, source_target_pairs={{0,4},{1,5},{2,6},{3,7},{4,0},{5,1},{6,2},{7,3},{8,12},{9,13},{10,... | collective-permute-start | bytes 811016 | tf_op jit(solution)/shard_map/ppermute | solution.py:21
  36.3 12.5 %collective-permute-start.6 = (s16[528,256]{1,0:T(8,128)(2,1)S(1)}, s16[528,256]{1,0:T(8,128)(2,1)S(1)}, u32[]{:S(2)}, u32[]{:S(2)}) collective-permute-start(s16[528,256]{1,0:T(8,128)(2,1)S(1)} %get-tuple-element.12), channel_id=1, source_target_pairs={{0,6},{1,7},{2,4},{3,5},{4,2},{5,3},{6,0},{7,1},{8,14},{9,15},{10,... | collective-permute-start | bytes 811016 | tf_op jit(solution)/shard_map/ppermute | solution.py:21
  49.4 1.4 %collective-permute-start.7 = (f32[192,128]{1,0:T(8,128)S(1)}, f32[192,128]{1,0:T(8,128)S(1)}, u32[]{:S(2)}, u32[]{:S(2)}) collective-permute-start(f32[192,128]{1,0:T(8,128)S(1)} %get-tuple-element.14), channel_id=1, source_target_pairs={{0,1},{1,0},{2,3},{3,2},{4,5},{5,4},{6,7},{7,6},{8,9},{9,8},{10,11... | collective-permute-start | bytes 294920 | tf_op jit(solution)/shard_map/ppermute | solution.py:21
  50.8 6.5 %collective-permute-start.10 = (f32[192,128]{1,0:T(8,128)S(1)}, f32[192,128]{1,0:T(8,128)S(1)}, u32[]{:S(2)}, u32[]{:S(2)}) collective-permute-start(f32[192,128]{1,0:T(8,128)S(1)} %add.71), channel_id=1, source_target_pairs={{0,6},{1,7},{2,4},{3,5},{4,2},{5,3},{6,0},{7,1},{8,14},{9,15},{10,... | collective-permute-start | bytes 294920 | tf_op jit(solution)/shard_map/ppermute | solution.py:21
  52.4 6.4 %collective-permute-start.9 = (f32[192,128]{1,0:T(8,128)S(1)}, f32[192,128]{1,0:T(8,128)S(1)}, u32[]{:S(2)}, u32[]{:S(2)}) collective-permute-start(f32[192,128]{1,0:T(8,128)S(1)} %add.71), channel_id=1, source_target_pairs={{0,4},{1,5},{2,6},{3,7},{4,0},{5,1},{6,2},{7,3},{8,12},{9,13},{10,... | collective-permute-start | bytes 294920 | tf_op jit(solution)/shard_map/ppermute | solution.py:21
  53.6 5.3 %collective-permute-start.8 = (f32[192,128]{1,0:T(8,128)S(1)}, f32[192,128]{1,0:T(8,128)S(1)}, u32[]{:S(2)}, u32[]{:S(2)}) collective-permute-start(f32[192,128]{1,0:T(8,128)S(1)} %add.71), channel_id=1, source_target_pairs={{0,2},{1,3},{2,0},{3,1},{4,6},{5,7},{6,4},{7,5},{8,10},{9,11},{10,... | collective-permute-start | bytes 294920 | tf_op jit(solution)/shard_map/ppermute | solution.py:21
  58.9 6.7 %collective-permute-start.13 = (f32[192,128]{1,0:T(8,128)S(1)}, f32[192,128]{1,0:T(8,128)S(1)}, u32[]{:S(2)}, u32[]{:S(2)}) collective-permute-start(f32[192,128]{1,0:T(8,128)S(1)} %add_add_fusion.1), channel_id=1, source_target_pairs={{0,24},{8,16},{16,8},{24,0},{1,25},{9,17},{17,9},{25,1},{2,26},{10... | collective-permute-start | bytes 294920 | tf_op jit(solution)/shard_map/ppermute | solution.py:21
  62.1 9.3 %collective-permute-start.12 = (f32[192,128]{1,0:T(8,128)S(1)}, f32[192,128]{1,0:T(8,128)S(1)}, u32[]{:S(2)}, u32[]{:S(2)}) collective-permute-start(f32[192,128]{1,0:T(8,128)S(1)} %add_add_fusion.1), channel_id=1, source_target_pairs={{0,16},{8,24},{16,0},{24,8},{1,17},{9,25},{17,1},{25,9},{2,18},{10... | collective-permute-start | bytes 294920 | tf_op jit(solution)/shard_map/ppermute | solution.py:21
  62.3 9.1 %collective-permute-start.11 = (f32[192,128]{1,0:T(8,128)S(1)}, f32[192,128]{1,0:T(8,128)S(1)}, u32[]{:S(2)}, u32[]{:S(2)}) collective-permute-start(f32[192,128]{1,0:T(8,128)S(1)} %add_add_fusion.1), channel_id=1, source_target_pairs={{0,8},{8,0},{16,24},{24,16},{1,9},{9,1},{17,25},{25,17},{2,10},{10... | collective-permute-start | bytes 294920 | tf_op jit(solution)/shard_map/ppermute | solution.py:21
  71.4 1.4 %collective-permute-start.14 = (f32[192,128]{1,0:T(8,128)S(1)}, f32[192,128]{1,0:T(8,128)S(1)}, u32[]{:S(2)}, u32[]{:S(2)}) collective-permute-start(f32[192,128]{1,0:T(8,128)S(1)} %add_add_fusion.mine_ref), channel_id=1, source_target_pairs={{0,1},{1,0},{2,3},{3,2},{4,5},{5,4},{6,7},{7,6},{8,9},{9,8},{10,11... | collective-permute-start | bytes 294920 | tf_op jit(solution)/shard_map/ppermute | solution.py:21

commit v3 on v2

--- a/solution.py
+++ b/solution.py
@@ -14,6 +14,7 @@
 OCTAVE = 64.0
 DENSE_BYTES = 32 * 2**20
 STEP = 4
+PACK = 2 * PANEL + 16
 
 
 def exchange(value, axis, mask):
@@ -21,17 +22,25 @@
     return lax.ppermute(value, axis, [(i, i ^ mask) for i in range(size)])
 
 
-def scatter_kernel(slots, values, dense, sem):
+def scatter_kernel(slots, values, dense, taken, sem):
     n_slots = dense.shape[0]
     n_blocks = values.shape[0]
 
     @pl.loop(0, n_slots)
     def _(s):
-        dense[s] = jnp.zeros(dense.shape[1:], dense.dtype)
+        taken[s] = 0
 
     @pl.loop(0, n_blocks)
     def _(b):
-        pltpu.make_async_copy(values.at[b], dense.at[slots[b]], sem).start()
+        slot = slots[b]
+        taken[slot] = 1
+        pltpu.make_async_copy(values.at[b], dense.at[slot], sem).start()
+
+    @pl.loop(0, n_slots)
+    def _(s):
+        @pl.when(taken[s] == 0)
+        def _():
+            dense[s] = jnp.zeros(dense.shape[1:], dense.dtype)
 
     pltpu.make_async_copy(values, values, sem).wait()
 
@@ -45,21 +54,20 @@
             grid=(),
             in_specs=[pl.BlockSpec(memory_space=pltpu.HBM)],
             out_specs=pl.BlockSpec(memory_space=pltpu.VMEM),
-            scratch_shapes=[pltpu.SemaphoreType.DMA],
+            scratch_shapes=[pltpu.SMEM((n_slots,), jnp.int32), pltpu.SemaphoreType.DMA],
         ),
         compiler_params=pltpu.CompilerParams(vmem_limit_bytes=4 * 2**20),
         cost_estimate=pl.CostEstimate(flops=0, bytes_accessed=24 * 2**20, transcendentals=0),
     )(slots, pltpu.with_memory_space_constraint(values, pltpu.HBM))
 
 
-def dense_dot(a_ref, x_refs, chunk):
+def dense_dot(a_ref, x_refs, shards, chunk):
     group = a_ref.shape[1]
-    span = a_ref.shape[2] // len(x_refs)
     total = None
-    for k, x_ref in enumerate(x_refs):
+    for k, x_ref in zip(shards, x_refs):
         lhs = jnp.concatenate(
             [
-                jnp.concatenate([a_ref[chunk, r, k * span + c] for c in range(span)], axis=1)
+                jnp.concatenate([a_ref[chunk, r, k * group + c] for c in range(group)], axis=1)
                 for r in range(group)
             ],
             axis=0,
@@ -69,9 +77,10 @@
     return total
 
 
-def product_kernel(first, a_ref, *refs):
-    *x_refs, o_ref = refs
-    o_ref[0] = dense_dot(a_ref, x_refs, pl.program_id(0) + first)
+def product_kernel(first, shards, a_ref, *refs):
+    *in_refs, o_ref = refs
+    total = dense_dot(a_ref, in_refs, shards, pl.program_id(0) + first)
+    o_ref[0] = total + in_refs[-1][0] if len(in_refs) > len(shards) else total
 
 
 def quantize(total, o_ref):
@@ -134,9 +143,13 @@
     dot = functools.partial(lax.dot_general, dimension_numbers=dims, preferred_element_type=jnp.float32)
     cross = dot(high, low)
     gram = dot(high, high) + dot(low, low) + cross + cross.T
-    pack[0:PANEL, :] = gram[:PANEL, :PANEL]
+    row = lax.broadcasted_iota(jnp.int32, (PANEL, PANEL), 0)
+    lane = lax.broadcasted_iota(jnp.int32, (PANEL, PANEL), 1)
+    second = gram[PANEL:, PANEL:]
+    pack[0:PANEL, :] = jnp.where(lane >= row, gram[:PANEL, :PANEL], second)
     pack[PANEL : 2 * PANEL, :] = gram[:PANEL, PANEL:]
-    pack[2 * PANEL : 3 * PANEL, :] = gram[PANEL:, PANEL:]
+    diagonal = jnp.sum(jnp.where(lane == row, second, 0.0), axis=0, keepdims=True)
+    pack[2 * PANEL :, :] = jnp.broadcast_to(diagonal, (PACK - 2 * PANEL, PANEL))
 
 
 def split(x, terms):
@@ -222,7 +235,13 @@
     c = core[0]
     pack[pl.ds(pl.multiple_of(c * half, 8), half), :] = mine_ref[...] * scale
     pack[pl.ds(pl.multiple_of((1 - c) * half, 8), half), :] = other_ref[...] * scale
-    gram_one, cross, gram_two = (pack[i * PANEL : (i + 1) * PANEL, :] for i in range(3))
+    row = lax.broadcasted_iota(jnp.int32, (PANEL, PANEL), 0)
+    lane = lax.broadcasted_iota(jnp.int32, (PANEL, PANEL), 1)
+    both, cross = pack[0:PANEL, :], pack[PANEL : 2 * PANEL, :]
+    turned = both.T
+    gram_one = jnp.where(lane >= row, both, turned)
+    diagonal = jnp.broadcast_to(pack[2 * PANEL : 2 * PANEL + 1, :], both.shape)
+    gram_two = jnp.where(lane == row, diagonal, jnp.where(lane < row, both, turned))
     upper_one, low_one = factor(gram_one)
     coupling = full_dot(low_one, cross, NN)
     upper_two, low_two = factor(gram_two - full_dot(coupling, coupling, TN))
@@ -241,15 +260,15 @@
     return pl.BlockSpec(shape, lambda *_: (0,) * len(shape))
 
 
-def gather_row(value):
+def gather_row(value, ready):
     bits = lax.axis_size("row").bit_length() - 1
-    shards = [value]
+    shards = {0: value}
     for bit in reversed(range(bits)):
-        shards = shards + [exchange(v, "row", 1 << bit) for v in shards]
-    order = [0]
-    for bit in reversed(range(bits)):
-        order = order + [k | 1 << bit for k in order]
-    return [shards[order.index(k)] for k in range(2**bits)]
+        for k, v in list(shards.items()):
+            if bit == 0 and k:
+                v, ready = lax.optimization_barrier((v, ready))
+            shards[k | 1 << bit] = exchange(v, "row", 1 << bit)
+    return [shards[k] for k in range(2**bits)], ready
 
 
 def dense_sketch(gaussian_sketch, block_values, local_rows, local_cols, grid_rows, grid_cols):
@@ -266,8 +285,9 @@
     slots = place * grid_cols + shard * group + local_cols % group
     dense = scatter_blocks(slots, block_values, grid_rows * grid_cols)
     dense = dense.reshape(2 * chips, group, grid_cols, BS, BS)
-    shards = gather_row(gaussian_sketch)
-    n = len(shards)
+    shards, dense = gather_row(gaussian_sketch, dense)
+    late = [k for k in range(len(shards)) if k % 2 and k > 1]
+    early = [k for k in range(len(shards)) if k not in late]
 
     params = pltpu.CompilerParams(vmem_limit_bytes=12 * 2**20)
     flops = 2 * shard_rows * grid_cols * BS * width
@@ -278,19 +298,23 @@
 
     held = pl.BlockSpec(memory_space=pltpu.VMEM)
     r_block = (1, shard_rows, width)
-    def product(first):
+    def product(first, chosen, *added):
+        block = pl.BlockSpec(r_block, lambda i: (i, 0, 0))
         return pl.pallas_call(
-            functools.partial(product_kernel, first),
+            functools.partial(product_kernel, first, chosen),
             grid=(chips,),
-            in_specs=[held] * (n + 1),
-            out_specs=pl.BlockSpec(r_block, lambda i: (i, 0, 0)),
+            in_specs=[held] * (len(chosen) + 1) + [block] * len(added),
+            out_specs=block,
             out_shape=jax.ShapeDtypeStruct((chips, shard_rows, width), jnp.float32),
             compiler_params=params,
             cost_estimate=cost(chips),
-        )(dense, *shards)
-
-    peer_sum = exchange(product(0), "col", 1)
-    near_sum = product(chips)
+        )(dense, *[shards[k] for k in chosen], *added)
+
+    far, near = product(0, early), product(chips, early)
+    if late:
+        far = product(0, late, far)
+    peer_sum = exchange(far, "col", 1)
+    near_sum = product(chips, late, near) if late else near
     sent = jax.ShapeDtypeStruct((shard_rows + 16, width), jnp.int16)
     own_last = pl.BlockSpec(r_block, lambda i: ((i + 1) % chips, 0, 0))
     own_shape = (shard_rows, width)
@@ -367,7 +391,7 @@
         gaussian_sketch, block_values, local_rows, local_cols, grid_rows, grid_cols
     )
     core = lax.axis_index("col") % 2
-    half = jax.ShapeDtypeStruct((3 * PANEL // 2, PANEL), jnp.float32)
+    half = jax.ShapeDtypeStruct((PACK // 2, PANEL), jnp.float32)
     sketched, mine, other = pl.pallas_call(
         reduce_kernel,
         grid_spec=pltpu.PrefetchScalarGridSpec(
@@ -375,7 +399,7 @@
             grid=(1,),
             in_specs=[whole(t.shape) for t in terms],
             out_specs=[whole((shard_rows, width)), whole(half.shape), whole(half.shape)],
-            scratch_shapes=[pltpu.VMEM((3 * PANEL, PANEL), jnp.float32)],
+            scratch_shapes=[pltpu.VMEM((PACK, PANEL), jnp.float32)],
         ),
         out_shape=[jax.ShapeDtypeStruct((shard_rows, width), jnp.float32), half, half],
         compiler_params=pltpu.CompilerParams(vmem_limit_bytes=12 * 2**20),
@@ -389,7 +413,7 @@
             grid=(1,),
             in_specs=[whole(half.shape), whole(half.shape), whole(sketched.shape)],
             out_specs=[whole(sketched.shape), whole((width, width))],
-            scratch_shapes=[pltpu.VMEM((3 * PANEL, PANEL), jnp.float32)],
+            scratch_shapes=[pltpu.VMEM((PACK, PANEL), jnp.float32)],
         ),
         out_shape=[
             jax.ShapeDtypeStruct(sketched.shape, jnp.float32),

time: 83.7 us -> 79.2 us (0.946)
  waiting for transfers between devices: 39.1 us -> 27.6 us
  Pallas kernels: 24.6 us -> 31.9 us
    ppermute x15, waiting for transfers between devices: 39.1 us -> 27.6 us  [exchange(): return lax.ppermute(value, axis, [(i, i ^ mask) for i in range(size)])]
    pallas_call x1, Pallas kernels: 6.95 us -> 12.8 us  [scatter_blocks(): pl.pallas_call(scatter_kernel, out_shape=pltpu.VMEM((n_slots, BS, BS), va...]
    pallas_call x2 -> x4, Pallas kernels: 5.73 us -> 7.08 us  [product(): pl.pallas_call(functools.partial(product_kernel, first, chosen), grid=(ch...]
  transfers between devices with their start and end apart: 15 -> 15, of which waited for: 11 -> 11; matrix products, arithmetic and copies ran while one was open for 1% -> 1% of each run, Pallas kernels for 12% -> 24%
where the time goes in v3:
time: 79.2 us; the launch traced here: 79 us
  Pallas kernels  31.9 us (40%)
  waiting for transfers between devices  27.6 us (35%)
  starting transfers between devices  18 us (23%)
    ppermute x15, waiting for transfers between devices, exchange(): return lax.ppermute(value, axis, [(i, i ^ mask) for i in range(size)])  27.6 us
    ppermute x15, starting transfers between devices, exchange(): return lax.ppermute(value, axis, [(i, i ^ mask) for i in range(size)])  18 us
    pallas_call x1, Pallas kernels, scatter_blocks(): pl.pallas_call(scatter_kernel, out_shape=pltpu.VMEM((n_slots, BS, BS), va...  12.8 us
    pallas_call x1, Pallas kernels, on_device(): pl.pallas_call(functools.partial(tail_kernel, 1.0 / order_total), grid_sp...  10.7 us
    pallas_call x4, Pallas kernels, product(): pl.pallas_call(functools.partial(product_kernel, first, chosen), grid=(ch...  7.08 us
  transfers between devices with their start and end apart: 15, of which 11 were waited for; matrix products, arithmetic and copies ran while one was open for 1% of the time, Pallas kernels for 24%

profile of v3, /device:TPU:0, one launch (start us, length us, event | category | flops | bytes accessed | tf_op | source)
XLA Modules:
  0.0 79.0 jit_solution(13681395524803801515)
XLA Ops:
  0.6 4.1 %collective-permute-start = (bf16[512,256]{1,0:T(8,128)(2,1)}, bf16[512,256]{1,0:T(8,128)(2,1)S(1)}, u32[]{:S(2)}, u32[]{:S(2)}) collective-permute-start(bf16[512,256]{1,0:T(8,128)(2,1)} %refs_0_.3), channel_id=1, source_target_pairs={{0,16},{8,24},{16,0},{24,8},{1,17},{9,25},{17,1},{25,9},{2,18},{10... | collective-permute-start | bytes 786440 | tf_op jit(solution)/shard_map/ppermute | solution.py:22
  4.7 1.6 %collective-permute-start.2 = (bf16[512,256]{1,0:T(8,128)(2,1)}, bf16[512,256]{1,0:T(8,128)(2,1)S(1)}, u32[]{:S(2)}, u32[]{:S(2)}) collective-permute-start(bf16[512,256]{1,0:T(8,128)(2,1)} %refs_0_.3), channel_id=1, source_target_pairs={{0,8},{8,0},{16,24},{24,16},{1,9},{9,1},{17,25},{25,17},{2,10},{10... | collective-permute-start | bytes 786440 | tf_op jit(solution)/shard_map/ppermute | solution.py:22
  6.3 0.7 fusion.4.slots
  7.0 12.8 %shard_map.59 = bf16[512,128,128]{2,1,0:T(8,128)(2,1)S(1)} custom-call(s32[256]{0:T(256)S(1)} %fusion.4.slots, bf16[256,128,128]{2,1,0:T(8,128)(2,1)} %values.1), custom_call_target="tpu_custom_call" | custom-call | bytes 25165824 | tf_op jit(solution)/shard_map/pallas_call | solution.py:49
  19.9 0.5 collective-permute-start.1
  20.4 2.3 %shard_map.62.refs_1_ = f32[4,512,256]{2,1,0:T(8,128)S(1)} custom-call(bf16[8,4,16,128,128]{4,3,2,1,0:T(8,128)(2,1)S(1)} %bitcast.2, bf16[512,256]{1,0:T(8,128)(2,1)S(1)} %copy-done, bf16[512,256]{1,0:T(8,128)(2,1)S(1)} %collective-permute-done.2.refs_1_, bf16[512,256]{1,0:T(8,128)(2,1)S(1)} %collective-permute-done.refs_2_), custom_call_target="tpu_custom_call" | custom-call | flops 2147483648 | bytes 8388608 | tf_op jit(solution)/shard_map/pallas_call | solution.py:303
  22.7 4.7 %collective-permute-done.1.refs_0_ = bf16[512,256]{1,0:T(8,128)(2,1)S(1)} collective-permute-done((bf16[512,256]{1,0:T(8,128)(2,1)S(1)}, bf16[512,256]{1,0:T(8,128)(2,1)S(1)}, u32[]{:S(2)}, u32[]{:S(2)}) %collective-permute-start.1) | collective-permute-done | bytes 262176 | tf_op jit(solution)/shard_map/ppermute | solution.py:22
  27.4 1.2 %shard_map.63 = f32[4,512,256]{2,1,0:T(8,128)S(1)} custom-call(bf16[8,4,16,128,128]{4,3,2,1,0:T(8,128)(2,1)S(1)} %bitcast.3, bf16[512,256]{1,0:T(8,128)(2,1)S(1)} %collective-permute-done.1.refs_0_, f32[4,512,256]{2,1,0:T(8,128)S(1)} %shard_map.62.refs_1_), custom_call_target="tpu_custom_call" | custom-call | flops 2147483648 | bytes 8388608 | tf_op jit(solution)/shard_map/pallas_call | solution.py:303
  28.7 2.3 %shard_map.60.refs_1_ = f32[4,512,256]{2,1,0:T(8,128)S(1)} custom-call(bf16[8,4,16,128,128]{4,3,2,1,0:T(8,128)(2,1)S(1)} %bitcast.4, bf16[512,256]{1,0:T(8,128)(2,1)S(1)} %copy-done, bf16[512,256]{1,0:T(8,128)(2,1)S(1)} %collective-permute-done.2.refs_1_, bf16[512,256]{1,0:T(8,128)(2,1)S(1)} %collective-permute-done.refs_2_), custom_call_target="tpu_custom_call" | custom-call | flops 2147483648 | bytes 8388608 | tf_op jit(solution)/shard_map/pallas_call | solution.py:303
  31.1 1.2 %shard_map.61.a_ref = f32[4,512,256]{2,1,0:T(8,128)S(1)} custom-call(bf16[8,4,16,128,128]{4,3,2,1,0:T(8,128)(2,1)S(1)} %bitcast.5, bf16[512,256]{1,0:T(8,128)(2,1)S(1)} %collective-permute-done.1.refs_0_, f32[4,512,256]{2,1,0:T(8,128)S(1)} %shard_map.60.refs_1_), custom_call_target="tpu_custom_call" | custom-call | flops 2147483648 | bytes 8388608 | tf_op jit(solution)/shard_map/pallas_call | solution.py:303
  32.3 0.6 collective-permute-done.3.b_ref
  32.9 0.7 shard_map.64
  33.6 1.6 %collective-permute-start.4 = (s16[528,256]{1,0:T(8,128)(2,1)S(1)}, s16[528,256]{1,0:T(8,128)(2,1)S(1)}, u32[]{:S(2)}, u32[]{:S(2)}) collective-permute-start(s16[528,256]{1,0:T(8,128)(2,1)S(1)} %get-tuple-element.14), channel_id=1, source_target_pairs={{0,2},{1,3},{2,0},{3,1},{4,6},{5,7},{6,4},{7,5},{8,10},{9,11},{10,... | collective-permute-start | bytes 811016 | tf_op jit(solution)/shard_map/ppermute | solution.py:22
  35.1 1.5 %collective-permute-start.5 = (s16[528,256]{1,0:T(8,128)(2,1)S(1)}, s16[528,256]{1,0:T(8,128)(2,1)S(1)}, u32[]{:S(2)}, u32[]{:S(2)}) collective-permute-start(s16[528,256]{1,0:T(8,128)(2,1)S(1)} %get-tuple-element.15), channel_id=1, source_target_pairs={{0,4},{1,5},{2,6},{3,7},{4,0},{5,1},{6,2},{7,3},{8,12},{9,13},{10,... | collective-permute-start | bytes 811016 | tf_op jit(solution)/shard_map/ppermute | solution.py:22
  36.6 0.5 collective-permute-start.6
  37.1 5.8 %collective-permute-done.4.refs_1_ = s16[528,256]{1,0:T(8,128)(2,1)S(1)} collective-permute-done((s16[528,256]{1,0:T(8,128)(2,1)S(1)}, s16[528,256]{1,0:T(8,128)(2,1)S(1)}, u32[]{:S(2)}, u32[]{:S(2)}) %collective-permute-start.4) | collective-permute-done | bytes 270368 | tf_op jit(solution)/shard_map/ppermute | solution.py:22
  42.9 6.2 %collective-permute-done.5.refs_2_ = s16[528,256]{1,0:T(8,128)(2,1)S(1)} collective-permute-done((s16[528,256]{1,0:T(8,128)(2,1)S(1)}, s16[528,256]{1,0:T(8,128)(2,1)S(1)}, u32[]{:S(2)}, u32[]{:S(2)}) %collective-permute-start.5) | collective-permute-done | bytes 270368 | tf_op jit(solution)/shard_map/ppermute | solution.py:22
  49.2 0.6 shard_map.65
  49.9 1.2 %collective-permute-done.7 = f32[136,128]{1,0:T(8,128)S(1)} collective-permute-done((f32[136,128]{1,0:T(8,128)S(1)}, f32[136,128]{1,0:T(8,128)S(1)}, u32[]{:S(2)}, u32[]{:S(2)}) %collective-permute-start.7) | collective-permute-done | bytes 69664 | tf_op jit(solution)/shard_map/ppermute | solution.py:22
  51.1 1.6 %collective-permute-start.10 = (f32[136,128]{1,0:T(8,128)S(1)}, f32[136,128]{1,0:T(8,128)S(1)}, u32[]{:S(2)}, u32[]{:S(2)}) collective-permute-start(f32[136,128]{1,0:T(8,128)S(1)} %add.71), channel_id=1, source_target_pairs={{0,6},{1,7},{2,4},{3,5},{4,2},{5,3},{6,0},{7,1},{8,14},{9,15},{10,... | collective-permute-start | bytes 208904 | tf_op jit(solution)/shard_map/ppermute | solution.py:22
  52.7 1.2 %collective-permute-start.9 = (f32[136,128]{1,0:T(8,128)S(1)}, f32[136,128]{1,0:T(8,128)S(1)}, u32[]{:S(2)}, u32[]{:S(2)}) collective-permute-start(f32[136,128]{1,0:T(8,128)S(1)} %add.71), channel_id=1, source_target_pairs={{0,4},{1,5},{2,6},{3,7},{4,0},{5,1},{6,2},{7,3},{8,12},{9,13},{10,... | collective-permute-start | bytes 208904 | tf_op jit(solution)/shard_map/ppermute | solution.py:22
  53.9 0.8 %collective-permute-start.8 = (f32[136,128]{1,0:T(8,128)S(1)}, f32[136,128]{1,0:T(8,128)S(1)}, u32[]{:S(2)}, u32[]{:S(2)}) collective-permute-start(f32[136,128]{1,0:T(8,128)S(1)} %add.71), channel_id=1, source_target_pairs={{0,2},{1,3},{2,0},{3,1},{4,6},{5,7},{6,4},{7,5},{8,10},{9,11},{10,... | collective-permute-start | bytes 208904 | tf_op jit(solution)/shard_map/ppermute | solution.py:22
  54.7 1.8 %collective-permute-done.10 = f32[136,128]{1,0:T(8,128)S(1)} collective-permute-done((f32[136,128]{1,0:T(8,128)S(1)}, f32[136,128]{1,0:T(8,128)S(1)}, u32[]{:S(2)}, u32[]{:S(2)}) %collective-permute-start.10) | collective-permute-done | bytes 69664 | tf_op jit(solution)/shard_map/ppermute | solution.py:22
  56.5 1.3 %collective-permute-done.9 = f32[136,128]{1,0:T(8,128)S(1)} collective-permute-done((f32[136,128]{1,0:T(8,128)S(1)}, f32[136,128]{1,0:T(8,128)S(1)}, u32[]{:S(2)}, u32[]{:S(2)}) %collective-permute-start.9) | collective-permute-done | bytes 69664 | tf_op jit(solution)/shard_map/ppermute | solution.py:22
  57.8 0.4 collective-permute-done.8
  58.2 1.3 %collective-permute-start.13 = (f32[136,128]{1,0:T(8,128)S(1)}, f32[136,128]{1,0:T(8,128)S(1)}, u32[]{:S(2)}, u32[]{:S(2)}) collective-permute-start(f32[136,128]{1,0:T(8,128)S(1)} %add_add_fusion.1), channel_id=1, source_target_pairs={{0,24},{8,16},{16,8},{24,0},{1,25},{9,17},{17,9},{25,1},{2,26},{10... | collective-permute-start | bytes 208904 | tf_op jit(solution)/shard_map/ppermute | solution.py:22
  59.5 0.7 collective-permute-start.12
  60.2 2.5 %collective-permute-start.11 = (f32[136,128]{1,0:T(8,128)S(1)}, f32[136,128]{1,0:T(8,128)S(1)}, u32[]{:S(2)}, u32[]{:S(2)}) collective-permute-start(f32[136,128]{1,0:T(8,128)S(1)} %add_add_fusion.1), channel_id=1, source_target_pairs={{0,8},{8,0},{16,24},{24,16},{1,9},{9,1},{17,25},{25,17},{2,10},{10... | collective-permute-start | bytes 208904 | tf_op jit(solution)/shard_map/ppermute | solution.py:22
  62.7 2.6 %collective-permute-done.13 = f32[136,128]{1,0:T(8,128)S(1)} collective-permute-done((f32[136,128]{1,0:T(8,128)S(1)}, f32[136,128]{1,0:T(8,128)S(1)}, u32[]{:S(2)}, u32[]{:S(2)}) %collective-permute-start.13) | collective-permute-done | bytes 69664 | tf_op jit(solution)/shard_map/ppermute | solution.py:22
  65.2 1.7 %collective-permute-done.12 = f32[136,128]{1,0:T(8,128)S(1)} collective-permute-done((f32[136,128]{1,0:T(8,128)S(1)}, f32[136,128]{1,0:T(8,128)S(1)}, u32[]{:S(2)}, u32[]{:S(2)}) %collective-permute-start.12) | collective-permute-done | bytes 69664 | tf_op jit(solution)/shard_map/ppermute | solution.py:22
  67.0 1.2 %collective-permute-done.14.other_ref = f32[136,128]{1,0:T(8,128)S(1)} collective-permute-done((f32[136,128]{1,0:T(8,128)S(1)}, f32[136,128]{1,0:T(8,128)S(1)}, u32[]{:S(2)}, u32[]{:S(2)}) %collective-permute-start.14) | collective-permute-done | bytes 69664 | tf_op jit(solution)/shard_map/ppermute | solution.py:22
  68.3 10.7 %shard_map.66 = (f32[512,256]{1,0:T(8,128)}, f32[256,256]{1,0:T(8,128)}) custom-call(s32[1]{0:T(128)} %bitcast.core, f32[136,128]{1,0:T(8,128)S(1)} %add_add_fusion.mine_ref, f32[136,128]{1,0:T(8,128)S(1)} %collective-permute-done.14.other_ref, f32[512,256]{1,0:T(8,128)S(1)} %get-tuple-element.19.s_ref), custom_call_target="tpu_custom_call" | custom-call | tf_op jit(solution)/shard_map/pallas_call | solution.py:409
  (12 shorter events, 0.3 us)
Async XLA Ops:
  0.6 19.2 %collective-permute-start = (bf16[512,256]{1,0:T(8,128)(2,1)}, bf16[512,256]{1,0:T(8,128)(2,1)S(1)}, u32[]{:S(2)}, u32[]{:S(2)}) collective-permute-start(bf16[512,256]{1,0:T(8,128)(2,1)} %refs_0_.3), channel_id=1, source_target_pairs={{0,16},{8,24},{16,0},{24,8},{1,17},{9,25},{17,1},{25,9},{2,18},{10... | collective-permute-start | bytes 786440 | tf_op jit(solution)/shard_map/ppermute | solution.py:22
  4.7 15.7 %collective-permute-start.2 = (bf16[512,256]{1,0:T(8,128)(2,1)}, bf16[512,256]{1,0:T(8,128)(2,1)S(1)}, u32[]{:S(2)}, u32[]{:S(2)}) collective-permute-start(bf16[512,256]{1,0:T(8,128)(2,1)} %refs_0_.3), channel_id=1, source_target_pairs={{0,8},{8,0},{16,24},{24,16},{1,9},{9,1},{17,25},{25,17},{2,10},{10... | collective-permute-start | bytes 786440 | tf_op jit(solution)/shard_map/ppermute | solution.py:22
  7.0 13.4 %copy-start = (bf16[512,256]{1,0:T(8,128)(2,1)S(1)}, bf16[512,256]{1,0:T(8,128)(2,1)}, u32[]{:S(2)}) copy-start(bf16[512,256]{1,0:T(8,128)(2,1)} %refs_0_.3) | copy-start | bytes 786436
  19.9 7.6 %collective-permute-start.1 = (bf16[512,256]{1,0:T(8,128)(2,1)S(1)}, bf16[512,256]{1,0:T(8,128)(2,1)S(1)}, u32[]{:S(2)}, u32[]{:S(2)}) collective-permute-start(bf16[512,256]{1,0:T(8,128)(2,1)S(1)} %collective-permute-done.refs_2_), channel_id=1, source_target_pairs={{0,8},{8,0},{16,24},{24,16},{1,9},{9,1},{17,25},{25,17},{2,10},{10... | collective-permute-start | bytes 786440 | tf_op jit(solution)/shard_map/ppermute | solution.py:22
  28.7 4.2 %collective-permute-start.3 = (f32[4,512,256]{2,1,0:T(8,128)S(1)}, f32[4,512,256]{2,1,0:T(8,128)S(1)}, u32[]{:S(2)}, u32[]{:S(2)}) collective-permute-start(f32[4,512,256]{2,1,0:T(8,128)S(1)} %shard_map.63), channel_id=1, source_target_pairs={{0,1},{1,0},{2,3},{3,2},{4,5},{5,4},{6,7},{7,6},{8,9},{9,8},{10,11... | collective-permute-start | bytes 6291464 | tf_op jit(solution)/shard_map/ppermute | solution.py:22
  33.6 9.4 %collective-permute-start.4 = (s16[528,256]{1,0:T(8,128)(2,1)S(1)}, s16[528,256]{1,0:T(8,128)(2,1)S(1)}, u32[]{:S(2)}, u32[]{:S(2)}) collective-permute-start(s16[528,256]{1,0:T(8,128)(2,1)S(1)} %get-tuple-element.14), channel_id=1, source_target_pairs={{0,2},{1,3},{2,0},{3,1},{4,6},{5,7},{6,4},{7,5},{8,10},{9,11},{10,... | collective-permute-start | bytes 811016 | tf_op jit(solution)/shard_map/ppermute | solution.py:22
  35.1 14.0 %collective-permute-start.5 = (s16[528,256]{1,0:T(8,128)(2,1)S(1)}, s16[528,256]{1,0:T(8,128)(2,1)S(1)}, u32[]{:S(2)}, u32[]{:S(2)}) collective-permute-start(s16[528,256]{1,0:T(8,128)(2,1)S(1)} %get-tuple-element.15), channel_id=1, source_target_pairs={{0,4},{1,5},{2,6},{3,7},{4,0},{5,1},{6,2},{7,3},{8,12},{9,13},{10,... | collective-permute-start | bytes 811016 | tf_op jit(solution)/shard_map/ppermute | solution.py:22
  36.6 12.5 %collective-permute-start.6 = (s16[528,256]{1,0:T(8,128)(2,1)S(1)}, s16[528,256]{1,0:T(8,128)(2,1)S(1)}, u32[]{:S(2)}, u32[]{:S(2)}) collective-permute-start(s16[528,256]{1,0:T(8,128)(2,1)S(1)} %get-tuple-element.16), channel_id=1, source_target_pairs={{0,6},{1,7},{2,4},{3,5},{4,2},{5,3},{6,0},{7,1},{8,14},{9,15},{10,... | collective-permute-start | bytes 811016 | tf_op jit(solution)/shard_map/ppermute | solution.py:22
  49.8 1.3 %collective-permute-start.7 = (f32[136,128]{1,0:T(8,128)S(1)}, f32[136,128]{1,0:T(8,128)S(1)}, u32[]{:S(2)}, u32[]{:S(2)}) collective-permute-start(f32[136,128]{1,0:T(8,128)S(1)} %get-tuple-element.18), channel_id=1, source_target_pairs={{0,1},{1,0},{2,3},{3,2},{4,5},{5,4},{6,7},{7,6},{8,9},{9,8},{10,11... | collective-permute-start | bytes 208904 | tf_op jit(solution)/shard_map/ppermute | solution.py:22
  51.1 5.4 %collective-permute-start.10 = (f32[136,128]{1,0:T(8,128)S(1)}, f32[136,128]{1,0:T(8,128)S(1)}, u32[]{:S(2)}, u32[]{:S(2)}) collective-permute-start(f32[136,128]{1,0:T(8,128)S(1)} %add.71), channel_id=1, source_target_pairs={{0,6},{1,7},{2,4},{3,5},{4,2},{5,3},{6,0},{7,1},{8,14},{9,15},{10,... | collective-permute-start | bytes 208904 | tf_op jit(solution)/shard_map/ppermute | solution.py:22
  52.7 5.1 %collective-permute-start.9 = (f32[136,128]{1,0:T(8,128)S(1)}, f32[136,128]{1,0:T(8,128)S(1)}, u32[]{:S(2)}, u32[]{:S(2)}) collective-permute-start(f32[136,128]{1,0:T(8,128)S(1)} %add.71), channel_id=1, source_target_pairs={{0,4},{1,5},{2,6},{3,7},{4,0},{5,1},{6,2},{7,3},{8,12},{9,13},{10,... | collective-permute-start | bytes 208904 | tf_op jit(solution)/shard_map/ppermute | solution.py:22
  53.9 4.3 %collective-permute-start.8 = (f32[136,128]{1,0:T(8,128)S(1)}, f32[136,128]{1,0:T(8,128)S(1)}, u32[]{:S(2)}, u32[]{:S(2)}) collective-permute-start(f32[136,128]{1,0:T(8,128)S(1)} %add.71), channel_id=1, source_target_pairs={{0,2},{1,3},{2,0},{3,1},{4,6},{5,7},{6,4},{7,5},{8,10},{9,11},{10,... | collective-permute-start | bytes 208904 | tf_op jit(solution)/shard_map/ppermute | solution.py:22
  58.2 7.0 %collective-permute-start.13 = (f32[136,128]{1,0:T(8,128)S(1)}, f32[136,128]{1,0:T(8,128)S(1)}, u32[]{:S(2)}, u32[]{:S(2)}) collective-permute-start(f32[136,128]{1,0:T(8,128)S(1)} %add_add_fusion.1), channel_id=1, source_target_pairs={{0,24},{8,16},{16,8},{24,0},{1,25},{9,17},{17,9},{25,1},{2,26},{10... | collective-permute-start | bytes 208904 | tf_op jit(solution)/shard_map/ppermute | solution.py:22
  59.5 7.5 %collective-permute-start.12 = (f32[136,128]{1,0:T(8,128)S(1)}, f32[136,128]{1,0:T(8,128)S(1)}, u32[]{:S(2)}, u32[]{:S(2)}) collective-permute-start(f32[136,128]{1,0:T(8,128)S(1)} %add_add_fusion.1), channel_id=1, source_target_pairs={{0,16},{8,24},{16,0},{24,8},{1,17},{9,25},{17,1},{25,9},{2,18},{10... | collective-permute-start | bytes 208904 | tf_op jit(solution)/shard_map/ppermute | solution.py:22
  60.2 6.8 %collective-permute-start.11 = (f32[136,128]{1,0:T(8,128)S(1)}, f32[136,128]{1,0:T(8,128)S(1)}, u32[]{:S(2)}, u32[]{:S(2)}) collective-permute-start(f32[136,128]{1,0:T(8,128)S(1)} %add_add_fusion.1), channel_id=1, source_target_pairs={{0,8},{8,0},{16,24},{24,16},{1,9},{9,1},{17,25},{25,17},{2,10},{10... | collective-permute-start | bytes 208904 | tf_op jit(solution)/shard_map/ppermute | solution.py:22
  67.0 1.3 %collective-permute-start.14 = (f32[136,128]{1,0:T(8,128)S(1)}, f32[136,128]{1,0:T(8,128)S(1)}, u32[]{:S(2)}, u32[]{:S(2)}) collective-permute-start(f32[136,128]{1,0:T(8,128)S(1)} %add_add_fusion.mine_ref), channel_id=1, source_target_pairs={{0,1},{1,0},{2,3},{3,2},{4,5},{5,4},{6,7},{7,6},{8,9},{9,8},{10,11... | collective-permute-start | bytes 208904 | tf_op jit(solution)/shard_map/ppermute | solution.py:22

commit v4 on v3

--- a/solution.py
+++ b/solution.py
@@ -22,25 +22,18 @@
     return lax.ppermute(value, axis, [(i, i ^ mask) for i in range(size)])
 
 
-def scatter_kernel(slots, values, dense, taken, sem):
-    n_slots = dense.shape[0]
-    n_blocks = values.shape[0]
-
-    @pl.loop(0, n_slots)
+def scatter_kernel(slots, values, dense, sem):
+    step = math.gcd(8, math.gcd(dense.shape[0], values.shape[0]))
+
+    @pl.loop(0, dense.shape[0] // step)
     def _(s):
-        taken[s] = 0
-
-    @pl.loop(0, n_blocks)
+        dense[pl.ds(s * step, step)] = jnp.zeros((step, *dense.shape[1:]), dense.dtype)
+
+    @pl.loop(0, values.shape[0] // step)
     def _(b):
-        slot = slots[b]
-        taken[slot] = 1
-        pltpu.make_async_copy(values.at[b], dense.at[slot], sem).start()
-
-    @pl.loop(0, n_slots)
-    def _(s):
-        @pl.when(taken[s] == 0)
-        def _():
-            dense[s] = jnp.zeros(dense.shape[1:], dense.dtype)
+        for u in range(step):
+            block = b * step + u
+            pltpu.make_async_copy(values.at[block], dense.at[slots[block]], sem).start()
 
     pltpu.make_async_copy(values, values, sem).wait()
 
@@ -54,7 +47,7 @@
             grid=(),
             in_specs=[pl.BlockSpec(memory_space=pltpu.HBM)],
             out_specs=pl.BlockSpec(memory_space=pltpu.VMEM),
-            scratch_shapes=[pltpu.SMEM((n_slots,), jnp.int32), pltpu.SemaphoreType.DMA],
+            scratch_shapes=[pltpu.SemaphoreType.DMA],
         ),
         compiler_params=pltpu.CompilerParams(vmem_limit_bytes=4 * 2**20),
         cost_estimate=pl.CostEstimate(flops=0, bytes_accessed=24 * 2**20, transcendentals=0),
@@ -80,7 +73,8 @@
 def product_kernel(first, shards, a_ref, *refs):
     *in_refs, o_ref = refs
     total = dense_dot(a_ref, in_refs, shards, pl.program_id(0) + first)
-    o_ref[0] = total + in_refs[-1][0] if len(in_refs) > len(shards) else total
+    added = in_refs[len(shards) :]
+    o_ref[0] = total + added[0][0] if added else total
 
 
 def quantize(total, o_ref):
@@ -108,18 +102,16 @@
     return jnp.concatenate(parts, axis=0)
 
 
-def code_kernel(a_ref, b_ref, own_ref, *o_refs):
+def code_kernel(a_ref, b_ref, *o_refs):
     total = a_ref[0] + b_ref[0]
-    i = pl.program_id(0)
     for j, o_ref in enumerate(o_refs):
 
-        @pl.when(i == j)
+        @pl.when(pl.program_id(0) == j)
         def _(o_ref=o_ref):
-            quantize(total, o_ref)
-
-    @pl.when(i == len(o_refs))
-    def _():
-        own_ref[...] = total
+            if o_ref.dtype == jnp.int16:
+                quantize(total, o_ref)
+            else:
+                o_ref[...] = total
 
 
 def reduce_kernel(core, *refs):
@@ -166,6 +158,13 @@
 
 def factor(gram):
     n = gram.shape[0]
+    eye = lax.broadcasted_iota(jnp.int32, (n, n), 0) == lax.broadcasted_iota(jnp.int32, (n, n), 1)
+    picked = jnp.where(eye, gram, 0.0)
+    diagonal = jnp.sum(picked, axis=0, keepdims=True)
+    inverse_row = lax.rsqrt(diagonal)
+    inverse_col = lax.rsqrt(jnp.sum(picked, axis=1, keepdims=True))
+    gram = gram * inverse_row * inverse_col
+
     sub = lax.broadcasted_iota(jnp.int32, (8, n), 0)
     lane = lax.broadcasted_iota(jnp.int32, (8, n), 1)
     left = [gram[8 * i : 8 * i + 8] for i in range(n // 8)]
@@ -181,22 +180,27 @@
                 t: [jnp.broadcast_to(left[t][:, 8 * b + k : 8 * b + k + 1], (8, n)) for k in range(8)]
                 for t in range(b, last)
             }
-            for k in range(8):
-                pivot = row(cols[b][k], k)
-                root = lax.rsqrt(pivot)
-                root = root * (1.5 - 0.5 * pivot * root * root)
-                mult = {t: cols[t][k] * root for t in range(b, last)}
-                for j in range(k + 1, 8):
-                    other = row(mult[b], j)
+            for k in range(0, 8, 2):
+                p, q, r = row(cols[b][k], k), row(cols[b][k], k + 1), row(cols[b][k + 1], k + 1)
+                root_p = lax.rsqrt(p)
+                ratio = q * root_p
+                det = p * r - q * q
+                root_r = lax.rsqrt(det) * (p * root_p)
+                one = {t: cols[t][k] * root_p for t in range(b, last)}
+                two = {t: (cols[t][k + 1] - one[t] * ratio) * root_r for t in range(b, last)}
+                for j in range(k + 2, 8):
+                    u, v = row(one[b], j), row(two[b], j)
                     for t in range(b, last):
-                        cols[t][j] = cols[t][j] - mult[t] * other
-                top_left, top_right = row(left[b], k) * root, row(right[b], k) * root
-                below = jnp.where(sub > k, mult[b], 0.0)
-                left[b] = jnp.where(sub == k, top_left, left[b] - below * top_left)
-                right[b] = jnp.where(sub == k, top_right, right[b] - below * top_right)
-                for t in range(b + 1, last):
-                    left[t] = left[t] - mult[t] * top_left
-                    right[t] = right[t] - mult[t] * top_right
+                        cols[t][j] = cols[t][j] - one[t] * u - two[t] * v
+                below_one = jnp.where(sub > k + 1, one[b], 0.0)
+                below_two = jnp.where(sub > k + 1, two[b], 0.0)
+                for side in (left, right):
+                    top = row(side[b], k) * root_p
+                    low = (row(side[b], k + 1) - top * ratio) * root_r
+                    rest = side[b] - below_one * top - below_two * low
+                    side[b] = jnp.where(sub == k, top, jnp.where(sub == k + 1, low, rest))
+                    for t in range(b + 1, last):
+                        side[t] = side[t] - one[t] * top - two[t] * low
         if last < n // 8:
             u = split(jnp.concatenate(left[first:last], axis=0), 3)
             v = split(jnp.concatenate(right[first:last], axis=0), 3)
@@ -210,7 +214,7 @@
                 left[t] = left[t] - change[8 * t : 8 * t + 8, :n]
                 right[t] = right[t] - change[8 * t : 8 * t + 8, n:]
     upper = jnp.concatenate([jnp.where(lane >= sub + 8 * i, x, 0.0) for i, x in enumerate(left)], axis=0)
-    return upper, jnp.concatenate(right, axis=0)
+    return upper * (diagonal * inverse_row), jnp.concatenate(right, axis=0) * inverse_row
 
 
 def dot3(a, b, dims):
@@ -279,7 +283,7 @@
     me = lax.axis_index("col")
     owner = local_rows // group
     peer_core = (owner + me) % 2
-    near = (owner // 2) ^ (me // 2)
+    near = ((owner // 2 ^ me // 2) + chips - 1) % chips
     place = ((1 - peer_core) * chips + near) * group + local_rows % group
     shard = (local_cols // group) ^ lax.axis_index("row")
     slots = place * grid_cols + shard * group + local_cols % group
@@ -298,35 +302,40 @@
 
     held = pl.BlockSpec(memory_space=pltpu.VMEM)
     r_block = (1, shard_rows, width)
-    def product(first, chosen, *added):
-        block = pl.BlockSpec(r_block, lambda i: (i, 0, 0))
+    def block(first):
+        return pl.BlockSpec(r_block, lambda i: (i + first, 0, 0))
+
+    def product(first, count, chosen, *added):
         return pl.pallas_call(
             functools.partial(product_kernel, first, chosen),
-            grid=(chips,),
-            in_specs=[held] * (len(chosen) + 1) + [block] * len(added),
-            out_specs=block,
-            out_shape=jax.ShapeDtypeStruct((chips, shard_rows, width), jnp.float32),
+            grid=(count,),
+            in_specs=[held] * (len(chosen) + 1) + [block(first)] * len(added),
+            out_specs=block(0),
+            out_shape=jax.ShapeDtypeStruct((count, shard_rows, width), jnp.float32),
             compiler_params=params,
-            cost_estimate=cost(chips),
+            cost_estimate=cost(count),
         )(dense, *[shards[k] for k in chosen], *added)
 
-    far, near = product(0, early), product(chips, early)
-    if late:
-        far = product(0, late, far)
-    peer_sum = exchange(far, "col", 1)
-    near_sum = product(chips, late, near) if late else near
+    first_sum = product(0, 2 * chips, early)
+    parts = [(0, chips // 2), (chips // 2, chips - chips // 2)]
+    peer = [exchange(product(at, n, late, first_sum), "col", 1) for at, n in parts]
+    near = [product(chips + at, n, late, first_sum) for at, n in parts]
     sent = jax.ShapeDtypeStruct((shard_rows + 16, width), jnp.int16)
-    own_last = pl.BlockSpec(r_block, lambda i: ((i + 1) % chips, 0, 0))
-    own_shape = (shard_rows, width)
-    own, *coded = pl.pallas_call(
-        code_kernel,
-        grid=(chips,),
-        in_specs=[own_last, own_last],
-        out_specs=[whole(own_shape)] + [whole(sent.shape)] * (chips - 1),
-        out_shape=[jax.ShapeDtypeStruct(own_shape, jnp.float32)] + [sent] * (chips - 1),
-        compiler_params=params,
-    )(near_sum, peer_sum)
-    return [own] + [exchange(q, "col", 2 * (i + 1)) for i, q in enumerate(coded)]
+    kept = jax.ShapeDtypeStruct((shard_rows, width), jnp.float32)
+    terms = []
+    for (at, n), mine, theirs in zip(parts, near, peer):
+        shapes = [kept if at + i == chips - 1 else sent for i in range(n)]
+        done = pl.pallas_call(
+            code_kernel,
+            grid=(n,),
+            in_specs=[block(0), block(0)],
+            out_specs=[whole(x.shape) for x in shapes],
+            out_shape=shapes,
+            compiler_params=params,
+        )(mine, theirs)
+        for i, x in enumerate(done):
+            terms.append(x if x.dtype == jnp.float32 else exchange(x, "col", 2 * (at + i + 1)))
+    return terms
 
 
 def tile_product(sketch_blocks, block_values, local_rows, local_cols, tile_rows):

time: 79.2 us -> 74.8 us (0.944)
  Pallas kernels: 31.9 us -> 24.1 us
  starting transfers between devices: 18 us -> 19.8 us
  waiting for transfers between devices: 27.6 us -> 29.3 us
    pallas_call x1, Pallas kernels: 12.8 us -> 6.21 us  [scatter_blocks(): pl.pallas_call(scatter_kernel, out_shape=pltpu.VMEM((n_slots, BS, BS), va...]
    ppermute x15 -> x16, starting transfers between devices: 18 us -> 19.8 us  [exchange(): return lax.ppermute(value, axis, [(i, i ^ mask) for i in range(size)])]
    ppermute x15 -> x16, waiting for transfers between devices: 27.6 us -> 29.3 us  [exchange(): return lax.ppermute(value, axis, [(i, i ^ mask) for i in range(size)])]
    pallas_call x1, Pallas kernels: 10.7 us -> 9.6 us  [on_device(): pl.pallas_call(functools.partial(tail_kernel, 1.0 / order_total), grid_sp...]
    pallas_call x5 -> x7, Pallas kernels: 7.75 us -> 7.66 us  [the longest x5 7.08 us: product(): pl.pallas_call(functools.partial(product_kernel, first, chosen), grid=(co...]
  transfers between devices with their start and end apart: 15 -> 16, of which waited for: 11 -> 13; matrix products, arithmetic and copies ran while one was open for 1% -> 1% of each run, Pallas kernels for 24% -> 18%
where the time goes in v4:
time: 74.8 us; the launch traced here: 74.7 us
  waiting for transfers between devices  29.3 us (39%)
  Pallas kernels  24.1 us (32%)
  starting transfers between devices  19.8 us (26%)
  other arithmetic  0.78 us (1%)
  between operations  0.75 us (1%)
    ppermute x16, waiting for transfers between devices, exchange(): return lax.ppermute(value, axis, [(i, i ^ mask) for i in range(size)])  29.3 us
    ppermute x16, starting transfers between devices, exchange(): return lax.ppermute(value, axis, [(i, i ^ mask) for i in range(size)])  19.8 us
    pallas_call x1, Pallas kernels, on_device(): pl.pallas_call(functools.partial(tail_kernel, 1.0 / order_total), grid_sp...  9.6 us
    pallas_call x5, Pallas kernels, product(): pl.pallas_call(functools.partial(product_kernel, first, chosen), grid=(co...  7.08 us
    pallas_call x1, Pallas kernels, scatter_blocks(): pl.pallas_call(scatter_kernel, out_shape=pltpu.VMEM((n_slots, BS, BS), va...  6.21 us
  transfers between devices with their start and end apart: 16, of which 13 were waited for; matrix products, arithmetic and copies ran while one was open for 1% of the time, Pallas kernels for 18%

profile of v4, /device:TPU:0, one launch (start us, length us, event | category | flops | bytes accessed | tf_op | source)
XLA Modules:
  0.0 74.7 jit_solution(2593816078325953388)
XLA Ops:
  0.6 4.1 %collective-permute-start = (bf16[512,256]{1,0:T(8,128)(2,1)}, bf16[512,256]{1,0:T(8,128)(2,1)S(1)}, u32[]{:S(2)}, u32[]{:S(2)}) collective-permute-start(bf16[512,256]{1,0:T(8,128)(2,1)} %refs_0_.1), channel_id=1, source_target_pairs={{0,16},{8,24},{16,0},{24,8},{1,17},{9,25},{17,1},{25,9},{2,18},{10... | collective-permute-start | bytes 786440 | tf_op jit(solution)/shard_map/ppermute | solution.py:22
  4.7 1.6 %collective-permute-start.2 = (bf16[512,256]{1,0:T(8,128)(2,1)}, bf16[512,256]{1,0:T(8,128)(2,1)S(1)}, u32[]{:S(2)}, u32[]{:S(2)}) collective-permute-start(bf16[512,256]{1,0:T(8,128)(2,1)} %refs_0_.1), channel_id=1, source_target_pairs={{0,8},{8,0},{16,24},{24,16},{1,9},{9,1},{17,25},{25,17},{2,10},{10... | collective-permute-start | bytes 786440 | tf_op jit(solution)/shard_map/ppermute | solution.py:22
  6.3 0.7 fusion.4.slots
  7.0 6.2 %shard_map.59 = bf16[512,128,128]{2,1,0:T(8,128)(2,1)S(1)} custom-call(s32[256]{0:T(256)S(1)} %fusion.4.slots, bf16[256,128,128]{2,1,0:T(8,128)(2,1)} %values.1), custom_call_target="tpu_custom_call" | custom-call | bytes 25165824 | tf_op jit(solution)/shard_map/pallas_call | solution.py:42
  13.3 3.7 %collective-permute-done.refs_2_ = bf16[512,256]{1,0:T(8,128)(2,1)S(1)} collective-permute-done((bf16[512,256]{1,0:T(8,128)(2,1)}, bf16[512,256]{1,0:T(8,128)(2,1)S(1)}, u32[]{:S(2)}, u32[]{:S(2)}) %collective-permute-start) | collective-permute-done | bytes 262176 | tf_op jit(solution)/shard_map/ppermute | solution.py:22
  17.0 0.7 collective-permute-start.1
  17.7 4.6 %shard_map.60.refs_1_ = f32[8,512,256]{2,1,0:T(8,128)S(1)} custom-call(bf16[8,4,16,128,128]{4,3,2,1,0:T(8,128)(2,1)S(1)} %bitcast.2, bf16[512,256]{1,0:T(8,128)(2,1)S(1)} %copy-done, bf16[512,256]{1,0:T(8,128)(2,1)S(1)} %collective-permute-done.2.refs_1_, bf16[512,256]{1,0:T(8,128)(2,1)S(1)} %collective-permute-done.refs_2_), custom_call_target="tpu_custom_call" | custom-call | flops 4294967296 | bytes 16777216 | tf_op jit(solution)/shard_map/pallas_call | solution.py:309
  22.3 2.1 %collective-permute-done.1.refs_0_ = bf16[512,256]{1,0:T(8,128)(2,1)S(1)} collective-permute-done((bf16[512,256]{1,0:T(8,128)(2,1)S(1)}, bf16[512,256]{1,0:T(8,128)(2,1)S(1)}, u32[]{:S(2)}, u32[]{:S(2)}) %collective-permute-start.1) | collective-permute-done | bytes 262176 | tf_op jit(solution)/shard_map/ppermute | solution.py:22
  24.4 0.6 shard_map.65
  25.1 0.6 shard_map.62
  25.7 0.5 collective-permute-start.3
  26.3 0.6 shard_map.64.a_ref
  26.9 0.6 shard_map.61.a_ref
  28.0 2.3 %collective-permute-start.7 = (s16[528,256]{1,0:T(8,128)(2,1)S(1)}, s16[528,256]{1,0:T(8,128)(2,1)S(1)}, u32[]{:S(2)}, u32[]{:S(2)}) collective-permute-start(s16[528,256]{1,0:T(8,128)(2,1)S(1)} %get-tuple-element.15), channel_id=1, source_target_pairs={{0,6},{1,7},{2,4},{3,5},{4,2},{5,3},{6,0},{7,1},{8,14},{9,15},{10,... | collective-permute-start | bytes 811016 | tf_op jit(solution)/shard_map/ppermute | solution.py:22
  30.3 0.3 shard_map.63
  30.6 0.6 collective-permute-start.4
  31.2 1.2 %collective-permute-start.5 = (s16[528,256]{1,0:T(8,128)(2,1)S(1)}, s16[528,256]{1,0:T(8,128)(2,1)S(1)}, u32[]{:S(2)}, u32[]{:S(2)}) collective-permute-start(s16[528,256]{1,0:T(8,128)(2,1)S(1)} %get-tuple-element.14), channel_id=1, source_target_pairs={{0,4},{1,5},{2,6},{3,7},{4,0},{5,1},{6,2},{7,3},{8,12},{9,13},{10,... | collective-permute-start | bytes 811016 | tf_op jit(solution)/shard_map/ppermute | solution.py:22
  32.4 5.9 %collective-permute-done.7.refs_2_ = s16[528,256]{1,0:T(8,128)(2,1)S(1)} collective-permute-done((s16[528,256]{1,0:T(8,128)(2,1)S(1)}, s16[528,256]{1,0:T(8,128)(2,1)S(1)}, u32[]{:S(2)}, u32[]{:S(2)}) %collective-permute-start.7) | collective-permute-done | bytes 270368 | tf_op jit(solution)/shard_map/ppermute | solution.py:22
  38.3 4.8 %collective-permute-done.4.refs_0_ = s16[528,256]{1,0:T(8,128)(2,1)S(1)} collective-permute-done((s16[528,256]{1,0:T(8,128)(2,1)S(1)}, s16[528,256]{1,0:T(8,128)(2,1)S(1)}, u32[]{:S(2)}, u32[]{:S(2)}) %collective-permute-start.4) | collective-permute-done | bytes 270368 | tf_op jit(solution)/shard_map/ppermute | solution.py:22
  43.3 0.6 shard_map.67
  44.0 1.2 %collective-permute-done.8 = f32[136,128]{1,0:T(8,128)S(1)} collective-permute-done((f32[136,128]{1,0:T(8,128)S(1)}, f32[136,128]{1,0:T(8,128)S(1)}, u32[]{:S(2)}, u32[]{:S(2)}) %collective-permute-start.8) | collective-permute-done | bytes 69664 | tf_op jit(solution)/shard_map/ppermute | solution.py:22
  45.3 1.4 %collective-permute-start.10 = (f32[136,128]{1,0:T(8,128)S(1)}, f32[136,128]{1,0:T(8,128)S(1)}, u32[]{:S(2)}, u32[]{:S(2)}) collective-permute-start(f32[136,128]{1,0:T(8,128)S(1)} %add.80), channel_id=1, source_target_pairs={{0,4},{1,5},{2,6},{3,7},{4,0},{5,1},{6,2},{7,3},{8,12},{9,13},{10,... | collective-permute-start | bytes 208904 | tf_op jit(solution)/shard_map/ppermute | solution.py:22
  46.6 1.5 %collective-permute-start.11 = (f32[136,128]{1,0:T(8,128)S(1)}, f32[136,128]{1,0:T(8,128)S(1)}, u32[]{:S(2)}, u32[]{:S(2)}) collective-permute-start(f32[136,128]{1,0:T(8,128)S(1)} %add.80), channel_id=1, source_target_pairs={{0,6},{1,7},{2,4},{3,5},{4,2},{5,3},{6,0},{7,1},{8,14},{9,15},{10,... | collective-permute-start | bytes 208904 | tf_op jit(solution)/shard_map/ppermute | solution.py:22
  48.2 0.7 collective-permute-start.9
  48.8 0.8 %collective-permute-done.10 = f32[136,128]{1,0:T(8,128)S(1)} collective-permute-done((f32[136,128]{1,0:T(8,128)S(1)}, f32[136,128]{1,0:T(8,128)S(1)}, u32[]{:S(2)}, u32[]{:S(2)}) %collective-permute-start.10) | collective-permute-done | bytes 69664 | tf_op jit(solution)/shard_map/ppermute | solution.py:22
  49.7 2.8 %collective-permute-done.11 = f32[136,128]{1,0:T(8,128)S(1)} collective-permute-done((f32[136,128]{1,0:T(8,128)S(1)}, f32[136,128]{1,0:T(8,128)S(1)}, u32[]{:S(2)}, u32[]{:S(2)}) %collective-permute-start.11) | collective-permute-done | bytes 69664 | tf_op jit(solution)/shard_map/ppermute | solution.py:22
  52.6 1.7 %collective-permute-start.12 = (f32[136,128]{1,0:T(8,128)S(1)}, f32[136,128]{1,0:T(8,128)S(1)}, u32[]{:S(2)}, u32[]{:S(2)}) collective-permute-start(f32[136,128]{1,0:T(8,128)S(1)} %add_add_fusion.1), channel_id=1, source_target_pairs={{0,8},{8,0},{16,24},{24,16},{1,9},{9,1},{17,25},{25,17},{2,10},{10... | collective-permute-start | bytes 208904 | tf_op jit(solution)/shard_map/ppermute | solution.py:22
  54.3 3.3 %collective-permute-start.13 = (f32[136,128]{1,0:T(8,128)S(1)}, f32[136,128]{1,0:T(8,128)S(1)}, u32[]{:S(2)}, u32[]{:S(2)}) collective-permute-start(f32[136,128]{1,0:T(8,128)S(1)} %add_add_fusion.1), channel_id=1, source_target_pairs={{0,16},{8,24},{16,0},{24,8},{1,17},{9,25},{17,1},{25,9},{2,18},{10... | collective-permute-start | bytes 208904 | tf_op jit(solution)/shard_map/ppermute | solution.py:22
  57.6 4.4 %collective-permute-done.13 = f32[136,128]{1,0:T(8,128)S(1)} collective-permute-done((f32[136,128]{1,0:T(8,128)S(1)}, f32[136,128]{1,0:T(8,128)S(1)}, u32[]{:S(2)}, u32[]{:S(2)}) %collective-permute-start.13) | collective-permute-done | bytes 69664 | tf_op jit(solution)/shard_map/ppermute | solution.py:22
  62.0 1.7 %collective-permute-done.14 = f32[136,128]{1,0:T(8,128)S(1)} collective-permute-done((f32[136,128]{1,0:T(8,128)S(1)}, f32[136,128]{1,0:T(8,128)S(1)}, u32[]{:S(2)}, u32[]{:S(2)}) %collective-permute-start.14) | collective-permute-done | bytes 69664 | tf_op jit(solution)/shard_map/ppermute | solution.py:22
  63.8 1.2 %collective-permute-done.15.other_ref = f32[136,128]{1,0:T(8,128)S(1)} collective-permute-done((f32[136,128]{1,0:T(8,128)S(1)}, f32[136,128]{1,0:T(8,128)S(1)}, u32[]{:S(2)}, u32[]{:S(2)}) %collective-permute-start.15) | collective-permute-done | bytes 69664 | tf_op jit(solution)/shard_map/ppermute | solution.py:22
  65.1 9.6 %shard_map.68 = (f32[512,256]{1,0:T(8,128)}, f32[256,256]{1,0:T(8,128)}) custom-call(s32[1]{0:T(128)} %bitcast.core, f32[136,128]{1,0:T(8,128)S(1)} %add_add_fusion.mine_ref, f32[136,128]{1,0:T(8,128)S(1)} %collective-permute-done.15.other_ref, f32[512,256]{1,0:T(8,128)S(1)} %get-tuple-element.19.s_ref), custom_call_target="tpu_custom_call" | custom-call | tf_op jit(solution)/shard_map/pallas_call | solution.py:418
  (16 shorter events, 1.0 us)
Async XLA Ops:
  0.6 16.3 %collective-permute-start = (bf16[512,256]{1,0:T(8,128)(2,1)}, bf16[512,256]{1,0:T(8,128)(2,1)S(1)}, u32[]{:S(2)}, u32[]{:S(2)}) collective-permute-start(bf16[512,256]{1,0:T(8,128)(2,1)} %refs_0_.1), channel_id=1, source_target_pairs={{0,16},{8,24},{16,0},{24,8},{1,17},{9,25},{17,1},{25,9},{2,18},{10... | collective-permute-start | bytes 786440 | tf_op jit(solution)/shard_map/ppermute | solution.py:22
  4.7 13.0 %collective-permute-start.2 = (bf16[512,256]{1,0:T(8,128)(2,1)}, bf16[512,256]{1,0:T(8,128)(2,1)S(1)}, u32[]{:S(2)}, u32[]{:S(2)}) collective-permute-start(bf16[512,256]{1,0:T(8,128)(2,1)} %refs_0_.1), channel_id=1, source_target_pairs={{0,8},{8,0},{16,24},{24,16},{1,9},{9,1},{17,25},{25,17},{2,10},{10... | collective-permute-start | bytes 786440 | tf_op jit(solution)/shard_map/ppermute | solution.py:22
  7.0 10.7 %copy-start = (bf16[512,256]{1,0:T(8,128)(2,1)S(1)}, bf16[512,256]{1,0:T(8,128)(2,1)}, u32[]{:S(2)}) copy-start(bf16[512,256]{1,0:T(8,128)(2,1)} %refs_0_.1) | copy-start | bytes 786436
  17.0 7.4 %collective-permute-start.1 = (bf16[512,256]{1,0:T(8,128)(2,1)S(1)}, bf16[512,256]{1,0:T(8,128)(2,1)S(1)}, u32[]{:S(2)}, u32[]{:S(2)}) collective-permute-start(bf16[512,256]{1,0:T(8,128)(2,1)S(1)} %collective-permute-done.refs_2_), channel_id=1, source_target_pairs={{0,8},{8,0},{16,24},{24,16},{1,9},{9,1},{17,25},{25,17},{2,10},{10... | collective-permute-start | bytes 786440 | tf_op jit(solution)/shard_map/ppermute | solution.py:22
  25.0 2.7 %collective-permute-start.6 = (f32[2,512,256]{2,1,0:T(8,128)S(1)}, f32[2,512,256]{2,1,0:T(8,128)S(1)}, u32[]{:S(2)}, u32[]{:S(2)}) collective-permute-start(f32[2,512,256]{2,1,0:T(8,128)S(1)} %shard_map.65), channel_id=1, source_target_pairs={{0,1},{1,0},{2,3},{3,2},{4,5},{5,4},{6,7},{7,6},{8,9},{9,8},{10,11... | collective-permute-start | bytes 3145736 | tf_op jit(solution)/shard_map/ppermute | solution.py:22
  25.7 4.6 %collective-permute-start.3 = (f32[2,512,256]{2,1,0:T(8,128)S(1)}, f32[2,512,256]{2,1,0:T(8,128)S(1)}, u32[]{:S(2)}, u32[]{:S(2)}) collective-permute-start(f32[2,512,256]{2,1,0:T(8,128)S(1)} %shard_map.62), channel_id=1, source_target_pairs={{0,1},{1,0},{2,3},{3,2},{4,5},{5,4},{6,7},{7,6},{8,9},{9,8},{10,11... | collective-permute-start | bytes 3145736 | tf_op jit(solution)/shard_map/ppermute | solution.py:22
  28.0 10.3 %collective-permute-start.7 = (s16[528,256]{1,0:T(8,128)(2,1)S(1)}, s16[528,256]{1,0:T(8,128)(2,1)S(1)}, u32[]{:S(2)}, u32[]{:S(2)}) collective-permute-start(s16[528,256]{1,0:T(8,128)(2,1)S(1)} %get-tuple-element.15), channel_id=1, source_target_pairs={{0,6},{1,7},{2,4},{3,5},{4,2},{5,3},{6,0},{7,1},{8,14},{9,15},{10,... | collective-permute-start | bytes 811016 | tf_op jit(solution)/shard_map/ppermute | solution.py:22
  30.6 12.5 %collective-permute-start.4 = (s16[528,256]{1,0:T(8,128)(2,1)S(1)}, s16[528,256]{1,0:T(8,128)(2,1)S(1)}, u32[]{:S(2)}, u32[]{:S(2)}) collective-permute-start(s16[528,256]{1,0:T(8,128)(2,1)S(1)} %get-tuple-element.13), channel_id=1, source_target_pairs={{0,2},{1,3},{2,0},{3,1},{4,6},{5,7},{6,4},{7,5},{8,10},{9,11},{10,... | collective-permute-start | bytes 811016 | tf_op jit(solution)/shard_map/ppermute | solution.py:22
  31.2 12.1 %collective-permute-start.5 = (s16[528,256]{1,0:T(8,128)(2,1)S(1)}, s16[528,256]{1,0:T(8,128)(2,1)S(1)}, u32[]{:S(2)}, u32[]{:S(2)}) collective-permute-start(s16[528,256]{1,0:T(8,128)(2,1)S(1)} %get-tuple-element.14), channel_id=1, source_target_pairs={{0,4},{1,5},{2,6},{3,7},{4,0},{5,1},{6,2},{7,3},{8,12},{9,13},{10,... | collective-permute-start | bytes 811016 | tf_op jit(solution)/shard_map/ppermute | solution.py:22
  43.9 1.3 %collective-permute-start.8 = (f32[136,128]{1,0:T(8,128)S(1)}, f32[136,128]{1,0:T(8,128)S(1)}, u32[]{:S(2)}, u32[]{:S(2)}) collective-permute-start(f32[136,128]{1,0:T(8,128)S(1)} %get-tuple-element.18), channel_id=1, source_target_pairs={{0,1},{1,0},{2,3},{3,2},{4,5},{5,4},{6,7},{7,6},{8,9},{9,8},{10,11... | collective-permute-start | bytes 208904 | tf_op jit(solution)/shard_map/ppermute | solution.py:22
  45.3 4.4 %collective-permute-start.10 = (f32[136,128]{1,0:T(8,128)S(1)}, f32[136,128]{1,0:T(8,128)S(1)}, u32[]{:S(2)}, u32[]{:S(2)}) collective-permute-start(f32[136,128]{1,0:T(8,128)S(1)} %add.80), channel_id=1, source_target_pairs={{0,4},{1,5},{2,6},{3,7},{4,0},{5,1},{6,2},{7,3},{8,12},{9,13},{10,... | collective-permute-start | bytes 208904 | tf_op jit(solution)/shard_map/ppermute | solution.py:22
  46.6 5.8 %collective-permute-start.11 = (f32[136,128]{1,0:T(8,128)S(1)}, f32[136,128]{1,0:T(8,128)S(1)}, u32[]{:S(2)}, u32[]{:S(2)}) collective-permute-start(f32[136,128]{1,0:T(8,128)S(1)} %add.80), channel_id=1, source_target_pairs={{0,6},{1,7},{2,4},{3,5},{4,2},{5,3},{6,0},{7,1},{8,14},{9,15},{10,... | collective-permute-start | bytes 208904 | tf_op jit(solution)/shard_map/ppermute | solution.py:22
  48.2 4.4 %collective-permute-start.9 = (f32[136,128]{1,0:T(8,128)S(1)}, f32[136,128]{1,0:T(8,128)S(1)}, u32[]{:S(2)}, u32[]{:S(2)}) collective-permute-start(f32[136,128]{1,0:T(8,128)S(1)} %add.80), channel_id=1, source_target_pairs={{0,2},{1,3},{2,0},{3,1},{4,6},{5,7},{6,4},{7,5},{8,10},{9,11},{10,... | collective-permute-start | bytes 208904 | tf_op jit(solution)/shard_map/ppermute | solution.py:22
  52.6 5.0 %collective-permute-start.12 = (f32[136,128]{1,0:T(8,128)S(1)}, f32[136,128]{1,0:T(8,128)S(1)}, u32[]{:S(2)}, u32[]{:S(2)}) collective-permute-start(f32[136,128]{1,0:T(8,128)S(1)} %add_add_fusion.1), channel_id=1, source_target_pairs={{0,8},{8,0},{16,24},{24,16},{1,9},{9,1},{17,25},{25,17},{2,10},{10... | collective-permute-start | bytes 208904 | tf_op jit(solution)/shard_map/ppermute | solution.py:22
  54.3 7.7 %collective-permute-start.13 = (f32[136,128]{1,0:T(8,128)S(1)}, f32[136,128]{1,0:T(8,128)S(1)}, u32[]{:S(2)}, u32[]{:S(2)}) collective-permute-start(f32[136,128]{1,0:T(8,128)S(1)} %add_add_fusion.1), channel_id=1, source_target_pairs={{0,16},{8,24},{16,0},{24,8},{1,17},{9,25},{17,1},{25,9},{2,18},{10... | collective-permute-start | bytes 208904 | tf_op jit(solution)/shard_map/ppermute | solution.py:22
  57.6 6.1 %collective-permute-start.14 = (f32[136,128]{1,0:T(8,128)S(1)}, f32[136,128]{1,0:T(8,128)S(1)}, u32[]{:S(2)}, u32[]{:S(2)}) collective-permute-start(f32[136,128]{1,0:T(8,128)S(1)} %add_add_fusion.1), channel_id=1, source_target_pairs={{0,24},{8,16},{16,8},{24,0},{1,25},{9,17},{17,9},{25,1},{2,26},{10... | collective-permute-start | bytes 208904 | tf_op jit(solution)/shard_map/ppermute | solution.py:22
  63.7 1.3 %collective-permute-start.15 = (f32[136,128]{1,0:T(8,128)S(1)}, f32[136,128]{1,0:T(8,128)S(1)}, u32[]{:S(2)}, u32[]{:S(2)}) collective-permute-start(f32[136,128]{1,0:T(8,128)S(1)} %add_add_fusion.mine_ref), channel_id=1, source_target_pairs={{0,1},{1,0},{2,3},{3,2},{4,5},{5,4},{6,7},{7,6},{8,9},{9,8},{10,11... | collective-permute-start | bytes 208904 | tf_op jit(solution)/shard_map/ppermute | solution.py:22

commit v5 on v4

--- a/solution.py
+++ b/solution.py
@@ -54,14 +54,14 @@
     )(slots, pltpu.with_memory_space_constraint(values, pltpu.HBM))
 
 
-def dense_dot(a_ref, x_refs, shards, chunk):
-    group = a_ref.shape[1]
+def dense_dot(a_ref, x_refs, starts, chunk):
     total = None
-    for k, x_ref in zip(shards, x_refs):
+    for start, x_ref in zip(starts, x_refs):
+        span = x_ref.shape[0] // BS
         lhs = jnp.concatenate(
             [
-                jnp.concatenate([a_ref[chunk, r, k * group + c] for c in range(group)], axis=1)
-                for r in range(group)
+                jnp.concatenate([a_ref[chunk, r, start + c] for c in range(span)], axis=1)
+                for r in range(a_ref.shape[1])
             ],
             axis=0,
         )
@@ -70,10 +70,10 @@
     return total
 
 
-def product_kernel(first, shards, a_ref, *refs):
+def product_kernel(first, starts, a_ref, *refs):
     *in_refs, o_ref = refs
-    total = dense_dot(a_ref, in_refs, shards, pl.program_id(0) + first)
-    added = in_refs[len(shards) :]
+    total = dense_dot(a_ref, in_refs, starts, pl.program_id(0) + first)
+    added = in_refs[len(starts) :]
     o_ref[0] = total + added[0][0] if added else total
 
 
@@ -264,15 +264,16 @@
     return pl.BlockSpec(shape, lambda *_: (0,) * len(shape))
 
 
-def gather_row(value, ready):
+def gather_row(value):
     bits = lax.axis_size("row").bit_length() - 1
-    shards = {0: value}
-    for bit in reversed(range(bits)):
-        for k, v in list(shards.items()):
-            if bit == 0 and k:
-                v, ready = lax.optimization_barrier((v, ready))
-            shards[k | 1 << bit] = exchange(v, "row", 1 << bit)
-    return [shards[k] for k in range(2**bits)], ready
+    half = value.shape[0] // 2
+    shards = {0: [value], 1: [exchange(value, "row", 1)]}
+    for bit in reversed(range(1, bits)):
+        for k, pieces in list(shards.items()):
+            if k != 1:
+                pieces = pieces if k else [value[:half], value[half:]]
+                shards[k | 1 << bit] = [exchange(p, "row", 1 << bit) for p in pieces]
+    return shards
 
 
 def dense_sketch(gaussian_sketch, block_values, local_rows, local_cols, grid_rows, grid_cols):
@@ -289,9 +290,8 @@
     slots = place * grid_cols + shard * group + local_cols % group
     dense = scatter_blocks(slots, block_values, grid_rows * grid_cols)
     dense = dense.reshape(2 * chips, group, grid_cols, BS, BS)
-    shards, dense = gather_row(gaussian_sketch, dense)
-    late = [k for k in range(len(shards)) if k % 2 and k > 1]
-    early = [k for k in range(len(shards)) if k not in late]
+    shards = gather_row(gaussian_sketch)
+    relayed = [k for k in shards if k > 1]
 
     params = pltpu.CompilerParams(vmem_limit_bytes=12 * 2**20)
     flops = 2 * shard_rows * grid_cols * BS * width
@@ -305,21 +305,38 @@
     def block(first):
         return pl.BlockSpec(r_block, lambda i: (i + first, 0, 0))
 
-    def product(first, count, chosen, *added):
+    def product(first, count, pieces, *added):
+        starts, refs = zip(*pieces)
         return pl.pallas_call(
-            functools.partial(product_kernel, first, chosen),
+            functools.partial(product_kernel, first, starts),
             grid=(count,),
-            in_specs=[held] * (len(chosen) + 1) + [block(first)] * len(added),
+            in_specs=[held] * (len(refs) + 1) + [block(first)] * len(added),
             out_specs=block(0),
             out_shape=jax.ShapeDtypeStruct((count, shard_rows, width), jnp.float32),
             compiler_params=params,
             cost_estimate=cost(count),
-        )(dense, *[shards[k] for k in chosen], *added)
-
-    first_sum = product(0, 2 * chips, early)
+        )(dense, *refs, *added)
+
+    def placed(k, h, piece):
+        return (k * group + (h * group // 2), piece)
+
+    late, sums, now = [], [], [placed(k, 0, shards[k][0]) for k in (0, 1)]
+    for h in range(2 if relayed else 1):
+        for k in relayed:
+            piece, dense, *sums = lax.optimization_barrier((shards[k][h], dense, *sums))
+            late.append(placed(k + 1, h, exchange(piece, "row", 1)))
+            now.append(placed(k, h, piece))
+        sums = [product(0, 2 * chips, now, *sums)]
+        now = []
+    first_sum = sums[0]
     parts = [(0, chips // 2), (chips // 2, chips - chips // 2)]
-    peer = [exchange(product(at, n, late, first_sum), "col", 1) for at, n in parts]
-    near = [product(chips + at, n, late, first_sum) for at, n in parts]
+    def finish(first, count):
+        if late:
+            return product(first, count, late, first_sum)
+        return first_sum[first : first + count]
+
+    peer = [exchange(finish(at, n), "col", 1) for at, n in parts]
+    near = [finish(chips + at, n) for at, n in parts]
     sent = jax.ShapeDtypeStruct((shard_rows + 16, width), jnp.int16)
     kept = jax.ShapeDtypeStruct((shard_rows, width), jnp.float32)
     terms = []
@@ -364,7 +381,10 @@
 
 
 def direct_sum(value, axis, low_bit, bits):
-    terms = [value] + [exchange(value, axis, mask << low_bit) for mask in range(1, 2**bits)]
+    terms = {0: value}
+    for mask in reversed(range(1, 2**bits)):
+        terms[mask] = exchange(value, axis, mask << low_bit)
+    terms = [terms[mask] for mask in range(2**bits)]
     while len(terms) > 1:
         terms = [a + b for a, b in zip(terms[0::2], terms[1::2])]
     return terms[0]

time: 74.8 us -> 76 us (1.016)
  waiting for transfers between devices: 29.3 us -> 26.5 us
  starting transfers between devices: 19.8 us -> 21.3 us
  Pallas kernels: 24.1 us -> 25.5 us
  local copies, waits for them, and re-layouts: 0.01 us -> 1 us
    ppermute x16 -> x18, waiting for transfers between devices: 29.3 us -> 26.5 us  [exchange(): return lax.ppermute(value, axis, [(i, i ^ mask) for i in range(size)])]
    ppermute x16 -> x18, starting transfers between devices: 19.8 us -> 21.3 us  [exchange(): return lax.ppermute(value, axis, [(i, i ^ mask) for i in range(size)])]
    pallas_call x5 -> x6, Pallas kernels: 7.08 us -> 8.45 us  [product(): pl.pallas_call(functools.partial(product_kernel, first, starts), grid=(co...]
    slice x0 -> x1, local copies, waits for them, and re-layouts: none -> 0.99 us  [gather_row(): pieces = pieces if k else [value[:half], value[half:]]]
  transfers between devices with their start and end apart: 16 -> 18, of which waited for: 13 -> 11; matrix products, arithmetic and copies ran while one was open for 1% -> 2% of each run, Pallas kernels for 18% -> 19%
where the time goes in v5:
time: 76 us; the launch traced here: 75.8 us
  waiting for transfers between devices  26.5 us (35%)
  Pallas kernels  25.5 us (34%)
  starting transfers between devices  21.3 us (28%)
  local copies, waits for them, and re-layouts  1 us (1%)
  between operations  0.79 us (1%)
  other arithmetic  0.77 us (1%)
    ppermute x18, waiting for transfers between devices, exchange(): return lax.ppermute(value, axis, [(i, i ^ mask) for i in range(size)])  26.5 us
    ppermute x18, starting transfers between devices, exchange(): return lax.ppermute(value, axis, [(i, i ^ mask) for i in range(size)])  21.3 us
    pallas_call x1, Pallas kernels, on_device(): pl.pallas_call(functools.partial(tail_kernel, 1.0 / order_total), grid_sp...  9.6 us
    pallas_call x6, Pallas kernels, product(): pl.pallas_call(functools.partial(product_kernel, first, starts), grid=(co...  8.45 us
    pallas_call x1, Pallas kernels, scatter_blocks(): pl.pallas_call(scatter_kernel, out_shape=pltpu.VMEM((n_slots, BS, BS), va...  6.21 us
  transfers between devices with their start and end apart: 18, of which 11 were waited for; matrix products, arithmetic and copies ran while one was open for 2% of the time, Pallas kernels for 19%

profile of v5, /device:TPU:0, one launch (start us, length us, event | category | flops | bytes accessed | tf_op | source)
XLA Modules:
  0.0 75.8 jit_solution(11137971551595289680)
XLA Ops:
  0.6 3.1 %collective-permute-start.2 = (bf16[512,256]{1,0:T(8,128)(2,1)}, bf16[512,256]{1,0:T(8,128)(2,1)S(1)}, u32[]{:S(2)}, u32[]{:S(2)}) collective-permute-start(bf16[512,256]{1,0:T(8,128)(2,1)} %refs_0_.1), channel_id=1, source_target_pairs={{0,8},{8,0},{16,24},{24,16},{1,9},{9,1},{17,25},{25,17},{2,10},{10... | collective-permute-start | bytes 786440 | tf_op jit(solution)/shard_map/ppermute | solution.py:22
  3.7 1.0 %fusion.7 = (bf16[256,256]{1,0:T(8,128)(2,1)S(1)}, bf16[256,256]{1,0:T(8,128)(2,1)S(1)}) fusion(bf16[512,256]{1,0:T(8,128)(2,1)} %refs_0_.1), kind=kLoop, calls=%fused_computation.29 | loop fusion | bytes 524288 | tf_op jit(solution)/shard_map/slice | solution.py:274
  4.7 2.7 %collective-permute-start.1 = (bf16[256,256]{1,0:T(8,128)(2,1)S(1)}, bf16[256,256]{1,0:T(8,128)(2,1)S(1)}, u32[]{:S(2)}, u32[]{:S(2)}) collective-permute-start(bf16[256,256]{1,0:T(8,128)(2,1)S(1)} %get-tuple-element.26), channel_id=1, source_target_pairs={{0,16},{8,24},{16,0},{24,8},{1,17},{9,25},{17,1},{25,9},{2,18},{10... | collective-permute-start | bytes 393224 | tf_op jit(solution)/shard_map/ppermute | solution.py:22
  7.7 0.7 fusion.4.slots
  8.4 6.2 %shard_map.59 = bf16[512,128,128]{2,1,0:T(8,128)(2,1)S(1)} custom-call(s32[256]{0:T(256)S(1)} %fusion.4.slots, bf16[256,128,128]{2,1,0:T(8,128)(2,1)} %values.1), custom_call_target="tpu_custom_call" | custom-call | bytes 25165824 | tf_op jit(solution)/shard_map/pallas_call | solution.py:42
  14.7 2.7 %collective-permute-start.3 = (bf16[256,256]{1,0:T(8,128)(2,1)S(1)}, bf16[256,256]{1,0:T(8,128)(2,1)S(1)}, u32[]{:S(2)}, u32[]{:S(2)}) collective-permute-start(bf16[256,256]{1,0:T(8,128)(2,1)S(1)} %collective-permute-done.1.refs_2_), channel_id=1, source_target_pairs={{0,8},{8,0},{16,24},{24,16},{1,9},{9,1},{17,25},{25,17},{2,10},{10... | collective-permute-start | bytes 393224 | tf_op jit(solution)/shard_map/ppermute | solution.py:22
  17.4 4.1 %shard_map.60.refs_1_ = f32[8,512,256]{2,1,0:T(8,128)S(1)} custom-call(bf16[8,4,16,128,128]{4,3,2,1,0:T(8,128)(2,1)S(1)} %bitcast.2, bf16[512,256]{1,0:T(8,128)(2,1)S(1)} %copy-done, bf16[512,256]{1,0:T(8,128)(2,1)S(1)} %collective-permute-done.2.refs_1_, bf16[256,256]{1,0:T(8,128)(2,1)S(1)} %collective-permute-done.1.refs_2_), custom_call_target="tpu_custom_call" | custom-call | flops 4294967296 | bytes 16777216 | tf_op jit(solution)/shard_map/pallas_call | solution.py:310
  21.6 1.9 %shard_map.61.refs_2_ = f32[8,512,256]{2,1,0:T(8,128)S(1)} custom-call(bf16[8,4,16,128,128]{4,3,2,1,0:T(8,128)(2,1)S(1)} %bitcast.3, bf16[256,256]{1,0:T(8,128)(2,1)S(1)} %collective-permute-done.refs_0_, f32[8,512,256]{2,1,0:T(8,128)S(1)} %shard_map.60.refs_1_), custom_call_target="tpu_custom_call" | custom-call | flops 4294967296 | bytes 16777216 | tf_op jit(solution)/shard_map/pallas_call | solution.py:310
  23.5 3.1 %collective-permute-done.4.refs_1_ = bf16[256,256]{1,0:T(8,128)(2,1)S(1)} collective-permute-done((bf16[256,256]{1,0:T(8,128)(2,1)S(1)}, bf16[256,256]{1,0:T(8,128)(2,1)S(1)}, u32[]{:S(2)}, u32[]{:S(2)}) %collective-permute-start.4) | collective-permute-done | bytes 131104 | tf_op jit(solution)/shard_map/ppermute | solution.py:22
  26.6 0.6 shard_map.63
  27.3 0.6 shard_map.66
  28.4 0.6 shard_map.65.a_ref
  29.1 0.6 shard_map.62.a_ref
  30.2 1.6 %collective-permute-start.6 = (s16[528,256]{1,0:T(8,128)(2,1)S(1)}, s16[528,256]{1,0:T(8,128)(2,1)S(1)}, u32[]{:S(2)}, u32[]{:S(2)}) collective-permute-start(s16[528,256]{1,0:T(8,128)(2,1)S(1)} %get-tuple-element.19), channel_id=1, source_target_pairs={{0,2},{1,3},{2,0},{3,1},{4,6},{5,7},{6,4},{7,5},{8,10},{9,11},{10,... | collective-permute-start | bytes 811016 | tf_op jit(solution)/shard_map/ppermute | solution.py:22
  31.8 1.5 %collective-permute-start.7 = (s16[528,256]{1,0:T(8,128)(2,1)S(1)}, s16[528,256]{1,0:T(8,128)(2,1)S(1)}, u32[]{:S(2)}, u32[]{:S(2)}) collective-permute-start(s16[528,256]{1,0:T(8,128)(2,1)S(1)} %get-tuple-element.20), channel_id=1, source_target_pairs={{0,4},{1,5},{2,6},{3,7},{4,0},{5,1},{6,2},{7,3},{8,12},{9,13},{10,... | collective-permute-start | bytes 811016 | tf_op jit(solution)/shard_map/ppermute | solution.py:22
  33.6 0.6 collective-permute-start.9
  34.2 5.4 %collective-permute-done.6.refs_0_ = s16[528,256]{1,0:T(8,128)(2,1)S(1)} collective-permute-done((s16[528,256]{1,0:T(8,128)(2,1)S(1)}, s16[528,256]{1,0:T(8,128)(2,1)S(1)}, u32[]{:S(2)}, u32[]{:S(2)}) %collective-permute-start.6) | collective-permute-done | bytes 270368 | tf_op jit(solution)/shard_map/ppermute | solution.py:22
  39.6 6.2 %collective-permute-done.7.refs_1_ = s16[528,256]{1,0:T(8,128)(2,1)S(1)} collective-permute-done((s16[528,256]{1,0:T(8,128)(2,1)S(1)}, s16[528,256]{1,0:T(8,128)(2,1)S(1)}, u32[]{:S(2)}, u32[]{:S(2)}) %collective-permute-start.7) | collective-permute-done | bytes 270368 | tf_op jit(solution)/shard_map/ppermute | solution.py:22
  45.8 0.6 shard_map.68
  46.6 1.2 %collective-permute-done.10 = f32[136,128]{1,0:T(8,128)S(1)} collective-permute-done((f32[136,128]{1,0:T(8,128)S(1)}, f32[136,128]{1,0:T(8,128)S(1)}, u32[]{:S(2)}, u32[]{:S(2)}) %collective-permute-start.10) | collective-permute-done | bytes 69664 | tf_op jit(solution)/shard_map/ppermute | solution.py:22
  47.8 1.6 %collective-permute-start.13 = (f32[136,128]{1,0:T(8,128)S(1)}, f32[136,128]{1,0:T(8,128)S(1)}, u32[]{:S(2)}, u32[]{:S(2)}) collective-permute-start(f32[136,128]{1,0:T(8,128)S(1)} %add.80), channel_id=1, source_target_pairs={{0,6},{1,7},{2,4},{3,5},{4,2},{5,3},{6,0},{7,1},{8,14},{9,15},{10,... | collective-permute-start | bytes 208904 | tf_op jit(solution)/shard_map/ppermute | solution.py:22
  49.4 1.2 %collective-permute-start.12 = (f32[136,128]{1,0:T(8,128)S(1)}, f32[136,128]{1,0:T(8,128)S(1)}, u32[]{:S(2)}, u32[]{:S(2)}) collective-permute-start(f32[136,128]{1,0:T(8,128)S(1)} %add.80), channel_id=1, source_target_pairs={{0,4},{1,5},{2,6},{3,7},{4,0},{5,1},{6,2},{7,3},{8,12},{9,13},{10,... | collective-permute-start | bytes 208904 | tf_op jit(solution)/shard_map/ppermute | solution.py:22
  50.6 0.8 %collective-permute-start.11 = (f32[136,128]{1,0:T(8,128)S(1)}, f32[136,128]{1,0:T(8,128)S(1)}, u32[]{:S(2)}, u32[]{:S(2)}) collective-permute-start(f32[136,128]{1,0:T(8,128)S(1)} %add.80), channel_id=1, source_target_pairs={{0,2},{1,3},{2,0},{3,1},{4,6},{5,7},{6,4},{7,5},{8,10},{9,11},{10,... | collective-permute-start | bytes 208904 | tf_op jit(solution)/shard_map/ppermute | solution.py:22
  51.4 1.8 %collective-permute-done.13 = f32[136,128]{1,0:T(8,128)S(1)} collective-permute-done((f32[136,128]{1,0:T(8,128)S(1)}, f32[136,128]{1,0:T(8,128)S(1)}, u32[]{:S(2)}, u32[]{:S(2)}) %collective-permute-start.13) | collective-permute-done | bytes 69664 | tf_op jit(solution)/shard_map/ppermute | solution.py:22
  53.2 1.3 %collective-permute-done.12 = f32[136,128]{1,0:T(8,128)S(1)} collective-permute-done((f32[136,128]{1,0:T(8,128)S(1)}, f32[136,128]{1,0:T(8,128)S(1)}, u32[]{:S(2)}, u32[]{:S(2)}) %collective-permute-start.12) | collective-permute-done | bytes 69664 | tf_op jit(solution)/shard_map/ppermute | solution.py:22
  54.9 3.0 %collective-permute-start.16 = (f32[136,128]{1,0:T(8,128)S(1)}, f32[136,128]{1,0:T(8,128)S(1)}, u32[]{:S(2)}, u32[]{:S(2)}) collective-permute-start(f32[136,128]{1,0:T(8,128)S(1)} %add_add_fusion.1), channel_id=1, source_target_pairs={{0,24},{8,16},{16,8},{24,0},{1,25},{9,17},{17,9},{25,1},{2,26},{10... | collective-permute-start | bytes 208904 | tf_op jit(solution)/shard_map/ppermute | solution.py:22
  57.9 0.6 collective-permute-start.15
  58.5 0.9 %collective-permute-start.14 = (f32[136,128]{1,0:T(8,128)S(1)}, f32[136,128]{1,0:T(8,128)S(1)}, u32[]{:S(2)}, u32[]{:S(2)}) collective-permute-start(f32[136,128]{1,0:T(8,128)S(1)} %add_add_fusion.1), channel_id=1, source_target_pairs={{0,8},{8,0},{16,24},{24,16},{1,9},{9,1},{17,25},{25,17},{2,10},{10... | collective-permute-start | bytes 208904 | tf_op jit(solution)/shard_map/ppermute | solution.py:22
  59.4 1.9 %collective-permute-done.16 = f32[136,128]{1,0:T(8,128)S(1)} collective-permute-done((f32[136,128]{1,0:T(8,128)S(1)}, f32[136,128]{1,0:T(8,128)S(1)}, u32[]{:S(2)}, u32[]{:S(2)}) %collective-permute-start.16) | collective-permute-done | bytes 69664 | tf_op jit(solution)/shard_map/ppermute | solution.py:22
  61.3 3.6 %collective-permute-done.15 = f32[136,128]{1,0:T(8,128)S(1)} collective-permute-done((f32[136,128]{1,0:T(8,128)S(1)}, f32[136,128]{1,0:T(8,128)S(1)}, u32[]{:S(2)}, u32[]{:S(2)}) %collective-permute-start.15) | collective-permute-done | bytes 69664 | tf_op jit(solution)/shard_map/ppermute | solution.py:22
  65.0 1.2 %collective-permute-done.17.other_ref = f32[136,128]{1,0:T(8,128)S(1)} collective-permute-done((f32[136,128]{1,0:T(8,128)S(1)}, f32[136,128]{1,0:T(8,128)S(1)}, u32[]{:S(2)}, u32[]{:S(2)}) %collective-permute-start.17) | collective-permute-done | bytes 69664 | tf_op jit(solution)/shard_map/ppermute | solution.py:22
  66.2 9.6 %shard_map.69 = (f32[512,256]{1,0:T(8,128)}, f32[256,256]{1,0:T(8,128)}) custom-call(s32[1]{0:T(128)} %bitcast.core, f32[136,128]{1,0:T(8,128)S(1)} %add_add_fusion.mine_ref, f32[136,128]{1,0:T(8,128)S(1)} %collective-permute-done.17.other_ref, f32[512,256]{1,0:T(8,128)S(1)} %get-tuple-element.25.s_ref), custom_call_target="tpu_custom_call" | custom-call | tf_op jit(solution)/shard_map/pallas_call | solution.py:438
  (22 shorter events, 2.4 us)
Async XLA Ops:
  0.6 16.8 %collective-permute-start.2 = (bf16[512,256]{1,0:T(8,128)(2,1)}, bf16[512,256]{1,0:T(8,128)(2,1)S(1)}, u32[]{:S(2)}, u32[]{:S(2)}) collective-permute-start(bf16[512,256]{1,0:T(8,128)(2,1)} %refs_0_.1), channel_id=1, source_target_pairs={{0,8},{8,0},{16,24},{24,16},{1,9},{9,1},{17,25},{25,17},{2,10},{10... | collective-permute-start | bytes 786440 | tf_op jit(solution)/shard_map/ppermute | solution.py:22
  4.7 9.9 %collective-permute-start.1 = (bf16[256,256]{1,0:T(8,128)(2,1)S(1)}, bf16[256,256]{1,0:T(8,128)(2,1)S(1)}, u32[]{:S(2)}, u32[]{:S(2)}) collective-permute-start(bf16[256,256]{1,0:T(8,128)(2,1)S(1)} %get-tuple-element.26), channel_id=1, source_target_pairs={{0,16},{8,24},{16,0},{24,8},{1,17},{9,25},{17,1},{25,9},{2,18},{10... | collective-permute-start | bytes 393224 | tf_op jit(solution)/shard_map/ppermute | solution.py:22
  7.4 14.2 %collective-permute-start = (bf16[256,256]{1,0:T(8,128)(2,1)S(1)}, bf16[256,256]{1,0:T(8,128)(2,1)S(1)}, u32[]{:S(2)}, u32[]{:S(2)}) collective-permute-start(bf16[256,256]{1,0:T(8,128)(2,1)S(1)} %get-tuple-element.27), channel_id=1, source_target_pairs={{0,16},{8,24},{16,0},{24,8},{1,17},{9,25},{17,1},{25,9},{2,18},{10... | collective-permute-start | bytes 393224 | tf_op jit(solution)/shard_map/ppermute | solution.py:22
  8.4 9.0 %copy-start = (bf16[512,256]{1,0:T(8,128)(2,1)S(1)}, bf16[512,256]{1,0:T(8,128)(2,1)}, u32[]{:S(2)}) copy-start(bf16[512,256]{1,0:T(8,128)(2,1)} %refs_0_.1) | copy-start | bytes 786436
  14.7 8.8 %collective-permute-start.3 = (bf16[256,256]{1,0:T(8,128)(2,1)S(1)}, bf16[256,256]{1,0:T(8,128)(2,1)S(1)}, u32[]{:S(2)}, u32[]{:S(2)}) collective-permute-start(bf16[256,256]{1,0:T(8,128)(2,1)S(1)} %collective-permute-done.1.refs_2_), channel_id=1, source_target_pairs={{0,8},{8,0},{16,24},{24,16},{1,9},{9,1},{17,25},{25,17},{2,10},{10... | collective-permute-start | bytes 393224 | tf_op jit(solution)/shard_map/ppermute | solution.py:22
  21.5 5.0 %collective-permute-start.4 = (bf16[256,256]{1,0:T(8,128)(2,1)S(1)}, bf16[256,256]{1,0:T(8,128)(2,1)S(1)}, u32[]{:S(2)}, u32[]{:S(2)}) collective-permute-start(bf16[256,256]{1,0:T(8,128)(2,1)S(1)} %collective-permute-done.refs_0_), channel_id=1, source_target_pairs={{0,8},{8,0},{16,24},{24,16},{1,9},{9,1},{17,25},{25,17},{2,10},{10... | collective-permute-start | bytes 393224 | tf_op jit(solution)/shard_map/ppermute | solution.py:22
  27.2 2.7 %collective-permute-start.5 = (f32[2,512,256]{2,1,0:T(8,128)S(1)}, f32[2,512,256]{2,1,0:T(8,128)S(1)}, u32[]{:S(2)}, u32[]{:S(2)}) collective-permute-start(f32[2,512,256]{2,1,0:T(8,128)S(1)} %shard_map.63), channel_id=1, source_target_pairs={{0,1},{1,0},{2,3},{3,2},{4,5},{5,4},{6,7},{7,6},{8,9},{9,8},{10,11... | collective-permute-start | bytes 3145736 | tf_op jit(solution)/shard_map/ppermute | solution.py:22
  27.9 5.4 %collective-permute-start.8 = (f32[2,512,256]{2,1,0:T(8,128)S(1)}, f32[2,512,256]{2,1,0:T(8,128)S(1)}, u32[]{:S(2)}, u32[]{:S(2)}) collective-permute-start(f32[2,512,256]{2,1,0:T(8,128)S(1)} %shard_map.66), channel_id=1, source_target_pairs={{0,1},{1,0},{2,3},{3,2},{4,5},{5,4},{6,7},{7,6},{8,9},{9,8},{10,11... | collective-permute-start | bytes 3145736 | tf_op jit(solution)/shard_map/ppermute | solution.py:22
  30.2 9.4 %collective-permute-start.6 = (s16[528,256]{1,0:T(8,128)(2,1)S(1)}, s16[528,256]{1,0:T(8,128)(2,1)S(1)}, u32[]{:S(2)}, u32[]{:S(2)}) collective-permute-start(s16[528,256]{1,0:T(8,128)(2,1)S(1)} %get-tuple-element.19), channel_id=1, source_target_pairs={{0,2},{1,3},{2,0},{3,1},{4,6},{5,7},{6,4},{7,5},{8,10},{9,11},{10,... | collective-permute-start | bytes 811016 | tf_op jit(solution)/shard_map/ppermute | solution.py:22
  31.8 14.0 %collective-permute-start.7 = (s16[528,256]{1,0:T(8,128)(2,1)S(1)}, s16[528,256]{1,0:T(8,128)(2,1)S(1)}, u32[]{:S(2)}, u32[]{:S(2)}) collective-permute-start(s16[528,256]{1,0:T(8,128)(2,1)S(1)} %get-tuple-element.20), channel_id=1, source_target_pairs={{0,4},{1,5},{2,6},{3,7},{4,0},{5,1},{6,2},{7,3},{8,12},{9,13},{10,... | collective-permute-start | bytes 811016 | tf_op jit(solution)/shard_map/ppermute | solution.py:22
  33.6 12.2 %collective-permute-start.9 = (s16[528,256]{1,0:T(8,128)(2,1)S(1)}, s16[528,256]{1,0:T(8,128)(2,1)S(1)}, u32[]{:S(2)}, u32[]{:S(2)}) collective-permute-start(s16[528,256]{1,0:T(8,128)(2,1)S(1)} %get-tuple-element.21), channel_id=1, source_target_pairs={{0,6},{1,7},{2,4},{3,5},{4,2},{5,3},{6,0},{7,1},{8,14},{9,15},{10,... | collective-permute-start | bytes 811016 | tf_op jit(solution)/shard_map/ppermute | solution.py:22
  46.5 1.3 %collective-permute-start.10 = (f32[136,128]{1,0:T(8,128)S(1)}, f32[136,128]{1,0:T(8,128)S(1)}, u32[]{:S(2)}, u32[]{:S(2)}) collective-permute-start(f32[136,128]{1,0:T(8,128)S(1)} %get-tuple-element.24), channel_id=1, source_target_pairs={{0,1},{1,0},{2,3},{3,2},{4,5},{5,4},{6,7},{7,6},{8,9},{9,8},{10,11... | collective-permute-start | bytes 208904 | tf_op jit(solution)/shard_map/ppermute | solution.py:22
  47.8 5.4 %collective-permute-start.13 = (f32[136,128]{1,0:T(8,128)S(1)}, f32[136,128]{1,0:T(8,128)S(1)}, u32[]{:S(2)}, u32[]{:S(2)}) collective-permute-start(f32[136,128]{1,0:T(8,128)S(1)} %add.80), channel_id=1, source_target_pairs={{0,6},{1,7},{2,4},{3,5},{4,2},{5,3},{6,0},{7,1},{8,14},{9,15},{10,... | collective-permute-start | bytes 208904 | tf_op jit(solution)/shard_map/ppermute | solution.py:22
  49.4 5.1 %collective-permute-start.12 = (f32[136,128]{1,0:T(8,128)S(1)}, f32[136,128]{1,0:T(8,128)S(1)}, u32[]{:S(2)}, u32[]{:S(2)}) collective-permute-start(f32[136,128]{1,0:T(8,128)S(1)} %add.80), channel_id=1, source_target_pairs={{0,4},{1,5},{2,6},{3,7},{4,0},{5,1},{6,2},{7,3},{8,12},{9,13},{10,... | collective-permute-start | bytes 208904 | tf_op jit(solution)/shard_map/ppermute | solution.py:22
  50.6 4.3 %collective-permute-start.11 = (f32[136,128]{1,0:T(8,128)S(1)}, f32[136,128]{1,0:T(8,128)S(1)}, u32[]{:S(2)}, u32[]{:S(2)}) collective-permute-start(f32[136,128]{1,0:T(8,128)S(1)} %add.80), channel_id=1, source_target_pairs={{0,2},{1,3},{2,0},{3,1},{4,6},{5,7},{6,4},{7,5},{8,10},{9,11},{10,... | collective-permute-start | bytes 208904 | tf_op jit(solution)/shard_map/ppermute | solution.py:22
  54.9 6.4 %collective-permute-start.16 = (f32[136,128]{1,0:T(8,128)S(1)}, f32[136,128]{1,0:T(8,128)S(1)}, u32[]{:S(2)}, u32[]{:S(2)}) collective-permute-start(f32[136,128]{1,0:T(8,128)S(1)} %add_add_fusion.1), channel_id=1, source_target_pairs={{0,24},{8,16},{16,8},{24,0},{1,25},{9,17},{17,9},{25,1},{2,26},{10... | collective-permute-start | bytes 208904 | tf_op jit(solution)/shard_map/ppermute | solution.py:22
  57.9 7.0 %collective-permute-start.15 = (f32[136,128]{1,0:T(8,128)S(1)}, f32[136,128]{1,0:T(8,128)S(1)}, u32[]{:S(2)}, u32[]{:S(2)}) collective-permute-start(f32[136,128]{1,0:T(8,128)S(1)} %add_add_fusion.1), channel_id=1, source_target_pairs={{0,16},{8,24},{16,0},{24,8},{1,17},{9,25},{17,1},{25,9},{2,18},{10... | collective-permute-start | bytes 208904 | tf_op jit(solution)/shard_map/ppermute | solution.py:22
  58.5 6.4 %collective-permute-start.14 = (f32[136,128]{1,0:T(8,128)S(1)}, f32[136,128]{1,0:T(8,128)S(1)}, u32[]{:S(2)}, u32[]{:S(2)}) collective-permute-start(f32[136,128]{1,0:T(8,128)S(1)} %add_add_fusion.1), channel_id=1, source_target_pairs={{0,8},{8,0},{16,24},{24,16},{1,9},{9,1},{17,25},{25,17},{2,10},{10... | collective-permute-start | bytes 208904 | tf_op jit(solution)/shard_map/ppermute | solution.py:22
  64.9 1.3 %collective-permute-start.17 = (f32[136,128]{1,0:T(8,128)S(1)}, f32[136,128]{1,0:T(8,128)S(1)}, u32[]{:S(2)}, u32[]{:S(2)}) collective-permute-start(f32[136,128]{1,0:T(8,128)S(1)} %add_add_fusion.mine_ref), channel_id=1, source_target_pairs={{0,1},{1,0},{2,3},{3,2},{4,5},{5,4},{6,7},{7,6},{8,9},{9,8},{10,11... | collective-permute-start | bytes 208904 | tf_op jit(solution)/shard_map/ppermute | solution.py:22

commit v6 on v4

--- a/solution.py
+++ b/solution.py
@@ -15,6 +15,8 @@
 DENSE_BYTES = 32 * 2**20
 STEP = 4
 PACK = 2 * PANEL + 16
+TOP = PANEL // 2
+REST = PACK // 2 - TOP
 
 
 def exchange(value, axis, mask):
@@ -122,10 +124,9 @@
         total = term if total is None else total + term
     s_ref[...] = total
     gram_store(total, pack)
-    half = pack.shape[0] // 2
-    c = core[0]
-    mine_ref[...] = pack[pl.ds(pl.multiple_of(c * half, 8), half), :]
-    other_ref[...] = pack[pl.ds(pl.multiple_of((1 - c) * half, 8), half), :]
+    for ref, c in ((mine_ref, core[0]), (other_ref, 1 - core[0])):
+        ref[:TOP, :] = pack[pl.ds(pl.multiple_of(c * TOP, 8), TOP), :]
+        ref[TOP:, :] = pack[pl.ds(pl.multiple_of(2 * TOP + c * REST, 8), REST), :]
 
 
 def gram_store(total, pack):
@@ -234,30 +235,45 @@
 NN, NT, TN = ((1,), (0,)), ((1,), (1,)), ((0,), (0,))
 
 
-def tail_kernel(scale, core, mine_ref, other_ref, s_ref, basis_ref, upper_ref, pack):
-    half = pack.shape[0] // 2
-    c = core[0]
-    pack[pl.ds(pl.multiple_of(c * half, 8), half), :] = mine_ref[...] * scale
-    pack[pl.ds(pl.multiple_of((1 - c) * half, 8), half), :] = other_ref[...] * scale
+def joined(scale, core, mine_ref, other_ref, both):
+    half = mine_ref.shape[0]
+    both[pl.ds(pl.multiple_of(core[0] * half, 8), half), :] = mine_ref[...] * scale
+    both[pl.ds(pl.multiple_of((1 - core[0]) * half, 8), half), :] = other_ref[...] * scale
+    return both[...]
+
+
+def place():
     row = lax.broadcasted_iota(jnp.int32, (PANEL, PANEL), 0)
-    lane = lax.broadcasted_iota(jnp.int32, (PANEL, PANEL), 1)
-    both, cross = pack[0:PANEL, :], pack[PANEL : 2 * PANEL, :]
-    turned = both.T
-    gram_one = jnp.where(lane >= row, both, turned)
-    diagonal = jnp.broadcast_to(pack[2 * PANEL : 2 * PANEL + 1, :], both.shape)
-    gram_two = jnp.where(lane == row, diagonal, jnp.where(lane < row, both, turned))
-    upper_one, low_one = factor(gram_one)
-    coupling = full_dot(low_one, cross, NN)
+    return row, lax.broadcasted_iota(jnp.int32, (PANEL, PANEL), 1)
+
+
+def first_kernel(scale, core, mine_ref, other_ref, s_ref, upper_ref, low_ref, basis_ref, side_ref, both):
+    triangles = joined(scale, core, mine_ref, other_ref, both)
+    row, lane = place()
+    turned = triangles.T
+    upper_ref[...], low = factor(jnp.where(lane >= row, triangles, turned))
+    low_ref[...] = low
+    side_ref[...] = jnp.where(lane < row, triangles, turned)
+    basis_ref[...] = dot3(s_ref[:, 0:PANEL], low, NT)
+
+
+def second_kernel(
+    scale, core, mine_ref, other_ref, s_ref, first_ref, low_ref, one_ref, side_ref, basis_ref, upper_ref, both
+):
+    rest = joined(scale, core, mine_ref, other_ref, both)
+    row, lane = place()
+    low_one = low_ref[...]
+    coupling = full_dot(low_one, rest[:PANEL], NN)
+    diagonal = jnp.broadcast_to(rest[PANEL : PANEL + 1], (PANEL, PANEL))
+    gram_two = jnp.where(lane == row, diagonal, side_ref[...])
     upper_two, low_two = factor(gram_two - full_dot(coupling, coupling, TN))
     mixed = -full_dot(low_two, full_dot(coupling, low_one, TN), NN)
-    zero = jnp.zeros_like(upper_one)
-    upper_ref[0:PANEL, 0:PANEL] = upper_one
+    upper_ref[0:PANEL, 0:PANEL] = first_ref[...]
     upper_ref[0:PANEL, PANEL:] = coupling
-    upper_ref[PANEL:, 0:PANEL] = zero
+    upper_ref[PANEL:, 0:PANEL] = jnp.zeros_like(coupling)
     upper_ref[PANEL:, PANEL:] = upper_two
-    first, second = s_ref[:, 0:PANEL], s_ref[...]
-    basis_ref[:, 0:PANEL] = dot3(first, low_one, NT)
-    basis_ref[:, PANEL:] = dot3(second, jnp.concatenate([mixed, low_two], axis=1), NT)
+    basis_ref[:, 0:PANEL] = one_ref[...]
+    basis_ref[:, PANEL:] = dot3(s_ref[...], jnp.concatenate([mixed, low_two], axis=1), NT)
 
 
 def whole(shape):
@@ -363,27 +379,30 @@
     return [lax.psum_scatter(partial_value, "col", scatter_dimension=0, tiled=True)]
 
 
-def direct_sum(value, axis, low_bit, bits):
-    terms = [value] + [exchange(value, axis, mask << low_bit) for mask in range(1, 2**bits)]
+def direct_terms(value, axis, low_bit, bits):
+    terms = {0: value}
+    for mask in reversed(range(1, 2**bits)):
+        terms[mask] = exchange(value, axis, mask << low_bit)
+    return [terms[mask] for mask in range(2**bits)]
+
+
+def pair_sum(terms):
     while len(terms) > 1:
         terms = [a + b for a, b in zip(terms[0::2], terms[1::2])]
     return terms[0]
 
 
-def sum_over_axis(value, axis, low_bit):
+def axis_terms(value, axis, low_bit):
     bits = lax.axis_size(axis).bit_length() - 1
-    while low_bit < bits:
-        take = min(2, bits - low_bit)
-        value = direct_sum(value, axis, low_bit, take)
-        low_bit += take
-    return value
-
-
-def sum_over_mesh(mine, other, core):
-    mine = mine + exchange(other, "col", 1)
-    mine = sum_over_axis(mine, "col", 1)
-    mine = sum_over_axis(mine, "row", 0)
-    return mine, exchange(mine, "col", 1)
+    while bits - low_bit > 2:
+        value = pair_sum(direct_terms(value, axis, low_bit, 2))
+        low_bit += 2
+    return direct_terms(value, axis, low_bit, bits - low_bit)
+
+
+def finish_sum(terms):
+    value = pair_sum(terms)
+    return value, exchange(value, "col", 1)
 
 
 def on_device(gaussian_sketch, block_values, block_rows, block_columns):
@@ -414,22 +433,46 @@
         compiler_params=pltpu.CompilerParams(vmem_limit_bytes=12 * 2**20),
     )(core.reshape(1), *terms)
     order_total = shard_rows * size_row * size_col
-    mine, other = sum_over_mesh(mine, other, core)
-    range_basis, upper_factor = pl.pallas_call(
-        functools.partial(tail_kernel, 1.0 / order_total),
-        grid_spec=pltpu.PrefetchScalarGridSpec(
-            num_scalar_prefetch=1,
-            grid=(1,),
-            in_specs=[whole(half.shape), whole(half.shape), whole(sketched.shape)],
-            out_specs=[whole(sketched.shape), whole((width, width))],
-            scratch_shapes=[pltpu.VMEM((PACK, PANEL), jnp.float32)],
-        ),
-        out_shape=[
-            jax.ShapeDtypeStruct(sketched.shape, jnp.float32),
+    mine = mine + exchange(other, "col", 1)
+    mine = pair_sum(axis_terms(mine, "col", 1))
+    triangles = finish_sum(axis_terms(mine[:TOP], "row", 0))
+    rest = axis_terms(mine[TOP:], "row", 0)
+    square = jax.ShapeDtypeStruct((PANEL, PANEL), jnp.float32)
+    one = jax.ShapeDtypeStruct((shard_rows, PANEL), jnp.float32)
+
+    def solve(kernel, outs, rows, *args):
+        return pl.pallas_call(
+            functools.partial(kernel, 1.0 / order_total),
+            grid_spec=pltpu.PrefetchScalarGridSpec(
+                num_scalar_prefetch=1,
+                grid=(1,),
+                in_specs=[whole(x.shape) for x in args],
+                out_specs=[whole(x.shape) for x in outs],
+                scratch_shapes=[pltpu.VMEM((rows, PANEL), jnp.float32)],
+            ),
+            out_shape=outs,
+            compiler_params=pltpu.CompilerParams(vmem_limit_bytes=12 * 2**20),
+            cost_estimate=pl.CostEstimate(flops=2**32, bytes_accessed=2**21, transcendentals=0),
+        )(core.reshape(1), *args)
+
+    upper_one, low_one, basis_one, side = solve(
+        first_kernel, [square, square, one, square], PANEL, *triangles, sketched
+    )
+    *rest, low_one = lax.optimization_barrier((*rest, low_one))
+    range_basis, upper_factor = solve(
+        second_kernel,
+        [
+            jax.ShapeDtypeStruct((shard_rows, width), jnp.float32),
             jax.ShapeDtypeStruct((width, width), jnp.float32),
         ],
-        compiler_params=pltpu.CompilerParams(vmem_limit_bytes=16 * 2**20),
-    )(core.reshape(1), mine, other, sketched)
+        2 * REST,
+        *finish_sum(rest),
+        sketched,
+        upper_one,
+        low_one,
+        basis_one,
+        side,
+    )
     return (range_basis, upper_factor)
 
 

time: 74.8 us -> 79 us (1.056)
  starting transfers between devices: 19.8 us -> 24.3 us
    ppermute x16 -> x20, starting transfers between devices: 19.8 us -> 24.3 us  [exchange(): return lax.ppermute(value, axis, [(i, i ^ mask) for i in range(size)])]
    ppermute x16 -> x20, waiting for transfers between devices: 29.3 us -> 28.8 us  [exchange(): return lax.ppermute(value, axis, [(i, i ^ mask) for i in range(size)])]
    pallas_call x1 -> x2, Pallas kernels: 9.6 us -> 9.66 us  [solve(): pl.pallas_call(functools.partial(kernel, 1.0 / order_total), grid_spec=pl...]
  transfers between devices with their start and end apart: 16 -> 20, of which waited for: 13 -> 13; matrix products, arithmetic and copies ran while one was open for 1% -> 1% of each run, Pallas kernels for 18% -> 22%
where the time goes in v6:
time: 79 us; the launch traced here: 78.9 us
  waiting for transfers between devices  28.8 us (36%)
  starting transfers between devices  24.3 us (31%)
  Pallas kernels  24.2 us (31%)
  between operations  0.82 us (1%)
    ppermute x20, waiting for transfers between devices, exchange(): return lax.ppermute(value, axis, [(i, i ^ mask) for i in range(size)])  28.8 us
    ppermute x20, starting transfers between devices, exchange(): return lax.ppermute(value, axis, [(i, i ^ mask) for i in range(size)])  24.3 us
    pallas_call x2, Pallas kernels, solve(): pl.pallas_call(functools.partial(kernel, 1.0 / order_total), grid_spec=pl...  9.66 us
    pallas_call x5, Pallas kernels, product(): pl.pallas_call(functools.partial(product_kernel, first, chosen), grid=(co...  7.08 us
    pallas_call x1, Pallas kernels, scatter_blocks(): pl.pallas_call(scatter_kernel, out_shape=pltpu.VMEM((n_slots, BS, BS), va...  6.21 us
  transfers between devices with their start and end apart: 20, of which 13 were waited for; matrix products, arithmetic and copies ran while one was open for 1% of the time, Pallas kernels for 22%

profile of v6, /device:TPU:0, one launch (start us, length us, event | category | flops | bytes accessed | tf_op | source)
XLA Modules:
  0.0 78.9 jit_solution(18148790816076408583)
XLA Ops:
  0.6 4.1 %collective-permute-start = (bf16[512,256]{1,0:T(8,128)(2,1)}, bf16[512,256]{1,0:T(8,128)(2,1)S(1)}, u32[]{:S(2)}, u32[]{:S(2)}) collective-permute-start(bf16[512,256]{1,0:T(8,128)(2,1)} %refs_0_.1), channel_id=1, source_target_pairs={{0,16},{8,24},{16,0},{24,8},{1,17},{9,25},{17,1},{25,9},{2,18},{10... | collective-permute-start | bytes 786440 | tf_op jit(solution)/shard_map/ppermute | solution.py:24
  4.7 1.6 %collective-permute-start.2 = (bf16[512,256]{1,0:T(8,128)(2,1)}, bf16[512,256]{1,0:T(8,128)(2,1)S(1)}, u32[]{:S(2)}, u32[]{:S(2)}) collective-permute-start(bf16[512,256]{1,0:T(8,128)(2,1)} %refs_0_.1), channel_id=1, source_target_pairs={{0,8},{8,0},{16,24},{24,16},{1,9},{9,1},{17,25},{25,17},{2,10},{10... | collective-permute-start | bytes 786440 | tf_op jit(solution)/shard_map/ppermute | solution.py:24
  6.3 0.7 fusion.4.slots
  7.0 6.2 %shard_map.59 = bf16[512,128,128]{2,1,0:T(8,128)(2,1)S(1)} custom-call(s32[256]{0:T(256)S(1)} %fusion.4.slots, bf16[256,128,128]{2,1,0:T(8,128)(2,1)} %values.1), custom_call_target="tpu_custom_call" | custom-call | bytes 25165824 | tf_op jit(solution)/shard_map/pallas_call | solution.py:44
  13.3 3.7 %collective-permute-done.refs_2_ = bf16[512,256]{1,0:T(8,128)(2,1)S(1)} collective-permute-done((bf16[512,256]{1,0:T(8,128)(2,1)}, bf16[512,256]{1,0:T(8,128)(2,1)S(1)}, u32[]{:S(2)}, u32[]{:S(2)}) %collective-permute-start) | collective-permute-done | bytes 262176 | tf_op jit(solution)/shard_map/ppermute | solution.py:24
  17.0 0.7 collective-permute-start.1
  17.7 4.6 %shard_map.60.refs_1_ = f32[8,512,256]{2,1,0:T(8,128)S(1)} custom-call(bf16[8,4,16,128,128]{4,3,2,1,0:T(8,128)(2,1)S(1)} %bitcast.2, bf16[512,256]{1,0:T(8,128)(2,1)S(1)} %copy-done, bf16[512,256]{1,0:T(8,128)(2,1)S(1)} %collective-permute-done.2.refs_1_, bf16[512,256]{1,0:T(8,128)(2,1)S(1)} %collective-permute-done.refs_2_), custom_call_target="tpu_custom_call" | custom-call | flops 4294967296 | bytes 16777216 | tf_op jit(solution)/shard_map/pallas_call | solution.py:325
  22.3 2.1 %collective-permute-done.1.refs_0_ = bf16[512,256]{1,0:T(8,128)(2,1)S(1)} collective-permute-done((bf16[512,256]{1,0:T(8,128)(2,1)S(1)}, bf16[512,256]{1,0:T(8,128)(2,1)S(1)}, u32[]{:S(2)}, u32[]{:S(2)}) %collective-permute-start.1) | collective-permute-done | bytes 262176 | tf_op jit(solution)/shard_map/ppermute | solution.py:24
  25.1 0.6 shard_map.62
  26.3 0.6 shard_map.64.a_ref
  26.9 0.6 shard_map.61.a_ref
  28.0 2.3 %collective-permute-start.7 = (s16[528,256]{1,0:T(8,128)(2,1)S(1)}, s16[528,256]{1,0:T(8,128)(2,1)S(1)}, u32[]{:S(2)}, u32[]{:S(2)}) collective-permute-start(s16[528,256]{1,0:T(8,128)(2,1)S(1)} %get-tuple-element.24), channel_id=1, source_target_pairs={{0,6},{1,7},{2,4},{3,5},{4,2},{5,3},{6,0},{7,1},{8,14},{9,15},{10,... | collective-permute-start | bytes 811016 | tf_op jit(solution)/shard_map/ppermute | solution.py:24
  30.6 0.6 collective-permute-start.4
  31.2 1.2 %collective-permute-start.5 = (s16[528,256]{1,0:T(8,128)(2,1)S(1)}, s16[528,256]{1,0:T(8,128)(2,1)S(1)}, u32[]{:S(2)}, u32[]{:S(2)}) collective-permute-start(s16[528,256]{1,0:T(8,128)(2,1)S(1)} %get-tuple-element.23), channel_id=1, source_target_pairs={{0,4},{1,5},{2,6},{3,7},{4,0},{5,1},{6,2},{7,3},{8,12},{9,13},{10,... | collective-permute-start | bytes 811016 | tf_op jit(solution)/shard_map/ppermute | solution.py:24
  32.4 5.9 %collective-permute-done.7.refs_2_ = s16[528,256]{1,0:T(8,128)(2,1)S(1)} collective-permute-done((s16[528,256]{1,0:T(8,128)(2,1)S(1)}, s16[528,256]{1,0:T(8,128)(2,1)S(1)}, u32[]{:S(2)}, u32[]{:S(2)}) %collective-permute-start.7) | collective-permute-done | bytes 270368 | tf_op jit(solution)/shard_map/ppermute | solution.py:24
  38.3 4.8 %collective-permute-done.4.refs_0_ = s16[528,256]{1,0:T(8,128)(2,1)S(1)} collective-permute-done((s16[528,256]{1,0:T(8,128)(2,1)S(1)}, s16[528,256]{1,0:T(8,128)(2,1)S(1)}, u32[]{:S(2)}, u32[]{:S(2)}) %collective-permute-start.4) | collective-permute-done | bytes 270368 | tf_op jit(solution)/shard_map/ppermute | solution.py:24
  43.3 0.6 shard_map.67
  44.0 1.2 %collective-permute-done.8 = f32[136,128]{1,0:T(8,128)S(1)} collective-permute-done((f32[136,128]{1,0:T(8,128)S(1)}, f32[136,128]{1,0:T(8,128)S(1)}, u32[]{:S(2)}, u32[]{:S(2)}) %collective-permute-start.8) | collective-permute-done | bytes 69664 | tf_op jit(solution)/shard_map/ppermute | solution.py:24
  45.3 1.4 %collective-permute-start.10 = (f32[136,128]{1,0:T(8,128)S(1)}, f32[136,128]{1,0:T(8,128)S(1)}, u32[]{:S(2)}, u32[]{:S(2)}) collective-permute-start(f32[136,128]{1,0:T(8,128)S(1)} %add.89), channel_id=1, source_target_pairs={{0,4},{1,5},{2,6},{3,7},{4,0},{5,1},{6,2},{7,3},{8,12},{9,13},{10,... | collective-permute-start | bytes 208904 | tf_op jit(solution)/shard_map/ppermute | solution.py:24
  46.6 1.5 %collective-permute-start.11 = (f32[136,128]{1,0:T(8,128)S(1)}, f32[136,128]{1,0:T(8,128)S(1)}, u32[]{:S(2)}, u32[]{:S(2)}) collective-permute-start(f32[136,128]{1,0:T(8,128)S(1)} %add.89), channel_id=1, source_target_pairs={{0,6},{1,7},{2,4},{3,5},{4,2},{5,3},{6,0},{7,1},{8,14},{9,15},{10,... | collective-permute-start | bytes 208904 | tf_op jit(solution)/shard_map/ppermute | solution.py:24
  48.2 0.7 collective-permute-start.9
  48.8 0.8 %collective-permute-done.10 = f32[136,128]{1,0:T(8,128)S(1)} collective-permute-done((f32[136,128]{1,0:T(8,128)S(1)}, f32[136,128]{1,0:T(8,128)S(1)}, u32[]{:S(2)}, u32[]{:S(2)}) %collective-permute-start.10) | collective-permute-done | bytes 69664 | tf_op jit(solution)/shard_map/ppermute | solution.py:24
  49.7 2.8 %collective-permute-done.11 = f32[136,128]{1,0:T(8,128)S(1)} collective-permute-done((f32[136,128]{1,0:T(8,128)S(1)}, f32[136,128]{1,0:T(8,128)S(1)}, u32[]{:S(2)}, u32[]{:S(2)}) %collective-permute-start.11) | collective-permute-done | bytes 69664 | tf_op jit(solution)/shard_map/ppermute | solution.py:24
  52.6 1.7 %collective-permute-start.15 = (f32[64,128]{1,0:T(8,128)S(1)}, f32[64,128]{1,0:T(8,128)S(1)}, u32[]{:S(2)}, u32[]{:S(2)}) collective-permute-start(f32[64,128]{1,0:T(8,128)S(1)} %slice.9), channel_id=1, source_target_pairs={{0,8},{8,0},{16,24},{24,16},{1,9},{9,1},{17,25},{25,17},{2,10},{10... | collective-permute-start | bytes 98312 | tf_op jit(solution)/shard_map/ppermute | solution.py:24
  54.3 3.3 %collective-permute-start.16 = (f32[64,128]{1,0:T(8,128)S(1)}, f32[64,128]{1,0:T(8,128)S(1)}, u32[]{:S(2)}, u32[]{:S(2)}) collective-permute-start(f32[64,128]{1,0:T(8,128)S(1)} %slice.9), channel_id=1, source_target_pairs={{0,16},{8,24},{16,0},{24,8},{1,17},{9,25},{17,1},{25,9},{2,18},{10... | collective-permute-start | bytes 98312 | tf_op jit(solution)/shard_map/ppermute | solution.py:24
  57.6 2.2 %collective-permute-done.16 = f32[64,128]{1,0:T(8,128)S(1)} collective-permute-done((f32[64,128]{1,0:T(8,128)S(1)}, f32[64,128]{1,0:T(8,128)S(1)}, u32[]{:S(2)}, u32[]{:S(2)}) %collective-permute-start.16) | collective-permute-done | bytes 32800 | tf_op jit(solution)/shard_map/ppermute | solution.py:24
  59.9 3.5 %collective-permute-done.17 = f32[64,128]{1,0:T(8,128)S(1)} collective-permute-done((f32[64,128]{1,0:T(8,128)S(1)}, f32[64,128]{1,0:T(8,128)S(1)}, u32[]{:S(2)}, u32[]{:S(2)}) %collective-permute-start.17) | collective-permute-done | bytes 32800 | tf_op jit(solution)/shard_map/ppermute | solution.py:24
  63.5 0.9 %collective-permute-start.13 = (f32[72,128]{1,0:T(8,128)S(1)}, f32[72,128]{1,0:T(8,128)S(1)}, u32[]{:S(2)}, u32[]{:S(2)}) collective-permute-start(f32[72,128]{1,0:T(8,128)S(1)} %slice.8), channel_id=1, source_target_pairs={{0,16},{8,24},{16,0},{24,8},{1,17},{9,25},{17,1},{25,9},{2,18},{10... | collective-permute-start | bytes 110600 | tf_op jit(solution)/shard_map/ppermute | solution.py:24
  64.4 3.5 %collective-permute-start.14 = (f32[72,128]{1,0:T(8,128)S(1)}, f32[72,128]{1,0:T(8,128)S(1)}, u32[]{:S(2)}, u32[]{:S(2)}) collective-permute-start(f32[72,128]{1,0:T(8,128)S(1)} %slice.8), channel_id=1, source_target_pairs={{0,24},{8,16},{16,8},{24,0},{1,25},{9,17},{17,9},{25,1},{2,26},{10... | collective-permute-start | bytes 110600 | tf_op jit(solution)/shard_map/ppermute | solution.py:24
  67.9 4.0 %shard_map.68 = (f32[128,128]{1,0:T(8,128)S(1)}, f32[128,128]{1,0:T(8,128)S(1)}, f32[512,128]{1,0:T(8,128)S(1)}, f32[128,128]{1,0:T(8,128)S(1)}) custom-call(s32[1]{0:T(128)} %bitcast.core, f32[64,128]{1,0:T(8,128)S(1)} %add_add_fusion.2.mine_ref, f32[64,128]{1,0:T(8,128)S(1)} %collective-permute-done.18.other_ref, f32[512,256]{1,0:T(8,128)S(1)} %get-tuple-element.28.s_ref), custom_call_target="tpu_custom_call" | custom-call | flops 4294967296 | bytes 2097152 | tf_op jit(solution)/shard_map/pallas_call | solution.py:444
  72.0 1.2 %collective-permute-done.19.other_ref = f32[72,128]{1,0:T(8,128)S(1)} collective-permute-done((f32[72,128]{1,0:T(8,128)S(1)}, f32[72,128]{1,0:T(8,128)S(1)}, u32[]{:S(2)}, u32[]{:S(2)}) %collective-permute-start.19) | collective-permute-done | bytes 36896 | tf_op jit(solution)/shard_map/ppermute | solution.py:24
  73.2 5.6 %shard_map.69 = (f32[512,256]{1,0:T(8,128)}, f32[256,256]{1,0:T(8,128)}) custom-call(s32[1]{0:T(128)} %bitcast.core, f32[72,128]{1,0:T(8,128)S(1)} %add_add_fusion.1.mine_ref, f32[72,128]{1,0:T(8,128)S(1)} %collective-permute-done.19.other_ref, f32[512,256]{1,0:T(8,128)S(1)} %get-tuple-element.28.s_ref, f32[128,128]{1,0:T(8,128)S(1)} %get-tuple-element.34.first_ref, ...), custom_call_target="tpu_custom_call" | custom-call | flops 4294967296 | bytes 2097152 | tf_op jit(solution)/shard_map/pallas_call | solution.py:444
  (28 shorter events, 2.6 us)
Async XLA Ops:
  0.6 16.3 %collective-permute-start = (bf16[512,256]{1,0:T(8,128)(2,1)}, bf16[512,256]{1,0:T(8,128)(2,1)S(1)}, u32[]{:S(2)}, u32[]{:S(2)}) collective-permute-start(bf16[512,256]{1,0:T(8,128)(2,1)} %refs_0_.1), channel_id=1, source_target_pairs={{0,16},{8,24},{16,0},{24,8},{1,17},{9,25},{17,1},{25,9},{2,18},{10... | collective-permute-start | bytes 786440 | tf_op jit(solution)/shard_map/ppermute | solution.py:24
  4.7 13.0 %collective-permute-start.2 = (bf16[512,256]{1,0:T(8,128)(2,1)}, bf16[512,256]{1,0:T(8,128)(2,1)S(1)}, u32[]{:S(2)}, u32[]{:S(2)}) collective-permute-start(bf16[512,256]{1,0:T(8,128)(2,1)} %refs_0_.1), channel_id=1, source_target_pairs={{0,8},{8,0},{16,24},{24,16},{1,9},{9,1},{17,25},{25,17},{2,10},{10... | collective-permute-start | bytes 786440 | tf_op jit(solution)/shard_map/ppermute | solution.py:24
  7.0 10.7 %copy-start = (bf16[512,256]{1,0:T(8,128)(2,1)S(1)}, bf16[512,256]{1,0:T(8,128)(2,1)}, u32[]{:S(2)}) copy-start(bf16[512,256]{1,0:T(8,128)(2,1)} %refs_0_.1) | copy-start | bytes 786436
  17.0 7.4 %collective-permute-start.1 = (bf16[512,256]{1,0:T(8,128)(2,1)S(1)}, bf16[512,256]{1,0:T(8,128)(2,1)S(1)}, u32[]{:S(2)}, u32[]{:S(2)}) collective-permute-start(bf16[512,256]{1,0:T(8,128)(2,1)S(1)} %collective-permute-done.refs_2_), channel_id=1, source_target_pairs={{0,8},{8,0},{16,24},{24,16},{1,9},{9,1},{17,25},{25,17},{2,10},{10... | collective-permute-start | bytes 786440 | tf_op jit(solution)/shard_map/ppermute | solution.py:24
  25.0 2.7 %collective-permute-start.6 = (f32[2,512,256]{2,1,0:T(8,128)S(1)}, f32[2,512,256]{2,1,0:T(8,128)S(1)}, u32[]{:S(2)}, u32[]{:S(2)}) collective-permute-start(f32[2,512,256]{2,1,0:T(8,128)S(1)} %shard_map.65), channel_id=1, source_target_pairs={{0,1},{1,0},{2,3},{3,2},{4,5},{5,4},{6,7},{7,6},{8,9},{9,8},{10,11... | collective-permute-start | bytes 3145736 | tf_op jit(solution)/shard_map/ppermute | solution.py:24
  25.7 4.6 %collective-permute-start.3 = (f32[2,512,256]{2,1,0:T(8,128)S(1)}, f32[2,512,256]{2,1,0:T(8,128)S(1)}, u32[]{:S(2)}, u32[]{:S(2)}) collective-permute-start(f32[2,512,256]{2,1,0:T(8,128)S(1)} %shard_map.62), channel_id=1, source_target_pairs={{0,1},{1,0},{2,3},{3,2},{4,5},{5,4},{6,7},{7,6},{8,9},{9,8},{10,11... | collective-permute-start | bytes 3145736 | tf_op jit(solution)/shard_map/ppermute | solution.py:24
  28.0 10.3 %collective-permute-start.7 = (s16[528,256]{1,0:T(8,128)(2,1)S(1)}, s16[528,256]{1,0:T(8,128)(2,1)S(1)}, u32[]{:S(2)}, u32[]{:S(2)}) collective-permute-start(s16[528,256]{1,0:T(8,128)(2,1)S(1)} %get-tuple-element.24), channel_id=1, source_target_pairs={{0,6},{1,7},{2,4},{3,5},{4,2},{5,3},{6,0},{7,1},{8,14},{9,15},{10,... | collective-permute-start | bytes 811016 | tf_op jit(solution)/shard_map/ppermute | solution.py:24
  30.6 12.5 %collective-permute-start.4 = (s16[528,256]{1,0:T(8,128)(2,1)S(1)}, s16[528,256]{1,0:T(8,128)(2,1)S(1)}, u32[]{:S(2)}, u32[]{:S(2)}) collective-permute-start(s16[528,256]{1,0:T(8,128)(2,1)S(1)} %get-tuple-element.22), channel_id=1, source_target_pairs={{0,2},{1,3},{2,0},{3,1},{4,6},{5,7},{6,4},{7,5},{8,10},{9,11},{10,... | collective-permute-start | bytes 811016 | tf_op jit(solution)/shard_map/ppermute | solution.py:24
  31.2 12.1 %collective-permute-start.5 = (s16[528,256]{1,0:T(8,128)(2,1)S(1)}, s16[528,256]{1,0:T(8,128)(2,1)S(1)}, u32[]{:S(2)}, u32[]{:S(2)}) collective-permute-start(s16[528,256]{1,0:T(8,128)(2,1)S(1)} %get-tuple-element.23), channel_id=1, source_target_pairs={{0,4},{1,5},{2,6},{3,7},{4,0},{5,1},{6,2},{7,3},{8,12},{9,13},{10,... | collective-permute-start | bytes 811016 | tf_op jit(solution)/shard_map/ppermute | solution.py:24
  43.9 1.3 %collective-permute-start.8 = (f32[136,128]{1,0:T(8,128)S(1)}, f32[136,128]{1,0:T(8,128)S(1)}, u32[]{:S(2)}, u32[]{:S(2)}) collective-permute-start(f32[136,128]{1,0:T(8,128)S(1)} %get-tuple-element.27), channel_id=1, source_target_pairs={{0,1},{1,0},{2,3},{3,2},{4,5},{5,4},{6,7},{7,6},{8,9},{9,8},{10,11... | collective-permute-start | bytes 208904 | tf_op jit(solution)/shard_map/ppermute | solution.py:24
  45.3 4.4 %collective-permute-start.10 = (f32[136,128]{1,0:T(8,128)S(1)}, f32[136,128]{1,0:T(8,128)S(1)}, u32[]{:S(2)}, u32[]{:S(2)}) collective-permute-start(f32[136,128]{1,0:T(8,128)S(1)} %add.89), channel_id=1, source_target_pairs={{0,4},{1,5},{2,6},{3,7},{4,0},{5,1},{6,2},{7,3},{8,12},{9,13},{10,... | collective-permute-start | bytes 208904 | tf_op jit(solution)/shard_map/ppermute | solution.py:24
  46.6 5.8 %collective-permute-start.11 = (f32[136,128]{1,0:T(8,128)S(1)}, f32[136,128]{1,0:T(8,128)S(1)}, u32[]{:S(2)}, u32[]{:S(2)}) collective-permute-start(f32[136,128]{1,0:T(8,128)S(1)} %add.89), channel_id=1, source_target_pairs={{0,6},{1,7},{2,4},{3,5},{4,2},{5,3},{6,0},{7,1},{8,14},{9,15},{10,... | collective-permute-start | bytes 208904 | tf_op jit(solution)/shard_map/ppermute | solution.py:24
  48.2 4.4 %collective-permute-start.9 = (f32[136,128]{1,0:T(8,128)S(1)}, f32[136,128]{1,0:T(8,128)S(1)}, u32[]{:S(2)}, u32[]{:S(2)}) collective-permute-start(f32[136,128]{1,0:T(8,128)S(1)} %add.89), channel_id=1, source_target_pairs={{0,2},{1,3},{2,0},{3,1},{4,6},{5,7},{6,4},{7,5},{8,10},{9,11},{10,... | collective-permute-start | bytes 208904 | tf_op jit(solution)/shard_map/ppermute | solution.py:24
  52.6 5.0 %collective-permute-start.15 = (f32[64,128]{1,0:T(8,128)S(1)}, f32[64,128]{1,0:T(8,128)S(1)}, u32[]{:S(2)}, u32[]{:S(2)}) collective-permute-start(f32[64,128]{1,0:T(8,128)S(1)} %slice.9), channel_id=1, source_target_pairs={{0,8},{8,0},{16,24},{24,16},{1,9},{9,1},{17,25},{25,17},{2,10},{10... | collective-permute-start | bytes 98312 | tf_op jit(solution)/shard_map/ppermute | solution.py:24
  54.3 5.5 %collective-permute-start.16 = (f32[64,128]{1,0:T(8,128)S(1)}, f32[64,128]{1,0:T(8,128)S(1)}, u32[]{:S(2)}, u32[]{:S(2)}) collective-permute-start(f32[64,128]{1,0:T(8,128)S(1)} %slice.9), channel_id=1, source_target_pairs={{0,16},{8,24},{16,0},{24,8},{1,17},{9,25},{17,1},{25,9},{2,18},{10... | collective-permute-start | bytes 98312 | tf_op jit(solution)/shard_map/ppermute | solution.py:24
  57.6 5.7 %collective-permute-start.17 = (f32[64,128]{1,0:T(8,128)S(1)}, f32[64,128]{1,0:T(8,128)S(1)}, u32[]{:S(2)}, u32[]{:S(2)}) collective-permute-start(f32[64,128]{1,0:T(8,128)S(1)} %slice.9), channel_id=1, source_target_pairs={{0,24},{8,16},{16,8},{24,0},{1,25},{9,17},{17,9},{25,1},{2,26},{10... | collective-permute-start | bytes 98312 | tf_op jit(solution)/shard_map/ppermute | solution.py:24
  63.3 4.5 %collective-permute-start.18 = (f32[64,128]{1,0:T(8,128)S(1)}, f32[64,128]{1,0:T(8,128)S(1)}, u32[]{:S(2)}, u32[]{:S(2)}) collective-permute-start(f32[64,128]{1,0:T(8,128)S(1)} %add_add_fusion.2.mine_ref), channel_id=1, source_target_pairs={{0,1},{1,0},{2,3},{3,2},{4,5},{5,4},{6,7},{7,6},{8,9},{9,8},{10,11... | collective-permute-start | bytes 98312 | tf_op jit(solution)/shard_map/ppermute | solution.py:24
  63.4 8.5 %collective-permute-start.12 = (f32[72,128]{1,0:T(8,128)S(1)}, f32[72,128]{1,0:T(8,128)S(1)}, u32[]{:S(2)}, u32[]{:S(2)}) collective-permute-start(f32[72,128]{1,0:T(8,128)S(1)} %slice.8), channel_id=1, source_target_pairs={{0,8},{8,0},{16,24},{24,16},{1,9},{9,1},{17,25},{25,17},{2,10},{10... | collective-permute-start | bytes 110600 | tf_op jit(solution)/shard_map/ppermute | solution.py:24
  63.5 8.4 %collective-permute-start.13 = (f32[72,128]{1,0:T(8,128)S(1)}, f32[72,128]{1,0:T(8,128)S(1)}, u32[]{:S(2)}, u32[]{:S(2)}) collective-permute-start(f32[72,128]{1,0:T(8,128)S(1)} %slice.8), channel_id=1, source_target_pairs={{0,16},{8,24},{16,0},{24,8},{1,17},{9,25},{17,1},{25,9},{2,18},{10... | collective-permute-start | bytes 110600 | tf_op jit(solution)/shard_map/ppermute | solution.py:24
  64.4 7.5 %collective-permute-start.14 = (f32[72,128]{1,0:T(8,128)S(1)}, f32[72,128]{1,0:T(8,128)S(1)}, u32[]{:S(2)}, u32[]{:S(2)}) collective-permute-start(f32[72,128]{1,0:T(8,128)S(1)} %slice.8), channel_id=1, source_target_pairs={{0,24},{8,16},{16,8},{24,0},{1,25},{9,17},{17,9},{25,1},{2,26},{10... | collective-permute-start | bytes 110600 | tf_op jit(solution)/shard_map/ppermute | solution.py:24
  72.0 1.3 %collective-permute-start.19 = (f32[72,128]{1,0:T(8,128)S(1)}, f32[72,128]{1,0:T(8,128)S(1)}, u32[]{:S(2)}, u32[]{:S(2)}) collective-permute-start(f32[72,128]{1,0:T(8,128)S(1)} %add_add_fusion.1.mine_ref), channel_id=1, source_target_pairs={{0,1},{1,0},{2,3},{3,2},{4,5},{5,4},{6,7},{7,6},{8,9},{9,8},{10,11... | collective-permute-start | bytes 110600 | tf_op jit(solution)/shard_map/ppermute | solution.py:24

commit v7 on v4

--- a/solution.py
+++ b/solution.py
@@ -248,16 +248,15 @@
     gram_two = jnp.where(lane == row, diagonal, jnp.where(lane < row, both, turned))
     upper_one, low_one = factor(gram_one)
     coupling = full_dot(low_one, cross, NN)
+    basis_one = dot3(s_ref[:, 0:PANEL], low_one, NT)
+    basis_ref[:, 0:PANEL] = basis_one
+    remainder = s_ref[:, PANEL:] - dot3(basis_one, coupling, NN)
     upper_two, low_two = factor(gram_two - full_dot(coupling, coupling, TN))
-    mixed = -full_dot(low_two, full_dot(coupling, low_one, TN), NN)
-    zero = jnp.zeros_like(upper_one)
     upper_ref[0:PANEL, 0:PANEL] = upper_one
     upper_ref[0:PANEL, PANEL:] = coupling
-    upper_ref[PANEL:, 0:PANEL] = zero
+    upper_ref[PANEL:, 0:PANEL] = jnp.zeros_like(upper_one)
     upper_ref[PANEL:, PANEL:] = upper_two
-    first, second = s_ref[:, 0:PANEL], s_ref[...]
-    basis_ref[:, 0:PANEL] = dot3(first, low_one, NT)
-    basis_ref[:, PANEL:] = dot3(second, jnp.concatenate([mixed, low_two], axis=1), NT)
+    basis_ref[:, PANEL:] = dot3(remainder, low_two, NT)
 
 
 def whole(shape):
@@ -364,10 +363,12 @@
 
 
 def direct_sum(value, axis, low_bit, bits):
-    terms = [value] + [exchange(value, axis, mask << low_bit) for mask in range(1, 2**bits)]
-    while len(terms) > 1:
-        terms = [a + b for a, b in zip(terms[0::2], terms[1::2])]
-    return terms[0]
+    t = [value] + [exchange(value, axis, mask << low_bit) for mask in range(1, 2**bits)]
+    if bits == 1:
+        return t[0] + t[1]
+    if axis == "col":
+        return (t[2] + t[3]) + (t[0] + t[1])
+    return (t[3] + t[2]) + (t[1] + t[0])
 
 
 def sum_over_axis(value, axis, low_bit):

time: 74.8 us -> 73.1 us (0.977)
  waiting for transfers between devices: 29.3 us -> 27.6 us
    ppermute x16, waiting for transfers between devices: 29.3 us -> 27.6 us  [exchange(): return lax.ppermute(value, axis, [(i, i ^ mask) for i in range(size)])]
where the time goes in v7:
time: 73.1 us; the launch traced here: 73 us
  waiting for transfers between devices  27.6 us (38%)
  Pallas kernels  23.9 us (33%)
  starting transfers between devices  19.9 us (27%)
  other arithmetic  0.77 us (1%)
  between operations  0.75 us (1%)
    ppermute x16, waiting for transfers between devices, exchange(): return lax.ppermute(value, axis, [(i, i ^ mask) for i in range(size)])  27.6 us
    ppermute x16, starting transfers between devices, exchange(): return lax.ppermute(value, axis, [(i, i ^ mask) for i in range(size)])  19.9 us
    pallas_call x1, Pallas kernels, on_device(): pl.pallas_call(functools.partial(tail_kernel, 1.0 / order_total), grid_sp...  9.37 us
    pallas_call x5, Pallas kernels, product(): pl.pallas_call(functools.partial(product_kernel, first, chosen), grid=(co...  7.08 us
    pallas_call x1, Pallas kernels, scatter_blocks(): pl.pallas_call(scatter_kernel, out_shape=pltpu.VMEM((n_slots, BS, BS), va...  6.21 us
  transfers between devices with their start and end apart: 16, of which 13 were waited for; matrix products, arithmetic and copies ran while one was open for 1% of the time, Pallas kernels for 18%

profile of v7, /device:TPU:0, one launch (start us, length us, event | category | flops | bytes accessed | tf_op | source)
XLA Modules:
  0.0 73.0 jit_solution(12335540993387009686)
XLA Ops:
  0.6 4.1 %collective-permute-start = (bf16[512,256]{1,0:T(8,128)(2,1)}, bf16[512,256]{1,0:T(8,128)(2,1)S(1)}, u32[]{:S(2)}, u32[]{:S(2)}) collective-permute-start(bf16[512,256]{1,0:T(8,128)(2,1)} %refs_0_.1), channel_id=1, source_target_pairs={{0,16},{8,24},{16,0},{24,8},{1,17},{9,25},{17,1},{25,9},{2,18},{10... | collective-permute-start | bytes 786440 | tf_op jit(solution)/shard_map/ppermute | solution.py:22
  4.7 1.6 %collective-permute-start.2 = (bf16[512,256]{1,0:T(8,128)(2,1)}, bf16[512,256]{1,0:T(8,128)(2,1)S(1)}, u32[]{:S(2)}, u32[]{:S(2)}) collective-permute-start(bf16[512,256]{1,0:T(8,128)(2,1)} %refs_0_.1), channel_id=1, source_target_pairs={{0,8},{8,0},{16,24},{24,16},{1,9},{9,1},{17,25},{25,17},{2,10},{10... | collective-permute-start | bytes 786440 | tf_op jit(solution)/shard_map/ppermute | solution.py:22
  6.3 0.7 fusion.4.slots
  7.0 6.2 %shard_map.59 = bf16[512,128,128]{2,1,0:T(8,128)(2,1)S(1)} custom-call(s32[256]{0:T(256)S(1)} %fusion.4.slots, bf16[256,128,128]{2,1,0:T(8,128)(2,1)} %values.1), custom_call_target="tpu_custom_call" | custom-call | bytes 25165824 | tf_op jit(solution)/shard_map/pallas_call | solution.py:42
  13.3 3.7 %collective-permute-done.refs_2_ = bf16[512,256]{1,0:T(8,128)(2,1)S(1)} collective-permute-done((bf16[512,256]{1,0:T(8,128)(2,1)}, bf16[512,256]{1,0:T(8,128)(2,1)S(1)}, u32[]{:S(2)}, u32[]{:S(2)}) %collective-permute-start) | collective-permute-done | bytes 262176 | tf_op jit(solution)/shard_map/ppermute | solution.py:22
  17.0 0.7 collective-permute-start.1
  17.7 4.6 %shard_map.60.refs_1_ = f32[8,512,256]{2,1,0:T(8,128)S(1)} custom-call(bf16[8,4,16,128,128]{4,3,2,1,0:T(8,128)(2,1)S(1)} %bitcast.2, bf16[512,256]{1,0:T(8,128)(2,1)S(1)} %copy-done, bf16[512,256]{1,0:T(8,128)(2,1)S(1)} %collective-permute-done.2.refs_1_, bf16[512,256]{1,0:T(8,128)(2,1)S(1)} %collective-permute-done.refs_2_), custom_call_target="tpu_custom_call" | custom-call | flops 4294967296 | bytes 16777216 | tf_op jit(solution)/shard_map/pallas_call | solution.py:308
  22.3 2.1 %collective-permute-done.1.refs_0_ = bf16[512,256]{1,0:T(8,128)(2,1)S(1)} collective-permute-done((bf16[512,256]{1,0:T(8,128)(2,1)S(1)}, bf16[512,256]{1,0:T(8,128)(2,1)S(1)}, u32[]{:S(2)}, u32[]{:S(2)}) %collective-permute-start.1) | collective-permute-done | bytes 262176 | tf_op jit(solution)/shard_map/ppermute | solution.py:22
  24.4 0.6 shard_map.65
  25.1 0.6 shard_map.62
  25.7 0.5 collective-permute-start.3
  26.3 0.6 shard_map.64.a_ref
  26.9 0.6 shard_map.61.a_ref
  28.0 2.3 %collective-permute-start.7 = (s16[528,256]{1,0:T(8,128)(2,1)S(1)}, s16[528,256]{1,0:T(8,128)(2,1)S(1)}, u32[]{:S(2)}, u32[]{:S(2)}) collective-permute-start(s16[528,256]{1,0:T(8,128)(2,1)S(1)} %get-tuple-element.15), channel_id=1, source_target_pairs={{0,6},{1,7},{2,4},{3,5},{4,2},{5,3},{6,0},{7,1},{8,14},{9,15},{10,... | collective-permute-start | bytes 811016 | tf_op jit(solution)/shard_map/ppermute | solution.py:22
  30.6 0.6 collective-permute-start.4
  31.2 1.2 %collective-permute-start.5 = (s16[528,256]{1,0:T(8,128)(2,1)S(1)}, s16[528,256]{1,0:T(8,128)(2,1)S(1)}, u32[]{:S(2)}, u32[]{:S(2)}) collective-permute-start(s16[528,256]{1,0:T(8,128)(2,1)S(1)} %get-tuple-element.14), channel_id=1, source_target_pairs={{0,4},{1,5},{2,6},{3,7},{4,0},{5,1},{6,2},{7,3},{8,12},{9,13},{10,... | collective-permute-start | bytes 811016 | tf_op jit(solution)/shard_map/ppermute | solution.py:22
  32.4 5.9 %collective-permute-done.7.refs_2_ = s16[528,256]{1,0:T(8,128)(2,1)S(1)} collective-permute-done((s16[528,256]{1,0:T(8,128)(2,1)S(1)}, s16[528,256]{1,0:T(8,128)(2,1)S(1)}, u32[]{:S(2)}, u32[]{:S(2)}) %collective-permute-start.7) | collective-permute-done | bytes 270368 | tf_op jit(solution)/shard_map/ppermute | solution.py:22
  38.3 4.8 %collective-permute-done.4.refs_0_ = s16[528,256]{1,0:T(8,128)(2,1)S(1)} collective-permute-done((s16[528,256]{1,0:T(8,128)(2,1)S(1)}, s16[528,256]{1,0:T(8,128)(2,1)S(1)}, u32[]{:S(2)}, u32[]{:S(2)}) %collective-permute-start.4) | collective-permute-done | bytes 270368 | tf_op jit(solution)/shard_map/ppermute | solution.py:22
  43.3 0.6 shard_map.67
  44.0 1.2 %collective-permute-done.8 = f32[136,128]{1,0:T(8,128)S(1)} collective-permute-done((f32[136,128]{1,0:T(8,128)S(1)}, f32[136,128]{1,0:T(8,128)S(1)}, u32[]{:S(2)}, u32[]{:S(2)}) %collective-permute-start.8) | collective-permute-done | bytes 69664 | tf_op jit(solution)/shard_map/ppermute | solution.py:22
  45.3 2.3 %collective-permute-start.10 = (f32[136,128]{1,0:T(8,128)S(1)}, f32[136,128]{1,0:T(8,128)S(1)}, u32[]{:S(2)}, u32[]{:S(2)}) collective-permute-start(f32[136,128]{1,0:T(8,128)S(1)} %add.80), channel_id=1, source_target_pairs={{0,6},{1,7},{2,4},{3,5},{4,2},{5,3},{6,0},{7,1},{8,14},{9,15},{10,... | collective-permute-start | bytes 208904 | tf_op jit(solution)/shard_map/ppermute | solution.py:22
  47.6 0.5 collective-permute-start.11
  48.1 0.7 collective-permute-start.9
  48.8 2.2 %collective-permute-done.10 = f32[136,128]{1,0:T(8,128)S(1)} collective-permute-done((f32[136,128]{1,0:T(8,128)S(1)}, f32[136,128]{1,0:T(8,128)S(1)}, u32[]{:S(2)}, u32[]{:S(2)}) %collective-permute-start.10) | collective-permute-done | bytes 69664 | tf_op jit(solution)/shard_map/ppermute | solution.py:22
  51.0 0.9 %collective-permute-done.11 = f32[136,128]{1,0:T(8,128)S(1)} collective-permute-done((f32[136,128]{1,0:T(8,128)S(1)}, f32[136,128]{1,0:T(8,128)S(1)}, u32[]{:S(2)}, u32[]{:S(2)}) %collective-permute-start.11) | collective-permute-done | bytes 69664 | tf_op jit(solution)/shard_map/ppermute | solution.py:22
  51.9 0.5 collective-permute-done.9
  52.4 4.5 %collective-permute-start.12 = (f32[136,128]{1,0:T(8,128)S(1)}, f32[136,128]{1,0:T(8,128)S(1)}, u32[]{:S(2)}, u32[]{:S(2)}) collective-permute-start(f32[136,128]{1,0:T(8,128)S(1)} %add_add_fusion.1), channel_id=1, source_target_pairs={{0,24},{8,16},{16,8},{24,0},{1,25},{9,17},{17,9},{25,1},{2,26},{10... | collective-permute-start | bytes 208904 | tf_op jit(solution)/shard_map/ppermute | solution.py:22
  57.0 0.6 collective-permute-start.14
  57.6 2.0 %collective-permute-done.12 = f32[136,128]{1,0:T(8,128)S(1)} collective-permute-done((f32[136,128]{1,0:T(8,128)S(1)}, f32[136,128]{1,0:T(8,128)S(1)}, u32[]{:S(2)}, u32[]{:S(2)}) %collective-permute-start.12) | collective-permute-done | bytes 69664 | tf_op jit(solution)/shard_map/ppermute | solution.py:22
  59.6 2.7 %collective-permute-done.13 = f32[136,128]{1,0:T(8,128)S(1)} collective-permute-done((f32[136,128]{1,0:T(8,128)S(1)}, f32[136,128]{1,0:T(8,128)S(1)}, u32[]{:S(2)}, u32[]{:S(2)}) %collective-permute-start.13) | collective-permute-done | bytes 69664 | tf_op jit(solution)/shard_map/ppermute | solution.py:22
  62.4 1.2 %collective-permute-done.15.other_ref = f32[136,128]{1,0:T(8,128)S(1)} collective-permute-done((f32[136,128]{1,0:T(8,128)S(1)}, f32[136,128]{1,0:T(8,128)S(1)}, u32[]{:S(2)}, u32[]{:S(2)}) %collective-permute-start.15) | collective-permute-done | bytes 69664 | tf_op jit(solution)/shard_map/ppermute | solution.py:22
  63.6 9.4 %shard_map.68 = (f32[512,256]{1,0:T(8,128)}, f32[256,256]{1,0:T(8,128)}) custom-call(s32[1]{0:T(128)} %bitcast.core, f32[136,128]{1,0:T(8,128)S(1)} %add_add_fusion.mine_ref, f32[136,128]{1,0:T(8,128)S(1)} %collective-permute-done.15.other_ref, f32[512,256]{1,0:T(8,128)S(1)} %get-tuple-element.19.s_ref), custom_call_target="tpu_custom_call" | custom-call | tf_op jit(solution)/shard_map/pallas_call | solution.py:419
  (16 shorter events, 1.2 us)
Async XLA Ops:
  0.6 16.3 %collective-permute-start = (bf16[512,256]{1,0:T(8,128)(2,1)}, bf16[512,256]{1,0:T(8,128)(2,1)S(1)}, u32[]{:S(2)}, u32[]{:S(2)}) collective-permute-start(bf16[512,256]{1,0:T(8,128)(2,1)} %refs_0_.1), channel_id=1, source_target_pairs={{0,16},{8,24},{16,0},{24,8},{1,17},{9,25},{17,1},{25,9},{2,18},{10... | collective-permute-start | bytes 786440 | tf_op jit(solution)/shard_map/ppermute | solution.py:22
  4.7 13.0 %collective-permute-start.2 = (bf16[512,256]{1,0:T(8,128)(2,1)}, bf16[512,256]{1,0:T(8,128)(2,1)S(1)}, u32[]{:S(2)}, u32[]{:S(2)}) collective-permute-start(bf16[512,256]{1,0:T(8,128)(2,1)} %refs_0_.1), channel_id=1, source_target_pairs={{0,8},{8,0},{16,24},{24,16},{1,9},{9,1},{17,25},{25,17},{2,10},{10... | collective-permute-start | bytes 786440 | tf_op jit(solution)/shard_map/ppermute | solution.py:22
  7.0 10.7 %copy-start = (bf16[512,256]{1,0:T(8,128)(2,1)S(1)}, bf16[512,256]{1,0:T(8,128)(2,1)}, u32[]{:S(2)}) copy-start(bf16[512,256]{1,0:T(8,128)(2,1)} %refs_0_.1) | copy-start | bytes 786436
  17.0 7.4 %collective-permute-start.1 = (bf16[512,256]{1,0:T(8,128)(2,1)S(1)}, bf16[512,256]{1,0:T(8,128)(2,1)S(1)}, u32[]{:S(2)}, u32[]{:S(2)}) collective-permute-start(bf16[512,256]{1,0:T(8,128)(2,1)S(1)} %collective-permute-done.refs_2_), channel_id=1, source_target_pairs={{0,8},{8,0},{16,24},{24,16},{1,9},{9,1},{17,25},{25,17},{2,10},{10... | collective-permute-start | bytes 786440 | tf_op jit(solution)/shard_map/ppermute | solution.py:22
  25.0 2.7 %collective-permute-start.6 = (f32[2,512,256]{2,1,0:T(8,128)S(1)}, f32[2,512,256]{2,1,0:T(8,128)S(1)}, u32[]{:S(2)}, u32[]{:S(2)}) collective-permute-start(f32[2,512,256]{2,1,0:T(8,128)S(1)} %shard_map.65), channel_id=1, source_target_pairs={{0,1},{1,0},{2,3},{3,2},{4,5},{5,4},{6,7},{7,6},{8,9},{9,8},{10,11... | collective-permute-start | bytes 3145736 | tf_op jit(solution)/shard_map/ppermute | solution.py:22
  25.7 4.6 %collective-permute-start.3 = (f32[2,512,256]{2,1,0:T(8,128)S(1)}, f32[2,512,256]{2,1,0:T(8,128)S(1)}, u32[]{:S(2)}, u32[]{:S(2)}) collective-permute-start(f32[2,512,256]{2,1,0:T(8,128)S(1)} %shard_map.62), channel_id=1, source_target_pairs={{0,1},{1,0},{2,3},{3,2},{4,5},{5,4},{6,7},{7,6},{8,9},{9,8},{10,11... | collective-permute-start | bytes 3145736 | tf_op jit(solution)/shard_map/ppermute | solution.py:22
  28.0 10.3 %collective-permute-start.7 = (s16[528,256]{1,0:T(8,128)(2,1)S(1)}, s16[528,256]{1,0:T(8,128)(2,1)S(1)}, u32[]{:S(2)}, u32[]{:S(2)}) collective-permute-start(s16[528,256]{1,0:T(8,128)(2,1)S(1)} %get-tuple-element.15), channel_id=1, source_target_pairs={{0,6},{1,7},{2,4},{3,5},{4,2},{5,3},{6,0},{7,1},{8,14},{9,15},{10,... | collective-permute-start | bytes 811016 | tf_op jit(solution)/shard_map/ppermute | solution.py:22
  30.6 12.5 %collective-permute-start.4 = (s16[528,256]{1,0:T(8,128)(2,1)S(1)}, s16[528,256]{1,0:T(8,128)(2,1)S(1)}, u32[]{:S(2)}, u32[]{:S(2)}) collective-permute-start(s16[528,256]{1,0:T(8,128)(2,1)S(1)} %get-tuple-element.13), channel_id=1, source_target_pairs={{0,2},{1,3},{2,0},{3,1},{4,6},{5,7},{6,4},{7,5},{8,10},{9,11},{10,... | collective-permute-start | bytes 811016 | tf_op jit(solution)/shard_map/ppermute | solution.py:22
  31.2 12.1 %collective-permute-start.5 = (s16[528,256]{1,0:T(8,128)(2,1)S(1)}, s16[528,256]{1,0:T(8,128)(2,1)S(1)}, u32[]{:S(2)}, u32[]{:S(2)}) collective-permute-start(s16[528,256]{1,0:T(8,128)(2,1)S(1)} %get-tuple-element.14), channel_id=1, source_target_pairs={{0,4},{1,5},{2,6},{3,7},{4,0},{5,1},{6,2},{7,3},{8,12},{9,13},{10,... | collective-permute-start | bytes 811016 | tf_op jit(solution)/shard_map/ppermute | solution.py:22
  43.9 1.3 %collective-permute-start.8 = (f32[136,128]{1,0:T(8,128)S(1)}, f32[136,128]{1,0:T(8,128)S(1)}, u32[]{:S(2)}, u32[]{:S(2)}) collective-permute-start(f32[136,128]{1,0:T(8,128)S(1)} %get-tuple-element.18), channel_id=1, source_target_pairs={{0,1},{1,0},{2,3},{3,2},{4,5},{5,4},{6,7},{7,6},{8,9},{9,8},{10,11... | collective-permute-start | bytes 208904 | tf_op jit(solution)/shard_map/ppermute | solution.py:22
  45.3 5.7 %collective-permute-start.10 = (f32[136,128]{1,0:T(8,128)S(1)}, f32[136,128]{1,0:T(8,128)S(1)}, u32[]{:S(2)}, u32[]{:S(2)}) collective-permute-start(f32[136,128]{1,0:T(8,128)S(1)} %add.80), channel_id=1, source_target_pairs={{0,6},{1,7},{2,4},{3,5},{4,2},{5,3},{6,0},{7,1},{8,14},{9,15},{10,... | collective-permute-start | bytes 208904 | tf_op jit(solution)/shard_map/ppermute | solution.py:22
  47.6 4.3 %collective-permute-start.11 = (f32[136,128]{1,0:T(8,128)S(1)}, f32[136,128]{1,0:T(8,128)S(1)}, u32[]{:S(2)}, u32[]{:S(2)}) collective-permute-start(f32[136,128]{1,0:T(8,128)S(1)} %add.80), channel_id=1, source_target_pairs={{0,2},{1,3},{2,0},{3,1},{4,6},{5,7},{6,4},{7,5},{8,10},{9,11},{10,... | collective-permute-start | bytes 208904 | tf_op jit(solution)/shard_map/ppermute | solution.py:22
  48.1 4.3 %collective-permute-start.9 = (f32[136,128]{1,0:T(8,128)S(1)}, f32[136,128]{1,0:T(8,128)S(1)}, u32[]{:S(2)}, u32[]{:S(2)}) collective-permute-start(f32[136,128]{1,0:T(8,128)S(1)} %add.80), channel_id=1, source_target_pairs={{0,4},{1,5},{2,6},{3,7},{4,0},{5,1},{6,2},{7,3},{8,12},{9,13},{10,... | collective-permute-start | bytes 208904 | tf_op jit(solution)/shard_map/ppermute | solution.py:22
  52.4 7.2 %collective-permute-start.12 = (f32[136,128]{1,0:T(8,128)S(1)}, f32[136,128]{1,0:T(8,128)S(1)}, u32[]{:S(2)}, u32[]{:S(2)}) collective-permute-start(f32[136,128]{1,0:T(8,128)S(1)} %add_add_fusion.1), channel_id=1, source_target_pairs={{0,24},{8,16},{16,8},{24,0},{1,25},{9,17},{17,9},{25,1},{2,26},{10... | collective-permute-start | bytes 208904 | tf_op jit(solution)/shard_map/ppermute | solution.py:22
  57.0 5.3 %collective-permute-start.13 = (f32[136,128]{1,0:T(8,128)S(1)}, f32[136,128]{1,0:T(8,128)S(1)}, u32[]{:S(2)}, u32[]{:S(2)}) collective-permute-start(f32[136,128]{1,0:T(8,128)S(1)} %add_add_fusion.1), channel_id=1, source_target_pairs={{0,16},{8,24},{16,0},{24,8},{1,17},{9,25},{17,1},{25,9},{2,18},{10... | collective-permute-start | bytes 208904 | tf_op jit(solution)/shard_map/ppermute | solution.py:22
  57.0 5.3 %collective-permute-start.14 = (f32[136,128]{1,0:T(8,128)S(1)}, f32[136,128]{1,0:T(8,128)S(1)}, u32[]{:S(2)}, u32[]{:S(2)}) collective-permute-start(f32[136,128]{1,0:T(8,128)S(1)} %add_add_fusion.1), channel_id=1, source_target_pairs={{0,8},{8,0},{16,24},{24,16},{1,9},{9,1},{17,25},{25,17},{2,10},{10... | collective-permute-start | bytes 208904 | tf_op jit(solution)/shard_map/ppermute | solution.py:22
  62.3 1.3 %collective-permute-start.15 = (f32[136,128]{1,0:T(8,128)S(1)}, f32[136,128]{1,0:T(8,128)S(1)}, u32[]{:S(2)}, u32[]{:S(2)}) collective-permute-start(f32[136,128]{1,0:T(8,128)S(1)} %add_add_fusion.mine_ref), channel_id=1, source_target_pairs={{0,1},{1,0},{2,3},{3,2},{4,5},{5,4},{6,7},{7,6},{8,9},{9,8},{10,11... | collective-permute-start | bytes 208904 | tf_op jit(solution)/shard_map/ppermute | solution.py:22

commit v8 on v7

--- a/solution.py
+++ b/solution.py
@@ -13,7 +13,7 @@
 LEVELS = 32700.0
 OCTAVE = 64.0
 DENSE_BYTES = 32 * 2**20
-STEP = 4
+STEP = 8
 PACK = 2 * PANEL + 16
 
 
@@ -156,6 +156,10 @@
 PAIRS = ((0, 0), (0, 1), (1, 0), (1, 1), (0, 2), (2, 0))
 
 
+def lane_copy(x, k):
+    return jnp.take_along_axis(x, jnp.full(x.shape, k, jnp.int32), axis=1, mode="promise_in_bounds")
+
+
 def factor(gram):
     n = gram.shape[0]
     eye = lax.broadcasted_iota(jnp.int32, (n, n), 0) == lax.broadcasted_iota(jnp.int32, (n, n), 1)
@@ -177,30 +181,40 @@
         last = first + STEP
         for b in range(first, last):
             cols = {
-                t: [jnp.broadcast_to(left[t][:, 8 * b + k : 8 * b + k + 1], (8, n)) for k in range(8)]
+                t: [lane_copy(left[t], 8 * b + k) for k in range(8)]
                 for t in range(b, last)
             }
+            spread = {(i, j): row(cols[b][j], i) for j in range(8) for i in range(j, 8)}
+            low, root = {}, {}
             for k in range(0, 8, 2):
-                p, q, r = row(cols[b][k], k), row(cols[b][k], k + 1), row(cols[b][k + 1], k + 1)
-                root_p = lax.rsqrt(p)
-                ratio = q * root_p
-                det = p * r - q * q
-                root_r = lax.rsqrt(det) * (p * root_p)
-                one = {t: cols[t][k] * root_p for t in range(b, last)}
-                two = {t: (cols[t][k + 1] - one[t] * ratio) * root_r for t in range(b, last)}
+                p, q, r = spread[k, k], spread[k + 1, k], spread[k + 1, k + 1]
+                root[k] = lax.rsqrt(p)
+                low[k + 1, k] = q * root[k]
+                root[k + 1] = lax.rsqrt(p * r - q * q) * (p * root[k])
+                for i in range(k + 2, 8):
+                    low[i, k] = spread[i, k] * root[k]
+                    low[i, k + 1] = (spread[i, k + 1] - low[i, k] * low[k + 1, k]) * root[k + 1]
                 for j in range(k + 2, 8):
-                    u, v = row(one[b], j), row(two[b], j)
-                    for t in range(b, last):
-                        cols[t][j] = cols[t][j] - one[t] * u - two[t] * v
-                below_one = jnp.where(sub > k + 1, one[b], 0.0)
-                below_two = jnp.where(sub > k + 1, two[b], 0.0)
-                for side in (left, right):
-                    top = row(side[b], k) * root_p
-                    low = (row(side[b], k + 1) - top * ratio) * root_r
-                    rest = side[b] - below_one * top - below_two * low
-                    side[b] = jnp.where(sub == k, top, jnp.where(sub == k + 1, low, rest))
-                    for t in range(b + 1, last):
-                        side[t] = side[t] - one[t] * top - two[t] * low
+                    for i in range(j, 8):
+                        spread[i, j] = spread[i, j] - low[i, k] * low[j, k] - low[i, k + 1] * low[j, k + 1]
+
+            def solve(terms):
+                done = []
+                for k, term in enumerate(terms):
+                    for j in range(k):
+                        term = term - done[j] * low[k, j]
+                    done.append(term * root[k])
+                return done
+
+            mult = {t: solve(cols[t]) for t in range(b + 1, last)}
+            for side in (left, right):
+                tops = solve([row(side[b], k) for k in range(8)])
+                side[b] = tops[0]
+                for k in range(1, 8):
+                    side[b] = jnp.where(sub == k, tops[k], side[b])
+                for t in range(b + 1, last):
+                    for k in range(8):
+                        side[t] = side[t] - mult[t][k] * tops[k]
         if last < n // 8:
             u = split(jnp.concatenate(left[first:last], axis=0), 3)
             v = split(jnp.concatenate(right[first:last], axis=0), 3)

time: 73.1 us -> 71.1 us (0.973)
  Pallas kernels: 23.9 us -> 21.9 us
    pallas_call x1, Pallas kernels: 9.37 us -> 7.37 us  [on_device(): pl.pallas_call(functools.partial(tail_kernel, 1.0 / order_total), grid_sp...]
  transfers between devices with their start and end apart: 16 -> 16, of which waited for: 13 -> 13; matrix products, arithmetic and copies ran while one was open for 1% -> 1% of each run, Pallas kernels for 18% -> 19%
where the time goes in v8:
time: 71.1 us; the launch traced here: 71 us
  waiting for transfers between devices  27.6 us (39%)
  Pallas kernels  21.9 us (31%)
  starting transfers between devices  19.9 us (28%)
  other arithmetic  0.77 us (1%)
  between operations  0.75 us (1%)
    ppermute x16, waiting for transfers between devices, exchange(): return lax.ppermute(value, axis, [(i, i ^ mask) for i in range(size)])  27.6 us
    ppermute x16, starting transfers between devices, exchange(): return lax.ppermute(value, axis, [(i, i ^ mask) for i in range(size)])  19.9 us
    pallas_call x1, Pallas kernels, on_device(): pl.pallas_call(functools.partial(tail_kernel, 1.0 / order_total), grid_sp...  7.37 us
    pallas_call x5, Pallas kernels, product(): pl.pallas_call(functools.partial(product_kernel, first, chosen), grid=(co...  7.08 us
    pallas_call x1, Pallas kernels, scatter_blocks(): pl.pallas_call(scatter_kernel, out_shape=pltpu.VMEM((n_slots, BS, BS), va...  6.21 us
  transfers between devices with their start and end apart: 16, of which 13 were waited for; matrix products, arithmetic and copies ran while one was open for 1% of the time, Pallas kernels for 19%

profile of v8, /device:TPU:0, one launch (start us, length us, event | category | flops | bytes accessed | tf_op | source)
XLA Modules:
  0.0 71.0 jit_solution(7757279827941047681)
XLA Ops:
  0.6 4.1 %collective-permute-start = (bf16[512,256]{1,0:T(8,128)(2,1)}, bf16[512,256]{1,0:T(8,128)(2,1)S(1)}, u32[]{:S(2)}, u32[]{:S(2)}) collective-permute-start(bf16[512,256]{1,0:T(8,128)(2,1)} %refs_0_.1), channel_id=1, source_target_pairs={{0,16},{8,24},{16,0},{24,8},{1,17},{9,25},{17,1},{25,9},{2,18},{10... | collective-permute-start | bytes 786440 | tf_op jit(solution)/shard_map/ppermute | solution.py:22
  4.7 1.6 %collective-permute-start.2 = (bf16[512,256]{1,0:T(8,128)(2,1)}, bf16[512,256]{1,0:T(8,128)(2,1)S(1)}, u32[]{:S(2)}, u32[]{:S(2)}) collective-permute-start(bf16[512,256]{1,0:T(8,128)(2,1)} %refs_0_.1), channel_id=1, source_target_pairs={{0,8},{8,0},{16,24},{24,16},{1,9},{9,1},{17,25},{25,17},{2,10},{10... | collective-permute-start | bytes 786440 | tf_op jit(solution)/shard_map/ppermute | solution.py:22
  6.3 0.7 %fusion.4.slots = s32[256]{0:T(256)S(1)} fusion(s32[256]{0:T(256)} %param.7, s32[256]{0:T(256)} %param.6, s32[]{:T(128)S(6)} %axis_index.17, s32[]{:T(128)S(6)} %mul.26, s32[]{:T(128)S(6)} %select_n.44, s32[]{:T(128)S(6)} %axis_index.14, s32[]{:T(128)S(6)} %mul.21), kind=kLoop, calls=%fused_computation.26 | loop fusion | flops 23040 | bytes 3092 | tf_op jit(solution)/shard_map/add | solution.py:302
  7.0 6.2 %shard_map.59 = bf16[512,128,128]{2,1,0:T(8,128)(2,1)S(1)} custom-call(s32[256]{0:T(256)S(1)} %fusion.4.slots, bf16[256,128,128]{2,1,0:T(8,128)(2,1)} %values.1), custom_call_target="tpu_custom_call" | custom-call | bytes 25165824 | tf_op jit(solution)/shard_map/pallas_call | solution.py:42
  13.3 3.7 %collective-permute-done.refs_2_ = bf16[512,256]{1,0:T(8,128)(2,1)S(1)} collective-permute-done((bf16[512,256]{1,0:T(8,128)(2,1)}, bf16[512,256]{1,0:T(8,128)(2,1)S(1)}, u32[]{:S(2)}, u32[]{:S(2)}) %collective-permute-start) | collective-permute-done | bytes 262176 | tf_op jit(solution)/shard_map/ppermute | solution.py:22
  17.0 0.7 %collective-permute-start.1 = (bf16[512,256]{1,0:T(8,128)(2,1)S(1)}, bf16[512,256]{1,0:T(8,128)(2,1)S(1)}, u32[]{:S(2)}, u32[]{:S(2)}) collective-permute-start(bf16[512,256]{1,0:T(8,128)(2,1)S(1)} %collective-permute-done.refs_2_), channel_id=1, source_target_pairs={{0,8},{8,0},{16,24},{24,16},{1,9},{9,1},{17,25},{25,17},{2,10},{10... | collective-permute-start | bytes 786440 | tf_op jit(solution)/shard_map/ppermute | solution.py:22
  17.7 4.6 %shard_map.60.refs_1_ = f32[8,512,256]{2,1,0:T(8,128)S(1)} custom-call(bf16[8,4,16,128,128]{4,3,2,1,0:T(8,128)(2,1)S(1)} %bitcast.2, bf16[512,256]{1,0:T(8,128)(2,1)S(1)} %copy-done, bf16[512,256]{1,0:T(8,128)(2,1)S(1)} %collective-permute-done.2.refs_1_, bf16[512,256]{1,0:T(8,128)(2,1)S(1)} %collective-permute-done.refs_2_), custom_call_target="tpu_custom_call" | custom-call | flops 4294967296 | bytes 16777216 | tf_op jit(solution)/shard_map/pallas_call | solution.py:322
  22.3 2.1 %collective-permute-done.1.refs_0_ = bf16[512,256]{1,0:T(8,128)(2,1)S(1)} collective-permute-done((bf16[512,256]{1,0:T(8,128)(2,1)S(1)}, bf16[512,256]{1,0:T(8,128)(2,1)S(1)}, u32[]{:S(2)}, u32[]{:S(2)}) %collective-permute-start.1) | collective-permute-done | bytes 262176 | tf_op jit(solution)/shard_map/ppermute | solution.py:22
  24.4 0.6 shard_map.65
  25.1 0.6 shard_map.62
  25.7 0.5 collective-permute-start.3
  26.3 0.6 shard_map.64.a_ref
  26.9 0.6 shard_map.61.a_ref
  28.0 2.3 %collective-permute-start.7 = (s16[528,256]{1,0:T(8,128)(2,1)S(1)}, s16[528,256]{1,0:T(8,128)(2,1)S(1)}, u32[]{:S(2)}, u32[]{:S(2)}) collective-permute-start(s16[528,256]{1,0:T(8,128)(2,1)S(1)} %get-tuple-element.15), channel_id=1, source_target_pairs={{0,6},{1,7},{2,4},{3,5},{4,2},{5,3},{6,0},{7,1},{8,14},{9,15},{10,... | collective-permute-start | bytes 811016 | tf_op jit(solution)/shard_map/ppermute | solution.py:22
  30.6 0.6 collective-permute-start.4
  31.2 1.2 %collective-permute-start.5 = (s16[528,256]{1,0:T(8,128)(2,1)S(1)}, s16[528,256]{1,0:T(8,128)(2,1)S(1)}, u32[]{:S(2)}, u32[]{:S(2)}) collective-permute-start(s16[528,256]{1,0:T(8,128)(2,1)S(1)} %get-tuple-element.14), channel_id=1, source_target_pairs={{0,4},{1,5},{2,6},{3,7},{4,0},{5,1},{6,2},{7,3},{8,12},{9,13},{10,... | collective-permute-start | bytes 811016 | tf_op jit(solution)/shard_map/ppermute | solution.py:22
  32.4 5.9 %collective-permute-done.7.refs_2_ = s16[528,256]{1,0:T(8,128)(2,1)S(1)} collective-permute-done((s16[528,256]{1,0:T(8,128)(2,1)S(1)}, s16[528,256]{1,0:T(8,128)(2,1)S(1)}, u32[]{:S(2)}, u32[]{:S(2)}) %collective-permute-start.7) | collective-permute-done | bytes 270368 | tf_op jit(solution)/shard_map/ppermute | solution.py:22
  38.3 4.8 %collective-permute-done.4.refs_0_ = s16[528,256]{1,0:T(8,128)(2,1)S(1)} collective-permute-done((s16[528,256]{1,0:T(8,128)(2,1)S(1)}, s16[528,256]{1,0:T(8,128)(2,1)S(1)}, u32[]{:S(2)}, u32[]{:S(2)}) %collective-permute-start.4) | collective-permute-done | bytes 270368 | tf_op jit(solution)/shard_map/ppermute | solution.py:22
  43.3 0.6 shard_map.67
  44.0 1.2 %collective-permute-done.8 = f32[136,128]{1,0:T(8,128)S(1)} collective-permute-done((f32[136,128]{1,0:T(8,128)S(1)}, f32[136,128]{1,0:T(8,128)S(1)}, u32[]{:S(2)}, u32[]{:S(2)}) %collective-permute-start.8) | collective-permute-done | bytes 69664 | tf_op jit(solution)/shard_map/ppermute | solution.py:22
  45.3 2.3 %collective-permute-start.10 = (f32[136,128]{1,0:T(8,128)S(1)}, f32[136,128]{1,0:T(8,128)S(1)}, u32[]{:S(2)}, u32[]{:S(2)}) collective-permute-start(f32[136,128]{1,0:T(8,128)S(1)} %add.80), channel_id=1, source_target_pairs={{0,6},{1,7},{2,4},{3,5},{4,2},{5,3},{6,0},{7,1},{8,14},{9,15},{10,... | collective-permute-start | bytes 208904 | tf_op jit(solution)/shard_map/ppermute | solution.py:22
  47.6 0.5 collective-permute-start.11
  48.1 0.7 %collective-permute-start.9 = (f32[136,128]{1,0:T(8,128)S(1)}, f32[136,128]{1,0:T(8,128)S(1)}, u32[]{:S(2)}, u32[]{:S(2)}) collective-permute-start(f32[136,128]{1,0:T(8,128)S(1)} %add.80), channel_id=1, source_target_pairs={{0,4},{1,5},{2,6},{3,7},{4,0},{5,1},{6,2},{7,3},{8,12},{9,13},{10,... | collective-permute-start | bytes 208904 | tf_op jit(solution)/shard_map/ppermute | solution.py:22
  48.8 2.2 %collective-permute-done.10 = f32[136,128]{1,0:T(8,128)S(1)} collective-permute-done((f32[136,128]{1,0:T(8,128)S(1)}, f32[136,128]{1,0:T(8,128)S(1)}, u32[]{:S(2)}, u32[]{:S(2)}) %collective-permute-start.10) | collective-permute-done | bytes 69664 | tf_op jit(solution)/shard_map/ppermute | solution.py:22
  51.0 0.9 %collective-permute-done.11 = f32[136,128]{1,0:T(8,128)S(1)} collective-permute-done((f32[136,128]{1,0:T(8,128)S(1)}, f32[136,128]{1,0:T(8,128)S(1)}, u32[]{:S(2)}, u32[]{:S(2)}) %collective-permute-start.11) | collective-permute-done | bytes 69664 | tf_op jit(solution)/shard_map/ppermute | solution.py:22
  51.9 0.5 collective-permute-done.9
  52.4 4.5 %collective-permute-start.12 = (f32[136,128]{1,0:T(8,128)S(1)}, f32[136,128]{1,0:T(8,128)S(1)}, u32[]{:S(2)}, u32[]{:S(2)}) collective-permute-start(f32[136,128]{1,0:T(8,128)S(1)} %add_add_fusion.1), channel_id=1, source_target_pairs={{0,24},{8,16},{16,8},{24,0},{1,25},{9,17},{17,9},{25,1},{2,26},{10... | collective-permute-start | bytes 208904 | tf_op jit(solution)/shard_map/ppermute | solution.py:22
  57.0 0.6 collective-permute-start.14
  57.6 2.0 %collective-permute-done.12 = f32[136,128]{1,0:T(8,128)S(1)} collective-permute-done((f32[136,128]{1,0:T(8,128)S(1)}, f32[136,128]{1,0:T(8,128)S(1)}, u32[]{:S(2)}, u32[]{:S(2)}) %collective-permute-start.12) | collective-permute-done | bytes 69664 | tf_op jit(solution)/shard_map/ppermute | solution.py:22
  59.6 2.7 %collective-permute-done.13 = f32[136,128]{1,0:T(8,128)S(1)} collective-permute-done((f32[136,128]{1,0:T(8,128)S(1)}, f32[136,128]{1,0:T(8,128)S(1)}, u32[]{:S(2)}, u32[]{:S(2)}) %collective-permute-start.13) | collective-permute-done | bytes 69664 | tf_op jit(solution)/shard_map/ppermute | solution.py:22
  62.4 1.2 %collective-permute-done.15.other_ref = f32[136,128]{1,0:T(8,128)S(1)} collective-permute-done((f32[136,128]{1,0:T(8,128)S(1)}, f32[136,128]{1,0:T(8,128)S(1)}, u32[]{:S(2)}, u32[]{:S(2)}) %collective-permute-start.15) | collective-permute-done | bytes 69664 | tf_op jit(solution)/shard_map/ppermute | solution.py:22
  63.6 7.4 %shard_map.68 = (f32[512,256]{1,0:T(8,128)}, f32[256,256]{1,0:T(8,128)}) custom-call(s32[1]{0:T(128)} %bitcast.core, f32[136,128]{1,0:T(8,128)S(1)} %add_add_fusion.mine_ref, f32[136,128]{1,0:T(8,128)S(1)} %collective-permute-done.15.other_ref, f32[512,256]{1,0:T(8,128)S(1)} %get-tuple-element.19.s_ref), custom_call_target="tpu_custom_call" | custom-call | tf_op jit(solution)/shard_map/pallas_call | solution.py:433
  (16 shorter events, 1.2 us)
Async XLA Ops:
  0.6 16.3 %collective-permute-start = (bf16[512,256]{1,0:T(8,128)(2,1)}, bf16[512,256]{1,0:T(8,128)(2,1)S(1)}, u32[]{:S(2)}, u32[]{:S(2)}) collective-permute-start(bf16[512,256]{1,0:T(8,128)(2,1)} %refs_0_.1), channel_id=1, source_target_pairs={{0,16},{8,24},{16,0},{24,8},{1,17},{9,25},{17,1},{25,9},{2,18},{10... | collective-permute-start | bytes 786440 | tf_op jit(solution)/shard_map/ppermute | solution.py:22
  4.7 13.0 %collective-permute-start.2 = (bf16[512,256]{1,0:T(8,128)(2,1)}, bf16[512,256]{1,0:T(8,128)(2,1)S(1)}, u32[]{:S(2)}, u32[]{:S(2)}) collective-permute-start(bf16[512,256]{1,0:T(8,128)(2,1)} %refs_0_.1), channel_id=1, source_target_pairs={{0,8},{8,0},{16,24},{24,16},{1,9},{9,1},{17,25},{25,17},{2,10},{10... | collective-permute-start | bytes 786440 | tf_op jit(solution)/shard_map/ppermute | solution.py:22
  7.0 10.7 %copy-start = (bf16[512,256]{1,0:T(8,128)(2,1)S(1)}, bf16[512,256]{1,0:T(8,128)(2,1)}, u32[]{:S(2)}) copy-start(bf16[512,256]{1,0:T(8,128)(2,1)} %refs_0_.1) | copy-start | bytes 786436
  17.0 7.4 %collective-permute-start.1 = (bf16[512,256]{1,0:T(8,128)(2,1)S(1)}, bf16[512,256]{1,0:T(8,128)(2,1)S(1)}, u32[]{:S(2)}, u32[]{:S(2)}) collective-permute-start(bf16[512,256]{1,0:T(8,128)(2,1)S(1)} %collective-permute-done.refs_2_), channel_id=1, source_target_pairs={{0,8},{8,0},{16,24},{24,16},{1,9},{9,1},{17,25},{25,17},{2,10},{10... | collective-permute-start | bytes 786440 | tf_op jit(solution)/shard_map/ppermute | solution.py:22
  25.0 2.7 %collective-permute-start.6 = (f32[2,512,256]{2,1,0:T(8,128)S(1)}, f32[2,512,256]{2,1,0:T(8,128)S(1)}, u32[]{:S(2)}, u32[]{:S(2)}) collective-permute-start(f32[2,512,256]{2,1,0:T(8,128)S(1)} %shard_map.65), channel_id=1, source_target_pairs={{0,1},{1,0},{2,3},{3,2},{4,5},{5,4},{6,7},{7,6},{8,9},{9,8},{10,11... | collective-permute-start | bytes 3145736 | tf_op jit(solution)/shard_map/ppermute | solution.py:22
  25.7 4.6 %collective-permute-start.3 = (f32[2,512,256]{2,1,0:T(8,128)S(1)}, f32[2,512,256]{2,1,0:T(8,128)S(1)}, u32[]{:S(2)}, u32[]{:S(2)}) collective-permute-start(f32[2,512,256]{2,1,0:T(8,128)S(1)} %shard_map.62), channel_id=1, source_target_pairs={{0,1},{1,0},{2,3},{3,2},{4,5},{5,4},{6,7},{7,6},{8,9},{9,8},{10,11... | collective-permute-start | bytes 3145736 | tf_op jit(solution)/shard_map/ppermute | solution.py:22
  28.0 10.3 %collective-permute-start.7 = (s16[528,256]{1,0:T(8,128)(2,1)S(1)}, s16[528,256]{1,0:T(8,128)(2,1)S(1)}, u32[]{:S(2)}, u32[]{:S(2)}) collective-permute-start(s16[528,256]{1,0:T(8,128)(2,1)S(1)} %get-tuple-element.15), channel_id=1, source_target_pairs={{0,6},{1,7},{2,4},{3,5},{4,2},{5,3},{6,0},{7,1},{8,14},{9,15},{10,... | collective-permute-start | bytes 811016 | tf_op jit(solution)/shard_map/ppermute | solution.py:22
  30.6 12.5 %collective-permute-start.4 = (s16[528,256]{1,0:T(8,128)(2,1)S(1)}, s16[528,256]{1,0:T(8,128)(2,1)S(1)}, u32[]{:S(2)}, u32[]{:S(2)}) collective-permute-start(s16[528,256]{1,0:T(8,128)(2,1)S(1)} %get-tuple-element.13), channel_id=1, source_target_pairs={{0,2},{1,3},{2,0},{3,1},{4,6},{5,7},{6,4},{7,5},{8,10},{9,11},{10,... | collective-permute-start | bytes 811016 | tf_op jit(solution)/shard_map/ppermute | solution.py:22
  31.2 12.1 %collective-permute-start.5 = (s16[528,256]{1,0:T(8,128)(2,1)S(1)}, s16[528,256]{1,0:T(8,128)(2,1)S(1)}, u32[]{:S(2)}, u32[]{:S(2)}) collective-permute-start(s16[528,256]{1,0:T(8,128)(2,1)S(1)} %get-tuple-element.14), channel_id=1, source_target_pairs={{0,4},{1,5},{2,6},{3,7},{4,0},{5,1},{6,2},{7,3},{8,12},{9,13},{10,... | collective-permute-start | bytes 811016 | tf_op jit(solution)/shard_map/ppermute | solution.py:22
  43.9 1.3 %collective-permute-start.8 = (f32[136,128]{1,0:T(8,128)S(1)}, f32[136,128]{1,0:T(8,128)S(1)}, u32[]{:S(2)}, u32[]{:S(2)}) collective-permute-start(f32[136,128]{1,0:T(8,128)S(1)} %get-tuple-element.18), channel_id=1, source_target_pairs={{0,1},{1,0},{2,3},{3,2},{4,5},{5,4},{6,7},{7,6},{8,9},{9,8},{10,11... | collective-permute-start | bytes 208904 | tf_op jit(solution)/shard_map/ppermute | solution.py:22
  45.3 5.7 %collective-permute-start.10 = (f32[136,128]{1,0:T(8,128)S(1)}, f32[136,128]{1,0:T(8,128)S(1)}, u32[]{:S(2)}, u32[]{:S(2)}) collective-permute-start(f32[136,128]{1,0:T(8,128)S(1)} %add.80), channel_id=1, source_target_pairs={{0,6},{1,7},{2,4},{3,5},{4,2},{5,3},{6,0},{7,1},{8,14},{9,15},{10,... | collective-permute-start | bytes 208904 | tf_op jit(solution)/shard_map/ppermute | solution.py:22
  47.6 4.3 %collective-permute-start.11 = (f32[136,128]{1,0:T(8,128)S(1)}, f32[136,128]{1,0:T(8,128)S(1)}, u32[]{:S(2)}, u32[]{:S(2)}) collective-permute-start(f32[136,128]{1,0:T(8,128)S(1)} %add.80), channel_id=1, source_target_pairs={{0,2},{1,3},{2,0},{3,1},{4,6},{5,7},{6,4},{7,5},{8,10},{9,11},{10,... | collective-permute-start | bytes 208904 | tf_op jit(solution)/shard_map/ppermute | solution.py:22
  48.1 4.3 %collective-permute-start.9 = (f32[136,128]{1,0:T(8,128)S(1)}, f32[136,128]{1,0:T(8,128)S(1)}, u32[]{:S(2)}, u32[]{:S(2)}) collective-permute-start(f32[136,128]{1,0:T(8,128)S(1)} %add.80), channel_id=1, source_target_pairs={{0,4},{1,5},{2,6},{3,7},{4,0},{5,1},{6,2},{7,3},{8,12},{9,13},{10,... | collective-permute-start | bytes 208904 | tf_op jit(solution)/shard_map/ppermute | solution.py:22
  52.4 7.2 %collective-permute-start.12 = (f32[136,128]{1,0:T(8,128)S(1)}, f32[136,128]{1,0:T(8,128)S(1)}, u32[]{:S(2)}, u32[]{:S(2)}) collective-permute-start(f32[136,128]{1,0:T(8,128)S(1)} %add_add_fusion.1), channel_id=1, source_target_pairs={{0,24},{8,16},{16,8},{24,0},{1,25},{9,17},{17,9},{25,1},{2,26},{10... | collective-permute-start | bytes 208904 | tf_op jit(solution)/shard_map/ppermute | solution.py:22
  57.0 5.3 %collective-permute-start.13 = (f32[136,128]{1,0:T(8,128)S(1)}, f32[136,128]{1,0:T(8,128)S(1)}, u32[]{:S(2)}, u32[]{:S(2)}) collective-permute-start(f32[136,128]{1,0:T(8,128)S(1)} %add_add_fusion.1), channel_id=1, source_target_pairs={{0,16},{8,24},{16,0},{24,8},{1,17},{9,25},{17,1},{25,9},{2,18},{10... | collective-permute-start | bytes 208904 | tf_op jit(solution)/shard_map/ppermute | solution.py:22
  57.0 5.3 %collective-permute-start.14 = (f32[136,128]{1,0:T(8,128)S(1)}, f32[136,128]{1,0:T(8,128)S(1)}, u32[]{:S(2)}, u32[]{:S(2)}) collective-permute-start(f32[136,128]{1,0:T(8,128)S(1)} %add_add_fusion.1), channel_id=1, source_target_pairs={{0,8},{8,0},{16,24},{24,16},{1,9},{9,1},{17,25},{25,17},{2,10},{10... | collective-permute-start | bytes 208904 | tf_op jit(solution)/shard_map/ppermute | solution.py:22
  62.3 1.3 %collective-permute-start.15 = (f32[136,128]{1,0:T(8,128)S(1)}, f32[136,128]{1,0:T(8,128)S(1)}, u32[]{:S(2)}, u32[]{:S(2)}) collective-permute-start(f32[136,128]{1,0:T(8,128)S(1)} %add_add_fusion.mine_ref), channel_id=1, source_target_pairs={{0,1},{1,0},{2,3},{3,2},{4,5},{5,4},{6,7},{7,6},{8,9},{9,8},{10,11... | collective-permute-start | bytes 208904 | tf_op jit(solution)/shard_map/ppermute | solution.py:22

commit v9 on v8

--- a/solution.py
+++ b/solution.py
@@ -380,15 +380,13 @@
     t = [value] + [exchange(value, axis, mask << low_bit) for mask in range(1, 2**bits)]
     if bits == 1:
         return t[0] + t[1]
-    if axis == "col":
-        return (t[2] + t[3]) + (t[0] + t[1])
-    return (t[3] + t[2]) + (t[1] + t[0])
+    return (t[2] + t[3]) + (t[0] + t[1])
 
 
 def sum_over_axis(value, axis, low_bit):
     bits = lax.axis_size(axis).bit_length() - 1
     while low_bit < bits:
-        take = min(2, bits - low_bit)
+        take = min(2 if axis == "col" else 1, bits - low_bit)
         value = direct_sum(value, axis, low_bit, take)
         low_bit += take
     return value

time: 71.1 us -> 71.3 us (level)
    ppermute x16 -> x15, waiting for transfers between devices: 27.6 us -> 27.8 us  [exchange(): return lax.ppermute(value, axis, [(i, i ^ mask) for i in range(size)])]
    ppermute x16 -> x15, starting transfers between devices: 19.9 us -> 19.9 us  [exchange(): return lax.ppermute(value, axis, [(i, i ^ mask) for i in range(size)])]
  transfers between devices with their start and end apart: 16 -> 15, of which waited for: 13 -> 13; matrix products, arithmetic and copies ran while one was open for 1% -> 1% of each run, Pallas kernels for 19% -> 19%
where the time goes in v9:
time: 71.3 us; the launch traced here: 71.1 us
  waiting for transfers between devices  27.8 us (39%)
  Pallas kernels  21.9 us (31%)
  starting transfers between devices  19.9 us (28%)
  other arithmetic  0.78 us (1%)
  between operations  0.75 us (1%)
    ppermute x15, waiting for transfers between devices, exchange(): return lax.ppermute(value, axis, [(i, i ^ mask) for i in range(size)])  27.8 us
    ppermute x15, starting transfers between devices, exchange(): return lax.ppermute(value, axis, [(i, i ^ mask) for i in range(size)])  19.9 us
    pallas_call x1, Pallas kernels, on_device(): pl.pallas_call(functools.partial(tail_kernel, 1.0 / order_total), grid_sp...  7.37 us
    pallas_call x5, Pallas kernels, product(): pl.pallas_call(functools.partial(product_kernel, first, chosen), grid=(co...  7.08 us
    pallas_call x1, Pallas kernels, scatter_blocks(): pl.pallas_call(scatter_kernel, out_shape=pltpu.VMEM((n_slots, BS, BS), va...  6.21 us
  transfers between devices with their start and end apart: 15, of which 13 were waited for; matrix products, arithmetic and copies ran while one was open for 1% of the time, Pallas kernels for 19%

profile of v9, /device:TPU:0, one launch (start us, length us, event | category | flops | bytes accessed | tf_op | source)
XLA Modules:
  0.0 71.1 jit_solution(3833889263573175487)
XLA Ops:
  0.6 4.1 %collective-permute-start = (bf16[512,256]{1,0:T(8,128)(2,1)}, bf16[512,256]{1,0:T(8,128)(2,1)S(1)}, u32[]{:S(2)}, u32[]{:S(2)}) collective-permute-start(bf16[512,256]{1,0:T(8,128)(2,1)} %refs_0_.1), channel_id=1, source_target_pairs={{0,16},{8,24},{16,0},{24,8},{1,17},{9,25},{17,1},{25,9},{2,18},{10... | collective-permute-start | bytes 786440 | tf_op jit(solution)/shard_map/ppermute | solution.py:22
  4.7 1.6 %collective-permute-start.2 = (bf16[512,256]{1,0:T(8,128)(2,1)}, bf16[512,256]{1,0:T(8,128)(2,1)S(1)}, u32[]{:S(2)}, u32[]{:S(2)}) collective-permute-start(bf16[512,256]{1,0:T(8,128)(2,1)} %refs_0_.1), channel_id=1, source_target_pairs={{0,8},{8,0},{16,24},{24,16},{1,9},{9,1},{17,25},{25,17},{2,10},{10... | collective-permute-start | bytes 786440 | tf_op jit(solution)/shard_map/ppermute | solution.py:22
  6.3 0.7 %fusion.4.slots = s32[256]{0:T(256)S(1)} fusion(s32[256]{0:T(256)} %param.7, s32[256]{0:T(256)} %param.6, s32[]{:T(128)S(6)} %axis_index.17, s32[]{:T(128)S(6)} %mul.26, s32[]{:T(128)S(6)} %select_n.44, s32[]{:T(128)S(6)} %axis_index.14, s32[]{:T(128)S(6)} %mul.21), kind=kLoop, calls=%fused_computation.25 | loop fusion | flops 23040 | bytes 3092 | tf_op jit(solution)/shard_map/add | solution.py:302
  7.0 6.2 %shard_map.59 = bf16[512,128,128]{2,1,0:T(8,128)(2,1)S(1)} custom-call(s32[256]{0:T(256)S(1)} %fusion.4.slots, bf16[256,128,128]{2,1,0:T(8,128)(2,1)} %values.1), custom_call_target="tpu_custom_call" | custom-call | bytes 25165824 | tf_op jit(solution)/shard_map/pallas_call | solution.py:42
  13.3 3.7 %collective-permute-done.refs_2_ = bf16[512,256]{1,0:T(8,128)(2,1)S(1)} collective-permute-done((bf16[512,256]{1,0:T(8,128)(2,1)}, bf16[512,256]{1,0:T(8,128)(2,1)S(1)}, u32[]{:S(2)}, u32[]{:S(2)}) %collective-permute-start) | collective-permute-done | bytes 262176 | tf_op jit(solution)/shard_map/ppermute | solution.py:22
  17.0 0.7 %collective-permute-start.1 = (bf16[512,256]{1,0:T(8,128)(2,1)S(1)}, bf16[512,256]{1,0:T(8,128)(2,1)S(1)}, u32[]{:S(2)}, u32[]{:S(2)}) collective-permute-start(bf16[512,256]{1,0:T(8,128)(2,1)S(1)} %collective-permute-done.refs_2_), channel_id=1, source_target_pairs={{0,8},{8,0},{16,24},{24,16},{1,9},{9,1},{17,25},{25,17},{2,10},{10... | collective-permute-start | bytes 786440 | tf_op jit(solution)/shard_map/ppermute | solution.py:22
  17.7 4.6 %shard_map.60.refs_1_ = f32[8,512,256]{2,1,0:T(8,128)S(1)} custom-call(bf16[8,4,16,128,128]{4,3,2,1,0:T(8,128)(2,1)S(1)} %bitcast.2, bf16[512,256]{1,0:T(8,128)(2,1)S(1)} %copy-done, bf16[512,256]{1,0:T(8,128)(2,1)S(1)} %collective-permute-done.2.refs_1_, bf16[512,256]{1,0:T(8,128)(2,1)S(1)} %collective-permute-done.refs_2_), custom_call_target="tpu_custom_call" | custom-call | flops 4294967296 | bytes 16777216 | tf_op jit(solution)/shard_map/pallas_call | solution.py:322
  22.3 2.1 %collective-permute-done.1.refs_0_ = bf16[512,256]{1,0:T(8,128)(2,1)S(1)} collective-permute-done((bf16[512,256]{1,0:T(8,128)(2,1)S(1)}, bf16[512,256]{1,0:T(8,128)(2,1)S(1)}, u32[]{:S(2)}, u32[]{:S(2)}) %collective-permute-start.1) | collective-permute-done | bytes 262176 | tf_op jit(solution)/shard_map/ppermute | solution.py:22
  24.4 0.6 shard_map.65
  25.1 0.6 shard_map.62
  25.7 0.5 collective-permute-start.3
  26.3 0.6 shard_map.64.a_ref
  26.9 0.6 shard_map.61.a_ref
  28.0 2.3 %collective-permute-start.7 = (s16[528,256]{1,0:T(8,128)(2,1)S(1)}, s16[528,256]{1,0:T(8,128)(2,1)S(1)}, u32[]{:S(2)}, u32[]{:S(2)}) collective-permute-start(s16[528,256]{1,0:T(8,128)(2,1)S(1)} %get-tuple-element.15), channel_id=1, source_target_pairs={{0,6},{1,7},{2,4},{3,5},{4,2},{5,3},{6,0},{7,1},{8,14},{9,15},{10,... | collective-permute-start | bytes 811016 | tf_op jit(solution)/shard_map/ppermute | solution.py:22
  30.6 0.6 collective-permute-start.4
  31.2 1.2 %collective-permute-start.5 = (s16[528,256]{1,0:T(8,128)(2,1)S(1)}, s16[528,256]{1,0:T(8,128)(2,1)S(1)}, u32[]{:S(2)}, u32[]{:S(2)}) collective-permute-start(s16[528,256]{1,0:T(8,128)(2,1)S(1)} %get-tuple-element.14), channel_id=1, source_target_pairs={{0,4},{1,5},{2,6},{3,7},{4,0},{5,1},{6,2},{7,3},{8,12},{9,13},{10,... | collective-permute-start | bytes 811016 | tf_op jit(solution)/shard_map/ppermute | solution.py:22
  32.4 5.9 %collective-permute-done.7.refs_2_ = s16[528,256]{1,0:T(8,128)(2,1)S(1)} collective-permute-done((s16[528,256]{1,0:T(8,128)(2,1)S(1)}, s16[528,256]{1,0:T(8,128)(2,1)S(1)}, u32[]{:S(2)}, u32[]{:S(2)}) %collective-permute-start.7) | collective-permute-done | bytes 270368 | tf_op jit(solution)/shard_map/ppermute | solution.py:22
  38.3 4.8 %collective-permute-done.4.refs_0_ = s16[528,256]{1,0:T(8,128)(2,1)S(1)} collective-permute-done((s16[528,256]{1,0:T(8,128)(2,1)S(1)}, s16[528,256]{1,0:T(8,128)(2,1)S(1)}, u32[]{:S(2)}, u32[]{:S(2)}) %collective-permute-start.4) | collective-permute-done | bytes 270368 | tf_op jit(solution)/shard_map/ppermute | solution.py:22
  43.3 0.6 shard_map.67
  44.0 1.2 %collective-permute-done.8 = f32[136,128]{1,0:T(8,128)S(1)} collective-permute-done((f32[136,128]{1,0:T(8,128)S(1)}, f32[136,128]{1,0:T(8,128)S(1)}, u32[]{:S(2)}, u32[]{:S(2)}) %collective-permute-start.8) | collective-permute-done | bytes 69664 | tf_op jit(solution)/shard_map/ppermute | solution.py:22
  45.3 2.3 %collective-permute-start.10 = (f32[136,128]{1,0:T(8,128)S(1)}, f32[136,128]{1,0:T(8,128)S(1)}, u32[]{:S(2)}, u32[]{:S(2)}) collective-permute-start(f32[136,128]{1,0:T(8,128)S(1)} %add.77), channel_id=1, source_target_pairs={{0,6},{1,7},{2,4},{3,5},{4,2},{5,3},{6,0},{7,1},{8,14},{9,15},{10,... | collective-permute-start | bytes 208904 | tf_op jit(solution)/shard_map/ppermute | solution.py:22
  47.6 0.5 collective-permute-start.11
  48.1 0.7 %collective-permute-start.9 = (f32[136,128]{1,0:T(8,128)S(1)}, f32[136,128]{1,0:T(8,128)S(1)}, u32[]{:S(2)}, u32[]{:S(2)}) collective-permute-start(f32[136,128]{1,0:T(8,128)S(1)} %add.77), channel_id=1, source_target_pairs={{0,4},{1,5},{2,6},{3,7},{4,0},{5,1},{6,2},{7,3},{8,12},{9,13},{10,... | collective-permute-start | bytes 208904 | tf_op jit(solution)/shard_map/ppermute | solution.py:22
  48.8 2.2 %collective-permute-done.10 = f32[136,128]{1,0:T(8,128)S(1)} collective-permute-done((f32[136,128]{1,0:T(8,128)S(1)}, f32[136,128]{1,0:T(8,128)S(1)}, u32[]{:S(2)}, u32[]{:S(2)}) %collective-permute-start.10) | collective-permute-done | bytes 69664 | tf_op jit(solution)/shard_map/ppermute | solution.py:22
  51.0 0.9 %collective-permute-done.11 = f32[136,128]{1,0:T(8,128)S(1)} collective-permute-done((f32[136,128]{1,0:T(8,128)S(1)}, f32[136,128]{1,0:T(8,128)S(1)}, u32[]{:S(2)}, u32[]{:S(2)}) %collective-permute-start.11) | collective-permute-done | bytes 69664 | tf_op jit(solution)/shard_map/ppermute | solution.py:22
  51.9 0.5 collective-permute-done.9
  52.4 1.8 %collective-permute-start.12 = (f32[136,128]{1,0:T(8,128)S(1)}, f32[136,128]{1,0:T(8,128)S(1)}, u32[]{:S(2)}, u32[]{:S(2)}) collective-permute-start(f32[136,128]{1,0:T(8,128)S(1)} %add_add_fusion), channel_id=1, source_target_pairs={{0,8},{8,0},{16,24},{24,16},{1,9},{9,1},{17,25},{25,17},{2,10},{10... | collective-permute-start | bytes 208904 | tf_op jit(solution)/shard_map/ppermute | solution.py:22
  54.2 2.6 %collective-permute-done.12 = f32[136,128]{1,0:T(8,128)S(1)} collective-permute-done((f32[136,128]{1,0:T(8,128)S(1)}, f32[136,128]{1,0:T(8,128)S(1)}, u32[]{:S(2)}, u32[]{:S(2)}) %collective-permute-start.12) | collective-permute-done | bytes 69664 | tf_op jit(solution)/shard_map/ppermute | solution.py:22
  56.8 3.3 %collective-permute-start.13 = (f32[136,128]{1,0:T(8,128)S(1)}, f32[136,128]{1,0:T(8,128)S(1)}, u32[]{:S(2)}, u32[]{:S(2)}) collective-permute-start(f32[136,128]{1,0:T(8,128)S(1)} %add.81), channel_id=1, source_target_pairs={{0,16},{8,24},{16,0},{24,8},{1,17},{9,25},{17,1},{25,9},{2,18},{10... | collective-permute-start | bytes 208904 | tf_op jit(solution)/shard_map/ppermute | solution.py:22
  60.2 2.3 %collective-permute-done.13 = f32[136,128]{1,0:T(8,128)S(1)} collective-permute-done((f32[136,128]{1,0:T(8,128)S(1)}, f32[136,128]{1,0:T(8,128)S(1)}, u32[]{:S(2)}, u32[]{:S(2)}) %collective-permute-start.13) | collective-permute-done | bytes 69664 | tf_op jit(solution)/shard_map/ppermute | solution.py:22
  62.5 1.2 %collective-permute-done.14.other_ref = f32[136,128]{1,0:T(8,128)S(1)} collective-permute-done((f32[136,128]{1,0:T(8,128)S(1)}, f32[136,128]{1,0:T(8,128)S(1)}, u32[]{:S(2)}, u32[]{:S(2)}) %collective-permute-start.14) | collective-permute-done | bytes 69664 | tf_op jit(solution)/shard_map/ppermute | solution.py:22
  63.8 7.4 %shard_map.68 = (f32[512,256]{1,0:T(8,128)}, f32[256,256]{1,0:T(8,128)}) custom-call(s32[1]{0:T(128)} %bitcast.core, f32[136,128]{1,0:T(8,128)S(1)} %add.82.mine_ref, f32[136,128]{1,0:T(8,128)S(1)} %collective-permute-done.14.other_ref, f32[512,256]{1,0:T(8,128)S(1)} %get-tuple-element.19.s_ref), custom_call_target="tpu_custom_call" | custom-call | tf_op jit(solution)/shard_map/pallas_call | solution.py:431
  (15 shorter events, 1.2 us)
Async XLA Ops:
  0.6 16.3 %collective-permute-start = (bf16[512,256]{1,0:T(8,128)(2,1)}, bf16[512,256]{1,0:T(8,128)(2,1)S(1)}, u32[]{:S(2)}, u32[]{:S(2)}) collective-permute-start(bf16[512,256]{1,0:T(8,128)(2,1)} %refs_0_.1), channel_id=1, source_target_pairs={{0,16},{8,24},{16,0},{24,8},{1,17},{9,25},{17,1},{25,9},{2,18},{10... | collective-permute-start | bytes 786440 | tf_op jit(solution)/shard_map/ppermute | solution.py:22
  4.7 13.0 %collective-permute-start.2 = (bf16[512,256]{1,0:T(8,128)(2,1)}, bf16[512,256]{1,0:T(8,128)(2,1)S(1)}, u32[]{:S(2)}, u32[]{:S(2)}) collective-permute-start(bf16[512,256]{1,0:T(8,128)(2,1)} %refs_0_.1), channel_id=1, source_target_pairs={{0,8},{8,0},{16,24},{24,16},{1,9},{9,1},{17,25},{25,17},{2,10},{10... | collective-permute-start | bytes 786440 | tf_op jit(solution)/shard_map/ppermute | solution.py:22
  7.0 10.7 %copy-start = (bf16[512,256]{1,0:T(8,128)(2,1)S(1)}, bf16[512,256]{1,0:T(8,128)(2,1)}, u32[]{:S(2)}) copy-start(bf16[512,256]{1,0:T(8,128)(2,1)} %refs_0_.1) | copy-start | bytes 786436
  17.0 7.4 %collective-permute-start.1 = (bf16[512,256]{1,0:T(8,128)(2,1)S(1)}, bf16[512,256]{1,0:T(8,128)(2,1)S(1)}, u32[]{:S(2)}, u32[]{:S(2)}) collective-permute-start(bf16[512,256]{1,0:T(8,128)(2,1)S(1)} %collective-permute-done.refs_2_), channel_id=1, source_target_pairs={{0,8},{8,0},{16,24},{24,16},{1,9},{9,1},{17,25},{25,17},{2,10},{10... | collective-permute-start | bytes 786440 | tf_op jit(solution)/shard_map/ppermute | solution.py:22
  25.0 2.7 %collective-permute-start.6 = (f32[2,512,256]{2,1,0:T(8,128)S(1)}, f32[2,512,256]{2,1,0:T(8,128)S(1)}, u32[]{:S(2)}, u32[]{:S(2)}) collective-permute-start(f32[2,512,256]{2,1,0:T(8,128)S(1)} %shard_map.65), channel_id=1, source_target_pairs={{0,1},{1,0},{2,3},{3,2},{4,5},{5,4},{6,7},{7,6},{8,9},{9,8},{10,11... | collective-permute-start | bytes 3145736 | tf_op jit(solution)/shard_map/ppermute | solution.py:22
  25.7 4.6 %collective-permute-start.3 = (f32[2,512,256]{2,1,0:T(8,128)S(1)}, f32[2,512,256]{2,1,0:T(8,128)S(1)}, u32[]{:S(2)}, u32[]{:S(2)}) collective-permute-start(f32[2,512,256]{2,1,0:T(8,128)S(1)} %shard_map.62), channel_id=1, source_target_pairs={{0,1},{1,0},{2,3},{3,2},{4,5},{5,4},{6,7},{7,6},{8,9},{9,8},{10,11... | collective-permute-start | bytes 3145736 | tf_op jit(solution)/shard_map/ppermute | solution.py:22
  28.0 10.3 %collective-permute-start.7 = (s16[528,256]{1,0:T(8,128)(2,1)S(1)}, s16[528,256]{1,0:T(8,128)(2,1)S(1)}, u32[]{:S(2)}, u32[]{:S(2)}) collective-permute-start(s16[528,256]{1,0:T(8,128)(2,1)S(1)} %get-tuple-element.15), channel_id=1, source_target_pairs={{0,6},{1,7},{2,4},{3,5},{4,2},{5,3},{6,0},{7,1},{8,14},{9,15},{10,... | collective-permute-start | bytes 811016 | tf_op jit(solution)/shard_map/ppermute | solution.py:22
  30.6 12.5 %collective-permute-start.4 = (s16[528,256]{1,0:T(8,128)(2,1)S(1)}, s16[528,256]{1,0:T(8,128)(2,1)S(1)}, u32[]{:S(2)}, u32[]{:S(2)}) collective-permute-start(s16[528,256]{1,0:T(8,128)(2,1)S(1)} %get-tuple-element.13), channel_id=1, source_target_pairs={{0,2},{1,3},{2,0},{3,1},{4,6},{5,7},{6,4},{7,5},{8,10},{9,11},{10,... | collective-permute-start | bytes 811016 | tf_op jit(solution)/shard_map/ppermute | solution.py:22
  31.2 12.1 %collective-permute-start.5 = (s16[528,256]{1,0:T(8,128)(2,1)S(1)}, s16[528,256]{1,0:T(8,128)(2,1)S(1)}, u32[]{:S(2)}, u32[]{:S(2)}) collective-permute-start(s16[528,256]{1,0:T(8,128)(2,1)S(1)} %get-tuple-element.14), channel_id=1, source_target_pairs={{0,4},{1,5},{2,6},{3,7},{4,0},{5,1},{6,2},{7,3},{8,12},{9,13},{10,... | collective-permute-start | bytes 811016 | tf_op jit(solution)/shard_map/ppermute | solution.py:22
  43.9 1.3 %collective-permute-start.8 = (f32[136,128]{1,0:T(8,128)S(1)}, f32[136,128]{1,0:T(8,128)S(1)}, u32[]{:S(2)}, u32[]{:S(2)}) collective-permute-start(f32[136,128]{1,0:T(8,128)S(1)} %get-tuple-element.18), channel_id=1, source_target_pairs={{0,1},{1,0},{2,3},{3,2},{4,5},{5,4},{6,7},{7,6},{8,9},{9,8},{10,11... | collective-permute-start | bytes 208904 | tf_op jit(solution)/shard_map/ppermute | solution.py:22
  45.3 5.7 %collective-permute-start.10 = (f32[136,128]{1,0:T(8,128)S(1)}, f32[136,128]{1,0:T(8,128)S(1)}, u32[]{:S(2)}, u32[]{:S(2)}) collective-permute-start(f32[136,128]{1,0:T(8,128)S(1)} %add.77), channel_id=1, source_target_pairs={{0,6},{1,7},{2,4},{3,5},{4,2},{5,3},{6,0},{7,1},{8,14},{9,15},{10,... | collective-permute-start | bytes 208904 | tf_op jit(solution)/shard_map/ppermute | solution.py:22
  47.6 4.3 %collective-permute-start.11 = (f32[136,128]{1,0:T(8,128)S(1)}, f32[136,128]{1,0:T(8,128)S(1)}, u32[]{:S(2)}, u32[]{:S(2)}) collective-permute-start(f32[136,128]{1,0:T(8,128)S(1)} %add.77), channel_id=1, source_target_pairs={{0,2},{1,3},{2,0},{3,1},{4,6},{5,7},{6,4},{7,5},{8,10},{9,11},{10,... | collective-permute-start | bytes 208904 | tf_op jit(solution)/shard_map/ppermute | solution.py:22
  48.1 4.3 %collective-permute-start.9 = (f32[136,128]{1,0:T(8,128)S(1)}, f32[136,128]{1,0:T(8,128)S(1)}, u32[]{:S(2)}, u32[]{:S(2)}) collective-permute-start(f32[136,128]{1,0:T(8,128)S(1)} %add.77), channel_id=1, source_target_pairs={{0,4},{1,5},{2,6},{3,7},{4,0},{5,1},{6,2},{7,3},{8,12},{9,13},{10,... | collective-permute-start | bytes 208904 | tf_op jit(solution)/shard_map/ppermute | solution.py:22
  52.4 4.4 %collective-permute-start.12 = (f32[136,128]{1,0:T(8,128)S(1)}, f32[136,128]{1,0:T(8,128)S(1)}, u32[]{:S(2)}, u32[]{:S(2)}) collective-permute-start(f32[136,128]{1,0:T(8,128)S(1)} %add_add_fusion), channel_id=1, source_target_pairs={{0,8},{8,0},{16,24},{24,16},{1,9},{9,1},{17,25},{25,17},{2,10},{10... | collective-permute-start | bytes 208904 | tf_op jit(solution)/shard_map/ppermute | solution.py:22
  56.8 5.6 %collective-permute-start.13 = (f32[136,128]{1,0:T(8,128)S(1)}, f32[136,128]{1,0:T(8,128)S(1)}, u32[]{:S(2)}, u32[]{:S(2)}) collective-permute-start(f32[136,128]{1,0:T(8,128)S(1)} %add.81), channel_id=1, source_target_pairs={{0,16},{8,24},{16,0},{24,8},{1,17},{9,25},{17,1},{25,9},{2,18},{10... | collective-permute-start | bytes 208904 | tf_op jit(solution)/shard_map/ppermute | solution.py:22
  62.5 1.3 %collective-permute-start.14 = (f32[136,128]{1,0:T(8,128)S(1)}, f32[136,128]{1,0:T(8,128)S(1)}, u32[]{:S(2)}, u32[]{:S(2)}) collective-permute-start(f32[136,128]{1,0:T(8,128)S(1)} %add.82.mine_ref), channel_id=1, source_target_pairs={{0,1},{1,0},{2,3},{3,2},{4,5},{5,4},{6,7},{7,6},{8,9},{9,8},{10,11... | collective-permute-start | bytes 208904 | tf_op jit(solution)/shard_map/ppermute | solution.py:22

commit v10 on v8

--- a/solution.py
+++ b/solution.py
@@ -92,34 +92,46 @@
     o_ref[n * BS :, :] = tail.astype(jnp.int32).astype(jnp.int16)
 
 
-def dequantize(q_ref):
-    n = (q_ref.shape[0] - 16) // BS
-    tail = q_ref[n * BS :, :].astype(jnp.int32).astype(jnp.float32)
+def dequantize(q_ref, first, count):
+    rows = q_ref.shape[0] - 16
+    tail = q_ref[rows:, :].astype(jnp.int32).astype(jnp.float32)
     parts = []
-    for b in range(n):
+    for b in range(first, first + count):
         scale = jnp.exp(tail[b : b + 1] * (math.log(2.0) / OCTAVE)) * (1.0 / LEVELS)
         parts.append(q_ref[b * BS : (b + 1) * BS, :].astype(jnp.int32).astype(jnp.float32) * scale)
     return jnp.concatenate(parts, axis=0)
 
 
-def code_kernel(a_ref, b_ref, *o_refs):
-    total = a_ref[0] + b_ref[0]
-    for j, o_ref in enumerate(o_refs):
-
-        @pl.when(pl.program_id(0) == j)
-        def _(o_ref=o_ref):
-            if o_ref.dtype == jnp.int16:
-                quantize(total, o_ref)
-            else:
-                o_ref[...] = total
+def code_x_kernel(a_ref, b_ref, q_ref, keep_ref, pass_ref):
+    near, diagonal = a_ref[0] + b_ref[0], a_ref[1] + b_ref[1]
+    quantize(jnp.concatenate([diagonal[:, :PANEL], near[:, :PANEL]], axis=0), q_ref)
+    keep_ref[...] = near[:, PANEL:]
+    pass_ref[...] = diagonal[:, PANEL:]
+
+
+def code_y_kernel(a_ref, b_ref, pass_ref, q_ref, keep_ref, own_ref):
+    near = a_ref[0] + b_ref[0]
+    quantize(jnp.concatenate([pass_ref[...], near[:, PANEL:]], axis=0), q_ref)
+    keep_ref[...] = near[:, :PANEL]
+    own_ref[...] = a_ref[1] + b_ref[1]
+
+
+def merge_kernel(keep_ref, q_ref, o_ref):
+    quantize(keep_ref[...] + dequantize(q_ref, 0, keep_ref.shape[0] // BS), o_ref)
+
+
+def all_terms(own_ref, x_ref=None, y_ref=None, late_y_ref=None, late_x_ref=None):
+    if x_ref is None:
+        return own_ref[...]
+    n = own_ref.shape[0] // BS
+    first = dequantize(x_ref, n, n) + dequantize(late_y_ref, 0, n)
+    second = dequantize(y_ref, n, n) + dequantize(late_x_ref, 0, n)
+    return own_ref[...] + jnp.concatenate([first, second], axis=1)
 
 
 def reduce_kernel(core, *refs):
     *in_refs, s_ref, mine_ref, other_ref, pack = refs
-    total = None
-    for ref in in_refs:
-        term = dequantize(ref) if ref.dtype == jnp.int16 else ref[...]
-        total = term if total is None else total + term
+    total = all_terms(*in_refs)
     s_ref[...] = total
     gram_store(total, pack)
     half = pack.shape[0] // 2
@@ -296,7 +308,8 @@
     me = lax.axis_index("col")
     owner = local_rows // group
     peer_core = (owner + me) % 2
-    near = ((owner // 2 ^ me // 2) + chips - 1) % chips
+    near = owner // 2 ^ me // 2
+    near = ((near ^ near // 2) + chips - 1) % chips
     place = ((1 - peer_core) * chips + near) * group + local_rows % group
     shard = (local_cols // group) ^ lax.axis_index("row")
     slots = place * grid_cols + shard * group + local_cols % group
@@ -330,25 +343,29 @@
         )(dense, *[shards[k] for k in chosen], *added)
 
     first_sum = product(0, 2 * chips, early)
-    parts = [(0, chips // 2), (chips // 2, chips - chips // 2)]
-    peer = [exchange(product(at, n, late, first_sum), "col", 1) for at, n in parts]
-    near = [product(chips + at, n, late, first_sum) for at, n in parts]
-    sent = jax.ShapeDtypeStruct((shard_rows + 16, width), jnp.int16)
+    peer = [exchange(product(at, 2, late, first_sum), "col", 1) for at in (0, 2)]
+    near = [product(chips + at, 2, late, first_sum) for at in (0, 2)]
+
+    def call(kernel, outs, *args):
+        return pl.pallas_call(
+            kernel,
+            grid=(1,),
+            in_specs=[whole(x.shape) for x in args],
+            out_specs=[whole(x.shape) for x in outs],
+            out_shape=outs,
+            compiler_params=params,
+        )(*args)
+
+    panel = jax.ShapeDtypeStruct((shard_rows, PANEL), jnp.float32)
     kept = jax.ShapeDtypeStruct((shard_rows, width), jnp.float32)
-    terms = []
-    for (at, n), mine, theirs in zip(parts, near, peer):
-        shapes = [kept if at + i == chips - 1 else sent for i in range(n)]
-        done = pl.pallas_call(
-            code_kernel,
-            grid=(n,),
-            in_specs=[block(0), block(0)],
-            out_specs=[whole(x.shape) for x in shapes],
-            out_shape=shapes,
-            compiler_params=params,
-        )(mine, theirs)
-        for i, x in enumerate(done):
-            terms.append(x if x.dtype == jnp.float32 else exchange(x, "col", 2 * (at + i + 1)))
-    return terms
+    two = jax.ShapeDtypeStruct((2 * shard_rows + 16, PANEL), jnp.int16)
+    single = jax.ShapeDtypeStruct((shard_rows + 16, PANEL), jnp.int16)
+    coded_x, keep_x, passed = call(code_x_kernel, [two, panel, panel], near[0], peer[0])
+    coded_y, keep_y, own = call(code_y_kernel, [two, panel, kept], near[1], peer[1], passed)
+    from_x, from_y = exchange(coded_x, "col", 2), exchange(coded_y, "col", 4)
+    late_y = exchange(call(merge_kernel, [single], keep_y, from_x)[0], "col", 4)
+    late_x = exchange(call(merge_kernel, [single], keep_x, from_y)[0], "col", 2)
+    return [own, from_x, from_y, late_y, late_x]
 
 
 def tile_product(sketch_blocks, block_values, local_rows, local_cols, tile_rows):
@@ -409,7 +426,7 @@
     grid_cols = shard_rows * size_row // BS
     local_rows = block_rows - lax.axis_index("row") * grid_rows
     local_cols = block_columns - lax.axis_index("col") * grid_cols
-    dense = 2 * grid_rows * grid_cols * BS * BS <= DENSE_BYTES
+    dense = 2 * grid_rows * grid_cols * BS * BS <= DENSE_BYTES and size_col == 8 and width == 2 * PANEL
     sketch = dense_sketch if dense else looped_sketch
     terms = sketch(
         gaussian_sketch, block_values, local_rows, local_cols, grid_rows, grid_cols

time: 71.1 us -> 72.3 us (1.017)
  starting transfers between devices: 19.9 us -> 21.6 us
    ppermute x16 -> x17, starting transfers between devices: 19.9 us -> 21.6 us  [exchange(): return lax.ppermute(value, axis, [(i, i ^ mask) for i in range(size)])]
    ppermute x16 -> x17, waiting for transfers between devices: 27.6 us -> 27.2 us  [exchange(): return lax.ppermute(value, axis, [(i, i ^ mask) for i in range(size)])]
  transfers between devices with their start and end apart: 16 -> 17, of which waited for: 13 -> 13; matrix products, arithmetic and copies ran while one was open for 1% -> 1% of each run, Pallas kernels for 19% -> 18%
where the time goes in v10:
time: 72.3 us; the launch traced here: 72.1 us
  waiting for transfers between devices  27.2 us (38%)
  Pallas kernels  21.8 us (30%)
  starting transfers between devices  21.6 us (30%)
  other arithmetic  0.78 us (1%)
  between operations  0.76 us (1%)
    ppermute x17, waiting for transfers between devices, exchange(): return lax.ppermute(value, axis, [(i, i ^ mask) for i in range(size)])  27.2 us
    ppermute x17, starting transfers between devices, exchange(): return lax.ppermute(value, axis, [(i, i ^ mask) for i in range(size)])  21.6 us
    pallas_call x1, Pallas kernels, on_device(): pl.pallas_call(functools.partial(tail_kernel, 1.0 / order_total), grid_sp...  7.37 us
    pallas_call x5, Pallas kernels, product(): pl.pallas_call(functools.partial(product_kernel, first, chosen), grid=(co...  7.08 us
    pallas_call x1, Pallas kernels, scatter_blocks(): pl.pallas_call(scatter_kernel, out_shape=pltpu.VMEM((n_slots, BS, BS), va...  6.21 us
  transfers between devices with their start and end apart: 17, of which 13 were waited for; matrix products, arithmetic and copies ran while one was open for 1% of the time, Pallas kernels for 18%

profile of v10, /device:TPU:0, one launch (start us, length us, event | category | flops | bytes accessed | tf_op | source)
XLA Modules:
  0.0 72.1 jit_solution(4154694060012533393)
XLA Ops:
  0.6 4.1 %collective-permute-start = (bf16[512,256]{1,0:T(8,128)(2,1)}, bf16[512,256]{1,0:T(8,128)(2,1)S(1)}, u32[]{:S(2)}, u32[]{:S(2)}) collective-permute-start(bf16[512,256]{1,0:T(8,128)(2,1)} %refs_0_.1), channel_id=1, source_target_pairs={{0,16},{8,24},{16,0},{24,8},{1,17},{9,25},{17,1},{25,9},{2,18},{10... | collective-permute-start | bytes 786440 | tf_op jit(solution)/shard_map/ppermute | solution.py:22
  4.7 1.6 %collective-permute-start.2 = (bf16[512,256]{1,0:T(8,128)(2,1)}, bf16[512,256]{1,0:T(8,128)(2,1)S(1)}, u32[]{:S(2)}, u32[]{:S(2)}) collective-permute-start(bf16[512,256]{1,0:T(8,128)(2,1)} %refs_0_.1), channel_id=1, source_target_pairs={{0,8},{8,0},{16,24},{24,16},{1,9},{9,1},{17,25},{25,17},{2,10},{10... | collective-permute-start | bytes 786440 | tf_op jit(solution)/shard_map/ppermute | solution.py:22
  6.3 0.7 %fusion.5.slots = s32[256]{0:T(256)S(1)} fusion(s32[256]{0:T(256)} %param.7, s32[256]{0:T(256)} %param.6, s32[]{:T(128)S(6)} %axis_index.17, s32[]{:T(128)S(6)} %mul.26, s32[]{:T(128)S(6)} %select_n.47, s32[]{:T(128)S(6)} %axis_index.14, s32[]{:T(128)S(6)} %mul.21), kind=kLoop, calls=%fused_computation.31 | loop fusion | flops 27136 | bytes 3092 | tf_op jit(solution)/shard_map/add | solution.py:315
  7.1 6.2 %shard_map.59 = bf16[512,128,128]{2,1,0:T(8,128)(2,1)S(1)} custom-call(s32[256]{0:T(256)S(1)} %fusion.5.slots, bf16[256,128,128]{2,1,0:T(8,128)(2,1)} %values.1), custom_call_target="tpu_custom_call" | custom-call | bytes 25165824 | tf_op jit(solution)/shard_map/pallas_call | solution.py:42
  13.3 3.7 %collective-permute-done.refs_2_ = bf16[512,256]{1,0:T(8,128)(2,1)S(1)} collective-permute-done((bf16[512,256]{1,0:T(8,128)(2,1)}, bf16[512,256]{1,0:T(8,128)(2,1)S(1)}, u32[]{:S(2)}, u32[]{:S(2)}) %collective-permute-start) | collective-permute-done | bytes 262176 | tf_op jit(solution)/shard_map/ppermute | solution.py:22
  17.0 0.7 collective-permute-start.1
  17.7 4.6 %shard_map.60.refs_1_ = f32[8,512,256]{2,1,0:T(8,128)S(1)} custom-call(bf16[8,4,16,128,128]{4,3,2,1,0:T(8,128)(2,1)S(1)} %bitcast.2, bf16[512,256]{1,0:T(8,128)(2,1)S(1)} %copy-done, bf16[512,256]{1,0:T(8,128)(2,1)S(1)} %collective-permute-done.2.refs_1_, bf16[512,256]{1,0:T(8,128)(2,1)S(1)} %collective-permute-done.refs_2_), custom_call_target="tpu_custom_call" | custom-call | flops 4294967296 | bytes 16777216 | tf_op jit(solution)/shard_map/pallas_call | solution.py:335
  22.3 2.1 %collective-permute-done.1.refs_0_ = bf16[512,256]{1,0:T(8,128)(2,1)S(1)} collective-permute-done((bf16[512,256]{1,0:T(8,128)(2,1)S(1)}, bf16[512,256]{1,0:T(8,128)(2,1)S(1)}, u32[]{:S(2)}, u32[]{:S(2)}) %collective-permute-start.1) | collective-permute-done | bytes 262176 | tf_op jit(solution)/shard_map/ppermute | solution.py:22
  24.4 0.6 shard_map.64
  25.1 0.6 shard_map.62
  26.3 0.6 shard_map.63.a_ref
  26.9 0.6 shard_map.61.a_ref
  28.0 1.3 %collective-permute-done.3.b_ref = f32[2,512,256]{2,1,0:T(8,128)S(1)} collective-permute-done((f32[2,512,256]{2,1,0:T(8,128)S(1)}, f32[2,512,256]{2,1,0:T(8,128)S(1)}, u32[]{:S(2)}, u32[]{:S(2)}) %collective-permute-start.3) | collective-permute-done | bytes 1048608 | tf_op jit(solution)/shard_map/ppermute | solution.py:22
  29.4 1.4 %collective-permute-start.6 = (s16[1040,128]{1,0:T(8,128)(2,1)S(1)}, s16[1040,128]{1,0:T(8,128)(2,1)S(1)}, u32[]{:S(2)}, u32[]{:S(2)}) collective-permute-start(s16[1040,128]{1,0:T(8,128)(2,1)S(1)} %get-tuple-element.18), channel_id=1, source_target_pairs={{0,4},{1,5},{2,6},{3,7},{4,0},{5,1},{6,2},{7,3},{8,12},{9,13},{10,... | collective-permute-start | bytes 798728 | tf_op jit(solution)/shard_map/ppermute | solution.py:22
  30.8 1.5 %collective-permute-start.5 = (s16[1040,128]{1,0:T(8,128)(2,1)S(1)}, s16[1040,128]{1,0:T(8,128)(2,1)S(1)}, u32[]{:S(2)}, u32[]{:S(2)}) collective-permute-start(s16[1040,128]{1,0:T(8,128)(2,1)S(1)} %get-tuple-element.17), channel_id=1, source_target_pairs={{0,2},{1,3},{2,0},{3,1},{4,6},{5,7},{6,4},{7,5},{8,10},{9,11},{10,... | collective-permute-start | bytes 798728 | tf_op jit(solution)/shard_map/ppermute | solution.py:22
  32.3 5.6 %collective-permute-done.6.q_ref.refs_2_ = s16[1040,128]{1,0:T(8,128)(2,1)S(1)} collective-permute-done((s16[1040,128]{1,0:T(8,128)(2,1)S(1)}, s16[1040,128]{1,0:T(8,128)(2,1)S(1)}, u32[]{:S(2)}, u32[]{:S(2)}) %collective-permute-start.6) | collective-permute-done | bytes 266272 | tf_op jit(solution)/shard_map/ppermute | solution.py:22
  38.0 1.3 %collective-permute-start.8 = (s16[528,128]{1,0:T(8,128)(2,1)S(1)}, s16[528,128]{1,0:T(8,128)(2,1)S(1)}, u32[]{:S(2)}, u32[]{:S(2)}) collective-permute-start(s16[528,128]{1,0:T(8,128)(2,1)S(1)} %shard_map.68), channel_id=1, source_target_pairs={{0,2},{1,3},{2,0},{3,1},{4,6},{5,7},{6,4},{7,5},{8,10},{9,11},{10,... | collective-permute-start | bytes 405512 | tf_op jit(solution)/shard_map/ppermute | solution.py:22
  39.5 1.6 %collective-permute-start.7 = (s16[528,128]{1,0:T(8,128)(2,1)S(1)}, s16[528,128]{1,0:T(8,128)(2,1)S(1)}, u32[]{:S(2)}, u32[]{:S(2)}) collective-permute-start(s16[528,128]{1,0:T(8,128)(2,1)S(1)} %shard_map.67), channel_id=1, source_target_pairs={{0,4},{1,5},{2,6},{3,7},{4,0},{5,1},{6,2},{7,3},{8,12},{9,13},{10,... | collective-permute-start | bytes 405512 | tf_op jit(solution)/shard_map/ppermute | solution.py:22
  41.0 2.1 %collective-permute-done.8.refs_4_ = s16[528,128]{1,0:T(8,128)(2,1)S(1)} collective-permute-done((s16[528,128]{1,0:T(8,128)(2,1)S(1)}, s16[528,128]{1,0:T(8,128)(2,1)S(1)}, u32[]{:S(2)}, u32[]{:S(2)}) %collective-permute-start.8) | collective-permute-done | bytes 135200 | tf_op jit(solution)/shard_map/ppermute | solution.py:22
  43.1 1.4 %collective-permute-done.7.refs_3_ = s16[528,128]{1,0:T(8,128)(2,1)S(1)} collective-permute-done((s16[528,128]{1,0:T(8,128)(2,1)S(1)}, s16[528,128]{1,0:T(8,128)(2,1)S(1)}, u32[]{:S(2)}, u32[]{:S(2)}) %collective-permute-start.7) | collective-permute-done | bytes 135200 | tf_op jit(solution)/shard_map/ppermute | solution.py:22
  45.2 1.2 %collective-permute-done.9 = f32[136,128]{1,0:T(8,128)S(1)} collective-permute-done((f32[136,128]{1,0:T(8,128)S(1)}, f32[136,128]{1,0:T(8,128)S(1)}, u32[]{:S(2)}, u32[]{:S(2)}) %collective-permute-start.9) | collective-permute-done | bytes 69664 | tf_op jit(solution)/shard_map/ppermute | solution.py:22
  46.4 1.6 %collective-permute-start.10 = (f32[136,128]{1,0:T(8,128)S(1)}, f32[136,128]{1,0:T(8,128)S(1)}, u32[]{:S(2)}, u32[]{:S(2)}) collective-permute-start(f32[136,128]{1,0:T(8,128)S(1)} %add.81), channel_id=1, source_target_pairs={{0,4},{1,5},{2,6},{3,7},{4,0},{5,1},{6,2},{7,3},{8,12},{9,13},{10,... | collective-permute-start | bytes 208904 | tf_op jit(solution)/shard_map/ppermute | solution.py:22
  48.0 1.0 %collective-permute-start.11 = (f32[136,128]{1,0:T(8,128)S(1)}, f32[136,128]{1,0:T(8,128)S(1)}, u32[]{:S(2)}, u32[]{:S(2)}) collective-permute-start(f32[136,128]{1,0:T(8,128)S(1)} %add.81), channel_id=1, source_target_pairs={{0,6},{1,7},{2,4},{3,5},{4,2},{5,3},{6,0},{7,1},{8,14},{9,15},{10,... | collective-permute-start | bytes 208904 | tf_op jit(solution)/shard_map/ppermute | solution.py:22
  49.0 1.0 %collective-permute-start.12 = (f32[136,128]{1,0:T(8,128)S(1)}, f32[136,128]{1,0:T(8,128)S(1)}, u32[]{:S(2)}, u32[]{:S(2)}) collective-permute-start(f32[136,128]{1,0:T(8,128)S(1)} %add.81), channel_id=1, source_target_pairs={{0,2},{1,3},{2,0},{3,1},{4,6},{5,7},{6,4},{7,5},{8,10},{9,11},{10,... | collective-permute-start | bytes 208904 | tf_op jit(solution)/shard_map/ppermute | solution.py:22
  50.0 0.8 %collective-permute-done.10 = f32[136,128]{1,0:T(8,128)S(1)} collective-permute-done((f32[136,128]{1,0:T(8,128)S(1)}, f32[136,128]{1,0:T(8,128)S(1)}, u32[]{:S(2)}, u32[]{:S(2)}) %collective-permute-start.10) | collective-permute-done | bytes 69664 | tf_op jit(solution)/shard_map/ppermute | solution.py:22
  50.8 2.8 %collective-permute-done.11 = f32[136,128]{1,0:T(8,128)S(1)} collective-permute-done((f32[136,128]{1,0:T(8,128)S(1)}, f32[136,128]{1,0:T(8,128)S(1)}, u32[]{:S(2)}, u32[]{:S(2)}) %collective-permute-start.11) | collective-permute-done | bytes 69664 | tf_op jit(solution)/shard_map/ppermute | solution.py:22
  53.7 4.5 %collective-permute-start.13 = (f32[136,128]{1,0:T(8,128)S(1)}, f32[136,128]{1,0:T(8,128)S(1)}, u32[]{:S(2)}, u32[]{:S(2)}) collective-permute-start(f32[136,128]{1,0:T(8,128)S(1)} %add_add_fusion.1), channel_id=1, source_target_pairs={{0,24},{8,16},{16,8},{24,0},{1,25},{9,17},{17,9},{25,1},{2,26},{10... | collective-permute-start | bytes 208904 | tf_op jit(solution)/shard_map/ppermute | solution.py:22
  58.2 0.6 collective-permute-start.15
  58.8 1.8 %collective-permute-done.13 = f32[136,128]{1,0:T(8,128)S(1)} collective-permute-done((f32[136,128]{1,0:T(8,128)S(1)}, f32[136,128]{1,0:T(8,128)S(1)}, u32[]{:S(2)}, u32[]{:S(2)}) %collective-permute-start.13) | collective-permute-done | bytes 69664 | tf_op jit(solution)/shard_map/ppermute | solution.py:22
  60.6 2.8 %collective-permute-done.14 = f32[136,128]{1,0:T(8,128)S(1)} collective-permute-done((f32[136,128]{1,0:T(8,128)S(1)}, f32[136,128]{1,0:T(8,128)S(1)}, u32[]{:S(2)}, u32[]{:S(2)}) %collective-permute-start.14) | collective-permute-done | bytes 69664 | tf_op jit(solution)/shard_map/ppermute | solution.py:22
  63.5 1.2 %collective-permute-done.16.other_ref = f32[136,128]{1,0:T(8,128)S(1)} collective-permute-done((f32[136,128]{1,0:T(8,128)S(1)}, f32[136,128]{1,0:T(8,128)S(1)}, u32[]{:S(2)}, u32[]{:S(2)}) %collective-permute-start.16) | collective-permute-done | bytes 69664 | tf_op jit(solution)/shard_map/ppermute | solution.py:22
  64.8 7.4 %shard_map.70 = (f32[512,256]{1,0:T(8,128)}, f32[256,256]{1,0:T(8,128)}) custom-call(s32[1]{0:T(128)} %bitcast.core, f32[136,128]{1,0:T(8,128)S(1)} %add_add_fusion.mine_ref, f32[136,128]{1,0:T(8,128)S(1)} %collective-permute-done.16.other_ref, f32[512,256]{1,0:T(8,128)S(1)} %get-tuple-element.23.s_ref), custom_call_target="tpu_custom_call" | custom-call | tf_op jit(solution)/shard_map/pallas_call | solution.py:450
  (20 shorter events, 2.2 us)
Async XLA Ops:
  0.6 16.3 %collective-permute-start = (bf16[512,256]{1,0:T(8,128)(2,1)}, bf16[512,256]{1,0:T(8,128)(2,1)S(1)}, u32[]{:S(2)}, u32[]{:S(2)}) collective-permute-start(bf16[512,256]{1,0:T(8,128)(2,1)} %refs_0_.1), channel_id=1, source_target_pairs={{0,16},{8,24},{16,0},{24,8},{1,17},{9,25},{17,1},{25,9},{2,18},{10... | collective-permute-start | bytes 786440 | tf_op jit(solution)/shard_map/ppermute | solution.py:22
  4.7 13.0 %collective-permute-start.2 = (bf16[512,256]{1,0:T(8,128)(2,1)}, bf16[512,256]{1,0:T(8,128)(2,1)S(1)}, u32[]{:S(2)}, u32[]{:S(2)}) collective-permute-start(bf16[512,256]{1,0:T(8,128)(2,1)} %refs_0_.1), channel_id=1, source_target_pairs={{0,8},{8,0},{16,24},{24,16},{1,9},{9,1},{17,25},{25,17},{2,10},{10... | collective-permute-start | bytes 786440 | tf_op jit(solution)/shard_map/ppermute | solution.py:22
  7.0 10.7 %copy-start = (bf16[512,256]{1,0:T(8,128)(2,1)S(1)}, bf16[512,256]{1,0:T(8,128)(2,1)}, u32[]{:S(2)}) copy-start(bf16[512,256]{1,0:T(8,128)(2,1)} %refs_0_.1) | copy-start | bytes 786436
  17.0 7.4 %collective-permute-start.1 = (bf16[512,256]{1,0:T(8,128)(2,1)S(1)}, bf16[512,256]{1,0:T(8,128)(2,1)S(1)}, u32[]{:S(2)}, u32[]{:S(2)}) collective-permute-start(bf16[512,256]{1,0:T(8,128)(2,1)S(1)} %collective-permute-done.refs_2_), channel_id=1, source_target_pairs={{0,8},{8,0},{16,24},{24,16},{1,9},{9,1},{17,25},{25,17},{2,10},{10... | collective-permute-start | bytes 786440 | tf_op jit(solution)/shard_map/ppermute | solution.py:22
  25.0 2.7 %collective-permute-start.4 = (f32[2,512,256]{2,1,0:T(8,128)S(1)}, f32[2,512,256]{2,1,0:T(8,128)S(1)}, u32[]{:S(2)}, u32[]{:S(2)}) collective-permute-start(f32[2,512,256]{2,1,0:T(8,128)S(1)} %shard_map.64), channel_id=1, source_target_pairs={{0,1},{1,0},{2,3},{3,2},{4,5},{5,4},{6,7},{7,6},{8,9},{9,8},{10,11... | collective-permute-start | bytes 3145736 | tf_op jit(solution)/shard_map/ppermute | solution.py:22
  25.7 3.5 %collective-permute-start.3 = (f32[2,512,256]{2,1,0:T(8,128)S(1)}, f32[2,512,256]{2,1,0:T(8,128)S(1)}, u32[]{:S(2)}, u32[]{:S(2)}) collective-permute-start(f32[2,512,256]{2,1,0:T(8,128)S(1)} %shard_map.62), channel_id=1, source_target_pairs={{0,1},{1,0},{2,3},{3,2},{4,5},{5,4},{6,7},{7,6},{8,9},{9,8},{10,11... | collective-permute-start | bytes 3145736 | tf_op jit(solution)/shard_map/ppermute | solution.py:22
  29.4 8.5 %collective-permute-start.6 = (s16[1040,128]{1,0:T(8,128)(2,1)S(1)}, s16[1040,128]{1,0:T(8,128)(2,1)S(1)}, u32[]{:S(2)}, u32[]{:S(2)}) collective-permute-start(s16[1040,128]{1,0:T(8,128)(2,1)S(1)} %get-tuple-element.18), channel_id=1, source_target_pairs={{0,4},{1,5},{2,6},{3,7},{4,0},{5,1},{6,2},{7,3},{8,12},{9,13},{10,... | collective-permute-start | bytes 798728 | tf_op jit(solution)/shard_map/ppermute | solution.py:22
  30.8 8.6 %collective-permute-start.5 = (s16[1040,128]{1,0:T(8,128)(2,1)S(1)}, s16[1040,128]{1,0:T(8,128)(2,1)S(1)}, u32[]{:S(2)}, u32[]{:S(2)}) collective-permute-start(s16[1040,128]{1,0:T(8,128)(2,1)S(1)} %get-tuple-element.17), channel_id=1, source_target_pairs={{0,2},{1,3},{2,0},{3,1},{4,6},{5,7},{6,4},{7,5},{8,10},{9,11},{10,... | collective-permute-start | bytes 798728 | tf_op jit(solution)/shard_map/ppermute | solution.py:22
  38.0 5.1 %collective-permute-start.8 = (s16[528,128]{1,0:T(8,128)(2,1)S(1)}, s16[528,128]{1,0:T(8,128)(2,1)S(1)}, u32[]{:S(2)}, u32[]{:S(2)}) collective-permute-start(s16[528,128]{1,0:T(8,128)(2,1)S(1)} %shard_map.68), channel_id=1, source_target_pairs={{0,2},{1,3},{2,0},{3,1},{4,6},{5,7},{6,4},{7,5},{8,10},{9,11},{10,... | collective-permute-start | bytes 405512 | tf_op jit(solution)/shard_map/ppermute | solution.py:22
  39.5 5.1 %collective-permute-start.7 = (s16[528,128]{1,0:T(8,128)(2,1)S(1)}, s16[528,128]{1,0:T(8,128)(2,1)S(1)}, u32[]{:S(2)}, u32[]{:S(2)}) collective-permute-start(s16[528,128]{1,0:T(8,128)(2,1)S(1)} %shard_map.67), channel_id=1, source_target_pairs={{0,4},{1,5},{2,6},{3,7},{4,0},{5,1},{6,2},{7,3},{8,12},{9,13},{10,... | collective-permute-start | bytes 405512 | tf_op jit(solution)/shard_map/ppermute | solution.py:22
  45.1 1.3 %collective-permute-start.9 = (f32[136,128]{1,0:T(8,128)S(1)}, f32[136,128]{1,0:T(8,128)S(1)}, u32[]{:S(2)}, u32[]{:S(2)}) collective-permute-start(f32[136,128]{1,0:T(8,128)S(1)} %get-tuple-element.22), channel_id=1, source_target_pairs={{0,1},{1,0},{2,3},{3,2},{4,5},{5,4},{6,7},{7,6},{8,9},{9,8},{10,11... | collective-permute-start | bytes 208904 | tf_op jit(solution)/shard_map/ppermute | solution.py:22
  46.4 4.4 %collective-permute-start.10 = (f32[136,128]{1,0:T(8,128)S(1)}, f32[136,128]{1,0:T(8,128)S(1)}, u32[]{:S(2)}, u32[]{:S(2)}) collective-permute-start(f32[136,128]{1,0:T(8,128)S(1)} %add.81), channel_id=1, source_target_pairs={{0,4},{1,5},{2,6},{3,7},{4,0},{5,1},{6,2},{7,3},{8,12},{9,13},{10,... | collective-permute-start | bytes 208904 | tf_op jit(solution)/shard_map/ppermute | solution.py:22
  48.0 5.6 %collective-permute-start.11 = (f32[136,128]{1,0:T(8,128)S(1)}, f32[136,128]{1,0:T(8,128)S(1)}, u32[]{:S(2)}, u32[]{:S(2)}) collective-permute-start(f32[136,128]{1,0:T(8,128)S(1)} %add.81), channel_id=1, source_target_pairs={{0,6},{1,7},{2,4},{3,5},{4,2},{5,3},{6,0},{7,1},{8,14},{9,15},{10,... | collective-permute-start | bytes 208904 | tf_op jit(solution)/shard_map/ppermute | solution.py:22
  49.0 4.6 %collective-permute-start.12 = (f32[136,128]{1,0:T(8,128)S(1)}, f32[136,128]{1,0:T(8,128)S(1)}, u32[]{:S(2)}, u32[]{:S(2)}) collective-permute-start(f32[136,128]{1,0:T(8,128)S(1)} %add.81), channel_id=1, source_target_pairs={{0,2},{1,3},{2,0},{3,1},{4,6},{5,7},{6,4},{7,5},{8,10},{9,11},{10,... | collective-permute-start | bytes 208904 | tf_op jit(solution)/shard_map/ppermute | solution.py:22
  53.7 6.9 %collective-permute-start.13 = (f32[136,128]{1,0:T(8,128)S(1)}, f32[136,128]{1,0:T(8,128)S(1)}, u32[]{:S(2)}, u32[]{:S(2)}) collective-permute-start(f32[136,128]{1,0:T(8,128)S(1)} %add_add_fusion.1), channel_id=1, source_target_pairs={{0,24},{8,16},{16,8},{24,0},{1,25},{9,17},{17,9},{25,1},{2,26},{10... | collective-permute-start | bytes 208904 | tf_op jit(solution)/shard_map/ppermute | solution.py:22
  58.2 5.2 %collective-permute-start.14 = (f32[136,128]{1,0:T(8,128)S(1)}, f32[136,128]{1,0:T(8,128)S(1)}, u32[]{:S(2)}, u32[]{:S(2)}) collective-permute-start(f32[136,128]{1,0:T(8,128)S(1)} %add_add_fusion.1), channel_id=1, source_target_pairs={{0,16},{8,24},{16,0},{24,8},{1,17},{9,25},{17,1},{25,9},{2,18},{10... | collective-permute-start | bytes 208904 | tf_op jit(solution)/shard_map/ppermute | solution.py:22
  58.2 5.2 %collective-permute-start.15 = (f32[136,128]{1,0:T(8,128)S(1)}, f32[136,128]{1,0:T(8,128)S(1)}, u32[]{:S(2)}, u32[]{:S(2)}) collective-permute-start(f32[136,128]{1,0:T(8,128)S(1)} %add_add_fusion.1), channel_id=1, source_target_pairs={{0,8},{8,0},{16,24},{24,16},{1,9},{9,1},{17,25},{25,17},{2,10},{10... | collective-permute-start | bytes 208904 | tf_op jit(solution)/shard_map/ppermute | solution.py:22
  63.4 1.3 %collective-permute-start.16 = (f32[136,128]{1,0:T(8,128)S(1)}, f32[136,128]{1,0:T(8,128)S(1)}, u32[]{:S(2)}, u32[]{:S(2)}) collective-permute-start(f32[136,128]{1,0:T(8,128)S(1)} %add_add_fusion.mine_ref), channel_id=1, source_target_pairs={{0,1},{1,0},{2,3},{3,2},{4,5},{5,4},{6,7},{7,6},{8,9},{9,8},{10,11... | collective-permute-start | bytes 208904 | tf_op jit(solution)/shard_map/ppermute | solution.py:22

commit v11 on v8

--- a/solution.py
+++ b/solution.py
@@ -381,7 +381,7 @@
     if bits == 1:
         return t[0] + t[1]
     if axis == "col":
-        return (t[2] + t[3]) + (t[0] + t[1])
+        return (t[0] + t[1]) + (t[3] + t[2])
     return (t[3] + t[2]) + (t[1] + t[0])
 
 

time: 71.1 us -> 71.3 us (level)
  no operation moved by 1% of the time
where the time goes in v11:
time: 71.3 us; the launch traced here: 71.1 us
  waiting for transfers between devices  27.8 us (39%)
  Pallas kernels  21.9 us (31%)
  starting transfers between devices  20 us (28%)
  other arithmetic  0.77 us (1%)
  between operations  0.75 us (1%)
    ppermute x16, waiting for transfers between devices, exchange(): return lax.ppermute(value, axis, [(i, i ^ mask) for i in range(size)])  27.8 us
    ppermute x16, starting transfers between devices, exchange(): return lax.ppermute(value, axis, [(i, i ^ mask) for i in range(size)])  20 us
    pallas_call x1, Pallas kernels, on_device(): pl.pallas_call(functools.partial(tail_kernel, 1.0 / order_total), grid_sp...  7.37 us
    pallas_call x5, Pallas kernels, product(): pl.pallas_call(functools.partial(product_kernel, first, chosen), grid=(co...  7.08 us
    pallas_call x1, Pallas kernels, scatter_blocks(): pl.pallas_call(scatter_kernel, out_shape=pltpu.VMEM((n_slots, BS, BS), va...  6.21 us
  transfers between devices with their start and end apart: 16, of which 13 were waited for; matrix products, arithmetic and copies ran while one was open for 1% of the time, Pallas kernels for 19%

profile of v11, /device:TPU:0, one launch (start us, length us, event | category | flops | bytes accessed | tf_op | source)
XLA Modules:
  0.0 71.1 jit_solution(515008814900746277)
XLA Ops:
  0.6 4.1 %collective-permute-start = (bf16[512,256]{1,0:T(8,128)(2,1)}, bf16[512,256]{1,0:T(8,128)(2,1)S(1)}, u32[]{:S(2)}, u32[]{:S(2)}) collective-permute-start(bf16[512,256]{1,0:T(8,128)(2,1)} %refs_0_.1), channel_id=1, source_target_pairs={{0,16},{8,24},{16,0},{24,8},{1,17},{9,25},{17,1},{25,9},{2,18},{10... | collective-permute-start | bytes 786440 | tf_op jit(solution)/shard_map/ppermute | solution.py:22
  4.7 1.6 %collective-permute-start.2 = (bf16[512,256]{1,0:T(8,128)(2,1)}, bf16[512,256]{1,0:T(8,128)(2,1)S(1)}, u32[]{:S(2)}, u32[]{:S(2)}) collective-permute-start(bf16[512,256]{1,0:T(8,128)(2,1)} %refs_0_.1), channel_id=1, source_target_pairs={{0,8},{8,0},{16,24},{24,16},{1,9},{9,1},{17,25},{25,17},{2,10},{10... | collective-permute-start | bytes 786440 | tf_op jit(solution)/shard_map/ppermute | solution.py:22
  6.3 0.7 %fusion.4.slots = s32[256]{0:T(256)S(1)} fusion(s32[256]{0:T(256)} %param.7, s32[256]{0:T(256)} %param.6, s32[]{:T(128)S(6)} %axis_index.17, s32[]{:T(128)S(6)} %mul.26, s32[]{:T(128)S(6)} %select_n.44, s32[]{:T(128)S(6)} %axis_index.14, s32[]{:T(128)S(6)} %mul.21), kind=kLoop, calls=%fused_computation.26 | loop fusion | flops 23040 | bytes 3092 | tf_op jit(solution)/shard_map/add | solution.py:302
  7.0 6.2 %shard_map.59 = bf16[512,128,128]{2,1,0:T(8,128)(2,1)S(1)} custom-call(s32[256]{0:T(256)S(1)} %fusion.4.slots, bf16[256,128,128]{2,1,0:T(8,128)(2,1)} %values.1), custom_call_target="tpu_custom_call" | custom-call | bytes 25165824 | tf_op jit(solution)/shard_map/pallas_call | solution.py:42
  13.3 3.7 %collective-permute-done.refs_2_ = bf16[512,256]{1,0:T(8,128)(2,1)S(1)} collective-permute-done((bf16[512,256]{1,0:T(8,128)(2,1)}, bf16[512,256]{1,0:T(8,128)(2,1)S(1)}, u32[]{:S(2)}, u32[]{:S(2)}) %collective-permute-start) | collective-permute-done | bytes 262176 | tf_op jit(solution)/shard_map/ppermute | solution.py:22
  17.0 0.7 %collective-permute-start.1 = (bf16[512,256]{1,0:T(8,128)(2,1)S(1)}, bf16[512,256]{1,0:T(8,128)(2,1)S(1)}, u32[]{:S(2)}, u32[]{:S(2)}) collective-permute-start(bf16[512,256]{1,0:T(8,128)(2,1)S(1)} %collective-permute-done.refs_2_), channel_id=1, source_target_pairs={{0,8},{8,0},{16,24},{24,16},{1,9},{9,1},{17,25},{25,17},{2,10},{10... | collective-permute-start | bytes 786440 | tf_op jit(solution)/shard_map/ppermute | solution.py:22
  17.7 4.6 %shard_map.60.refs_1_ = f32[8,512,256]{2,1,0:T(8,128)S(1)} custom-call(bf16[8,4,16,128,128]{4,3,2,1,0:T(8,128)(2,1)S(1)} %bitcast.2, bf16[512,256]{1,0:T(8,128)(2,1)S(1)} %copy-done, bf16[512,256]{1,0:T(8,128)(2,1)S(1)} %collective-permute-done.2.refs_1_, bf16[512,256]{1,0:T(8,128)(2,1)S(1)} %collective-permute-done.refs_2_), custom_call_target="tpu_custom_call" | custom-call | flops 4294967296 | bytes 16777216 | tf_op jit(solution)/shard_map/pallas_call | solution.py:322
  22.3 2.1 %collective-permute-done.1.refs_0_ = bf16[512,256]{1,0:T(8,128)(2,1)S(1)} collective-permute-done((bf16[512,256]{1,0:T(8,128)(2,1)S(1)}, bf16[512,256]{1,0:T(8,128)(2,1)S(1)}, u32[]{:S(2)}, u32[]{:S(2)}) %collective-permute-start.1) | collective-permute-done | bytes 262176 | tf_op jit(solution)/shard_map/ppermute | solution.py:22
  24.4 0.6 shard_map.65
  25.1 0.6 shard_map.62
  25.7 0.5 collective-permute-start.3
  26.3 0.6 shard_map.64.a_ref
  26.9 0.6 shard_map.61.a_ref
  28.0 2.3 %collective-permute-start.7 = (s16[528,256]{1,0:T(8,128)(2,1)S(1)}, s16[528,256]{1,0:T(8,128)(2,1)S(1)}, u32[]{:S(2)}, u32[]{:S(2)}) collective-permute-start(s16[528,256]{1,0:T(8,128)(2,1)S(1)} %get-tuple-element.15), channel_id=1, source_target_pairs={{0,6},{1,7},{2,4},{3,5},{4,2},{5,3},{6,0},{7,1},{8,14},{9,15},{10,... | collective-permute-start | bytes 811016 | tf_op jit(solution)/shard_map/ppermute | solution.py:22
  30.6 0.6 collective-permute-start.4
  31.2 1.2 %collective-permute-start.5 = (s16[528,256]{1,0:T(8,128)(2,1)S(1)}, s16[528,256]{1,0:T(8,128)(2,1)S(1)}, u32[]{:S(2)}, u32[]{:S(2)}) collective-permute-start(s16[528,256]{1,0:T(8,128)(2,1)S(1)} %get-tuple-element.14), channel_id=1, source_target_pairs={{0,4},{1,5},{2,6},{3,7},{4,0},{5,1},{6,2},{7,3},{8,12},{9,13},{10,... | collective-permute-start | bytes 811016 | tf_op jit(solution)/shard_map/ppermute | solution.py:22
  32.4 5.9 %collective-permute-done.7.refs_2_ = s16[528,256]{1,0:T(8,128)(2,1)S(1)} collective-permute-done((s16[528,256]{1,0:T(8,128)(2,1)S(1)}, s16[528,256]{1,0:T(8,128)(2,1)S(1)}, u32[]{:S(2)}, u32[]{:S(2)}) %collective-permute-start.7) | collective-permute-done | bytes 270368 | tf_op jit(solution)/shard_map/ppermute | solution.py:22
  38.3 4.8 %collective-permute-done.4.refs_0_ = s16[528,256]{1,0:T(8,128)(2,1)S(1)} collective-permute-done((s16[528,256]{1,0:T(8,128)(2,1)S(1)}, s16[528,256]{1,0:T(8,128)(2,1)S(1)}, u32[]{:S(2)}, u32[]{:S(2)}) %collective-permute-start.4) | collective-permute-done | bytes 270368 | tf_op jit(solution)/shard_map/ppermute | solution.py:22
  43.3 0.6 shard_map.67
  44.0 1.2 %collective-permute-done.8 = f32[136,128]{1,0:T(8,128)S(1)} collective-permute-done((f32[136,128]{1,0:T(8,128)S(1)}, f32[136,128]{1,0:T(8,128)S(1)}, u32[]{:S(2)}, u32[]{:S(2)}) %collective-permute-start.8) | collective-permute-done | bytes 69664 | tf_op jit(solution)/shard_map/ppermute | solution.py:22
  45.3 2.3 %collective-permute-start.10 = (f32[136,128]{1,0:T(8,128)S(1)}, f32[136,128]{1,0:T(8,128)S(1)}, u32[]{:S(2)}, u32[]{:S(2)}) collective-permute-start(f32[136,128]{1,0:T(8,128)S(1)} %add.80), channel_id=1, source_target_pairs={{0,6},{1,7},{2,4},{3,5},{4,2},{5,3},{6,0},{7,1},{8,14},{9,15},{10,... | collective-permute-start | bytes 208904 | tf_op jit(solution)/shard_map/ppermute | solution.py:22
  47.6 0.6 collective-permute-start.11
  48.2 0.7 collective-permute-start.9
  48.8 1.8 %collective-permute-done.10 = f32[136,128]{1,0:T(8,128)S(1)} collective-permute-done((f32[136,128]{1,0:T(8,128)S(1)}, f32[136,128]{1,0:T(8,128)S(1)}, u32[]{:S(2)}, u32[]{:S(2)}) %collective-permute-start.10) | collective-permute-done | bytes 69664 | tf_op jit(solution)/shard_map/ppermute | solution.py:22
  50.6 1.4 %collective-permute-done.11 = f32[136,128]{1,0:T(8,128)S(1)} collective-permute-done((f32[136,128]{1,0:T(8,128)S(1)}, f32[136,128]{1,0:T(8,128)S(1)}, u32[]{:S(2)}, u32[]{:S(2)}) %collective-permute-start.11) | collective-permute-done | bytes 69664 | tf_op jit(solution)/shard_map/ppermute | solution.py:22
  52.0 0.4 collective-permute-done.9
  52.5 4.5 %collective-permute-start.12 = (f32[136,128]{1,0:T(8,128)S(1)}, f32[136,128]{1,0:T(8,128)S(1)}, u32[]{:S(2)}, u32[]{:S(2)}) collective-permute-start(f32[136,128]{1,0:T(8,128)S(1)} %add_add_fusion.1), channel_id=1, source_target_pairs={{0,24},{8,16},{16,8},{24,0},{1,25},{9,17},{17,9},{25,1},{2,26},{10... | collective-permute-start | bytes 208904 | tf_op jit(solution)/shard_map/ppermute | solution.py:22
  57.0 0.6 collective-permute-start.14
  57.7 1.8 %collective-permute-done.12 = f32[136,128]{1,0:T(8,128)S(1)} collective-permute-done((f32[136,128]{1,0:T(8,128)S(1)}, f32[136,128]{1,0:T(8,128)S(1)}, u32[]{:S(2)}, u32[]{:S(2)}) %collective-permute-start.12) | collective-permute-done | bytes 69664 | tf_op jit(solution)/shard_map/ppermute | solution.py:22
  59.5 2.9 %collective-permute-done.13 = f32[136,128]{1,0:T(8,128)S(1)} collective-permute-done((f32[136,128]{1,0:T(8,128)S(1)}, f32[136,128]{1,0:T(8,128)S(1)}, u32[]{:S(2)}, u32[]{:S(2)}) %collective-permute-start.13) | collective-permute-done | bytes 69664 | tf_op jit(solution)/shard_map/ppermute | solution.py:22
  62.5 1.2 %collective-permute-done.15.other_ref = f32[136,128]{1,0:T(8,128)S(1)} collective-permute-done((f32[136,128]{1,0:T(8,128)S(1)}, f32[136,128]{1,0:T(8,128)S(1)}, u32[]{:S(2)}, u32[]{:S(2)}) %collective-permute-start.15) | collective-permute-done | bytes 69664 | tf_op jit(solution)/shard_map/ppermute | solution.py:22
  63.7 7.4 %shard_map.68 = (f32[512,256]{1,0:T(8,128)}, f32[256,256]{1,0:T(8,128)}) custom-call(s32[1]{0:T(128)} %bitcast.core, f32[136,128]{1,0:T(8,128)S(1)} %add_add_fusion.mine_ref, f32[136,128]{1,0:T(8,128)S(1)} %collective-permute-done.15.other_ref, f32[512,256]{1,0:T(8,128)S(1)} %get-tuple-element.19.s_ref), custom_call_target="tpu_custom_call" | custom-call | tf_op jit(solution)/shard_map/pallas_call | solution.py:433
  (16 shorter events, 1.2 us)
Async XLA Ops:
  0.6 16.3 %collective-permute-start = (bf16[512,256]{1,0:T(8,128)(2,1)}, bf16[512,256]{1,0:T(8,128)(2,1)S(1)}, u32[]{:S(2)}, u32[]{:S(2)}) collective-permute-start(bf16[512,256]{1,0:T(8,128)(2,1)} %refs_0_.1), channel_id=1, source_target_pairs={{0,16},{8,24},{16,0},{24,8},{1,17},{9,25},{17,1},{25,9},{2,18},{10... | collective-permute-start | bytes 786440 | tf_op jit(solution)/shard_map/ppermute | solution.py:22
  4.7 13.0 %collective-permute-start.2 = (bf16[512,256]{1,0:T(8,128)(2,1)}, bf16[512,256]{1,0:T(8,128)(2,1)S(1)}, u32[]{:S(2)}, u32[]{:S(2)}) collective-permute-start(bf16[512,256]{1,0:T(8,128)(2,1)} %refs_0_.1), channel_id=1, source_target_pairs={{0,8},{8,0},{16,24},{24,16},{1,9},{9,1},{17,25},{25,17},{2,10},{10... | collective-permute-start | bytes 786440 | tf_op jit(solution)/shard_map/ppermute | solution.py:22
  7.0 10.7 %copy-start = (bf16[512,256]{1,0:T(8,128)(2,1)S(1)}, bf16[512,256]{1,0:T(8,128)(2,1)}, u32[]{:S(2)}) copy-start(bf16[512,256]{1,0:T(8,128)(2,1)} %refs_0_.1) | copy-start | bytes 786436
  17.0 7.4 %collective-permute-start.1 = (bf16[512,256]{1,0:T(8,128)(2,1)S(1)}, bf16[512,256]{1,0:T(8,128)(2,1)S(1)}, u32[]{:S(2)}, u32[]{:S(2)}) collective-permute-start(bf16[512,256]{1,0:T(8,128)(2,1)S(1)} %collective-permute-done.refs_2_), channel_id=1, source_target_pairs={{0,8},{8,0},{16,24},{24,16},{1,9},{9,1},{17,25},{25,17},{2,10},{10... | collective-permute-start | bytes 786440 | tf_op jit(solution)/shard_map/ppermute | solution.py:22
  25.0 2.7 %collective-permute-start.6 = (f32[2,512,256]{2,1,0:T(8,128)S(1)}, f32[2,512,256]{2,1,0:T(8,128)S(1)}, u32[]{:S(2)}, u32[]{:S(2)}) collective-permute-start(f32[2,512,256]{2,1,0:T(8,128)S(1)} %shard_map.65), channel_id=1, source_target_pairs={{0,1},{1,0},{2,3},{3,2},{4,5},{5,4},{6,7},{7,6},{8,9},{9,8},{10,11... | collective-permute-start | bytes 3145736 | tf_op jit(solution)/shard_map/ppermute | solution.py:22
  25.7 4.6 %collective-permute-start.3 = (f32[2,512,256]{2,1,0:T(8,128)S(1)}, f32[2,512,256]{2,1,0:T(8,128)S(1)}, u32[]{:S(2)}, u32[]{:S(2)}) collective-permute-start(f32[2,512,256]{2,1,0:T(8,128)S(1)} %shard_map.62), channel_id=1, source_target_pairs={{0,1},{1,0},{2,3},{3,2},{4,5},{5,4},{6,7},{7,6},{8,9},{9,8},{10,11... | collective-permute-start | bytes 3145736 | tf_op jit(solution)/shard_map/ppermute | solution.py:22
  28.0 10.3 %collective-permute-start.7 = (s16[528,256]{1,0:T(8,128)(2,1)S(1)}, s16[528,256]{1,0:T(8,128)(2,1)S(1)}, u32[]{:S(2)}, u32[]{:S(2)}) collective-permute-start(s16[528,256]{1,0:T(8,128)(2,1)S(1)} %get-tuple-element.15), channel_id=1, source_target_pairs={{0,6},{1,7},{2,4},{3,5},{4,2},{5,3},{6,0},{7,1},{8,14},{9,15},{10,... | collective-permute-start | bytes 811016 | tf_op jit(solution)/shard_map/ppermute | solution.py:22
  30.6 12.5 %collective-permute-start.4 = (s16[528,256]{1,0:T(8,128)(2,1)S(1)}, s16[528,256]{1,0:T(8,128)(2,1)S(1)}, u32[]{:S(2)}, u32[]{:S(2)}) collective-permute-start(s16[528,256]{1,0:T(8,128)(2,1)S(1)} %get-tuple-element.13), channel_id=1, source_target_pairs={{0,2},{1,3},{2,0},{3,1},{4,6},{5,7},{6,4},{7,5},{8,10},{9,11},{10,... | collective-permute-start | bytes 811016 | tf_op jit(solution)/shard_map/ppermute | solution.py:22
  31.2 12.1 %collective-permute-start.5 = (s16[528,256]{1,0:T(8,128)(2,1)S(1)}, s16[528,256]{1,0:T(8,128)(2,1)S(1)}, u32[]{:S(2)}, u32[]{:S(2)}) collective-permute-start(s16[528,256]{1,0:T(8,128)(2,1)S(1)} %get-tuple-element.14), channel_id=1, source_target_pairs={{0,4},{1,5},{2,6},{3,7},{4,0},{5,1},{6,2},{7,3},{8,12},{9,13},{10,... | collective-permute-start | bytes 811016 | tf_op jit(solution)/shard_map/ppermute | solution.py:22
  43.9 1.3 %collective-permute-start.8 = (f32[136,128]{1,0:T(8,128)S(1)}, f32[136,128]{1,0:T(8,128)S(1)}, u32[]{:S(2)}, u32[]{:S(2)}) collective-permute-start(f32[136,128]{1,0:T(8,128)S(1)} %get-tuple-element.18), channel_id=1, source_target_pairs={{0,1},{1,0},{2,3},{3,2},{4,5},{5,4},{6,7},{7,6},{8,9},{9,8},{10,11... | collective-permute-start | bytes 208904 | tf_op jit(solution)/shard_map/ppermute | solution.py:22
  45.3 5.3 %collective-permute-start.10 = (f32[136,128]{1,0:T(8,128)S(1)}, f32[136,128]{1,0:T(8,128)S(1)}, u32[]{:S(2)}, u32[]{:S(2)}) collective-permute-start(f32[136,128]{1,0:T(8,128)S(1)} %add.80), channel_id=1, source_target_pairs={{0,6},{1,7},{2,4},{3,5},{4,2},{5,3},{6,0},{7,1},{8,14},{9,15},{10,... | collective-permute-start | bytes 208904 | tf_op jit(solution)/shard_map/ppermute | solution.py:22
  47.6 4.5 %collective-permute-start.11 = (f32[136,128]{1,0:T(8,128)S(1)}, f32[136,128]{1,0:T(8,128)S(1)}, u32[]{:S(2)}, u32[]{:S(2)}) collective-permute-start(f32[136,128]{1,0:T(8,128)S(1)} %add.80), channel_id=1, source_target_pairs={{0,4},{1,5},{2,6},{3,7},{4,0},{5,1},{6,2},{7,3},{8,12},{9,13},{10,... | collective-permute-start | bytes 208904 | tf_op jit(solution)/shard_map/ppermute | solution.py:22
  48.2 4.3 %collective-permute-start.9 = (f32[136,128]{1,0:T(8,128)S(1)}, f32[136,128]{1,0:T(8,128)S(1)}, u32[]{:S(2)}, u32[]{:S(2)}) collective-permute-start(f32[136,128]{1,0:T(8,128)S(1)} %add.80), channel_id=1, source_target_pairs={{0,2},{1,3},{2,0},{3,1},{4,6},{5,7},{6,4},{7,5},{8,10},{9,11},{10,... | collective-permute-start | bytes 208904 | tf_op jit(solution)/shard_map/ppermute | solution.py:22
  52.5 7.0 %collective-permute-start.12 = (f32[136,128]{1,0:T(8,128)S(1)}, f32[136,128]{1,0:T(8,128)S(1)}, u32[]{:S(2)}, u32[]{:S(2)}) collective-permute-start(f32[136,128]{1,0:T(8,128)S(1)} %add_add_fusion.1), channel_id=1, source_target_pairs={{0,24},{8,16},{16,8},{24,0},{1,25},{9,17},{17,9},{25,1},{2,26},{10... | collective-permute-start | bytes 208904 | tf_op jit(solution)/shard_map/ppermute | solution.py:22
  57.0 5.4 %collective-permute-start.13 = (f32[136,128]{1,0:T(8,128)S(1)}, f32[136,128]{1,0:T(8,128)S(1)}, u32[]{:S(2)}, u32[]{:S(2)}) collective-permute-start(f32[136,128]{1,0:T(8,128)S(1)} %add_add_fusion.1), channel_id=1, source_target_pairs={{0,16},{8,24},{16,0},{24,8},{1,17},{9,25},{17,1},{25,9},{2,18},{10... | collective-permute-start | bytes 208904 | tf_op jit(solution)/shard_map/ppermute | solution.py:22
  57.0 5.4 %collective-permute-start.14 = (f32[136,128]{1,0:T(8,128)S(1)}, f32[136,128]{1,0:T(8,128)S(1)}, u32[]{:S(2)}, u32[]{:S(2)}) collective-permute-start(f32[136,128]{1,0:T(8,128)S(1)} %add_add_fusion.1), channel_id=1, source_target_pairs={{0,8},{8,0},{16,24},{24,16},{1,9},{9,1},{17,25},{25,17},{2,10},{10... | collective-permute-start | bytes 208904 | tf_op jit(solution)/shard_map/ppermute | solution.py:22
  62.4 1.3 %collective-permute-start.15 = (f32[136,128]{1,0:T(8,128)S(1)}, f32[136,128]{1,0:T(8,128)S(1)}, u32[]{:S(2)}, u32[]{:S(2)}) collective-permute-start(f32[136,128]{1,0:T(8,128)S(1)} %add_add_fusion.mine_ref), channel_id=1, source_target_pairs={{0,1},{1,0},{2,3},{3,2},{4,5},{5,4},{6,7},{7,6},{8,9},{9,8},{10,11... | collective-permute-start | bytes 208904 | tf_op jit(solution)/shard_map/ppermute | solution.py:22

commit v12 on v8

--- a/solution.py
+++ b/solution.py
@@ -80,8 +80,8 @@
 def quantize(total, o_ref):
     n = total.shape[0] // BS
     width = total.shape[1]
-    row = lax.broadcasted_iota(jnp.int32, (16, width), 0)
-    tail = jnp.zeros((16, width), jnp.float32)
+    row = lax.broadcasted_iota(jnp.int32, (8, width), 0)
+    tail = jnp.zeros((8, width), jnp.float32)
     for b in range(n):
         part = total[b * BS : (b + 1) * BS]
         top = jnp.maximum(jnp.max(jnp.abs(part), axis=0, keepdims=True), 1e-30)
@@ -93,7 +93,7 @@
 
 
 def dequantize(q_ref):
-    n = (q_ref.shape[0] - 16) // BS
+    n = (q_ref.shape[0] - 8) // BS
     tail = q_ref[n * BS :, :].astype(jnp.int32).astype(jnp.float32)
     parts = []
     for b in range(n):
@@ -240,9 +240,11 @@
 
 
 def full_dot(a, b, dims):
-    return lax.dot_general(
-        a, b, (dims, ((), ())), precision=lax.Precision.HIGHEST, preferred_element_type=jnp.float32
-    )
+    (da,), (db,) = dims
+    sa, sb = split(a, 3), split(b, 3)
+    lhs = jnp.concatenate([sa[i] for i, _ in PAIRS], axis=da)
+    rhs = jnp.concatenate([sb[j] for _, j in PAIRS], axis=db)
+    return lax.dot_general(lhs, rhs, (dims, ((), ())), preferred_element_type=jnp.float32)
 
 
 NN, NT, TN = ((1,), (0,)), ((1,), (1,)), ((0,), (0,))
@@ -333,7 +335,7 @@
     parts = [(0, chips // 2), (chips // 2, chips - chips // 2)]
     peer = [exchange(product(at, n, late, first_sum), "col", 1) for at, n in parts]
     near = [product(chips + at, n, late, first_sum) for at, n in parts]
-    sent = jax.ShapeDtypeStruct((shard_rows + 16, width), jnp.int16)
+    sent = jax.ShapeDtypeStruct((shard_rows + 8, width), jnp.int16)
     kept = jax.ShapeDtypeStruct((shard_rows, width), jnp.float32)
     terms = []
     for (at, n), mine, theirs in zip(parts, near, peer):

time: 71.1 us -> 70.9 us (level)
  no operation moved by 1% of the time
where the time goes in v12:
time: 70.9 us; the launch traced here: 70.8 us
  waiting for transfers between devices  27.5 us (39%)
  Pallas kernels  21.8 us (31%)
  starting transfers between devices  20 us (28%)
  other arithmetic  0.77 us (1%)
  between operations  0.75 us (1%)
    ppermute x16, waiting for transfers between devices, exchange(): return lax.ppermute(value, axis, [(i, i ^ mask) for i in range(size)])  27.5 us
    ppermute x16, starting transfers between devices, exchange(): return lax.ppermute(value, axis, [(i, i ^ mask) for i in range(size)])  20 us
    pallas_call x1, Pallas kernels, on_device(): pl.pallas_call(functools.partial(tail_kernel, 1.0 / order_total), grid_sp...  7.31 us
    pallas_call x5, Pallas kernels, product(): pl.pallas_call(functools.partial(product_kernel, first, chosen), grid=(co...  7.08 us
    pallas_call x1, Pallas kernels, scatter_blocks(): pl.pallas_call(scatter_kernel, out_shape=pltpu.VMEM((n_slots, BS, BS), va...  6.21 us
  transfers between devices with their start and end apart: 16, of which 13 were waited for; matrix products, arithmetic and copies ran while one was open for 1% of the time, Pallas kernels for 19%

profile of v12, /device:TPU:0, one launch (start us, length us, event | category | flops | bytes accessed | tf_op | source)
XLA Modules:
  0.0 70.8 jit_solution(15952519238001307533)
XLA Ops:
  0.6 4.1 %collective-permute-start = (bf16[512,256]{1,0:T(8,128)(2,1)}, bf16[512,256]{1,0:T(8,128)(2,1)S(1)}, u32[]{:S(2)}, u32[]{:S(2)}) collective-permute-start(bf16[512,256]{1,0:T(8,128)(2,1)} %refs_0_.1), channel_id=1, source_target_pairs={{0,16},{8,24},{16,0},{24,8},{1,17},{9,25},{17,1},{25,9},{2,18},{10... | collective-permute-start | bytes 786440 | tf_op jit(solution)/shard_map/ppermute | solution.py:22
  4.7 1.6 %collective-permute-start.2 = (bf16[512,256]{1,0:T(8,128)(2,1)}, bf16[512,256]{1,0:T(8,128)(2,1)S(1)}, u32[]{:S(2)}, u32[]{:S(2)}) collective-permute-start(bf16[512,256]{1,0:T(8,128)(2,1)} %refs_0_.1), channel_id=1, source_target_pairs={{0,8},{8,0},{16,24},{24,16},{1,9},{9,1},{17,25},{25,17},{2,10},{10... | collective-permute-start | bytes 786440 | tf_op jit(solution)/shard_map/ppermute | solution.py:22
  6.3 0.7 %fusion.4.slots = s32[256]{0:T(256)S(1)} fusion(s32[256]{0:T(256)} %param.7, s32[256]{0:T(256)} %param.6, s32[]{:T(128)S(6)} %axis_index.17, s32[]{:T(128)S(6)} %mul.26, s32[]{:T(128)S(6)} %select_n.44, s32[]{:T(128)S(6)} %axis_index.14, s32[]{:T(128)S(6)} %mul.21), kind=kLoop, calls=%fused_computation.26 | loop fusion | flops 23040 | bytes 3092 | tf_op jit(solution)/shard_map/add | solution.py:304
  7.0 6.2 %shard_map.59 = bf16[512,128,128]{2,1,0:T(8,128)(2,1)S(1)} custom-call(s32[256]{0:T(256)S(1)} %fusion.4.slots, bf16[256,128,128]{2,1,0:T(8,128)(2,1)} %values.1), custom_call_target="tpu_custom_call" | custom-call | bytes 25165824 | tf_op jit(solution)/shard_map/pallas_call | solution.py:42
  13.3 3.7 %collective-permute-done.refs_2_ = bf16[512,256]{1,0:T(8,128)(2,1)S(1)} collective-permute-done((bf16[512,256]{1,0:T(8,128)(2,1)}, bf16[512,256]{1,0:T(8,128)(2,1)S(1)}, u32[]{:S(2)}, u32[]{:S(2)}) %collective-permute-start) | collective-permute-done | bytes 262176 | tf_op jit(solution)/shard_map/ppermute | solution.py:22
  17.0 0.7 %collective-permute-start.1 = (bf16[512,256]{1,0:T(8,128)(2,1)S(1)}, bf16[512,256]{1,0:T(8,128)(2,1)S(1)}, u32[]{:S(2)}, u32[]{:S(2)}) collective-permute-start(bf16[512,256]{1,0:T(8,128)(2,1)S(1)} %collective-permute-done.refs_2_), channel_id=1, source_target_pairs={{0,8},{8,0},{16,24},{24,16},{1,9},{9,1},{17,25},{25,17},{2,10},{10... | collective-permute-start | bytes 786440 | tf_op jit(solution)/shard_map/ppermute | solution.py:22
  17.7 4.6 %shard_map.60.refs_1_ = f32[8,512,256]{2,1,0:T(8,128)S(1)} custom-call(bf16[8,4,16,128,128]{4,3,2,1,0:T(8,128)(2,1)S(1)} %bitcast.2, bf16[512,256]{1,0:T(8,128)(2,1)S(1)} %copy-done, bf16[512,256]{1,0:T(8,128)(2,1)S(1)} %collective-permute-done.2.refs_1_, bf16[512,256]{1,0:T(8,128)(2,1)S(1)} %collective-permute-done.refs_2_), custom_call_target="tpu_custom_call" | custom-call | flops 4294967296 | bytes 16777216 | tf_op jit(solution)/shard_map/pallas_call | solution.py:324
  22.3 2.1 %collective-permute-done.1.refs_0_ = bf16[512,256]{1,0:T(8,128)(2,1)S(1)} collective-permute-done((bf16[512,256]{1,0:T(8,128)(2,1)S(1)}, bf16[512,256]{1,0:T(8,128)(2,1)S(1)}, u32[]{:S(2)}, u32[]{:S(2)}) %collective-permute-start.1) | collective-permute-done | bytes 262176 | tf_op jit(solution)/shard_map/ppermute | solution.py:22
  24.4 0.6 shard_map.65
  25.1 0.6 shard_map.62
  25.7 0.5 collective-permute-start.3
  26.3 0.6 shard_map.64.a_ref
  26.9 0.6 shard_map.61.a_ref
  28.0 2.3 %collective-permute-start.7 = (s16[520,256]{1,0:T(8,128)(2,1)S(1)}, s16[520,256]{1,0:T(8,128)(2,1)S(1)}, u32[]{:S(2)}, u32[]{:S(2)}) collective-permute-start(s16[520,256]{1,0:T(8,128)(2,1)S(1)} %get-tuple-element.15), channel_id=1, source_target_pairs={{0,6},{1,7},{2,4},{3,5},{4,2},{5,3},{6,0},{7,1},{8,14},{9,15},{10,... | collective-permute-start | bytes 798728 | tf_op jit(solution)/shard_map/ppermute | solution.py:22
  30.6 0.6 collective-permute-start.4
  31.2 1.2 %collective-permute-start.5 = (s16[520,256]{1,0:T(8,128)(2,1)S(1)}, s16[520,256]{1,0:T(8,128)(2,1)S(1)}, u32[]{:S(2)}, u32[]{:S(2)}) collective-permute-start(s16[520,256]{1,0:T(8,128)(2,1)S(1)} %get-tuple-element.14), channel_id=1, source_target_pairs={{0,4},{1,5},{2,6},{3,7},{4,0},{5,1},{6,2},{7,3},{8,12},{9,13},{10,... | collective-permute-start | bytes 798728 | tf_op jit(solution)/shard_map/ppermute | solution.py:22
  32.4 5.8 %collective-permute-done.7.refs_2_ = s16[520,256]{1,0:T(8,128)(2,1)S(1)} collective-permute-done((s16[520,256]{1,0:T(8,128)(2,1)S(1)}, s16[520,256]{1,0:T(8,128)(2,1)S(1)}, u32[]{:S(2)}, u32[]{:S(2)}) %collective-permute-start.7) | collective-permute-done | bytes 266272 | tf_op jit(solution)/shard_map/ppermute | solution.py:22
  38.3 4.7 %collective-permute-done.4.refs_0_ = s16[520,256]{1,0:T(8,128)(2,1)S(1)} collective-permute-done((s16[520,256]{1,0:T(8,128)(2,1)S(1)}, s16[520,256]{1,0:T(8,128)(2,1)S(1)}, u32[]{:S(2)}, u32[]{:S(2)}) %collective-permute-start.4) | collective-permute-done | bytes 266272 | tf_op jit(solution)/shard_map/ppermute | solution.py:22
  43.1 0.6 shard_map.67
  43.9 1.2 %collective-permute-done.8 = f32[136,128]{1,0:T(8,128)S(1)} collective-permute-done((f32[136,128]{1,0:T(8,128)S(1)}, f32[136,128]{1,0:T(8,128)S(1)}, u32[]{:S(2)}, u32[]{:S(2)}) %collective-permute-start.8) | collective-permute-done | bytes 69664 | tf_op jit(solution)/shard_map/ppermute | solution.py:22
  45.1 2.3 %collective-permute-start.10 = (f32[136,128]{1,0:T(8,128)S(1)}, f32[136,128]{1,0:T(8,128)S(1)}, u32[]{:S(2)}, u32[]{:S(2)}) collective-permute-start(f32[136,128]{1,0:T(8,128)S(1)} %add.80), channel_id=1, source_target_pairs={{0,6},{1,7},{2,4},{3,5},{4,2},{5,3},{6,0},{7,1},{8,14},{9,15},{10,... | collective-permute-start | bytes 208904 | tf_op jit(solution)/shard_map/ppermute | solution.py:22
  47.4 0.5 collective-permute-start.11
  47.9 0.7 %collective-permute-start.9 = (f32[136,128]{1,0:T(8,128)S(1)}, f32[136,128]{1,0:T(8,128)S(1)}, u32[]{:S(2)}, u32[]{:S(2)}) collective-permute-start(f32[136,128]{1,0:T(8,128)S(1)} %add.80), channel_id=1, source_target_pairs={{0,4},{1,5},{2,6},{3,7},{4,0},{5,1},{6,2},{7,3},{8,12},{9,13},{10,... | collective-permute-start | bytes 208904 | tf_op jit(solution)/shard_map/ppermute | solution.py:22
  48.7 2.2 %collective-permute-done.10 = f32[136,128]{1,0:T(8,128)S(1)} collective-permute-done((f32[136,128]{1,0:T(8,128)S(1)}, f32[136,128]{1,0:T(8,128)S(1)}, u32[]{:S(2)}, u32[]{:S(2)}) %collective-permute-start.10) | collective-permute-done | bytes 69664 | tf_op jit(solution)/shard_map/ppermute | solution.py:22
  50.9 0.9 %collective-permute-done.11 = f32[136,128]{1,0:T(8,128)S(1)} collective-permute-done((f32[136,128]{1,0:T(8,128)S(1)}, f32[136,128]{1,0:T(8,128)S(1)}, u32[]{:S(2)}, u32[]{:S(2)}) %collective-permute-start.11) | collective-permute-done | bytes 69664 | tf_op jit(solution)/shard_map/ppermute | solution.py:22
  51.7 0.5 collective-permute-done.9
  52.3 4.5 %collective-permute-start.12 = (f32[136,128]{1,0:T(8,128)S(1)}, f32[136,128]{1,0:T(8,128)S(1)}, u32[]{:S(2)}, u32[]{:S(2)}) collective-permute-start(f32[136,128]{1,0:T(8,128)S(1)} %add_add_fusion.1), channel_id=1, source_target_pairs={{0,24},{8,16},{16,8},{24,0},{1,25},{9,17},{17,9},{25,1},{2,26},{10... | collective-permute-start | bytes 208904 | tf_op jit(solution)/shard_map/ppermute | solution.py:22
  56.8 0.6 collective-permute-start.14
  57.4 2.0 %collective-permute-done.12 = f32[136,128]{1,0:T(8,128)S(1)} collective-permute-done((f32[136,128]{1,0:T(8,128)S(1)}, f32[136,128]{1,0:T(8,128)S(1)}, u32[]{:S(2)}, u32[]{:S(2)}) %collective-permute-start.12) | collective-permute-done | bytes 69664 | tf_op jit(solution)/shard_map/ppermute | solution.py:22
  59.4 2.7 %collective-permute-done.13 = f32[136,128]{1,0:T(8,128)S(1)} collective-permute-done((f32[136,128]{1,0:T(8,128)S(1)}, f32[136,128]{1,0:T(8,128)S(1)}, u32[]{:S(2)}, u32[]{:S(2)}) %collective-permute-start.13) | collective-permute-done | bytes 69664 | tf_op jit(solution)/shard_map/ppermute | solution.py:22
  62.2 1.2 %collective-permute-done.15.other_ref = f32[136,128]{1,0:T(8,128)S(1)} collective-permute-done((f32[136,128]{1,0:T(8,128)S(1)}, f32[136,128]{1,0:T(8,128)S(1)}, u32[]{:S(2)}, u32[]{:S(2)}) %collective-permute-start.15) | collective-permute-done | bytes 69664 | tf_op jit(solution)/shard_map/ppermute | solution.py:22
  63.4 7.3 %shard_map.68 = (f32[512,256]{1,0:T(8,128)}, f32[256,256]{1,0:T(8,128)}) custom-call(s32[1]{0:T(128)} %bitcast.core, f32[136,128]{1,0:T(8,128)S(1)} %add_add_fusion.mine_ref, f32[136,128]{1,0:T(8,128)S(1)} %collective-permute-done.15.other_ref, f32[512,256]{1,0:T(8,128)S(1)} %get-tuple-element.19.s_ref), custom_call_target="tpu_custom_call" | custom-call | tf_op jit(solution)/shard_map/pallas_call | solution.py:435
  (16 shorter events, 1.2 us)
Async XLA Ops:
  0.6 16.3 %collective-permute-start = (bf16[512,256]{1,0:T(8,128)(2,1)}, bf16[512,256]{1,0:T(8,128)(2,1)S(1)}, u32[]{:S(2)}, u32[]{:S(2)}) collective-permute-start(bf16[512,256]{1,0:T(8,128)(2,1)} %refs_0_.1), channel_id=1, source_target_pairs={{0,16},{8,24},{16,0},{24,8},{1,17},{9,25},{17,1},{25,9},{2,18},{10... | collective-permute-start | bytes 786440 | tf_op jit(solution)/shard_map/ppermute | solution.py:22
  4.7 13.0 %collective-permute-start.2 = (bf16[512,256]{1,0:T(8,128)(2,1)}, bf16[512,256]{1,0:T(8,128)(2,1)S(1)}, u32[]{:S(2)}, u32[]{:S(2)}) collective-permute-start(bf16[512,256]{1,0:T(8,128)(2,1)} %refs_0_.1), channel_id=1, source_target_pairs={{0,8},{8,0},{16,24},{24,16},{1,9},{9,1},{17,25},{25,17},{2,10},{10... | collective-permute-start | bytes 786440 | tf_op jit(solution)/shard_map/ppermute | solution.py:22
  7.0 10.7 %copy-start = (bf16[512,256]{1,0:T(8,128)(2,1)S(1)}, bf16[512,256]{1,0:T(8,128)(2,1)}, u32[]{:S(2)}) copy-start(bf16[512,256]{1,0:T(8,128)(2,1)} %refs_0_.1) | copy-start | bytes 786436
  17.0 7.4 %collective-permute-start.1 = (bf16[512,256]{1,0:T(8,128)(2,1)S(1)}, bf16[512,256]{1,0:T(8,128)(2,1)S(1)}, u32[]{:S(2)}, u32[]{:S(2)}) collective-permute-start(bf16[512,256]{1,0:T(8,128)(2,1)S(1)} %collective-permute-done.refs_2_), channel_id=1, source_target_pairs={{0,8},{8,0},{16,24},{24,16},{1,9},{9,1},{17,25},{25,17},{2,10},{10... | collective-permute-start | bytes 786440 | tf_op jit(solution)/shard_map/ppermute | solution.py:22
  25.0 2.7 %collective-permute-start.6 = (f32[2,512,256]{2,1,0:T(8,128)S(1)}, f32[2,512,256]{2,1,0:T(8,128)S(1)}, u32[]{:S(2)}, u32[]{:S(2)}) collective-permute-start(f32[2,512,256]{2,1,0:T(8,128)S(1)} %shard_map.65), channel_id=1, source_target_pairs={{0,1},{1,0},{2,3},{3,2},{4,5},{5,4},{6,7},{7,6},{8,9},{9,8},{10,11... | collective-permute-start | bytes 3145736 | tf_op jit(solution)/shard_map/ppermute | solution.py:22
  25.7 4.6 %collective-permute-start.3 = (f32[2,512,256]{2,1,0:T(8,128)S(1)}, f32[2,512,256]{2,1,0:T(8,128)S(1)}, u32[]{:S(2)}, u32[]{:S(2)}) collective-permute-start(f32[2,512,256]{2,1,0:T(8,128)S(1)} %shard_map.62), channel_id=1, source_target_pairs={{0,1},{1,0},{2,3},{3,2},{4,5},{5,4},{6,7},{7,6},{8,9},{9,8},{10,11... | collective-permute-start | bytes 3145736 | tf_op jit(solution)/shard_map/ppermute | solution.py:22
  28.0 10.2 %collective-permute-start.7 = (s16[520,256]{1,0:T(8,128)(2,1)S(1)}, s16[520,256]{1,0:T(8,128)(2,1)S(1)}, u32[]{:S(2)}, u32[]{:S(2)}) collective-permute-start(s16[520,256]{1,0:T(8,128)(2,1)S(1)} %get-tuple-element.15), channel_id=1, source_target_pairs={{0,6},{1,7},{2,4},{3,5},{4,2},{5,3},{6,0},{7,1},{8,14},{9,15},{10,... | collective-permute-start | bytes 798728 | tf_op jit(solution)/shard_map/ppermute | solution.py:22
  30.6 12.4 %collective-permute-start.4 = (s16[520,256]{1,0:T(8,128)(2,1)S(1)}, s16[520,256]{1,0:T(8,128)(2,1)S(1)}, u32[]{:S(2)}, u32[]{:S(2)}) collective-permute-start(s16[520,256]{1,0:T(8,128)(2,1)S(1)} %get-tuple-element.13), channel_id=1, source_target_pairs={{0,2},{1,3},{2,0},{3,1},{4,6},{5,7},{6,4},{7,5},{8,10},{9,11},{10,... | collective-permute-start | bytes 798728 | tf_op jit(solution)/shard_map/ppermute | solution.py:22
  31.2 11.9 %collective-permute-start.5 = (s16[520,256]{1,0:T(8,128)(2,1)S(1)}, s16[520,256]{1,0:T(8,128)(2,1)S(1)}, u32[]{:S(2)}, u32[]{:S(2)}) collective-permute-start(s16[520,256]{1,0:T(8,128)(2,1)S(1)} %get-tuple-element.14), channel_id=1, source_target_pairs={{0,4},{1,5},{2,6},{3,7},{4,0},{5,1},{6,2},{7,3},{8,12},{9,13},{10,... | collective-permute-start | bytes 798728 | tf_op jit(solution)/shard_map/ppermute | solution.py:22
  43.8 1.3 %collective-permute-start.8 = (f32[136,128]{1,0:T(8,128)S(1)}, f32[136,128]{1,0:T(8,128)S(1)}, u32[]{:S(2)}, u32[]{:S(2)}) collective-permute-start(f32[136,128]{1,0:T(8,128)S(1)} %get-tuple-element.18), channel_id=1, source_target_pairs={{0,1},{1,0},{2,3},{3,2},{4,5},{5,4},{6,7},{7,6},{8,9},{9,8},{10,11... | collective-permute-start | bytes 208904 | tf_op jit(solution)/shard_map/ppermute | solution.py:22
  45.1 5.7 %collective-permute-start.10 = (f32[136,128]{1,0:T(8,128)S(1)}, f32[136,128]{1,0:T(8,128)S(1)}, u32[]{:S(2)}, u32[]{:S(2)}) collective-permute-start(f32[136,128]{1,0:T(8,128)S(1)} %add.80), channel_id=1, source_target_pairs={{0,6},{1,7},{2,4},{3,5},{4,2},{5,3},{6,0},{7,1},{8,14},{9,15},{10,... | collective-permute-start | bytes 208904 | tf_op jit(solution)/shard_map/ppermute | solution.py:22
  47.4 4.3 %collective-permute-start.11 = (f32[136,128]{1,0:T(8,128)S(1)}, f32[136,128]{1,0:T(8,128)S(1)}, u32[]{:S(2)}, u32[]{:S(2)}) collective-permute-start(f32[136,128]{1,0:T(8,128)S(1)} %add.80), channel_id=1, source_target_pairs={{0,2},{1,3},{2,0},{3,1},{4,6},{5,7},{6,4},{7,5},{8,10},{9,11},{10,... | collective-permute-start | bytes 208904 | tf_op jit(solution)/shard_map/ppermute | solution.py:22
  47.9 4.3 %collective-permute-start.9 = (f32[136,128]{1,0:T(8,128)S(1)}, f32[136,128]{1,0:T(8,128)S(1)}, u32[]{:S(2)}, u32[]{:S(2)}) collective-permute-start(f32[136,128]{1,0:T(8,128)S(1)} %add.80), channel_id=1, source_target_pairs={{0,4},{1,5},{2,6},{3,7},{4,0},{5,1},{6,2},{7,3},{8,12},{9,13},{10,... | collective-permute-start | bytes 208904 | tf_op jit(solution)/shard_map/ppermute | solution.py:22
  52.3 7.2 %collective-permute-start.12 = (f32[136,128]{1,0:T(8,128)S(1)}, f32[136,128]{1,0:T(8,128)S(1)}, u32[]{:S(2)}, u32[]{:S(2)}) collective-permute-start(f32[136,128]{1,0:T(8,128)S(1)} %add_add_fusion.1), channel_id=1, source_target_pairs={{0,24},{8,16},{16,8},{24,0},{1,25},{9,17},{17,9},{25,1},{2,26},{10... | collective-permute-start | bytes 208904 | tf_op jit(solution)/shard_map/ppermute | solution.py:22
  56.8 5.3 %collective-permute-start.13 = (f32[136,128]{1,0:T(8,128)S(1)}, f32[136,128]{1,0:T(8,128)S(1)}, u32[]{:S(2)}, u32[]{:S(2)}) collective-permute-start(f32[136,128]{1,0:T(8,128)S(1)} %add_add_fusion.1), channel_id=1, source_target_pairs={{0,16},{8,24},{16,0},{24,8},{1,17},{9,25},{17,1},{25,9},{2,18},{10... | collective-permute-start | bytes 208904 | tf_op jit(solution)/shard_map/ppermute | solution.py:22
  56.8 5.3 %collective-permute-start.14 = (f32[136,128]{1,0:T(8,128)S(1)}, f32[136,128]{1,0:T(8,128)S(1)}, u32[]{:S(2)}, u32[]{:S(2)}) collective-permute-start(f32[136,128]{1,0:T(8,128)S(1)} %add_add_fusion.1), channel_id=1, source_target_pairs={{0,8},{8,0},{16,24},{24,16},{1,9},{9,1},{17,25},{25,17},{2,10},{10... | collective-permute-start | bytes 208904 | tf_op jit(solution)/shard_map/ppermute | solution.py:22
  62.1 1.3 %collective-permute-start.15 = (f32[136,128]{1,0:T(8,128)S(1)}, f32[136,128]{1,0:T(8,128)S(1)}, u32[]{:S(2)}, u32[]{:S(2)}) collective-permute-start(f32[136,128]{1,0:T(8,128)S(1)} %add_add_fusion.mine_ref), channel_id=1, source_target_pairs={{0,1},{1,0},{2,3},{3,2},{4,5},{5,4},{6,7},{7,6},{8,9},{9,8},{10,11... | collective-permute-start | bytes 208904 | tf_op jit(solution)/shard_map/ppermute | solution.py:22

commit v13 on v12

--- a/solution.py
+++ b/solution.py
@@ -334,20 +334,20 @@
     first_sum = product(0, 2 * chips, early)
     parts = [(0, chips // 2), (chips // 2, chips - chips // 2)]
     peer = [exchange(product(at, n, late, first_sum), "col", 1) for at, n in parts]
-    near = [product(chips + at, n, late, first_sum) for at, n in parts]
+    near = product(chips, chips, late, first_sum)
     sent = jax.ShapeDtypeStruct((shard_rows + 8, width), jnp.int16)
     kept = jax.ShapeDtypeStruct((shard_rows, width), jnp.float32)
     terms = []
-    for (at, n), mine, theirs in zip(parts, near, peer):
+    for (at, n), theirs in zip(parts, peer):
         shapes = [kept if at + i == chips - 1 else sent for i in range(n)]
         done = pl.pallas_call(
             code_kernel,
             grid=(n,),
-            in_specs=[block(0), block(0)],
+            in_specs=[block(at), block(0)],
             out_specs=[whole(x.shape) for x in shapes],
             out_shape=shapes,
             compiler_params=params,
-        )(mine, theirs)
+        )(near, theirs)
         for i, x in enumerate(done):
             terms.append(x if x.dtype == jnp.float32 else exchange(x, "col", 2 * (at + i + 1)))
     return terms

time: 70.9 us -> 70.9 us (level)
    pallas_call x5 -> x4, Pallas kernels: 7.08 us -> 7.05 us  [product(): pl.pallas_call(functools.partial(product_kernel, first, chosen), grid=(co...]
where the time goes in v13:
time: 70.9 us; the launch traced here: 70.8 us
  waiting for transfers between devices  27.5 us (39%)
  Pallas kernels  21.8 us (31%)
  starting transfers between devices  20 us (28%)
  other arithmetic  0.77 us (1%)
  between operations  0.74 us (1%)
    ppermute x16, waiting for transfers between devices, exchange(): return lax.ppermute(value, axis, [(i, i ^ mask) for i in range(size)])  27.5 us
    ppermute x16, starting transfers between devices, exchange(): return lax.ppermute(value, axis, [(i, i ^ mask) for i in range(size)])  20 us
    pallas_call x1, Pallas kernels, on_device(): pl.pallas_call(functools.partial(tail_kernel, 1.0 / order_total), grid_sp...  7.31 us
    pallas_call x4, Pallas kernels, product(): pl.pallas_call(functools.partial(product_kernel, first, chosen), grid=(co...  7.05 us
    pallas_call x1, Pallas kernels, scatter_blocks(): pl.pallas_call(scatter_kernel, out_shape=pltpu.VMEM((n_slots, BS, BS), va...  6.21 us
  transfers between devices with their start and end apart: 16, of which 13 were waited for; matrix products, arithmetic and copies ran while one was open for 1% of the time, Pallas kernels for 19%

profile of v13, /device:TPU:0, one launch (start us, length us, event | category | flops | bytes accessed | tf_op | source)
XLA Modules:
  0.0 70.8 jit_solution(4735344009572276877)
XLA Ops:
  0.6 4.1 %collective-permute-start = (bf16[512,256]{1,0:T(8,128)(2,1)}, bf16[512,256]{1,0:T(8,128)(2,1)S(1)}, u32[]{:S(2)}, u32[]{:S(2)}) collective-permute-start(bf16[512,256]{1,0:T(8,128)(2,1)} %refs_0_.1), channel_id=1, source_target_pairs={{0,16},{8,24},{16,0},{24,8},{1,17},{9,25},{17,1},{25,9},{2,18},{10... | collective-permute-start | bytes 786440 | tf_op jit(solution)/shard_map/ppermute | solution.py:22
  4.7 1.6 %collective-permute-start.2 = (bf16[512,256]{1,0:T(8,128)(2,1)}, bf16[512,256]{1,0:T(8,128)(2,1)S(1)}, u32[]{:S(2)}, u32[]{:S(2)}) collective-permute-start(bf16[512,256]{1,0:T(8,128)(2,1)} %refs_0_.1), channel_id=1, source_target_pairs={{0,8},{8,0},{16,24},{24,16},{1,9},{9,1},{17,25},{25,17},{2,10},{10... | collective-permute-start | bytes 786440 | tf_op jit(solution)/shard_map/ppermute | solution.py:22
  6.3 0.7 %fusion.4.slots = s32[256]{0:T(256)S(1)} fusion(s32[256]{0:T(256)} %param.7, s32[256]{0:T(256)} %param.6, s32[]{:T(128)S(6)} %axis_index.17, s32[]{:T(128)S(6)} %mul.26, s32[]{:T(128)S(6)} %select_n.44, s32[]{:T(128)S(6)} %axis_index.14, s32[]{:T(128)S(6)} %mul.21), kind=kLoop, calls=%fused_computation.26 | loop fusion | flops 23040 | bytes 3092 | tf_op jit(solution)/shard_map/add | solution.py:304
  7.0 6.2 %shard_map.59 = bf16[512,128,128]{2,1,0:T(8,128)(2,1)S(1)} custom-call(s32[256]{0:T(256)S(1)} %fusion.4.slots, bf16[256,128,128]{2,1,0:T(8,128)(2,1)} %values.1), custom_call_target="tpu_custom_call" | custom-call | bytes 25165824 | tf_op jit(solution)/shard_map/pallas_call | solution.py:42
  13.3 3.7 %collective-permute-done.refs_2_ = bf16[512,256]{1,0:T(8,128)(2,1)S(1)} collective-permute-done((bf16[512,256]{1,0:T(8,128)(2,1)}, bf16[512,256]{1,0:T(8,128)(2,1)S(1)}, u32[]{:S(2)}, u32[]{:S(2)}) %collective-permute-start) | collective-permute-done | bytes 262176 | tf_op jit(solution)/shard_map/ppermute | solution.py:22
  17.0 0.7 %collective-permute-start.1 = (bf16[512,256]{1,0:T(8,128)(2,1)S(1)}, bf16[512,256]{1,0:T(8,128)(2,1)S(1)}, u32[]{:S(2)}, u32[]{:S(2)}) collective-permute-start(bf16[512,256]{1,0:T(8,128)(2,1)S(1)} %collective-permute-done.refs_2_), channel_id=1, source_target_pairs={{0,8},{8,0},{16,24},{24,16},{1,9},{9,1},{17,25},{25,17},{2,10},{10... | collective-permute-start | bytes 786440 | tf_op jit(solution)/shard_map/ppermute | solution.py:22
  17.7 4.6 %shard_map.60.refs_1_ = f32[8,512,256]{2,1,0:T(8,128)S(1)} custom-call(bf16[8,4,16,128,128]{4,3,2,1,0:T(8,128)(2,1)S(1)} %bitcast.2, bf16[512,256]{1,0:T(8,128)(2,1)S(1)} %copy-done, bf16[512,256]{1,0:T(8,128)(2,1)S(1)} %collective-permute-done.2.refs_1_, bf16[512,256]{1,0:T(8,128)(2,1)S(1)} %collective-permute-done.refs_2_), custom_call_target="tpu_custom_call" | custom-call | flops 4294967296 | bytes 16777216 | tf_op jit(solution)/shard_map/pallas_call | solution.py:324
  22.3 2.1 %collective-permute-done.1.refs_0_ = bf16[512,256]{1,0:T(8,128)(2,1)S(1)} collective-permute-done((bf16[512,256]{1,0:T(8,128)(2,1)S(1)}, bf16[512,256]{1,0:T(8,128)(2,1)S(1)}, u32[]{:S(2)}, u32[]{:S(2)}) %collective-permute-start.1) | collective-permute-done | bytes 262176 | tf_op jit(solution)/shard_map/ppermute | solution.py:22
  24.4 0.6 shard_map.64
  25.1 0.6 shard_map.62
  25.7 0.5 collective-permute-start.3
  26.3 1.2 %shard_map.61.a_ref = f32[4,512,256]{2,1,0:T(8,128)S(1)} custom-call(bf16[8,4,16,128,128]{4,3,2,1,0:T(8,128)(2,1)S(1)} %bitcast.5, bf16[512,256]{1,0:T(8,128)(2,1)S(1)} %collective-permute-done.1.refs_0_, f32[8,512,256]{2,1,0:T(8,128)S(1)} %shard_map.60.refs_1_), custom_call_target="tpu_custom_call" | custom-call | flops 2147483648 | bytes 8388608 | tf_op jit(solution)/shard_map/pallas_call | solution.py:324
  28.0 2.3 %collective-permute-start.7 = (s16[520,256]{1,0:T(8,128)(2,1)S(1)}, s16[520,256]{1,0:T(8,128)(2,1)S(1)}, u32[]{:S(2)}, u32[]{:S(2)}) collective-permute-start(s16[520,256]{1,0:T(8,128)(2,1)S(1)} %get-tuple-element.15), channel_id=1, source_target_pairs={{0,6},{1,7},{2,4},{3,5},{4,2},{5,3},{6,0},{7,1},{8,14},{9,15},{10,... | collective-permute-start | bytes 798728 | tf_op jit(solution)/shard_map/ppermute | solution.py:22
  30.3 0.3 shard_map.63
  30.6 0.6 collective-permute-start.4
  31.2 1.2 %collective-permute-start.5 = (s16[520,256]{1,0:T(8,128)(2,1)S(1)}, s16[520,256]{1,0:T(8,128)(2,1)S(1)}, u32[]{:S(2)}, u32[]{:S(2)}) collective-permute-start(s16[520,256]{1,0:T(8,128)(2,1)S(1)} %get-tuple-element.14), channel_id=1, source_target_pairs={{0,4},{1,5},{2,6},{3,7},{4,0},{5,1},{6,2},{7,3},{8,12},{9,13},{10,... | collective-permute-start | bytes 798728 | tf_op jit(solution)/shard_map/ppermute | solution.py:22
  32.4 5.8 %collective-permute-done.7.refs_2_ = s16[520,256]{1,0:T(8,128)(2,1)S(1)} collective-permute-done((s16[520,256]{1,0:T(8,128)(2,1)S(1)}, s16[520,256]{1,0:T(8,128)(2,1)S(1)}, u32[]{:S(2)}, u32[]{:S(2)}) %collective-permute-start.7) | collective-permute-done | bytes 266272 | tf_op jit(solution)/shard_map/ppermute | solution.py:22
  38.3 4.7 %collective-permute-done.4.refs_0_ = s16[520,256]{1,0:T(8,128)(2,1)S(1)} collective-permute-done((s16[520,256]{1,0:T(8,128)(2,1)S(1)}, s16[520,256]{1,0:T(8,128)(2,1)S(1)}, u32[]{:S(2)}, u32[]{:S(2)}) %collective-permute-start.4) | collective-permute-done | bytes 266272 | tf_op jit(solution)/shard_map/ppermute | solution.py:22
  43.1 0.6 shard_map.66
  43.9 1.2 %collective-permute-done.8 = f32[136,128]{1,0:T(8,128)S(1)} collective-permute-done((f32[136,128]{1,0:T(8,128)S(1)}, f32[136,128]{1,0:T(8,128)S(1)}, u32[]{:S(2)}, u32[]{:S(2)}) %collective-permute-start.8) | collective-permute-done | bytes 69664 | tf_op jit(solution)/shard_map/ppermute | solution.py:22
  45.1 2.3 %collective-permute-start.10 = (f32[136,128]{1,0:T(8,128)S(1)}, f32[136,128]{1,0:T(8,128)S(1)}, u32[]{:S(2)}, u32[]{:S(2)}) collective-permute-start(f32[136,128]{1,0:T(8,128)S(1)} %add.80), channel_id=1, source_target_pairs={{0,6},{1,7},{2,4},{3,5},{4,2},{5,3},{6,0},{7,1},{8,14},{9,15},{10,... | collective-permute-start | bytes 208904 | tf_op jit(solution)/shard_map/ppermute | solution.py:22
  47.4 0.5 collective-permute-start.11
  47.9 0.7 %collective-permute-start.9 = (f32[136,128]{1,0:T(8,128)S(1)}, f32[136,128]{1,0:T(8,128)S(1)}, u32[]{:S(2)}, u32[]{:S(2)}) collective-permute-start(f32[136,128]{1,0:T(8,128)S(1)} %add.80), channel_id=1, source_target_pairs={{0,4},{1,5},{2,6},{3,7},{4,0},{5,1},{6,2},{7,3},{8,12},{9,13},{10,... | collective-permute-start | bytes 208904 | tf_op jit(solution)/shard_map/ppermute | solution.py:22
  48.7 2.2 %collective-permute-done.10 = f32[136,128]{1,0:T(8,128)S(1)} collective-permute-done((f32[136,128]{1,0:T(8,128)S(1)}, f32[136,128]{1,0:T(8,128)S(1)}, u32[]{:S(2)}, u32[]{:S(2)}) %collective-permute-start.10) | collective-permute-done | bytes 69664 | tf_op jit(solution)/shard_map/ppermute | solution.py:22
  50.9 0.9 %collective-permute-done.11 = f32[136,128]{1,0:T(8,128)S(1)} collective-permute-done((f32[136,128]{1,0:T(8,128)S(1)}, f32[136,128]{1,0:T(8,128)S(1)}, u32[]{:S(2)}, u32[]{:S(2)}) %collective-permute-start.11) | collective-permute-done | bytes 69664 | tf_op jit(solution)/shard_map/ppermute | solution.py:22
  51.7 0.5 collective-permute-done.9
  52.3 4.5 %collective-permute-start.12 = (f32[136,128]{1,0:T(8,128)S(1)}, f32[136,128]{1,0:T(8,128)S(1)}, u32[]{:S(2)}, u32[]{:S(2)}) collective-permute-start(f32[136,128]{1,0:T(8,128)S(1)} %add_add_fusion.1), channel_id=1, source_target_pairs={{0,24},{8,16},{16,8},{24,0},{1,25},{9,17},{17,9},{25,1},{2,26},{10... | collective-permute-start | bytes 208904 | tf_op jit(solution)/shard_map/ppermute | solution.py:22
  56.8 0.6 collective-permute-start.14
  57.4 2.0 %collective-permute-done.12 = f32[136,128]{1,0:T(8,128)S(1)} collective-permute-done((f32[136,128]{1,0:T(8,128)S(1)}, f32[136,128]{1,0:T(8,128)S(1)}, u32[]{:S(2)}, u32[]{:S(2)}) %collective-permute-start.12) | collective-permute-done | bytes 69664 | tf_op jit(solution)/shard_map/ppermute | solution.py:22
  59.4 2.7 %collective-permute-done.13 = f32[136,128]{1,0:T(8,128)S(1)} collective-permute-done((f32[136,128]{1,0:T(8,128)S(1)}, f32[136,128]{1,0:T(8,128)S(1)}, u32[]{:S(2)}, u32[]{:S(2)}) %collective-permute-start.13) | collective-permute-done | bytes 69664 | tf_op jit(solution)/shard_map/ppermute | solution.py:22
  62.2 1.2 %collective-permute-done.15.other_ref = f32[136,128]{1,0:T(8,128)S(1)} collective-permute-done((f32[136,128]{1,0:T(8,128)S(1)}, f32[136,128]{1,0:T(8,128)S(1)}, u32[]{:S(2)}, u32[]{:S(2)}) %collective-permute-start.15) | collective-permute-done | bytes 69664 | tf_op jit(solution)/shard_map/ppermute | solution.py:22
  63.4 7.3 %shard_map.67 = (f32[512,256]{1,0:T(8,128)}, f32[256,256]{1,0:T(8,128)}) custom-call(s32[1]{0:T(128)} %bitcast.core, f32[136,128]{1,0:T(8,128)S(1)} %add_add_fusion.mine_ref, f32[136,128]{1,0:T(8,128)S(1)} %collective-permute-done.15.other_ref, f32[512,256]{1,0:T(8,128)S(1)} %get-tuple-element.19.s_ref), custom_call_target="tpu_custom_call" | custom-call | tf_op jit(solution)/shard_map/pallas_call | solution.py:435
  (15 shorter events, 0.9 us)
Async XLA Ops:
  0.6 16.3 %collective-permute-start = (bf16[512,256]{1,0:T(8,128)(2,1)}, bf16[512,256]{1,0:T(8,128)(2,1)S(1)}, u32[]{:S(2)}, u32[]{:S(2)}) collective-permute-start(bf16[512,256]{1,0:T(8,128)(2,1)} %refs_0_.1), channel_id=1, source_target_pairs={{0,16},{8,24},{16,0},{24,8},{1,17},{9,25},{17,1},{25,9},{2,18},{10... | collective-permute-start | bytes 786440 | tf_op jit(solution)/shard_map/ppermute | solution.py:22
  4.7 13.0 %collective-permute-start.2 = (bf16[512,256]{1,0:T(8,128)(2,1)}, bf16[512,256]{1,0:T(8,128)(2,1)S(1)}, u32[]{:S(2)}, u32[]{:S(2)}) collective-permute-start(bf16[512,256]{1,0:T(8,128)(2,1)} %refs_0_.1), channel_id=1, source_target_pairs={{0,8},{8,0},{16,24},{24,16},{1,9},{9,1},{17,25},{25,17},{2,10},{10... | collective-permute-start | bytes 786440 | tf_op jit(solution)/shard_map/ppermute | solution.py:22
  7.0 10.7 %copy-start = (bf16[512,256]{1,0:T(8,128)(2,1)S(1)}, bf16[512,256]{1,0:T(8,128)(2,1)}, u32[]{:S(2)}) copy-start(bf16[512,256]{1,0:T(8,128)(2,1)} %refs_0_.1) | copy-start | bytes 786436
  17.0 7.4 %collective-permute-start.1 = (bf16[512,256]{1,0:T(8,128)(2,1)S(1)}, bf16[512,256]{1,0:T(8,128)(2,1)S(1)}, u32[]{:S(2)}, u32[]{:S(2)}) collective-permute-start(bf16[512,256]{1,0:T(8,128)(2,1)S(1)} %collective-permute-done.refs_2_), channel_id=1, source_target_pairs={{0,8},{8,0},{16,24},{24,16},{1,9},{9,1},{17,25},{25,17},{2,10},{10... | collective-permute-start | bytes 786440 | tf_op jit(solution)/shard_map/ppermute | solution.py:22
  25.0 2.7 %collective-permute-start.6 = (f32[2,512,256]{2,1,0:T(8,128)S(1)}, f32[2,512,256]{2,1,0:T(8,128)S(1)}, u32[]{:S(2)}, u32[]{:S(2)}) collective-permute-start(f32[2,512,256]{2,1,0:T(8,128)S(1)} %shard_map.64), channel_id=1, source_target_pairs={{0,1},{1,0},{2,3},{3,2},{4,5},{5,4},{6,7},{7,6},{8,9},{9,8},{10,11... | collective-permute-start | bytes 3145736 | tf_op jit(solution)/shard_map/ppermute | solution.py:22
  25.7 4.6 %collective-permute-start.3 = (f32[2,512,256]{2,1,0:T(8,128)S(1)}, f32[2,512,256]{2,1,0:T(8,128)S(1)}, u32[]{:S(2)}, u32[]{:S(2)}) collective-permute-start(f32[2,512,256]{2,1,0:T(8,128)S(1)} %shard_map.62), channel_id=1, source_target_pairs={{0,1},{1,0},{2,3},{3,2},{4,5},{5,4},{6,7},{7,6},{8,9},{9,8},{10,11... | collective-permute-start | bytes 3145736 | tf_op jit(solution)/shard_map/ppermute | solution.py:22
  28.0 10.2 %collective-permute-start.7 = (s16[520,256]{1,0:T(8,128)(2,1)S(1)}, s16[520,256]{1,0:T(8,128)(2,1)S(1)}, u32[]{:S(2)}, u32[]{:S(2)}) collective-permute-start(s16[520,256]{1,0:T(8,128)(2,1)S(1)} %get-tuple-element.15), channel_id=1, source_target_pairs={{0,6},{1,7},{2,4},{3,5},{4,2},{5,3},{6,0},{7,1},{8,14},{9,15},{10,... | collective-permute-start | bytes 798728 | tf_op jit(solution)/shard_map/ppermute | solution.py:22
  30.6 12.4 %collective-permute-start.4 = (s16[520,256]{1,0:T(8,128)(2,1)S(1)}, s16[520,256]{1,0:T(8,128)(2,1)S(1)}, u32[]{:S(2)}, u32[]{:S(2)}) collective-permute-start(s16[520,256]{1,0:T(8,128)(2,1)S(1)} %get-tuple-element.13), channel_id=1, source_target_pairs={{0,2},{1,3},{2,0},{3,1},{4,6},{5,7},{6,4},{7,5},{8,10},{9,11},{10,... | collective-permute-start | bytes 798728 | tf_op jit(solution)/shard_map/ppermute | solution.py:22
  31.2 11.9 %collective-permute-start.5 = (s16[520,256]{1,0:T(8,128)(2,1)S(1)}, s16[520,256]{1,0:T(8,128)(2,1)S(1)}, u32[]{:S(2)}, u32[]{:S(2)}) collective-permute-start(s16[520,256]{1,0:T(8,128)(2,1)S(1)} %get-tuple-element.14), channel_id=1, source_target_pairs={{0,4},{1,5},{2,6},{3,7},{4,0},{5,1},{6,2},{7,3},{8,12},{9,13},{10,... | collective-permute-start | bytes 798728 | tf_op jit(solution)/shard_map/ppermute | solution.py:22
  43.8 1.3 %collective-permute-start.8 = (f32[136,128]{1,0:T(8,128)S(1)}, f32[136,128]{1,0:T(8,128)S(1)}, u32[]{:S(2)}, u32[]{:S(2)}) collective-permute-start(f32[136,128]{1,0:T(8,128)S(1)} %get-tuple-element.18), channel_id=1, source_target_pairs={{0,1},{1,0},{2,3},{3,2},{4,5},{5,4},{6,7},{7,6},{8,9},{9,8},{10,11... | collective-permute-start | bytes 208904 | tf_op jit(solution)/shard_map/ppermute | solution.py:22
  45.1 5.7 %collective-permute-start.10 = (f32[136,128]{1,0:T(8,128)S(1)}, f32[136,128]{1,0:T(8,128)S(1)}, u32[]{:S(2)}, u32[]{:S(2)}) collective-permute-start(f32[136,128]{1,0:T(8,128)S(1)} %add.80), channel_id=1, source_target_pairs={{0,6},{1,7},{2,4},{3,5},{4,2},{5,3},{6,0},{7,1},{8,14},{9,15},{10,... | collective-permute-start | bytes 208904 | tf_op jit(solution)/shard_map/ppermute | solution.py:22
  47.4 4.3 %collective-permute-start.11 = (f32[136,128]{1,0:T(8,128)S(1)}, f32[136,128]{1,0:T(8,128)S(1)}, u32[]{:S(2)}, u32[]{:S(2)}) collective-permute-start(f32[136,128]{1,0:T(8,128)S(1)} %add.80), channel_id=1, source_target_pairs={{0,2},{1,3},{2,0},{3,1},{4,6},{5,7},{6,4},{7,5},{8,10},{9,11},{10,... | collective-permute-start | bytes 208904 | tf_op jit(solution)/shard_map/ppermute | solution.py:22
  47.9 4.3 %collective-permute-start.9 = (f32[136,128]{1,0:T(8,128)S(1)}, f32[136,128]{1,0:T(8,128)S(1)}, u32[]{:S(2)}, u32[]{:S(2)}) collective-permute-start(f32[136,128]{1,0:T(8,128)S(1)} %add.80), channel_id=1, source_target_pairs={{0,4},{1,5},{2,6},{3,7},{4,0},{5,1},{6,2},{7,3},{8,12},{9,13},{10,... | collective-permute-start | bytes 208904 | tf_op jit(solution)/shard_map/ppermute | solution.py:22
  52.3 7.2 %collective-permute-start.12 = (f32[136,128]{1,0:T(8,128)S(1)}, f32[136,128]{1,0:T(8,128)S(1)}, u32[]{:S(2)}, u32[]{:S(2)}) collective-permute-start(f32[136,128]{1,0:T(8,128)S(1)} %add_add_fusion.1), channel_id=1, source_target_pairs={{0,24},{8,16},{16,8},{24,0},{1,25},{9,17},{17,9},{25,1},{2,26},{10... | collective-permute-start | bytes 208904 | tf_op jit(solution)/shard_map/ppermute | solution.py:22
  56.8 5.3 %collective-permute-start.13 = (f32[136,128]{1,0:T(8,128)S(1)}, f32[136,128]{1,0:T(8,128)S(1)}, u32[]{:S(2)}, u32[]{:S(2)}) collective-permute-start(f32[136,128]{1,0:T(8,128)S(1)} %add_add_fusion.1), channel_id=1, source_target_pairs={{0,16},{8,24},{16,0},{24,8},{1,17},{9,25},{17,1},{25,9},{2,18},{10... | collective-permute-start | bytes 208904 | tf_op jit(solution)/shard_map/ppermute | solution.py:22
  56.8 5.3 %collective-permute-start.14 = (f32[136,128]{1,0:T(8,128)S(1)}, f32[136,128]{1,0:T(8,128)S(1)}, u32[]{:S(2)}, u32[]{:S(2)}) collective-permute-start(f32[136,128]{1,0:T(8,128)S(1)} %add_add_fusion.1), channel_id=1, source_target_pairs={{0,8},{8,0},{16,24},{24,16},{1,9},{9,1},{17,25},{25,17},{2,10},{10... | collective-permute-start | bytes 208904 | tf_op jit(solution)/shard_map/ppermute | solution.py:22
  62.1 1.3 %collective-permute-start.15 = (f32[136,128]{1,0:T(8,128)S(1)}, f32[136,128]{1,0:T(8,128)S(1)}, u32[]{:S(2)}, u32[]{:S(2)}) collective-permute-start(f32[136,128]{1,0:T(8,128)S(1)} %add_add_fusion.mine_ref), channel_id=1, source_target_pairs={{0,1},{1,0},{2,3},{3,2},{4,5},{5,4},{6,7},{7,6},{8,9},{9,8},{10,11... | collective-permute-start | bytes 208904 | tf_op jit(solution)/shard_map/ppermute | solution.py:22
